TPU v7x, 128 devices: a whole 4x4x4 slice. The times are simulated.
128 devices in a mesh: front: 32 (over y, x, core), enc: 4 (over z).
Axes of the slice: x: 4, y: 4, z: 4, core: 2. Of those that a mesh axis runs over, the one named last changes fastest.
Arguments:
- spectra: bfloat16 [4096, 56, 80], P('front'), may hold values from -6 to 6
- sub_weight: bfloat16 [640, 1024], P(None, 'enc'), may hold values from -0.25 to 0.25
- sub_bias: bfloat16 [1024], P('enc'), may hold values from -4 to 4
- key_cache: bfloat16 [4096, 70, 1024], P('front', None, 'enc'), may hold values from -1000 to 1000
- value_cache: bfloat16 [4096, 70, 1024], P('front', None, 'enc'), may hold values from -6 to 6
- conv_cache: bfloat16 [4096, 8, 1024], P('front', None, 'enc'), may hold values from -6 to 6
- new_slot: int32 [4096], P('front'), may hold values from 0 to 4095, as said below
- old_slot: int32 [4096], P('front'), may hold values from 0 to 4095, as said below
- valid_new: int32 [4096], P('front'), may hold values from 1 to 7
- cache_fill: int32 [4096], P('front'), may hold values from 0 to 70
- ln1_gain: float32 [1024], replicated, may hold values from 0.5 to 1.5
- w_query: bfloat16 [1024, 1024], P(None, 'enc'), may hold values from -0.1875 to 0.1875
- w_key: bfloat16 [1024, 1024], P(None, 'enc'), may hold values from -0.1875 to 0.1875
- w_value: bfloat16 [1024, 1024], P(None, 'enc'), may hold values from -0.1875 to 0.1875
- w_attn_out: bfloat16 [1024, 1024], P('enc'), may hold values from -0.1875 to 0.1875
- ln2_gain: float32 [1024], replicated, may hold values from 0.5 to 1.5
- w_glu_value: bfloat16 [1024, 1024], P(None, 'enc'), may hold values from -0.1875 to 0.1875
- w_glu_gate: bfloat16 [1024, 1024], P(None, 'enc'), may hold values from -0.1875 to 0.1875
- depth_kernel: float32 [9, 1024], P(None, 'enc'), may hold values from -2 to 2
- norm_scale: float32 [1024], P('enc'), may hold values from 0.1 to 1.9
- norm_shift: float32 [1024], P('enc'), may hold values from -3 to 3
- w_conv_out: bfloat16 [1024, 1024], P('enc'), may hold values from -0.1875 to 0.1875
Outputs:
- encoded: bfloat16 [4096, 7, 1024], P('front', None, 'enc')
- key_out: bfloat16 [4096, 70, 1024], P('front', None, 'enc')
- value_out: bfloat16 [4096, 70, 1024], P('front', None, 'enc')
- conv_out: bfloat16 [4096, 8, 1024], P('front', None, 'enc')
Inputs may be any that keep to these rules, and one draw needn't show every extreme that they name: `new_slot`: A permutation of the stream slots. Device f of front holds old slots and new slots f * 128 to (f + 1) * 128 - 1; a stream that stays on its device keeps its slot; each device hands at most 2 streams to any other device, to at most 16 other devices, and receives as many streams as it hands away. `old_slot`: the inverse permutation of new_slot.
All inputs are finite; a program needn't handle non-finite values.
Results may differ from a plain program's by a relative error of at most 0.0095.
Values may be sent and summed in bfloat16 or wider, within the bound.
No kernel may reach another device: no remote copies, remote signals or barrier semaphores. Data moves between devices by JAX's collectives and lax.ppermute only.
A program may use at most 128 MiB of HBM per device.

v0:
```python
import math

import jax
import jax.numpy as jnp
from jax import lax
from jax.sharding import PartitionSpec as P

MELS = 80
KERNEL = 9
SUB = 8
FRAMES = 7
CACHE = 70
CAP = 2
HEAD = 128
CONV_CACHE = 8


masked_score = -1e30


def layer_norm(values_in, scale_gain):
    average = jnp.mean(values_in, axis=-1, keepdims=True)
    centered = values_in - average
    spread = jnp.mean(centered * centered, axis=-1, keepdims=True)
    return centered * lax.rsqrt(spread + 1e-05) * scale_gain


def send_order(new_slot, own_index, peer_count, stream_count):
    target = new_slot // stream_count
    leaving = target != own_index
    onehot = (
        (target[:, None] == jnp.arange(peer_count, dtype=jnp.int32)[None, :]) & leaving[:, None]
    ).astype(jnp.int32)
    before = jnp.cumsum(onehot, axis=0) - onehot
    position = jnp.sum(before * onehot, axis=1)
    bucket = jnp.where(leaving, target * CAP + position, peer_count * CAP)
    chosen = (bucket[None, :] == jnp.arange(peer_count * CAP, dtype=jnp.int32)[:, None]).astype(
        jnp.int32
    )
    return jnp.sum(chosen * jnp.arange(stream_count, dtype=jnp.int32)[None, :], axis=1)


def arrival_rows(old_slot, own_index):
    stream_count = old_slot.shape[0]
    source = old_slot // stream_count
    staying = source == own_index
    earlier = (source[None, :] == source[:, None]) & (old_slot[None, :] < old_slot[:, None])
    position = jnp.sum(earlier.astype(jnp.int32), axis=1)
    arrival = jnp.where(staying, 0, source * CAP + position)
    return (arrival, staying)


def pick_rows(arrival, staying, resident, received):
    fetched = jnp.take(received, arrival, axis=0)
    keep = staying.reshape((-1,) + (1,) * (resident.ndim - 1))
    return jnp.where(keep, resident, fetched)


def trim_rows(block_all, offsets, length):
    return jax.vmap(
        lambda block_rows, offset_rows: lax.dynamic_slice_in_dim(block_rows, offset_rows, length, 0)
    )(block_all, offsets)


def on_device(
    spectra,
    sub_weight,
    sub_bias,
    key_cache,
    value_cache,
    conv_cache,
    new_slot,
    old_slot,
    valid_new,
    cache_fill,
    ln1_gain,
    w_query,
    w_key,
    w_value,
    w_attn_out,
    ln2_gain,
    w_glu_value,
    w_glu_gate,
    depth_kernel,
    norm_scale,
    norm_shift,
    w_conv_out,
):
    peer_count = lax.axis_size("front")
    own_index = lax.axis_index("front")
    member = lax.axis_index("enc")
    stream_count = spectra.shape[0]
    local_width = w_query.shape[1]
    heads_here = local_width // HEAD
    outgoing = send_order(new_slot, own_index, peer_count, stream_count)
    arrival, staying = arrival_rows(old_slot, own_index)
    stacked = spectra.reshape(stream_count * FRAMES, SUB * MELS)
    sliced = (
        jnp.dot(stacked, sub_weight, preferred_element_type=jnp.float32)
        + sub_bias.astype(jnp.float32)
    ).astype(jnp.bfloat16)
    sliced = sliced.reshape(stream_count, FRAMES, local_width)
    moved_frames, moved_keys, moved_values, moved_conv = (
        lax.all_to_all(
            jnp.take(sliced, outgoing, axis=0), "front", split_axis=0, concat_axis=0, tiled=True
        ),
        lax.all_to_all(
            jnp.take(key_cache, outgoing, axis=0), "front", split_axis=0, concat_axis=0, tiled=True
        ),
        lax.all_to_all(
            jnp.take(value_cache, outgoing, axis=0),
            "front",
            split_axis=0,
            concat_axis=0,
            tiled=True,
        ),
        lax.all_to_all(
            jnp.take(conv_cache, outgoing, axis=0), "front", split_axis=0, concat_axis=0, tiled=True
        ),
    )
    frames_new = pick_rows(arrival, staying, sliced, moved_frames)
    inputs = lax.all_gather(frames_new, "enc", axis=2, tiled=True)
    keys_old = pick_rows(arrival, staying, key_cache, moved_keys)
    values_old = pick_rows(arrival, staying, value_cache, moved_values)
    conv_old = pick_rows(arrival, staying, conv_cache, moved_conv)
    model_width = inputs.shape[2]
    flat_in = inputs.reshape(stream_count * FRAMES, model_width)
    normed = layer_norm(flat_in.astype(jnp.float32), ln1_gain).astype(jnp.bfloat16)
    queries = (
        jnp.dot(normed, w_query, preferred_element_type=jnp.float32)
        .astype(jnp.bfloat16)
        .reshape(stream_count, FRAMES, heads_here, HEAD)
    )
    key_flat = (
        jnp.dot(normed, w_key, preferred_element_type=jnp.float32)
        .astype(jnp.bfloat16)
        .reshape(stream_count, FRAMES, local_width)
    )
    value_flat = (
        jnp.dot(normed, w_value, preferred_element_type=jnp.float32)
        .astype(jnp.bfloat16)
        .reshape(stream_count, FRAMES, local_width)
    )
    keys_joined = jnp.concatenate([keys_old, key_flat], axis=1)
    values_joined = jnp.concatenate([values_old, value_flat], axis=1)
    keys_heads = keys_joined.reshape(stream_count, CACHE + FRAMES, heads_here, HEAD)
    values_heads = values_joined.reshape(stream_count, CACHE + FRAMES, heads_here, HEAD)
    scores = jnp.einsum(
        "sthd,sjhd->shtj", queries, keys_heads, preferred_element_type=jnp.float32
    ) / math.sqrt(HEAD)
    position = jnp.arange(CACHE + FRAMES, dtype=jnp.int32)[None, :]
    cache_ok = (position < CACHE) & (position >= CACHE - cache_fill[:, None])
    new_ok = (position >= CACHE) & (position - CACHE < valid_new[:, None])
    allowed = (cache_ok | new_ok)[:, None, None, :]
    scores = jnp.where(allowed, scores, masked_score)
    row_peak = jnp.max(scores, axis=-1, keepdims=True)
    exponent = jnp.where(allowed, jnp.exp(scores - row_peak), 0.0)
    weights = (exponent / jnp.sum(exponent, axis=-1, keepdims=True)).astype(jnp.bfloat16)
    context = jnp.einsum(
        "shtj,sjhd->sthd", weights, values_heads, preferred_element_type=jnp.float32
    ).astype(jnp.bfloat16)
    context = context.reshape(stream_count * FRAMES, local_width)
    partial_out = jnp.dot(context, w_attn_out, preferred_element_type=jnp.float32)
    attended = lax.psum_scatter(
        partial_out.astype(jnp.bfloat16), "enc", scatter_dimension=1, tiled=True
    ).astype(jnp.float32)
    own_inputs = lax.dynamic_slice_in_dim(flat_in, member * local_width, local_width, 1)
    middle_slice = (own_inputs.astype(jnp.float32) + attended).astype(jnp.bfloat16)
    middle = lax.all_gather(middle_slice, "enc", axis=1, tiled=True)
    normed_second = layer_norm(middle.astype(jnp.float32), ln2_gain).astype(jnp.bfloat16)
    glu_value = jnp.dot(normed_second, w_glu_value, preferred_element_type=jnp.float32)
    glu_gate = jnp.dot(normed_second, w_glu_gate, preferred_element_type=jnp.float32)
    gated = (
        (glu_value * jax.nn.sigmoid(glu_gate))
        .astype(jnp.bfloat16)
        .reshape(stream_count, FRAMES, local_width)
    )
    conv_in = jnp.concatenate([conv_old, gated], axis=1)
    depthwise = jnp.zeros((stream_count, FRAMES, local_width), jnp.float32)
    for kernel_tap in range(KERNEL):
        depthwise = depthwise + depth_kernel[kernel_tap] * conv_in[
            :, kernel_tap : kernel_tap + FRAMES
        ].astype(jnp.float32)
    shaped = depthwise * norm_scale + norm_shift
    activated = (
        (shaped * jax.nn.sigmoid(shaped))
        .astype(jnp.bfloat16)
        .reshape(stream_count * FRAMES, local_width)
    )
    conv_term = lax.psum_scatter(
        jnp.dot(activated, w_conv_out, preferred_element_type=jnp.float32).astype(jnp.bfloat16),
        "enc",
        scatter_dimension=1,
        tiled=True,
    ).astype(jnp.float32)
    frame_ok = (jnp.arange(FRAMES, dtype=jnp.int32)[None, :] < valid_new[:, None]).astype(
        jnp.float32
    )
    encoded = (
        (middle_slice.astype(jnp.float32) + conv_term).reshape(stream_count, FRAMES, local_width)
        * frame_ok[:, :, None]
    ).astype(jnp.bfloat16)
    key_out = trim_rows(keys_joined, valid_new, CACHE)
    value_out = trim_rows(values_joined, valid_new, CACHE)
    conv_out = trim_rows(conv_in, valid_new, CONV_CACHE)
    return (encoded, key_out, value_out, conv_out)


def solution(mesh):
    in_specs = (
        P("front", None, None),
        P(None, "enc"),
        P("enc"),
        P("front", None, "enc"),
        P("front", None, "enc"),
        P("front", None, "enc"),
        P("front"),
        P("front"),
        P("front"),
        P("front"),
        P(),
        P(None, "enc"),
        P(None, "enc"),
        P(None, "enc"),
        P("enc", None),
        P(),
        P(None, "enc"),
        P(None, "enc"),
        P(None, "enc"),
        P("enc"),
        P("enc"),
        P("enc", None),
    )
    out_specs = (
        P("front", None, "enc"),
        P("front", None, "enc"),
        P("front", None, "enc"),
        P("front", None, "enc"),
    )
    return jax.shard_map(
        on_device, mesh=mesh, in_specs=in_specs, out_specs=out_specs, check_vma=False
    )
```

profile of v0, /device:TPU:0, one launch (start us, length us, event | category | flops | bytes accessed | tf_op | source)
XLA Modules:
  0.0 337.4 jit_solution(11155208592910180405)
XLA Ops:
  8.5 2.9 copy.72
  11.4 1.4 reshape.252
  12.9 1.5 fusion.29
  16.0 8.0 %all-to-all-start = ((bf16[64,7,256]{2,1,0:T(8,128)(2,1)}), bf16[64,7,256]{2,1,0:T(8,128)(2,1)}, u32[]{:S(2)}, u32[]{:S(2)}) async-start(bf16[64,7,256]{2,1,0:T(8,128)(2,1)} %broadcast_select_fusion.3), calls=%async_computation | async-start | bytes 524288 | tf_op jit(solution)/shard_map/all_to_all | solution.py:104
  24.1 9.0 %gather_fusion.9 = bf16[64,70,256]{2,0,1:T(8,128)(2,1)S(1)} fusion(bf16[128,70,256]{2,0,1:T(8,128)(2,1)} %param.29, s32[1024]{0:T(1024)S(1)} %pad_clamp_fusion), kind=kCustom, calls=%fused_computation.2.clone | custom fusion | bytes 4587776 | tf_op jit(solution)/shard_map/jit(_take)/gather | solution.py:108
  33.1 11.6 %gather_fusion.7 = bf16[64,70,256]{2,0,1:T(8,128)(2,1)} fusion(bf16[128,70,256]{2,0,1:T(8,128)(2,1)} %param.30, s32[1024]{0:T(1024)S(1)} %pad_clamp_fusion), kind=kCustom, calls=%fused_computation.clone | custom fusion | bytes 4587776 | tf_op jit(solution)/shard_map/jit(_take)/gather | solution.py:111
  44.7 3.5 %broadcast_select_fusion = (bf16[64,70,256]{2,0,1:T(8,128)(2,1)S(1)}, bf16[64,70,256]{2,0,1:T(8,128)(2,1)}) fusion(bf16[64,70,256]{2,0,1:T(8,128)(2,1)S(1)} %gather_fusion.9, pred[64]{0:T(512)(128)(4,1)S(1)} %compare_and_fusion, bf16[64,70,256]{2,0,1:T(8,128)(2,1)} %gather_fusion.7), kind=kLoop, calls=%fused_computation.36 | loop fusion | flops 2293760 | bytes 9175104 | tf_op jit(solution)/shard_map/jit(_take)/select_n | solution.py:108
  48.2 2.7 copy.78
  51.0 7.7 %all-to-all-start.2 = ((bf16[64,70,256]{2,1,0:T(8,128)(2,1)}), bf16[64,70,256]{2,1,0:T(8,128)(2,1)S(1)}, u32[]{:S(2)}, u32[]{:S(2)}) async-start(bf16[64,70,256]{2,1,0:T(8,128)(2,1)} %copy.78), calls=%async_computation.2 | async-start | bytes 4718592 | tf_op jit(solution)/shard_map/all_to_all | solution.py:107
  58.7 4.3 %copy.73 = bf16[64,70,256]{2,1,0:T(8,128)(2,1)} copy(bf16[64,70,256]{2,0,1:T(8,128)(2,1)} %get-tuple-element.42) | data formatting | bytes 4587520 | tf_op jit(solution)/shard_map/jit(_take)/select_n | solution.py:111
  63.0 28.8 %all-to-all-done.2 = bf16[64,70,256]{2,1,0:T(8,128)(2,1)S(1)} async-done(((bf16[64,70,256]{2,1,0:T(8,128)(2,1)}), bf16[64,70,256]{2,1,0:T(8,128)(2,1)S(1)}, u32[]{:S(2)}, u32[]{:S(2)}) %all-to-all-start.2) | async-done | bytes 2293792 | tf_op jit(solution)/shard_map/all_to_all | solution.py:107
  91.8 5.0 %all-to-all-start.1 = ((bf16[64,70,256]{2,1,0:T(8,128)(2,1)}), bf16[64,70,256]{2,1,0:T(8,128)(2,1)}, u32[]{:S(2)}, u32[]{:S(2)}) async-start(bf16[64,70,256]{2,1,0:T(8,128)(2,1)} %copy.73), calls=%async_computation.1 | async-start | bytes 4718592 | tf_op jit(solution)/shard_map/all_to_all | solution.py:110
  97.1 2.4 gather_fusion.1
  99.5 2.2 select_select_fusion.1
  101.9 3.1 gather_fusion.10
  105.0 25.0 %all-to-all-done.1 = bf16[64,70,256]{2,1,0:T(8,128)(2,1)} async-done(((bf16[64,70,256]{2,1,0:T(8,128)(2,1)}), bf16[64,70,256]{2,1,0:T(8,128)(2,1)}, u32[]{:S(2)}, u32[]{:S(2)}) %all-to-all-start.1) | async-done | bytes 2293792 | tf_op jit(solution)/shard_map/all_to_all | solution.py:110
  130.0 4.6 %gather_fusion.8 = bf16[128,70,256]{2,1,0:T(8,128)(2,1)} fusion(bf16[64,70,256]{2,1,0:T(8,128)(2,1)} %all-to-all-done.1, s32[1024]{0:T(1024)S(1)} %pad_clamp_fusion.1), kind=kCustom, calls=%fused_computation.1.clone | custom fusion | bytes 9175552 | tf_op jit(solution)/shard_map/jit(_take)/gather | solution.py:54
  134.6 20.3 %copy_select_fusion = (bf16[128,70,256]{2,1,0:T(8,128)(2,1)}, bf16[128,70,256]{2,1,0:T(8,128)(2,1)}) fusion(bf16[128,70,256]{2,0,1:T(8,128)(2,1)} %param.29, bf16[128,70,256]{2,1,0:T(8,128)(2,1)} %gather_fusion.10, pred[128]{0:T(512)(128)(4,1)S(1)} %get-tuple-element.24, pred[128]{0:T(512)(128)(4,1)S(1)} %get-tuple-element.22, ...), kind=kLoop, calls=%fused_computation.24 | loop fusion | flops 9175040 | bytes 27525376 | tf_op jit(solution)/shard_map/jit(_where)/select_n | solution.py:56
  154.9 7.1 %copy.75 = bf16[128,70,256]{0,2,1:T(8,128)(2,1)} copy(bf16[128,70,256]{2,1,0:T(8,128)(2,1)} %get-tuple-element.38) | data formatting | bytes 9175040 | tf_op jit(solution)/shard_map/jit(_where)/select_n | solution.py:56
  162.0 7.0 %copy.76 = bf16[128,70,2,128]{3,1,2,0:T(8,128)(2,1)} copy(bf16[128,70,2,128]{0,3,2,1:T(8,128)(2,1)} %bitcast.53) | data formatting | bytes 9175040 | tf_op jit(solution)/shard_map/concatenate | solution.py:145
  168.9 7.1 %copy.80 = bf16[128,70,256]{0,2,1:T(8,128)(2,1)} copy(bf16[128,70,256]{2,1,0:T(8,128)(2,1)} %get-tuple-element.37) | data formatting | bytes 9175040 | tf_op jit(solution)/shard_map/jit(_where)/select_n | solution.py:56
  176.0 6.9 %copy.81 = bf16[128,70,2,128]{3,1,2,0:T(8,128)(2,1)} copy(bf16[128,70,2,128]{0,3,2,1:T(8,128)(2,1)} %bitcast.54) | data formatting | bytes 9175040 | tf_op jit(solution)/shard_map/concatenate | solution.py:144
  182.9 2.2 convert_reduce_fusion
  186.4 1.9 reshape.254
  188.4 2.2 multiply_convert_fusion
  190.6 1.2 copy-done.5
  192.7 2.1 convolution_convert_fusion.2
  195.1 2.2 convolution_convert_fusion.3
  197.4 6.3 %fusion.65 = (f32[128,2,7]{2,1,0:T(2,128)S(1)}, f32[128,2,7,77]{3,2,1,0:T(8,128)}) fusion(pred[128,77]{1,0:T(8,128)(4,1)S(1)} %fusion.49, bf16[128,7,2,128]{3,1,2,0:T(8,128)(2,1)S(1)} %copy.82, bf16[128,70,2,128]{3,1,2,0:T(8,128)(2,1)} %copy.81, bf16[128,7,2,128]{3,2,1,0:T(2,128)(2,1)S(1)} %reshape.255), kind=kOutput, calls=%fused_computation.146 | convolution fusion | flops 46106444 | bytes 6073984 | tf_op jit(solution)/shard_map/sub | solution.py:157
  203.7 4.2 %fusion.33 = bf16[128,7,2,128]{3,1,2,0:T(8,128)(2,1)S(1)} fusion(bf16[128,7,2,128]{3,1,2,0:T(8,128)(2,1)S(1)} %copy.77, bf16[128,70,2,128]{3,1,2,0:T(8,128)(2,1)} %copy.76, f32[128,2,7,77]{3,2,1,0:T(8,128)} %get-tuple-element.44, f32[128,2,7]{2,1,0:T(2,128)S(1)} %get-tuple-element.43), kind=kOutput, calls=%fused_computation.70 | convolution fusion | flops 45921792 | bytes 6064128 | tf_op jit(solution)/shard_map/shtj,sjhd->sthd/dot_general | solution.py:159
  208.3 1.9 convolution_convert_fusion.1
  210.3 25.8 %reduce-scatter.3.cloned.1.call-done = bf16[896,256]{1,0:T(8,128)(2,1)} async-done(((bf16[896,1024]{1,0:T(8,128)(2,1)}), bf16[896,256]{1,0:T(8,128)(2,1)}) %reduce-scatter.3.cloned.1.call-update) | async-done | bytes 458768 | tf_op jit(solution)/shard_map/reduce_scatter | solution.py:164
  236.1 2.0 add_convert_fusion
  239.7 7.1 %all-to-all-start.3 = ((bf16[64,8,256]{2,1,0:T(8,128)(2,1)}), bf16[64,8,256]{2,1,0:T(8,128)(2,1)S(1)}, u32[]{:S(2)}, u32[]{:S(2)}) async-start(bf16[64,8,256]{2,1,0:T(8,128)(2,1)} %broadcast_select_fusion.2), calls=%async_computation.4 | async-start | bytes 524288 | tf_op jit(solution)/shard_map/all_to_all | solution.py:117
  246.9 8.7 %all-to-all-done.3 = bf16[64,8,256]{2,1,0:T(8,128)(2,1)S(1)} async-done(((bf16[64,8,256]{2,1,0:T(8,128)(2,1)}), bf16[64,8,256]{2,1,0:T(8,128)(2,1)S(1)}, u32[]{:S(2)}, u32[]{:S(2)}) %all-to-all-start.3) | async-done | bytes 262176 | tf_op jit(solution)/shard_map/all_to_all | solution.py:117
  256.6 13.3 %all-gather.5.cloned.1.call-done = bf16[896,1024]{1,0:T(8,128)(2,1)} async-done(((bf16[896,256]{1,0:T(8,128)(2,1)}), bf16[896,1024]{1,0:T(8,128)(2,1)}) %all-gather.5.cloned.1.call-update) | async-done | bytes 1835024 | tf_op jit(solution)/shard_map/all_gather | solution.py:169
  269.9 2.0 convert_reduce_fusion.1
  271.9 2.1 fusion.13
  276.6 2.1 multiply_convert_fusion.2
  278.9 1.9 convolution_convert_fusion
  281.9 6.0 %pad_maximum_fusion = (bf16[128,77,256]{2,1,0:T(8,128)(2,1)S(1)}, bf16[128,77,256]{2,1,0:T(8,128)(2,1)S(1)}) fusion(bf16[128,7,256]{2,1,0:T(8,128)(2,1)S(1)} %reshape.260, bf16[128,70,256]{2,1,0:T(8,128)(2,1)} %get-tuple-element.37, bf16[128,7,256]{2,1,0:T(8,128)(2,1)S(1)} %reshape.261, bf16[128,70,256]{2,1,0:T(8,128)(2,1)} %get-tuple-element.38), kind=kLoop, calls=%fused_computation.22 | loop fusion | flops 20185088 | bytes 20185088 | tf_op jit(solution)/shard_map/concatenate | solution.py:144
  287.9 4.1 %copy.85 = bf16[128,77,256]{2,0,1:T(8,128)(2,1)} copy(bf16[128,77,256]{2,1,0:T(8,128)(2,1)S(1)} %get-tuple-element.45) | data formatting | bytes 10092544 | tf_op jit(solution)/shard_map/concatenate | solution.py:144
  291.9 4.1 %copy.86 = bf16[128,77,256]{2,0,1:T(8,128)(2,1)} copy(bf16[128,77,256]{2,1,0:T(8,128)(2,1)S(1)} %get-tuple-element.46) | data formatting | bytes 10092544 | tf_op jit(solution)/shard_map/concatenate | solution.py:145
  296.1 14.2 %gather_fusion.4 = bf16[128,70,256]{2,0,1:T(8,128)(2,1)} fusion(bf16[128,77,256]{2,0,1:T(8,128)(2,1)} %copy.85, s32[128]{0:T(128)S(1)} %get-tuple-element.40), kind=kCustom, calls=%fused_computation.8 | custom fusion | bytes 9176576 | tf_op jit(solution)/shard_map/vmap()/gather | solution.py:61
  310.2 13.9 %gather_fusion.5 = bf16[128,70,256]{2,0,1:T(8,128)(2,1)} fusion(bf16[128,77,256]{2,0,1:T(8,128)(2,1)} %copy.86, s32[128]{0:T(128)S(1)} %get-tuple-element.40), kind=kCustom, calls=%fused_computation.9 | custom fusion | bytes 9176576 | tf_op jit(solution)/shard_map/vmap()/gather | solution.py:61
  324.6 2.5 gather_fusion.6
  327.2 1.1 copy.89
  328.3 1.1 convert_add_fusion
  (118 shorter events, 14.3 us)
Async XLA Ops:
  7.2 201.2 %copy-start = (bf16[256,1024]{1,0:T(8,128)(2,1)S(1)}, bf16[256,1024]{1,0:T(8,128)(2,1)}, u32[]{:S(2)}) copy-start(bf16[256,1024]{1,0:T(8,128)(2,1)} %param.40) | copy-start | bytes 1572868
  7.2 5.7 %copy-start.24 = (bf16[256]{0:T(256)(128)(2,1)S(1)}, bf16[256]{0:T(256)(128)(2,1)}, u32[]{:S(2)}) copy-start(bf16[256]{0:T(256)(128)(2,1)} %param.28) | copy-start | bytes 1540
  8.5 36.2 %copy-start.12 = (pred[64]{0:T(512)(128)(4,1)}, pred[64]{0:T(512)(128)(4,1)S(1)}, u32[]{:S(2)}) copy-start(pred[64]{0:T(512)(128)(4,1)S(1)} %compare_and_fusion) | copy-start | bytes 196
  14.5 9.5 %copy-start.10 = (s32[1024]{0:T(1024)}, s32[1024]{0:T(1024)S(1)}, u32[]{:S(2)}) copy-start(s32[1024]{0:T(1024)S(1)} %pad_clamp_fusion.2) | copy-start | bytes 12292
  16.0 34.9 %all-to-all-start = ((bf16[64,7,256]{2,1,0:T(8,128)(2,1)}), bf16[64,7,256]{2,1,0:T(8,128)(2,1)}, u32[]{:S(2)}, u32[]{:S(2)}) async-start(bf16[64,7,256]{2,1,0:T(8,128)(2,1)} %broadcast_select_fusion.3), calls=%async_computation | async-start | bytes 524288 | tf_op jit(solution)/shard_map/all_to_all | solution.py:104
  51.0 40.9 %all-to-all-start.2 = ((bf16[64,70,256]{2,1,0:T(8,128)(2,1)}), bf16[64,70,256]{2,1,0:T(8,128)(2,1)S(1)}, u32[]{:S(2)}, u32[]{:S(2)}) async-start(bf16[64,70,256]{2,1,0:T(8,128)(2,1)} %copy.78), calls=%async_computation.2 | async-start | bytes 4718592 | tf_op jit(solution)/shard_map/all_to_all | solution.py:107
  58.6 38.2 %copy-start.14 = (s32[128]{0:T(128)S(1)}, s32[128]{0:T(128)}, u32[]{:S(2)}) copy-start(s32[128]{0:T(128)} %param.33) | copy-start | bytes 1540
  63.0 38.7 %copy-start.25 = (s32[128]{0:T(128)S(1)}, s32[128]{0:T(128)}, u32[]{:S(2)}) copy-start(s32[128]{0:T(128)} %param.35) | copy-start | bytes 1540
  63.0 38.8 %copy-start.17 = (s32[128]{0:T(128)S(1)}, s32[128]{0:T(128)}, u32[]{:S(2)}) copy-start(s32[128]{0:T(128)} %param.34) | copy-start | bytes 1540
  91.8 38.1 %all-to-all-start.1 = ((bf16[64,70,256]{2,1,0:T(8,128)(2,1)}), bf16[64,70,256]{2,1,0:T(8,128)(2,1)}, u32[]{:S(2)}, u32[]{:S(2)}) async-start(bf16[64,70,256]{2,1,0:T(8,128)(2,1)} %copy.73), calls=%async_computation.1 | async-start | bytes 4718592 | tf_op jit(solution)/shard_map/all_to_all | solution.py:110
  96.8 86.1 %all-gather.3.cloned.1.call-start = ((), (), s32[]{:S(2)}) async-start(), calls=%async_computation.6 | async-start | bytes 2621440 | tf_op jit(solution)/shard_map/all_gather | solution.py:122
  101.7 134.4 %reduce-scatter.3.cloned.1.call-start = ((), (), s32[]{:S(2)}) async-start(), calls=%async_computation.7 | async-start | bytes 2293760 | tf_op jit(solution)/shard_map/reduce_scatter | solution.py:164
  182.9 2.5 copy-start.2
  185.1 3.3 copy-start.15
  188.4 3.5 %copy-start.21 = (bf16[1024,256]{1,0:T(8,128)(2,1)S(1)}, bf16[1024,256]{1,0:T(8,128)(2,1)}, u32[]{:S(2)}) copy-start(bf16[1024,256]{1,0:T(8,128)(2,1)} %param.39) | copy-start | bytes 1572868
  188.4 4.3 %copy-start.22 = (bf16[1024,256]{1,0:T(8,128)(2,1)S(1)}, bf16[1024,256]{1,0:T(8,128)(2,1)}, u32[]{:S(2)}) copy-start(bf16[1024,256]{1,0:T(8,128)(2,1)} %param.38) | copy-start | bytes 1572868
  190.6 1.2 copy-start.5
  207.9 30.2 %copy-start.6 = (bf16[128,8,256]{2,1,0:T(8,128)(2,1)S(1)}, bf16[128,8,256]{2,1,0:T(8,128)(2,1)}, u32[]{:S(2)}) copy-start(bf16[128,8,256]{2,1,0:T(8,128)(2,1)} %param.31) | copy-start | bytes 1572868
  208.3 30.6 %copy-start.13 = (pred[64]{0:T(512)(128)(4,1)S(1)}, pred[64]{0:T(512)(128)(4,1)}, u32[]{:S(2)}) copy-start(pred[64]{0:T(512)(128)(4,1)} %copy-done.12) | copy-start | bytes 196
  208.3 38.6 %copy-start.11 = (f32[9,256]{1,0:T(8,128)S(1)}, f32[9,256]{1,0:T(8,128)}, u32[]{:S(2)}) copy-start(f32[9,256]{1,0:T(8,128)} %param.44) | copy-start | bytes 27652
  210.3 59.7 %all-gather.5.cloned.1.call-start = ((), (), s32[]{:S(2)}) async-start(), calls=%async_computation.8 | async-start | bytes 2293760 | tf_op jit(solution)/shard_map/all_gather | solution.py:169
  238.9 35.2 %copy-start.16 = (f32[1024]{0:T(1024)S(1)}, f32[1024]{0:T(1024)}, u32[]{:S(2)}) copy-start(f32[1024]{0:T(1024)} %param.41) | copy-start | bytes 12292
  239.7 15.9 %all-to-all-start.3 = ((bf16[64,8,256]{2,1,0:T(8,128)(2,1)}), bf16[64,8,256]{2,1,0:T(8,128)(2,1)S(1)}, u32[]{:S(2)}, u32[]{:S(2)}) async-start(bf16[64,8,256]{2,1,0:T(8,128)(2,1)} %broadcast_select_fusion.2), calls=%async_computation.4 | async-start | bytes 524288 | tf_op jit(solution)/shard_map/all_to_all | solution.py:117
  246.9 81.4 %reduce-scatter.5.cloned.1.call-start = ((), (), s32[]{:S(2)}) async-start(), calls=%async_computation.9 | async-start | bytes 2293760 | tf_op jit(solution)/shard_map/reduce_scatter | solution.py:190
  269.9 4.1 %copy-start.3 = (bf16[896,1024]{1,0:T(8,128)(2,1)S(1)}, bf16[896,1024]{1,0:T(8,128)(2,1)}, u32[]{:S(2)}) copy-start(bf16[896,1024]{1,0:T(8,128)(2,1)} %all-gather.5.cloned.1.call-done) | copy-start | bytes 5505028
  269.9 4.7 %copy-start.23 = (bf16[1024,256]{1,0:T(8,128)(2,1)S(1)}, bf16[1024,256]{1,0:T(8,128)(2,1)}, u32[]{:S(2)}) copy-start(bf16[1024,256]{1,0:T(8,128)(2,1)} %param.43) | copy-start | bytes 1572868
  274.7 1.0 copy-start.7
  275.7 0.8 copy-start.19
  275.7 0.9 copy-start.20
  276.4 2.5 copy-start.8
  276.6 4.2 %copy-start.18 = (s32[128]{0:T(128)S(1)}, s32[128]{0:T(128)}, u32[]{:S(2)}) copy-start(s32[128]{0:T(128)} %param.34) | copy-start | bytes 1540
  324.3 4.0 %copy-start.4 = (bf16[896,256]{1,0:T(8,128)(2,1)S(1)}, bf16[896,256]{1,0:T(8,128)(2,1)}, u32[]{:S(2)}) copy-start(bf16[896,256]{1,0:T(8,128)(2,1)} %add_convert_fusion) | copy-start | bytes 1376260
  324.6 4.9 %copy-start.9 = (f32[128,7]{1,0:T(8,128)S(1)}, f32[128,7]{1,0:T(8,128)}, u32[]{:S(2)}) copy-start(f32[128,7]{1,0:T(8,128)} %fusion.50) | copy-start | bytes 10756
  324.6 6.0 %copy-start.1 = (bf16[256,1024]{1,0:T(8,128)(2,1)S(1)}, bf16[256,1024]{1,0:T(8,128)(2,1)}, u32[]{:S(2)}) copy-start(bf16[256,1024]{1,0:T(8,128)(2,1)} %param.40) | copy-start | bytes 1572868
Sparse Core Ops, SparseCore 0:
  101.8 36.5 all-gather.2
  210.4 25.6 reduce-scatter.2
  238.3 31.5 all-gather.4
  280.9 28.5 reduce-scatter.4
where the time goes:
time: 342 us; the launch traced here: 337 us
  local copies, waits for them, and re-layouts  119 us (35%)
  waiting for transfers between devices  102 us (30%)
  other arithmetic  52 us (15%)
  starting transfers between devices  28 us (8%)
  matrix products  22.1 us (6%)
  between operations  14.8 us (4%)
    gather x3, local copies, waits for them, and re-layouts, trim_rows(): lax.dynamic_slice_in_dim(block_rows, offset_rows, length, 0)  30.6 us
    all_to_all x1, waiting for transfers between devices, on_device(): lax.all_to_all(jnp.take(key_cache, outgoing, axis=0), 'front', split_axis...  28.8 us
    reduce_scatter x1, waiting for transfers between devices, on_device(): lax.psum_scatter(partial_out.astype(jnp.bfloat16), 'enc', scatter_dimensi...  25.8 us
    all_to_all x1, waiting for transfers between devices, on_device(): lax.all_to_all(jnp.take(value_cache, outgoing, axis=0), 'front', split_ax...  25 us
    select_n x3, other arithmetic, pick_rows(): return jnp.where(keep, resident, fetched)  22.8 us
    select_n x2, local copies, waits for them, and re-layouts, pick_rows(): return jnp.where(keep, resident, fetched)  14.1 us
    all_gather x1, waiting for transfers between devices, on_device(): middle = lax.all_gather(middle_slice, 'enc', axis=1, tiled=True)  13.3 us
    gather x1, local copies, waits for them, and re-layouts, on_device(): jnp.take(value_cache, outgoing, axis=0)  11.6 us
  transfers between devices with their start and end apart: 8, of which 5 were waited for; matrix products, arithmetic and copies ran while one was open for 42% of the time, Pallas kernels for 0%

commit v1 on v0

v1 whole, which is shorter than its diff:
```python
import math

import jax
import jax.numpy as jnp
from jax import lax
from jax.experimental import pallas as pl
from jax.experimental.pallas import tpu as pltpu
from jax.sharding import PartitionSpec as P

MELS = 80
KERNEL = 9
SUB = 8
FRAMES = 7
CACHE = 70
CAP = 2
HEAD = 128
CONV_CACHE = 8
LANES = 128
BLOCK = 16
SPAN = 80
KEEP = 72
SLAB = 8
CHUNK = 10

masked_score = -1e30


def layer_norm(values_in, scale_gain):
    average = jnp.mean(values_in, axis=-1, keepdims=True)
    centered = values_in - average
    spread = jnp.mean(centered * centered, axis=-1, keepdims=True)
    return centered * lax.rsqrt(spread + 1e-05) * scale_gain


def send_slots(new_slot, own_index, peer_count):
    stream_count = new_slot.shape[0]
    target = new_slot // stream_count
    leaving = target != own_index
    order = jnp.arange(stream_count, dtype=jnp.int32)
    earlier = (target[None, :] == target[:, None]) & (order[None, :] < order[:, None])
    position = jnp.sum(earlier.astype(jnp.int32), axis=1)
    return jnp.where(leaving, target * CAP + position, peer_count * CAP)


def arrival_slots(old_slot, own_index):
    stream_count = old_slot.shape[0]
    source = old_slot // stream_count
    staying = source == own_index
    earlier = (source[None, :] == source[:, None]) & (old_slot[None, :] < old_slot[:, None])
    position = jnp.sum(earlier.astype(jnp.int32), axis=1)
    return jnp.where(staying, -1, source * CAP + position)


def shift_rows(rows, first, second, third):
    rows = jnp.where(first, rows[1:], rows[:-1])
    rows = jnp.where(second, rows[2:], rows[:-2])
    return jnp.where(third, rows[4:], rows[:-4])


def attend_body(
    valid_s,
    fill_s,
    slot_s,
    query_ref,
    key_new_ref,
    value_new_ref,
    key_ref,
    value_ref,
    valid_ref,
    context_ref,
    key_out_ref,
    value_out_ref,
    send_ref,
    key_f,
    value_f,
    query_f,
    context_f,
):
    base = pl.program_id(0) * BLOCK
    heads = key_f.shape[0]
    slots = send_ref.shape[0]
    shift = valid_ref[...] - 1
    first = ((shift & 1) != 0)[None]
    second = ((shift & 2) != 0)[None]
    third = ((shift & 4) != 0)[None]
    for h in range(heads):
        lanes = slice(h * LANES, (h + 1) * LANES)
        for old_ref, new_ref, dst in (
            (key_ref, key_new_ref, key_f),
            (value_ref, value_new_ref, value_f),
        ):
            for start in range(0, CACHE, CHUNK):
                dst[h, start * BLOCK : (start + CHUNK) * BLOCK, :] = (
                    old_ref[start : start + CHUNK, :, lanes]
                    .astype(jnp.float32)
                    .reshape(CHUNK * BLOCK, LANES)
                )
            dst[h, CACHE * BLOCK : (CACHE + FRAMES) * BLOCK, :] = (
                new_ref[:, :, lanes].astype(jnp.float32).reshape(FRAMES * BLOCK, LANES)
            )
            dst[h, (CACHE + FRAMES) * BLOCK :, :] = jnp.zeros(
                ((SPAN - CACHE - FRAMES) * BLOCK, LANES), jnp.float32
            )
        query_f[h, : FRAMES * BLOCK, :] = (
            query_ref[:, :, lanes].astype(jnp.float32).reshape(FRAMES * BLOCK, LANES)
        )
        query_f[h, FRAMES * BLOCK :, :] = jnp.zeros(((SLAB - FRAMES) * BLOCK, LANES), jnp.float32)
    place = lax.broadcasted_iota(jnp.int32, (SLAB, SPAN), 1)
    for s in range(BLOCK):
        fill = fill_s[base + s]
        valid = valid_s[base + s]
        allowed = (place >= CACHE - fill) & (place < CACHE + valid)
        for h in range(heads):
            keys = key_f[h, pl.ds(s, SPAN, stride=BLOCK), :].astype(jnp.bfloat16)
            query = query_f[h, pl.ds(s, SLAB, stride=BLOCK), :].astype(jnp.bfloat16)
            scores = lax.dot_general(
                query, keys, (((1,), (1,)), ((), ())), preferred_element_type=jnp.float32
            ) * (1.0 / math.sqrt(HEAD))
            scores = jnp.where(allowed, scores, masked_score)
            peak = jnp.max(scores, axis=1, keepdims=True)
            exponent = jnp.where(allowed, jnp.exp(scores - peak), 0.0)
            weights = (exponent / jnp.sum(exponent, axis=1, keepdims=True)).astype(jnp.bfloat16)
            values = value_f[h, pl.ds(s, SPAN, stride=BLOCK), :].astype(jnp.bfloat16)
            context_f[h, pl.ds(s, SLAB, stride=BLOCK), :] = lax.dot_general(
                weights, values, (((1,), (0,)), ((), ())), preferred_element_type=jnp.float32
            )
    for h in range(heads):
        lanes = slice(h * LANES, (h + 1) * LANES)
        context_ref[:, :, lanes] = (
            context_f[h, : FRAMES * BLOCK, :]
            .reshape(FRAMES, BLOCK, LANES)
            .astype(jnp.bfloat16)
        )
        for src, out_ref in ((key_f, key_out_ref), (value_f, value_out_ref)):
            for start in range(0, CACHE, CHUNK):
                rows = src[h, (start + 1) * BLOCK : (start + CHUNK + 8) * BLOCK, :]
                rows = rows.reshape(CHUNK + 7, BLOCK, LANES)
                out_ref[start : start + CHUNK, :, lanes] = shift_rows(
                    rows, first, second, third
                ).astype(jnp.bfloat16)

    def pack(s, carry):
        slot = slot_s[base + s]
        valid = valid_s[base + s]

        @pl.when(slot < slots)
        def _():
            for kind, src in enumerate((key_f, value_f)):
                for h in range(heads):
                    send_ref[slot, kind, :, h * LANES : (h + 1) * LANES] = src[
                        h, pl.ds(valid * BLOCK + s, KEEP, stride=BLOCK), :
                    ].astype(jnp.bfloat16)

        return carry

    lax.fori_loop(0, BLOCK, pack, 0)


def attend(valid_old, fill_old, bucket, queries, key_new, value_new, key_cache, value_cache, slots):
    stream_count = key_cache.shape[1]
    width = key_cache.shape[2]
    heads = width // HEAD
    wide_valid = jnp.broadcast_to(valid_old[:, None], (stream_count, LANES))

    def block(rows):
        return pl.BlockSpec((rows, BLOCK, width), lambda i, *_: (0, i, 0))

    return pl.pallas_call(
        attend_body,
        grid_spec=pltpu.PrefetchScalarGridSpec(
            num_scalar_prefetch=3,
            grid=(stream_count // BLOCK,),
            in_specs=[
                block(FRAMES),
                block(FRAMES),
                block(FRAMES),
                block(CACHE),
                block(CACHE),
                pl.BlockSpec((BLOCK, LANES), lambda i, *_: (i, 0)),
            ],
            out_specs=[
                block(FRAMES),
                block(CACHE),
                block(CACHE),
                pl.BlockSpec((slots, 2, KEEP, width), lambda i, *_: (0, 0, 0, 0)),
            ],
            scratch_shapes=[
                pltpu.VMEM((heads, SPAN * BLOCK, LANES), jnp.float32),
                pltpu.VMEM((heads, SPAN * BLOCK, LANES), jnp.float32),
                pltpu.VMEM((heads, SLAB * BLOCK, LANES), jnp.float32),
                pltpu.VMEM((heads, SLAB * BLOCK, LANES), jnp.float32),
            ],
        ),
        out_shape=[
            jax.ShapeDtypeStruct((FRAMES, stream_count, width), jnp.bfloat16),
            jax.ShapeDtypeStruct((CACHE, stream_count, width), jnp.bfloat16),
            jax.ShapeDtypeStruct((CACHE, stream_count, width), jnp.bfloat16),
            jax.ShapeDtypeStruct((slots, 2, KEEP, width), jnp.bfloat16),
        ],
        name="attend",
    )(
        valid_old,
        fill_old,
        bucket,
        queries,
        key_new,
        value_new,
        key_cache,
        value_cache,
        wide_valid,
    )


def place_body(arrival_s, got_ref, key_ref, value_ref, key_out_ref, value_out_ref, rows_f):
    base = pl.program_id(0) * BLOCK
    heads = rows_f.shape[1]
    for kind, src in enumerate((key_ref, value_ref)):
        for h in range(heads):
            lanes = slice(h * LANES, (h + 1) * LANES)
            for start in range(0, CACHE, CHUNK):
                rows_f[kind, h, start * BLOCK : (start + CHUNK) * BLOCK, :] = (
                    src[start : start + CHUNK, :, lanes]
                    .astype(jnp.float32)
                    .reshape(CHUNK * BLOCK, LANES)
                )

    def fetch(s, carry):
        slot = arrival_s[base + s]

        @pl.when(slot >= 0)
        def _():
            for kind in range(2):
                for h in range(heads):
                    rows_f[kind, h, pl.ds(s, KEEP, stride=BLOCK), :] = got_ref[
                        slot, kind, :, h * LANES : (h + 1) * LANES
                    ].astype(jnp.float32)

        return carry

    lax.fori_loop(0, BLOCK, fetch, 0)
    for kind, dst in enumerate((key_out_ref, value_out_ref)):
        for h in range(heads):
            lanes = slice(h * LANES, (h + 1) * LANES)
            for start in range(0, CACHE, CHUNK):
                dst[start : start + CHUNK, :, lanes] = (
                    rows_f[kind, h, start * BLOCK : (start + CHUNK) * BLOCK, :]
                    .reshape(CHUNK, BLOCK, LANES)
                    .astype(jnp.bfloat16)
                )


def place(arrival, received, key_rows, value_rows):
    stream_count = key_rows.shape[1]
    width = key_rows.shape[2]
    heads = width // HEAD
    slots = received.shape[0]
    block = pl.BlockSpec((CACHE, BLOCK, width), lambda i, *_: (0, i, 0))
    shape = jax.ShapeDtypeStruct((CACHE, stream_count, width), jnp.bfloat16)
    return pl.pallas_call(
        place_body,
        grid_spec=pltpu.PrefetchScalarGridSpec(
            num_scalar_prefetch=1,
            grid=(stream_count // BLOCK,),
            in_specs=[
                pl.BlockSpec((slots, 2, KEEP, width), lambda i, *_: (0, 0, 0, 0)),
                block,
                block,
            ],
            out_specs=[block, block],
            scratch_shapes=[pltpu.VMEM((2, heads, KEEP * BLOCK, LANES), jnp.float32)],
        ),
        out_shape=[shape, shape],
        name="place",
    )(arrival, received, key_rows, value_rows)


def on_device(
    spectra,
    sub_weight,
    sub_bias,
    key_cache,
    value_cache,
    conv_cache,
    new_slot,
    old_slot,
    valid_new,
    cache_fill,
    ln1_gain,
    w_query,
    w_key,
    w_value,
    w_attn_out,
    ln2_gain,
    w_glu_value,
    w_glu_gate,
    depth_kernel,
    norm_scale,
    norm_shift,
    w_conv_out,
):
    peer_count = lax.axis_size("front")
    own_index = lax.axis_index("front")
    member = lax.axis_index("enc")
    stream_count = spectra.shape[0]
    local_width = w_query.shape[1]
    slots = peer_count * CAP
    bucket = send_slots(new_slot, own_index, peer_count)
    arrival = arrival_slots(old_slot, own_index)
    both = lax.all_gather(valid_new * 128 + cache_fill, "front", axis=0, tiled=True)
    both_old = jnp.take(both, new_slot, axis=0)
    valid_old = both_old // 128
    fill_old = both_old % 128

    with_bias = jnp.concatenate(
        [sub_weight, jnp.broadcast_to(sub_bias[None, :], (16, local_width))], axis=0
    )
    with_bias = lax.all_gather(with_bias, "enc", axis=1, tiled=True)
    model_width = with_bias.shape[1]
    taps = SUB * MELS
    stacked = spectra.transpose(1, 2, 0).reshape(FRAMES, taps, stream_count)
    inputs = (
        jnp.einsum("tks,kc->tsc", stacked, with_bias[:taps], preferred_element_type=jnp.float32)
        + with_bias[taps].astype(jnp.float32)
    ).astype(jnp.bfloat16)
    flat_in = inputs.reshape(FRAMES * stream_count, model_width)
    normed = layer_norm(flat_in.astype(jnp.float32), ln1_gain).astype(jnp.bfloat16)

    def project(matrix):
        return (
            jnp.dot(normed, matrix, preferred_element_type=jnp.float32)
            .astype(jnp.bfloat16)
            .reshape(FRAMES, stream_count, local_width)
        )

    context, key_rows, value_rows, leaving_rows = attend(
        valid_old,
        fill_old,
        bucket,
        project(w_query),
        project(w_key),
        project(w_value),
        key_cache.transpose(1, 0, 2),
        value_cache.transpose(1, 0, 2),
        slots,
    )
    received = lax.all_to_all(leaving_rows, "front", split_axis=0, concat_axis=0, tiled=True)
    partial_out = jnp.dot(
        context.reshape(FRAMES * stream_count, local_width),
        w_attn_out,
        preferred_element_type=jnp.float32,
    )
    attended = lax.psum_scatter(
        partial_out.astype(jnp.bfloat16), "enc", scatter_dimension=1, tiled=True
    ).astype(jnp.float32)
    own_inputs = lax.dynamic_slice_in_dim(flat_in, member * local_width, local_width, 1)
    middle_slice = (own_inputs.astype(jnp.float32) + attended).astype(jnp.bfloat16)
    middle = lax.all_gather(middle_slice, "enc", axis=1, tiled=True)
    normed_second = layer_norm(middle.astype(jnp.float32), ln2_gain).astype(jnp.bfloat16)
    glu_value = jnp.dot(normed_second, w_glu_value, preferred_element_type=jnp.float32)
    glu_gate = jnp.dot(normed_second, w_glu_gate, preferred_element_type=jnp.float32)
    gated = (
        (glu_value * jax.nn.sigmoid(glu_gate))
        .astype(jnp.bfloat16)
        .reshape(FRAMES, stream_count, local_width)
    )
    conv_in = jnp.concatenate([conv_cache.transpose(1, 0, 2), gated], axis=0)
    depthwise = jnp.zeros((FRAMES, stream_count, local_width), jnp.float32)
    for kernel_tap in range(KERNEL):
        depthwise = depthwise + depth_kernel[kernel_tap] * conv_in[
            kernel_tap : kernel_tap + FRAMES
        ].astype(jnp.float32)
    shaped = depthwise * norm_scale + norm_shift
    activated = (
        (shaped * jax.nn.sigmoid(shaped))
        .astype(jnp.bfloat16)
        .reshape(FRAMES * stream_count, local_width)
    )
    conv_term = lax.psum_scatter(
        jnp.dot(activated, w_conv_out, preferred_element_type=jnp.float32).astype(jnp.bfloat16),
        "enc",
        scatter_dimension=1,
        tiled=True,
    ).astype(jnp.float32)
    frame_ok = jnp.arange(FRAMES, dtype=jnp.int32)[:, None] < valid_old[None, :]
    encoded = jnp.where(
        frame_ok[:, :, None],
        (middle_slice.astype(jnp.float32) + conv_term).reshape(
            FRAMES, stream_count, local_width
        ),
        0.0,
    ).astype(jnp.bfloat16)
    shift = (valid_old - 1)[None, :, None]
    conv_out = shift_rows(conv_in[1:], (shift & 1) != 0, (shift & 2) != 0, (shift & 4) != 0)
    conv_out = jnp.concatenate(
        [
            conv_out,
            jnp.where(shift == 6, conv_in[14:15], jnp.where(shift == 5, conv_in[13:14],
            jnp.where(shift == 4, conv_in[12:13], jnp.where(shift == 3, conv_in[11:12],
            jnp.where(shift == 2, conv_in[10:11], jnp.where(shift == 1, conv_in[9:10],
            conv_in[8:9]))))))
        ],
        axis=0,
    )
    finished = jnp.concatenate([encoded, conv_out], axis=0)
    picker = (
        bucket[None, :] == jnp.arange(slots, dtype=jnp.int32)[:, None]
    ).astype(jnp.bfloat16)
    leaving_end = jnp.einsum(
        "ls,tsc->ltc", picker, finished, preferred_element_type=jnp.float32
    ).astype(jnp.bfloat16)
    received_end = lax.all_to_all(leaving_end, "front", split_axis=0, concat_axis=0, tiled=True)
    placer = (
        arrival[:, None] == jnp.arange(slots, dtype=jnp.int32)[None, :]
    ).astype(jnp.bfloat16)
    placed = jnp.einsum(
        "sl,ltc->tsc", placer, received_end, preferred_element_type=jnp.float32
    ).astype(jnp.bfloat16)
    finished = jnp.where((arrival < 0)[None, :, None], finished, placed)
    key_done, value_done = place(arrival, received, key_rows, value_rows)
    return (
        finished[:FRAMES].transpose(1, 0, 2),
        key_done.transpose(1, 0, 2),
        value_done.transpose(1, 0, 2),
        finished[FRAMES:].transpose(1, 0, 2),
    )


def solution(mesh):
    in_specs = (
        P("front", None, None),
        P(None, "enc"),
        P("enc"),
        P("front", None, "enc"),
        P("front", None, "enc"),
        P("front", None, "enc"),
        P("front"),
        P("front"),
        P("front"),
        P("front"),
        P(),
        P(None, "enc"),
        P(None, "enc"),
        P(None, "enc"),
        P("enc", None),
        P(),
        P(None, "enc"),
        P(None, "enc"),
        P(None, "enc"),
        P("enc"),
        P("enc"),
        P("enc", None),
    )
    out_specs = (
        P("front", None, "enc"),
        P("front", None, "enc"),
        P("front", None, "enc"),
        P("front", None, "enc"),
    )
    return jax.shard_map(
        on_device, mesh=mesh, in_specs=in_specs, out_specs=out_specs, check_vma=False
    )
```

time: 342 us -> 277 us (0.81)
  local copies, waits for them, and re-layouts: 119 us -> 9.3 us
  Pallas kernels: 0 us -> 101 us
  other arithmetic: 52 us -> 13.5 us
  blocking collectives: 0 us -> 22 us
  waiting for transfers between devices: 102 us -> 85.9 us
  starting transfers between devices: 28 us -> 14.7 us
  matrix products: 22.1 us -> 14 us
    pallas_call x0 -> x2, Pallas kernels: none -> 101 us  [the longest x1 87.2 us: attend(): pl.pallas_call(attend_body, grid_spec=pltpu.PrefetchScalarGridSpec(num_sc...]
    all_to_all x4 -> x2, waiting for transfers between devices: 62.5 us -> 0.01 us  [the longest x1 0.01 us: on_device(): lax.all_to_all(leaving_rows, 'front', split_axis=0, concat_axis=0, tiled=...]
    gather x11 -> x1, local copies, waits for them, and re-layouts: 63.3 us -> 1.15 us  [on_device(): both_old = jnp.take(both, new_slot, axis=0)]
    reduce_scatter x1, waiting for transfers between devices: 0.01 us -> 28.1 us  [on_device(): lax.psum_scatter(jnp.dot(activated, w_conv_out, preferred_element_type=jn...]
    select_n x9 -> x7, other arithmetic: 28 us -> 1.19 us  [the longest x1 0.57 us: send_slots(): return jnp.where(leaving, target * CAP + position, peer_count * CAP)]
    concatenate x9 -> x0, local copies, waits for them, and re-layouts: 22.8 us -> none  [the longest x4 11.3 us: on_device(): values_joined = jnp.concatenate([values_old, value_flat], axis=1)]
    all_gather x0 -> x1, blocking collectives: none -> 22 us  [on_device(): lax.all_gather(valid_new * 128 + cache_fill, 'front', axis=0, tiled=True)]
    select_n x4 -> x0, local copies, waits for them, and re-layouts: 21.2 us -> none  [the longest x2 14.1 us: pick_rows(): return jnp.where(keep, resident, fetched)]
  transfers between devices with their start and end apart: 8 -> 6, of which waited for: 5 -> 4; matrix products, arithmetic and copies ran while one was open for 42% -> 6% of each run, Pallas kernels for 0% -> 5%
where the time goes in v1:
time: 277 us; the launch traced here: 274 us
  Pallas kernels  101 us (36%)
  waiting for transfers between devices  85.9 us (31%)
  blocking collectives  22 us (8%)
  starting transfers between devices  14.7 us (5%)
  between operations  14.2 us (5%)
  matrix products  14 us (5%)
  other arithmetic  13.5 us (5%)
  local copies, waits for them, and re-layouts  9.3 us (3%)
    pallas_call x1, Pallas kernels, attend(): pl.pallas_call(attend_body, grid_spec=pltpu.PrefetchScalarGridSpec(num_sc...  87.2 us
    reduce_scatter x1, waiting for transfers between devices, on_device(): lax.psum_scatter(partial_out.astype(jnp.bfloat16), 'enc', scatter_dimensi...  28.6 us
    reduce_scatter x1, waiting for transfers between devices, on_device(): lax.psum_scatter(jnp.dot(activated, w_conv_out, preferred_element_type=jn...  28.1 us
    all_gather x1, waiting for transfers between devices, on_device(): middle = lax.all_gather(middle_slice, 'enc', axis=1, tiled=True)  24.2 us
    all_gather x1, blocking collectives, on_device(): lax.all_gather(valid_new * 128 + cache_fill, 'front', axis=0, tiled=True)  22 us
    pallas_call x1, Pallas kernels, place(): pl.pallas_call(place_body, grid_spec=pltpu.PrefetchScalarGridSpec(num_sca...  13.4 us
    all_to_all x1, starting transfers between devices, on_device(): lax.all_to_all(leaving_rows, 'front', split_axis=0, concat_axis=0, tiled=...  7.24 us
    all_to_all x1, starting transfers between devices, on_device(): lax.all_to_all(leaving_end, 'front', split_axis=0, concat_axis=0, tiled=T...  7.1 us
  transfers between devices with their start and end apart: 6, of which 4 were waited for; matrix products, arithmetic and copies ran while one was open for 6% of the time, Pallas kernels for 5%

profile of v1, /device:TPU:0, one launch (start us, length us, event | category | flops | bytes accessed | tf_op | source)
XLA Modules:
  0.0 274.1 jit_solution(6397171608181489719)
XLA Ops:
  7.3 0.7 broadcast_in_dim.133
  8.0 1.7 pad_maximum_fusion.3
  9.8 2.1 copy.49
  11.9 22.0 %all-gather = s32[32,1,128]{2,1,0:T(1,128)S(1)} all-gather(s32[1,1,128]{2,1,0:T(1,128)S(1)} %add_bitcast_fusion), channel_id=1, replica_groups=mesh['front'=32,'enc'=4] {'front'}, dimensions={0}, use_global_device_ids=true | all-gather | bytes 16896 | tf_op jit(solution)/shard_map/all_gather | solution.py:309
  33.8 1.1 gather_fusion
  35.2 0.6 compare_select_fusion
  35.8 5.0 %all-gather.4.cloned.1.call-done = bf16[656,1024]{1,0:T(8,128)(2,1)} async-done(((bf16[656,256]{1,0:T(8,128)(2,1)}), bf16[656,1024]{1,0:T(8,128)(2,1)}) %all-gather.4.cloned.1.call-update) | async-done | bytes 1343504 | tf_op jit(solution)/shard_map/all_gather | solution.py:317
  40.7 0.7 slice_convert_fusion
  41.5 2.9 %fusion.12 = f32[1024,896]{0,1:S(1)} fusion(bf16[640,896]{0,1:T(8,128)(2,1)S(1)} %bitcast.87, bf16[656,1024]{1,0:T(8,128)(2,1)} %all-gather.4.cloned.1.call-done), kind=kOutput, calls=%fused_computation.38 | convolution fusion | flops 1174405120 | bytes 6127616
  44.4 0.4 convert_reduce_fusion.1
  44.8 0.6 fusion.6
  45.4 0.6 multiply_convert_fusion
  46.1 0.4 copy-done.18
  46.5 1.4 convolution_convert_fusion.6
  47.9 1.4 convolution_convert_fusion.5
  49.3 1.4 convolution_convert_fusion.4
  50.7 0.7 broadcast_in_dim.135.valid_ref
  51.4 87.2 %attend.1 = (bf16[7,128,256]{2,1,0:T(8,128)(2,1)}, bf16[70,128,256]{2,1,0:T(8,128)(2,1)}, bf16[70,128,256]{2,1,0:T(8,128)(2,1)}, bf16[64,2,72,256]{3,2,1,0:T(8,128)(2,1)}) custom-call(s32[128]{0:T(128)} %copy-done.7, s32[128]{0:T(128)} %get-tuple-element.61.fill_s, s32[128]{0:T(128)} %get-tuple-element.60.slot_s, bf16[7,128,256]{2,1,0:T(8,128)(2,1)} %bitcast.88, ...), custom_call_target="tpu_custom_call" | custom-call | tf_op jit(solution)/shard_map/attend/pallas_call | solution.py:168
  138.7 2.9 %convolution_convert_fusion.1 = bf16[896,1024]{1,0:T(8,128)(2,1)} fusion(bf16[896,256]{1,0:T(8,128)(2,1)} %bitcast.91, bf16[256,1024]{1,0:T(8,128)(2,1)S(1)} %copy-done), kind=kOutput, calls=%fused_computation.22 | convolution fusion | flops 470679552 | bytes 2818048 | tf_op jit(solution)/shard_map/dot_general | solution.py:347
  141.6 28.6 %reduce-scatter.3.cloned.1.call-done = bf16[896,256]{1,0:T(8,128)(2,1)} async-done(((bf16[896,1024]{1,0:T(8,128)(2,1)}), bf16[896,256]{1,0:T(8,128)(2,1)}) %reduce-scatter.3.cloned.1.call-update) | async-done | bytes 458768 | tf_op jit(solution)/shard_map/reduce_scatter | solution.py:352
  170.2 2.0 add_convert_fusion.1
  172.3 7.2 %all-to-all-start.1 = ((bf16[64,2,72,256]{3,2,1,0:T(8,128)(2,1)}), bf16[64,2,72,256]{3,2,1,0:T(8,128)(2,1)}, u32[]{:S(2)}, u32[]{:S(2)}) async-start(bf16[64,2,72,256]{3,2,1,0:T(8,128)(2,1)} %get-tuple-element.11), calls=%async_computation.3 | async-start | bytes 9437184 | tf_op jit(solution)/shard_map/all_to_all | solution.py:346
  179.6 0.2 reduce-scatter.5.cloned.1.call-start
  179.8 24.2 %all-gather.6.cloned.1.call-done = bf16[896,1024]{1,0:T(8,128)(2,1)} async-done(((bf16[896,256]{1,0:T(8,128)(2,1)}), bf16[896,1024]{1,0:T(8,128)(2,1)}) %all-gather.6.cloned.1.call-update) | async-done | bytes 1835024 | tf_op jit(solution)/shard_map/all_gather | solution.py:357
  204.1 1.9 convert_reduce_fusion
  206.1 0.6 fusion.2
  206.8 0.6 fusion.4
  207.4 0.4 copy-done.21
  207.8 0.7 fusion.11
  208.5 0.4 copy-done.4
  208.8 0.6 fusion.14
  209.5 0.8 multiply_convert_fusion.1
  210.3 0.2 copy-done.6
  210.5 1.9 convolution_convert_fusion
  212.5 0.2 fusion.29
  212.7 0.2 fusion.16
  213.1 28.1 %reduce-scatter.5.cloned.1.call-done = bf16[896,256]{1,0:T(8,128)(2,1)} async-done(((bf16[896,1024]{1,0:T(8,128)(2,1)}), bf16[896,256]{1,0:T(8,128)(2,1)}) %reduce-scatter.5.cloned.1.call-update) | async-done | bytes 458768 | tf_op jit(solution)/shard_map/reduce_scatter | solution.py:378
  241.2 1.1 convert_add_fusion
  242.3 0.2 select_convert_fusion
  242.5 0.3 convolution_convert_fusion.3
  242.8 1.1 copy.51
  243.9 7.1 %all-to-all-start = ((bf16[64,15,256]{2,1,0:T(8,128)(2,1)}), bf16[64,15,256]{2,1,0:T(8,128)(2,1)S(1)}, u32[]{:S(2)}, u32[]{:S(2)}) async-start(bf16[64,15,256]{2,1,0:T(8,128)(2,1)} %copy.51), calls=%async_computation.2 | async-start | bytes 1048576 | tf_op jit(solution)/shard_map/all_to_all | solution.py:411
  251.0 0.2 convert_reduce_fusion.3
  251.2 0.5 broadcast_compare_fusion.5
  251.7 13.4 %place.1 = (bf16[70,128,256]{2,1,0:T(8,128)(2,1)}, bf16[70,128,256]{2,1,0:T(8,128)(2,1)}) custom-call(s32[128]{0:T(128)} %get-tuple-element.38.arrival_s, bf16[64,2,72,256]{3,2,1,0:T(8,128)(2,1)} %all-to-all-done.1.got_ref, bf16[70,128,256]{2,1,0:T(8,128)(2,1)} %get-tuple-element.12.key_ref, bf16[70,128,256]{2,1,0:T(8,128)(2,1)} %get-tuple-element.13.value_ref), custom_call_target="tpu_custom_call" | custom-call | tf_op jit(solution)/shard_map/place/pallas_call | solution.py:259
  265.1 0.5 fusion.8
  265.6 0.8 slice_bitcast_fusion.1
  266.5 1.1 copy.54
  (70 shorter events, 1.1 us)
Async XLA Ops:
  7.2 131.5 %copy-start = (bf16[256,1024]{1,0:T(8,128)(2,1)S(1)}, bf16[256,1024]{1,0:T(8,128)(2,1)}, u32[]{:S(2)}) copy-start(bf16[256,1024]{1,0:T(8,128)(2,1)} %param.36) | copy-start | bytes 1572868
  7.2 4.6 %copy-start.22 = (s32[128]{0:T(128)S(1)}, s32[128]{0:T(128)}, u32[]{:S(2)}) copy-start(s32[128]{0:T(128)} %param.31) | copy-start | bytes 1540
  7.2 4.6 %copy-start.23 = (s32[128]{0:T(128)S(1)}, s32[128]{0:T(128)}, u32[]{:S(2)}) copy-start(s32[128]{0:T(128)} %param.30) | copy-start | bytes 1540
  7.2 26.6 %copy-start.17 = (s32[128]{0:T(128)S(1)}, s32[128]{0:T(128)}, u32[]{:S(2)}) copy-start(s32[128]{0:T(128)} %param.28) | copy-start | bytes 1540
  7.2 33.5 %all-gather.4.cloned.1.call-start = ((), (), s32[]{:S(2)}) async-start(), calls=%async_computation.4 | async-start | bytes 1679360 | tf_op jit(solution)/shard_map/all_gather | solution.py:317
  9.7 160.5 %reduce-scatter.3.cloned.1.call-start = ((), (), s32[]{:S(2)}) async-start(), calls=%async_computation.5 | async-start | bytes 2293760 | tf_op jit(solution)/shard_map/reduce_scatter | solution.py:352
  35.2 15.5 %copy-start.7 = (s32[128]{0:T(128)}, s32[128]{0:T(128)S(1)}, u32[]{:S(2)}) copy-start(s32[128]{0:T(128)S(1)} %get-tuple-element.33.valid_s) | copy-start | bytes 1540
  44.4 1.1 copy-start.11
  45.4 1.0 copy-start.18
  46.5 1.4 copy-start.19
  47.9 1.4 copy-start.20
  141.6 30.6 %copy-start.5 = (bf16[128,8,256]{2,1,0:T(8,128)(2,1)S(1)}, bf16[128,8,256]{2,1,0:T(8,128)(2,1)}, u32[]{:S(2)}) copy-start(bf16[128,8,256]{2,1,0:T(8,128)(2,1)} %param.27) | copy-start | bytes 1572868
  141.6 30.8 %copy-start.9 = (f32[9,256]{1,0:T(8,128)S(1)}, f32[9,256]{1,0:T(8,128)}, u32[]{:S(2)}) copy-start(f32[9,256]{1,0:T(8,128)} %param.40) | copy-start | bytes 27652
  141.6 62.5 %all-gather.6.cloned.1.call-start = ((), (), s32[]{:S(2)}) async-start(), calls=%async_computation.6 | async-start | bytes 2293760 | tf_op jit(solution)/shard_map/all_gather | solution.py:357
  172.3 71.6 %all-to-all-start.1 = ((bf16[64,2,72,256]{3,2,1,0:T(8,128)(2,1)}), bf16[64,2,72,256]{3,2,1,0:T(8,128)(2,1)}, u32[]{:S(2)}, u32[]{:S(2)}) async-start(bf16[64,2,72,256]{3,2,1,0:T(8,128)(2,1)} %get-tuple-element.11), calls=%async_computation.3 | async-start | bytes 9437184 | tf_op jit(solution)/shard_map/all_to_all | solution.py:346
  179.6 27.2 %copy-start.12 = (f32[1024]{0:T(1024)S(1)}, f32[1024]{0:T(1024)}, u32[]{:S(2)}) copy-start(f32[1024]{0:T(1024)} %param.37) | copy-start | bytes 12292
  179.6 61.6 %reduce-scatter.5.cloned.1.call-start = ((), (), s32[]{:S(2)}) async-start(), calls=%async_computation.7 | async-start | bytes 2293760 | tf_op jit(solution)/shard_map/reduce_scatter | solution.py:378
  204.1 2.1 copy-start.2
  206.7 1.0 copy-start.21
  207.8 1.0 copy-start.4
  208.8 0.7 copy-start.15
  208.8 0.7 copy-start.16
  209.5 1.0 copy-start.6
  210.5 1.9 copy-start.8
  212.9 28.3 %copy-start.3 = (bf16[896,256]{1,0:T(8,128)(2,1)S(1)}, bf16[896,256]{1,0:T(8,128)(2,1)}, u32[]{:S(2)}) copy-start(bf16[896,256]{1,0:T(8,128)(2,1)} %add_convert_fusion.1) | copy-start | bytes 1376260
  213.0 29.5 %copy-start.14 = (s32[128]{0:T(128)S(1)}, s32[128]{0:T(128)}, u32[]{:S(2)}) copy-start(s32[128]{0:T(128)} %get-tuple-element.60.slot_s) | copy-start | bytes 1540
  242.5 8.5 %copy-start.10 = (s32[128]{0:T(128)S(1)}, s32[128]{0:T(128)}, u32[]{:S(2)}) copy-start(s32[128]{0:T(128)} %param.29) | copy-start | bytes 1540
  243.9 21.2 %all-to-all-start = ((bf16[64,15,256]{2,1,0:T(8,128)(2,1)}), bf16[64,15,256]{2,1,0:T(8,128)(2,1)S(1)}, u32[]{:S(2)}, u32[]{:S(2)}) async-start(bf16[64,15,256]{2,1,0:T(8,128)(2,1)} %copy.51), calls=%async_computation.2 | async-start | bytes 1048576 | tf_op jit(solution)/shard_map/all_to_all | solution.py:411
  251.7 13.4 %copy-start.13 = (s32[128]{0:T(128)S(1)}, s32[128]{0:T(128)}, u32[]{:S(2)}) copy-start(s32[128]{0:T(128)} %get-tuple-element.38.arrival_s) | copy-start | bytes 1540
  265.1 2.4 copy-start.1
Sparse Core Ops, SparseCore 0:
  10.2 30.4 all-gather.3
  141.7 28.4 reduce-scatter.2
  172.4 31.5 all-gather.5
  212.6 28.5 reduce-scatter.4

commit v2 on v1

--- a/solution.py
+++ b/solution.py
@@ -6,6 +6,7 @@
 from jax.experimental import pallas as pl
 from jax.experimental.pallas import tpu as pltpu
 from jax.sharding import PartitionSpec as P
+
 
 MELS = 80
 KERNEL = 9
@@ -14,12 +15,10 @@
 CACHE = 70
 CAP = 2
 HEAD = 128
-CONV_CACHE = 8
 LANES = 128
 BLOCK = 16
 SPAN = 80
 KEEP = 72
-SLAB = 8
 CHUNK = 10
 
 masked_score = -1e30
@@ -58,8 +57,6 @@
 
 
 def attend_body(
-    valid_s,
-    fill_s,
     slot_s,
     query_ref,
     key_new_ref,
@@ -67,88 +64,87 @@
     key_ref,
     value_ref,
     valid_ref,
+    fill_ref,
     context_ref,
     key_out_ref,
     value_out_ref,
     send_ref,
-    key_f,
-    value_f,
-    query_f,
-    context_f,
+    rows_f,
 ):
     base = pl.program_id(0) * BLOCK
-    heads = key_f.shape[0]
+    width = query_ref.shape[2]
+    heads = width // LANES
     slots = send_ref.shape[0]
-    shift = valid_ref[...] - 1
+    span = SPAN * BLOCK
+    valid = valid_ref[...]
+    low = (CACHE - fill_ref[:, :1]) * BLOCK
+    high = (CACHE + valid[:, :1]) * BLOCK
+    offset = lax.broadcasted_iota(jnp.int32, (BLOCK, span), 1) - lax.broadcasted_iota(
+        jnp.int32, (BLOCK, span), 0
+    )
+    allowed = ((offset & (BLOCK - 1)) == 0) & (offset >= low) & (offset < high)
+    bias = jnp.where(allowed, 0.0, masked_score)[None]
+    padding = jnp.zeros(((SPAN - CACHE - FRAMES) * BLOCK, LANES), jnp.bfloat16)
+
+    def joined(old_ref, new_ref, lanes):
+        return jnp.concatenate(
+            [
+                old_ref[:, :, lanes].reshape(CACHE * BLOCK, LANES),
+                new_ref[:, :, lanes].reshape(FRAMES * BLOCK, LANES),
+                padding,
+            ],
+            axis=0,
+        )
+
+    for h in range(heads):
+        lanes = slice(h * LANES, (h + 1) * LANES)
+        scores = lax.dot_general(
+            query_ref[:, :, lanes].reshape(FRAMES * BLOCK, LANES),
+            joined(key_ref, key_new_ref, lanes),
+            (((1,), (1,)), ((), ())),
+            preferred_element_type=jnp.float32,
+        )
+        scores = scores.reshape(FRAMES, BLOCK, span) * (1.0 / math.sqrt(HEAD)) + bias
+        exponent = jnp.exp(scores - jnp.max(scores, axis=2, keepdims=True))
+        weights = exponent * (1.0 / jnp.sum(exponent, axis=2, keepdims=True))
+        context = lax.dot_general(
+            weights.astype(jnp.bfloat16).reshape(FRAMES * BLOCK, span),
+            joined(value_ref, value_new_ref, lanes),
+            (((1,), (0,)), ((), ())),
+            preferred_element_type=jnp.float32,
+        )
+        context_ref[:, :, lanes] = context.reshape(FRAMES, BLOCK, LANES).astype(jnp.bfloat16)
+
+    shift = valid - 1
     first = ((shift & 1) != 0)[None]
     second = ((shift & 2) != 0)[None]
     third = ((shift & 4) != 0)[None]
-    for h in range(heads):
-        lanes = slice(h * LANES, (h + 1) * LANES)
-        for old_ref, new_ref, dst in (
-            (key_ref, key_new_ref, key_f),
-            (value_ref, value_new_ref, value_f),
-        ):
+    for kind, (old_ref, new_ref, out_ref) in enumerate(
+        ((key_ref, key_new_ref, key_out_ref), (value_ref, value_new_ref, value_out_ref))
+    ):
+        for h in range(heads):
+            lanes = slice(h * LANES, (h + 1) * LANES)
             for start in range(0, CACHE, CHUNK):
-                dst[h, start * BLOCK : (start + CHUNK) * BLOCK, :] = (
-                    old_ref[start : start + CHUNK, :, lanes]
-                    .astype(jnp.float32)
-                    .reshape(CHUNK * BLOCK, LANES)
+                stop = start + CHUNK + 8
+                rows = old_ref[start + 1 : min(stop, CACHE), :, lanes].astype(jnp.float32)
+                if stop > CACHE:
+                    extra = new_ref[:, :, lanes].astype(jnp.float32)
+                    rows = jnp.concatenate([rows, extra, extra[:1]], axis=0)[: CHUNK + 7]
+                rows = shift_rows(rows, first, second, third)
+                out_ref[start : start + CHUNK, :, lanes] = rows.astype(jnp.bfloat16)
+                rows_f[kind, h, start * BLOCK : (start + CHUNK) * BLOCK, :] = rows.reshape(
+                    CHUNK * BLOCK, LANES
                 )
-            dst[h, CACHE * BLOCK : (CACHE + FRAMES) * BLOCK, :] = (
-                new_ref[:, :, lanes].astype(jnp.float32).reshape(FRAMES * BLOCK, LANES)
-            )
-            dst[h, (CACHE + FRAMES) * BLOCK :, :] = jnp.zeros(
-                ((SPAN - CACHE - FRAMES) * BLOCK, LANES), jnp.float32
-            )
-        query_f[h, : FRAMES * BLOCK, :] = (
-            query_ref[:, :, lanes].astype(jnp.float32).reshape(FRAMES * BLOCK, LANES)
-        )
-        query_f[h, FRAMES * BLOCK :, :] = jnp.zeros(((SLAB - FRAMES) * BLOCK, LANES), jnp.float32)
-    place = lax.broadcasted_iota(jnp.int32, (SLAB, SPAN), 1)
-    for s in range(BLOCK):
-        fill = fill_s[base + s]
-        valid = valid_s[base + s]
-        allowed = (place >= CACHE - fill) & (place < CACHE + valid)
-        for h in range(heads):
-            keys = key_f[h, pl.ds(s, SPAN, stride=BLOCK), :].astype(jnp.bfloat16)
-            query = query_f[h, pl.ds(s, SLAB, stride=BLOCK), :].astype(jnp.bfloat16)
-            scores = lax.dot_general(
-                query, keys, (((1,), (1,)), ((), ())), preferred_element_type=jnp.float32
-            ) * (1.0 / math.sqrt(HEAD))
-            scores = jnp.where(allowed, scores, masked_score)
-            peak = jnp.max(scores, axis=1, keepdims=True)
-            exponent = jnp.where(allowed, jnp.exp(scores - peak), 0.0)
-            weights = (exponent / jnp.sum(exponent, axis=1, keepdims=True)).astype(jnp.bfloat16)
-            values = value_f[h, pl.ds(s, SPAN, stride=BLOCK), :].astype(jnp.bfloat16)
-            context_f[h, pl.ds(s, SLAB, stride=BLOCK), :] = lax.dot_general(
-                weights, values, (((1,), (0,)), ((), ())), preferred_element_type=jnp.float32
-            )
-    for h in range(heads):
-        lanes = slice(h * LANES, (h + 1) * LANES)
-        context_ref[:, :, lanes] = (
-            context_f[h, : FRAMES * BLOCK, :]
-            .reshape(FRAMES, BLOCK, LANES)
-            .astype(jnp.bfloat16)
-        )
-        for src, out_ref in ((key_f, key_out_ref), (value_f, value_out_ref)):
-            for start in range(0, CACHE, CHUNK):
-                rows = src[h, (start + 1) * BLOCK : (start + CHUNK + 8) * BLOCK, :]
-                rows = rows.reshape(CHUNK + 7, BLOCK, LANES)
-                out_ref[start : start + CHUNK, :, lanes] = shift_rows(
-                    rows, first, second, third
-                ).astype(jnp.bfloat16)
 
     def pack(s, carry):
         slot = slot_s[base + s]
-        valid = valid_s[base + s]
 
         @pl.when(slot < slots)
         def _():
-            for kind, src in enumerate((key_f, value_f)):
+            for kind in range(2):
                 for h in range(heads):
-                    send_ref[slot, kind, :, h * LANES : (h + 1) * LANES] = src[
-                        h, pl.ds(valid * BLOCK + s, KEEP, stride=BLOCK), :
+                    send_ref[slot, kind, :, h * LANES : (h + 1) * LANES] = rows_f[
+                        kind, h, pl.ds(s, KEEP, stride=BLOCK), :
                     ].astype(jnp.bfloat16)
 
         return carry
@@ -160,15 +156,18 @@
     stream_count = key_cache.shape[1]
     width = key_cache.shape[2]
     heads = width // HEAD
-    wide_valid = jnp.broadcast_to(valid_old[:, None], (stream_count, LANES))
+
+    def wide(column):
+        return jnp.broadcast_to(column[:, None], (stream_count, LANES))
 
     def block(rows):
         return pl.BlockSpec((rows, BLOCK, width), lambda i, *_: (0, i, 0))
 
+    scalar = pl.BlockSpec((BLOCK, LANES), lambda i, *_: (i, 0))
     return pl.pallas_call(
         attend_body,
         grid_spec=pltpu.PrefetchScalarGridSpec(
-            num_scalar_prefetch=3,
+            num_scalar_prefetch=1,
             grid=(stream_count // BLOCK,),
             in_specs=[
                 block(FRAMES),
@@ -176,7 +175,8 @@
                 block(FRAMES),
                 block(CACHE),
                 block(CACHE),
-                pl.BlockSpec((BLOCK, LANES), lambda i, *_: (i, 0)),
+                scalar,
+                scalar,
             ],
             out_specs=[
                 block(FRAMES),
@@ -184,12 +184,7 @@
                 block(CACHE),
                 pl.BlockSpec((slots, 2, KEEP, width), lambda i, *_: (0, 0, 0, 0)),
             ],
-            scratch_shapes=[
-                pltpu.VMEM((heads, SPAN * BLOCK, LANES), jnp.float32),
-                pltpu.VMEM((heads, SPAN * BLOCK, LANES), jnp.float32),
-                pltpu.VMEM((heads, SLAB * BLOCK, LANES), jnp.float32),
-                pltpu.VMEM((heads, SLAB * BLOCK, LANES), jnp.float32),
-            ],
+            scratch_shapes=[pltpu.VMEM((2, heads, KEEP * BLOCK, LANES), jnp.float32)],
         ),
         out_shape=[
             jax.ShapeDtypeStruct((FRAMES, stream_count, width), jnp.bfloat16),
@@ -199,15 +194,14 @@
         ],
         name="attend",
     )(
-        valid_old,
-        fill_old,
         bucket,
         queries,
         key_new,
         value_new,
         key_cache,
         value_cache,
-        wide_valid,
+        wide(valid_old),
+        wide(fill_old),
     )
 
 
@@ -306,8 +300,18 @@
     slots = peer_count * CAP
     bucket = send_slots(new_slot, own_index, peer_count)
     arrival = arrival_slots(old_slot, own_index)
-    both = lax.all_gather(valid_new * 128 + cache_fill, "front", axis=0, tiled=True)
-    both_old = jnp.take(both, new_slot, axis=0)
+    slot_ids = jnp.arange(slots, dtype=jnp.int32)
+    both = valid_new * 128 + cache_fill
+    asked = jnp.sum(jnp.where(arrival[None, :] == slot_ids[:, None], both[None, :], 0), axis=1)
+    told = lax.all_to_all(
+        jnp.broadcast_to(asked[:, None], (slots, LANES)),
+        "front",
+        split_axis=0,
+        concat_axis=0,
+        tiled=True,
+    )[:, 0]
+    told = jnp.sum(jnp.where(bucket[:, None] == slot_ids[None, :], told[None, :], 0), axis=1)
+    both_old = jnp.where(bucket < slots, told, both)
     valid_old = both_old // 128
     fill_old = both_old % 128
 
@@ -456,6 +460,7 @@
         P("front", None, "enc"),
         P("front", None, "enc"),
     )
+
     return jax.shard_map(
         on_device, mesh=mesh, in_specs=in_specs, out_specs=out_specs, check_vma=False
     )

time: 277 us -> 210 us (0.76)
  Pallas kernels: 101 us -> 34.6 us
  blocking collectives: 22 us -> 0 us
  waiting for transfers between devices: 85.9 us -> 98.1 us
  starting transfers between devices: 14.7 us -> 22.1 us
    pallas_call x1, Pallas kernels: 87.2 us -> 21 us  [attend(): pl.pallas_call(attend_body, grid_spec=pltpu.PrefetchScalarGridSpec(num_sc...]
    all_gather x1 -> x0, blocking collectives: 22 us -> none  [on_device(): lax.all_gather(valid_new * 128 + cache_fill, 'front', axis=0, tiled=True)]
    all_to_all x0 -> x1, starting transfers between devices: none -> 7.43 us  [on_device(): lax.all_to_all(jnp.broadcast_to(asked[:, None], (slots, LANES)), 'front',...]
    all_gather x1, waiting for transfers between devices: 4.95 us -> 11.1 us  [on_device(): with_bias = lax.all_gather(with_bias, 'enc', axis=1, tiled=True)]
    all_to_all x0 -> x1, waiting for transfers between devices: none -> 5.87 us  [on_device(): lax.all_to_all(jnp.broadcast_to(asked[:, None], (slots, LANES)), 'front',...]
  transfers between devices with their start and end apart: 6 -> 7, of which waited for: 4 -> 5; matrix products, arithmetic and copies ran while one was open for 6% -> 8% of each run, Pallas kernels for 5% -> 7%
where the time goes in v2:
time: 210 us; the launch traced here: 208 us
  waiting for transfers between devices  98.1 us (47%)
  Pallas kernels  34.6 us (16%)
  starting transfers between devices  22.1 us (11%)
  other arithmetic  16 us (8%)
  between operations  14.2 us (7%)
  matrix products  14 us (7%)
  local copies, waits for them, and re-layouts  9.24 us (4%)
    reduce_scatter x1, waiting for transfers between devices, on_device(): lax.psum_scatter(partial_out.astype(jnp.bfloat16), 'enc', scatter_dimensi...  28.7 us
    reduce_scatter x1, waiting for transfers between devices, on_device(): lax.psum_scatter(jnp.dot(activated, w_conv_out, preferred_element_type=jn...  28.1 us
    all_gather x1, waiting for transfers between devices, on_device(): middle = lax.all_gather(middle_slice, 'enc', axis=1, tiled=True)  24.3 us
    pallas_call x1, Pallas kernels, attend(): pl.pallas_call(attend_body, grid_spec=pltpu.PrefetchScalarGridSpec(num_sc...  21 us
    pallas_call x1, Pallas kernels, place(): pl.pallas_call(place_body, grid_spec=pltpu.PrefetchScalarGridSpec(num_sca...  13.7 us
    all_gather x1, waiting for transfers between devices, on_device(): with_bias = lax.all_gather(with_bias, 'enc', axis=1, tiled=True)  11.1 us
    all_to_all x1, starting transfers between devices, on_device(): lax.all_to_all(jnp.broadcast_to(asked[:, None], (slots, LANES)), 'front',...  7.43 us
    all_to_all x1, starting transfers between devices, on_device(): lax.all_to_all(leaving_rows, 'front', split_axis=0, concat_axis=0, tiled=...  7.22 us
  transfers between devices with their start and end apart: 7, of which 5 were waited for; matrix products, arithmetic and copies ran while one was open for 8% of the time, Pallas kernels for 7%

profile of v2, /device:TPU:0, one launch (start us, length us, event | category | flops | bytes accessed | tf_op | source)
XLA Modules:
  0.0 208.2 jit_solution(5550440343916103755)
XLA Ops:
  7.2 0.8 broadcast_in_dim.176
  8.0 1.7 pad_maximum_fusion.3
  9.8 0.7 and_select_fusion.2
  10.6 0.7 and_select_fusion.3
  11.3 0.9 convert_reduce_fusion.3
  12.2 0.7 broadcast_compare_fusion.5
  12.9 0.7 compare_select_fusion.1
  13.8 0.7 broadcast_in_dim.171
  14.5 7.4 %all-to-all-start = ((s32[32,2,128]{2,1,0:T(2,128)}), s32[32,2,128]{2,1,0:T(2,128)S(1)}, u32[]{:S(2)}, u32[]{:S(2)}) async-start(s32[32,2,128]{2,1,0:T(2,128)} %broadcast_in_dim.171), calls=%async_computation | async-start | bytes 65536 | tf_op jit(solution)/shard_map/all_to_all | solution.py:306
  22.0 1.5 copy.53
  23.5 5.9 %all-to-all-done = s32[32,2,128]{2,1,0:T(2,128)S(1)} async-done(((s32[32,2,128]{2,1,0:T(2,128)}), s32[32,2,128]{2,1,0:T(2,128)S(1)}, u32[]{:S(2)}, u32[]{:S(2)}) %all-to-all-start) | async-done | bytes 32800 | tf_op jit(solution)/shard_map/all_to_all | solution.py:306
  29.6 11.1 %all-gather.3.cloned.1.call-done = bf16[656,1024]{1,0:T(8,128)(2,1)} async-done(((bf16[656,256]{1,0:T(8,128)(2,1)}), bf16[656,1024]{1,0:T(8,128)(2,1)}) %all-gather.3.cloned.1.call-update) | async-done | bytes 1343504 | tf_op jit(solution)/shard_map/all_gather | solution.py:321
  40.7 0.7 slice_convert_fusion
  41.4 2.9 %fusion.12 = f32[1024,896]{0,1:S(1)} fusion(bf16[640,896]{0,1:T(8,128)(2,1)S(1)} %bitcast.84, bf16[656,1024]{1,0:T(8,128)(2,1)} %all-gather.3.cloned.1.call-done), kind=kOutput, calls=%fused_computation.37 | convolution fusion | flops 1174405120 | bytes 6127616
  44.4 0.4 convert_reduce_fusion.1
  44.8 0.6 fusion.6
  45.4 0.6 multiply_convert_fusion
  46.1 0.4 copy-done.17
  46.5 1.4 convolution_convert_fusion.6
  47.9 1.4 convolution_convert_fusion.5
  49.3 1.4 convolution_convert_fusion.4
  50.7 0.7 broadcast_in_dim.177.valid_ref
  51.4 0.7 broadcast_in_dim.178.fill_ref
  52.1 21.0 %attend.1 = (bf16[7,128,256]{2,1,0:T(8,128)(2,1)}, bf16[70,128,256]{2,1,0:T(8,128)(2,1)}, bf16[70,128,256]{2,1,0:T(8,128)(2,1)}, bf16[64,2,72,256]{3,2,1,0:T(8,128)(2,1)}) custom-call(s32[128]{0:T(128)} %copy-done.9, bf16[7,128,256]{2,1,0:T(8,128)(2,1)} %bitcast.86, bf16[7,128,256]{2,1,0:T(8,128)(2,1)} %bitcast.87, bf16[7,128,256]{2,1,0:T(8,128)(2,1)} %bitcast.88, ...), custom_call_target="tpu_custom_call" | custom-call | tf_op jit(solution)/shard_map/attend/pallas_call | solution.py:167
  73.1 2.9 %convolution_convert_fusion.1 = bf16[896,1024]{1,0:T(8,128)(2,1)} fusion(bf16[896,256]{1,0:T(8,128)(2,1)} %bitcast.85, bf16[256,1024]{1,0:T(8,128)(2,1)S(1)} %copy-done), kind=kOutput, calls=%fused_computation.21 | convolution fusion | flops 470679552 | bytes 2818048 | tf_op jit(solution)/shard_map/dot_general | solution.py:351
  76.1 28.7 %reduce-scatter.3.cloned.1.call-done = bf16[896,256]{1,0:T(8,128)(2,1)} async-done(((bf16[896,1024]{1,0:T(8,128)(2,1)}), bf16[896,256]{1,0:T(8,128)(2,1)}) %reduce-scatter.3.cloned.1.call-update) | async-done | bytes 458768 | tf_op jit(solution)/shard_map/reduce_scatter | solution.py:356
  104.8 1.9 add_convert_fusion.1
  106.9 7.2 %all-to-all-start.2 = ((bf16[64,2,72,256]{3,2,1,0:T(8,128)(2,1)}), bf16[64,2,72,256]{3,2,1,0:T(8,128)(2,1)}, u32[]{:S(2)}, u32[]{:S(2)}) async-start(bf16[64,2,72,256]{3,2,1,0:T(8,128)(2,1)} %get-tuple-element.11), calls=%async_computation.4 | async-start | bytes 9437184 | tf_op jit(solution)/shard_map/all_to_all | solution.py:350
  114.1 0.2 reduce-scatter.5.cloned.1.call-start
  114.3 24.3 %all-gather.5.cloned.1.call-done = bf16[896,1024]{1,0:T(8,128)(2,1)} async-done(((bf16[896,256]{1,0:T(8,128)(2,1)}), bf16[896,1024]{1,0:T(8,128)(2,1)}) %all-gather.5.cloned.1.call-update) | async-done | bytes 1835024 | tf_op jit(solution)/shard_map/all_gather | solution.py:361
  138.6 1.9 convert_reduce_fusion
  140.7 0.6 fusion.2
  141.3 0.6 fusion.4
  141.9 0.4 copy-done.20
  142.3 0.7 fusion.11
  143.0 0.4 copy-done.5
  143.4 0.7 fusion.14
  144.1 0.8 multiply_convert_fusion.1
  145.1 1.9 convolution_convert_fusion
  147.7 28.1 %reduce-scatter.5.cloned.1.call-done = bf16[896,256]{1,0:T(8,128)(2,1)} async-done(((bf16[896,1024]{1,0:T(8,128)(2,1)}), bf16[896,256]{1,0:T(8,128)(2,1)}) %reduce-scatter.5.cloned.1.call-update) | async-done | bytes 458768 | tf_op jit(solution)/shard_map/reduce_scatter | solution.py:382
  175.7 1.1 convert_add_fusion
  177.1 0.3 convolution_convert_fusion.3
  177.3 1.1 copy.55
  178.4 7.1 %all-to-all-start.1 = ((bf16[64,15,256]{2,1,0:T(8,128)(2,1)}), bf16[64,15,256]{2,1,0:T(8,128)(2,1)S(1)}, u32[]{:S(2)}, u32[]{:S(2)}) async-start(bf16[64,15,256]{2,1,0:T(8,128)(2,1)} %copy.55), calls=%async_computation.3 | async-start | bytes 1048576 | tf_op jit(solution)/shard_map/all_to_all | solution.py:415
  185.5 13.7 %place.1 = (bf16[70,128,256]{2,1,0:T(8,128)(2,1)}, bf16[70,128,256]{2,1,0:T(8,128)(2,1)}) custom-call(s32[128]{0:T(128)} %copy-done.13, bf16[64,2,72,256]{3,2,1,0:T(8,128)(2,1)} %all-to-all-done.2.got_ref, bf16[70,128,256]{2,1,0:T(8,128)(2,1)} %get-tuple-element.12.key_ref, bf16[70,128,256]{2,1,0:T(8,128)(2,1)} %get-tuple-element.13.value_ref), custom_call_target="tpu_custom_call" | custom-call | tf_op jit(solution)/shard_map/place/pallas_call | solution.py:253
  199.2 0.5 fusion.8
  199.7 0.8 slice_bitcast_fusion.1
  200.6 1.1 copy.58
  (69 shorter events, 2.2 us)
Async XLA Ops:
  7.2 65.9 %copy-start = (bf16[256,1024]{1,0:T(8,128)(2,1)S(1)}, bf16[256,1024]{1,0:T(8,128)(2,1)}, u32[]{:S(2)}) copy-start(bf16[256,1024]{1,0:T(8,128)(2,1)} %param.36) | copy-start | bytes 1572868
  7.2 14.8 %copy-start.4 = (bf16[128,56,80]{0,2,1:T(8,128)(2,1)S(1)}, bf16[128,56,80]{0,2,1:T(8,128)(2,1)}, u32[]{:S(2)}) copy-start(bf16[128,56,80]{0,2,1:T(8,128)(2,1)} %param.22) | copy-start | bytes 3440644
  7.2 33.5 %all-gather.3.cloned.1.call-start = ((), (), s32[]{:S(2)}) async-start(), calls=%async_computation.5 | async-start | bytes 1679360 | tf_op jit(solution)/shard_map/all_gather | solution.py:321
  12.9 31.5 %copy-start.13 = (s32[128]{0:T(128)}, s32[128]{0:T(128)S(1)}, u32[]{:S(2)}) copy-start(s32[128]{0:T(128)S(1)} %get-tuple-element.42.arrival_s) | copy-start | bytes 1540
  13.6 30.8 %copy-start.9 = (s32[128]{0:T(128)}, s32[128]{0:T(128)S(1)}, u32[]{:S(2)}) copy-start(s32[128]{0:T(128)S(1)} %get-tuple-element.62.slot_s) | copy-start | bytes 1540
  14.5 14.9 %all-to-all-start = ((s32[32,2,128]{2,1,0:T(2,128)}), s32[32,2,128]{2,1,0:T(2,128)S(1)}, u32[]{:S(2)}, u32[]{:S(2)}) async-start(s32[32,2,128]{2,1,0:T(2,128)} %broadcast_in_dim.171), calls=%async_computation | async-start | bytes 65536 | tf_op jit(solution)/shard_map/all_to_all | solution.py:306
  22.0 82.8 %reduce-scatter.3.cloned.1.call-start = ((), (), s32[]{:S(2)}) async-start(), calls=%async_computation.6 | async-start | bytes 2293760 | tf_op jit(solution)/shard_map/reduce_scatter | solution.py:356
  44.4 1.1 copy-start.11
  45.4 1.0 copy-start.17
  46.5 1.4 copy-start.18
  47.9 1.4 copy-start.19
  76.0 30.7 %copy-start.6 = (bf16[128,8,256]{2,1,0:T(8,128)(2,1)S(1)}, bf16[128,8,256]{2,1,0:T(8,128)(2,1)}, u32[]{:S(2)}) copy-start(bf16[128,8,256]{2,1,0:T(8,128)(2,1)} %param.27) | copy-start | bytes 1572868
  76.0 30.9 %copy-start.8 = (f32[9,256]{1,0:T(8,128)S(1)}, f32[9,256]{1,0:T(8,128)}, u32[]{:S(2)}) copy-start(f32[9,256]{1,0:T(8,128)} %param.40) | copy-start | bytes 27652
  76.0 62.6 %all-gather.5.cloned.1.call-start = ((), (), s32[]{:S(2)}) async-start(), calls=%async_computation.7 | async-start | bytes 2293760 | tf_op jit(solution)/shard_map/all_gather | solution.py:361
  106.9 71.5 %all-to-all-start.2 = ((bf16[64,2,72,256]{3,2,1,0:T(8,128)(2,1)}), bf16[64,2,72,256]{3,2,1,0:T(8,128)(2,1)}, u32[]{:S(2)}, u32[]{:S(2)}) async-start(bf16[64,2,72,256]{3,2,1,0:T(8,128)(2,1)} %get-tuple-element.11), calls=%async_computation.4 | async-start | bytes 9437184 | tf_op jit(solution)/shard_map/all_to_all | solution.py:350
  114.1 27.2 %copy-start.12 = (f32[1024]{0:T(1024)S(1)}, f32[1024]{0:T(1024)}, u32[]{:S(2)}) copy-start(f32[1024]{0:T(1024)} %param.37) | copy-start | bytes 12292
  114.1 61.6 %reduce-scatter.5.cloned.1.call-start = ((), (), s32[]{:S(2)}) async-start(), calls=%async_computation.8 | async-start | bytes 2293760 | tf_op jit(solution)/shard_map/reduce_scatter | solution.py:382
  138.6 2.1 copy-start.2
  141.3 1.0 copy-start.20
  142.3 1.0 copy-start.5
  143.4 0.7 copy-start.15
  143.4 0.7 copy-start.16
  144.0 1.0 copy-start.7
  147.4 28.3 %copy-start.3 = (bf16[896,256]{1,0:T(8,128)(2,1)S(1)}, bf16[896,256]{1,0:T(8,128)(2,1)}, u32[]{:S(2)}) copy-start(bf16[896,256]{1,0:T(8,128)(2,1)} %add_convert_fusion.1) | copy-start | bytes 1376260
  147.5 29.5 %copy-start.10 = (s32[128]{0:T(128)S(1)}, s32[128]{0:T(128)}, u32[]{:S(2)}) copy-start(s32[128]{0:T(128)} %copy-done.9) | copy-start | bytes 1540
  178.4 20.8 %all-to-all-start.1 = ((bf16[64,15,256]{2,1,0:T(8,128)(2,1)}), bf16[64,15,256]{2,1,0:T(8,128)(2,1)S(1)}, u32[]{:S(2)}, u32[]{:S(2)}) async-start(bf16[64,15,256]{2,1,0:T(8,128)(2,1)} %copy.55), calls=%async_computation.3 | async-start | bytes 1048576 | tf_op jit(solution)/shard_map/all_to_all | solution.py:415
  185.5 13.7 %copy-start.14 = (s32[128]{0:T(128)S(1)}, s32[128]{0:T(128)}, u32[]{:S(2)}) copy-start(s32[128]{0:T(128)} %copy-done.13) | copy-start | bytes 1540
  199.2 2.4 %copy-start.1 = (bf16[256,1024]{1,0:T(8,128)(2,1)S(1)}, bf16[256,1024]{1,0:T(8,128)(2,1)}, u32[]{:S(2)}) copy-start(bf16[256,1024]{1,0:T(8,128)(2,1)} %param.36) | copy-start | bytes 1572868
Sparse Core Ops, SparseCore 0:
  10.2 30.4 all-gather.2
  76.1 28.5 reduce-scatter.2
  107.0 31.5 all-gather.4
  147.1 28.5 reduce-scatter.4

commit v3 on v2

--- a/solution.py
+++ b/solution.py
@@ -15,6 +15,7 @@
 CACHE = 70
 CAP = 2
 HEAD = 128
+CONV_CACHE = 8
 LANES = 128
 BLOCK = 16
 SPAN = 80
@@ -22,13 +23,6 @@
 CHUNK = 10
 
 masked_score = -1e30
-
-
-def layer_norm(values_in, scale_gain):
-    average = jnp.mean(values_in, axis=-1, keepdims=True)
-    centered = values_in - average
-    spread = jnp.mean(centered * centered, axis=-1, keepdims=True)
-    return centered * lax.rsqrt(spread + 1e-05) * scale_gain
 
 
 def send_slots(new_slot, own_index, peer_count):
@@ -113,7 +107,7 @@
             (((1,), (0,)), ((), ())),
             preferred_element_type=jnp.float32,
         )
-        context_ref[:, :, lanes] = context.reshape(FRAMES, BLOCK, LANES).astype(jnp.bfloat16)
+        context_ref[0, :, :, lanes] = context.reshape(FRAMES, BLOCK, LANES).astype(jnp.bfloat16)
 
     shift = valid - 1
     first = ((shift & 1) != 0)[None]
@@ -152,7 +146,9 @@
     lax.fori_loop(0, BLOCK, pack, 0)
 
 
-def attend(valid_old, fill_old, bucket, queries, key_new, value_new, key_cache, value_cache, slots):
+def attend(
+    valid_old, fill_old, bucket, queries, key_new, value_new, key_cache, value_cache, slots, groups
+):
     stream_count = key_cache.shape[1]
     width = key_cache.shape[2]
     heads = width // HEAD
@@ -163,6 +159,7 @@
     def block(rows):
         return pl.BlockSpec((rows, BLOCK, width), lambda i, *_: (0, i, 0))
 
+    per_group = stream_count // groups // BLOCK
     scalar = pl.BlockSpec((BLOCK, LANES), lambda i, *_: (i, 0))
     return pl.pallas_call(
         attend_body,
@@ -179,7 +176,9 @@
                 scalar,
             ],
             out_specs=[
-                block(FRAMES),
+                pl.BlockSpec(
+                    (1, FRAMES, BLOCK, width), lambda i, *_: (i // per_group, 0, i % per_group, 0)
+                ),
                 block(CACHE),
                 block(CACHE),
                 pl.BlockSpec((slots, 2, KEEP, width), lambda i, *_: (0, 0, 0, 0)),
@@ -187,7 +186,7 @@
             scratch_shapes=[pltpu.VMEM((2, heads, KEEP * BLOCK, LANES), jnp.float32)],
         ),
         out_shape=[
-            jax.ShapeDtypeStruct((FRAMES, stream_count, width), jnp.bfloat16),
+            jax.ShapeDtypeStruct((groups, FRAMES, stream_count // groups, width), jnp.bfloat16),
             jax.ShapeDtypeStruct((CACHE, stream_count, width), jnp.bfloat16),
             jax.ShapeDtypeStruct((CACHE, stream_count, width), jnp.bfloat16),
             jax.ShapeDtypeStruct((slots, 2, KEEP, width), jnp.bfloat16),
@@ -266,6 +265,181 @@
         out_shape=[shape, shape],
         name="place",
     )(arrival, received, key_rows, value_rows)
+
+
+def head_body(
+    place_s, frames_ref, own_ref, near_ref, far_ref, next_ref, gain_ref, *rest
+):
+    weights, outs, inputs_ref, raw = rest[:3], rest[3:6], rest[6], rest[7]
+    member = place_s[0]
+    groups = raw.shape[0]
+    taps = frames_ref.shape[2]
+    width = raw.shape[2]
+    frames = frames_ref[0]
+    for offset, piece in enumerate((own_ref, near_ref, far_ref, next_ref)):
+        total = jnp.dot(frames, piece[:taps, :], preferred_element_type=jnp.float32)
+        total = total + piece[taps : taps + 16, :].astype(jnp.float32)[:1]
+        raw[(member + groups - offset) % groups] = total.astype(jnp.bfloat16)
+    values = [raw[g].astype(jnp.float32) for g in range(groups)]
+    model_width = groups * width
+    average = sum(jnp.sum(v, axis=1, keepdims=True) for v in values) * (1.0 / model_width)
+    values = [v - average for v in values]
+    spread = sum(jnp.sum(v * v, axis=1, keepdims=True) for v in values) * (1.0 / model_width)
+    scale = lax.rsqrt(spread + 1e-05)
+    normed = [
+        (v * scale * gain_ref[:, g * width : (g + 1) * width]).astype(jnp.bfloat16)
+        for g, v in enumerate(values)
+    ]
+    normed = jnp.concatenate(normed, axis=1)
+    for matrix, out in zip(weights, outs):
+        out[0] = jnp.dot(normed, matrix[...], preferred_element_type=jnp.float32).astype(
+            jnp.bfloat16
+        )
+    share = inputs_ref.shape[1]
+    for g in range(groups):
+        inputs_ref[0, :, g * width : (g + 1) * width] = raw[
+            g, pl.ds(pl.multiple_of(member * share, share), share), :
+        ]
+
+
+def head(member, frames, pieces, gain, matrices):
+    count, streams, taps = frames.shape
+    width = matrices[0].shape[1]
+    groups = len(pieces)
+
+    def whole(array):
+        return pl.BlockSpec(array.shape, lambda i, *_: (0, 0))
+
+    per_frame = pl.BlockSpec((1, streams, width), lambda i, *_: (i, 0, 0))
+    shape = jax.ShapeDtypeStruct((count, streams, width), jnp.bfloat16)
+    gain = gain[None, :]
+    return pl.pallas_call(
+        head_body,
+        grid_spec=pltpu.PrefetchScalarGridSpec(
+            num_scalar_prefetch=1,
+            grid=(count,),
+            in_specs=[pl.BlockSpec((1, streams, taps), lambda i, *_: (i, 0, 0))]
+            + [whole(p) for p in pieces]
+            + [whole(gain)]
+            + [whole(w) for w in matrices],
+            out_specs=[per_frame, per_frame, per_frame]
+            + [pl.BlockSpec((1, streams // groups, groups * width), lambda i, *_: (i, 0, 0))],
+            scratch_shapes=[pltpu.VMEM((groups, streams, width), jnp.bfloat16)],
+        ),
+        out_shape=[shape, shape, shape]
+        + [jax.ShapeDtypeStruct((count, streams // groups, groups * width), jnp.bfloat16)],
+        name="head",
+    )(member[None], frames, *pieces, gain, *matrices)
+
+
+def tail_body(place_s, *refs):
+    contexts, caches, rest = refs[:4], refs[4:8], refs[8:]
+    inputs_ref, gain_ref, valid_ref, own_ref, near_ref, far_low, far_high, next_ref = rest[:8]
+    smalls, out_ref = rest[8:12], rest[12]
+    member = place_s[0]
+    groups = len(contexts)
+    _, share, width = contexts[0].shape
+    rows = FRAMES * share
+    size = groups * width
+    half = 2 * size
+    sources = tuple(
+        zip(
+            contexts,
+            caches,
+            (own_ref, near_ref, far_low, next_ref),
+            (own_ref, near_ref, far_high, next_ref),
+            (half, half, 0, half),
+            smalls,
+        )
+    )
+
+    def grouped(operand, low_ref, start, sums):
+        for n in range(groups):
+            block = low_ref[start + n * width : start + (n + 1) * width, :]
+            part = jnp.dot(operand, block, preferred_element_type=jnp.float32)
+            part = part.astype(jnp.bfloat16).astype(jnp.float32)
+            sums[n] = part if sums[n] is None else sums[n] + part
+
+    attended = [None] * groups
+    for context_ref, _, low_ref, _, _, _ in sources:
+        grouped(context_ref[...].reshape(rows, width), low_ref, 0, attended)
+    middle = []
+    for n in range(groups):
+        inputs = inputs_ref[:, :, n * width : (n + 1) * width].reshape(rows, width)
+        middle.append((inputs.astype(jnp.float32) + attended[n]).astype(jnp.bfloat16))
+    values = [m.astype(jnp.float32) for m in middle]
+    average = sum(jnp.sum(v, axis=1, keepdims=True) for v in values) * (1.0 / size)
+    values = [v - average for v in values]
+    spread = sum(jnp.sum(v * v, axis=1, keepdims=True) for v in values) * (1.0 / size)
+    scale = lax.rsqrt(spread + 1e-05)
+    normed = jnp.concatenate(
+        [
+            (v * scale * gain_ref[:, n * width : (n + 1) * width]).astype(jnp.bfloat16)
+            for n, v in enumerate(values)
+        ],
+        axis=1,
+    )
+    valid = valid_ref[...]
+    shift = valid - 1
+    first = ((shift & 1) != 0)[None]
+    second = ((shift & 2) != 0)[None]
+    third = ((shift & 4) != 0)[None]
+    conv_term = [None] * groups
+    for step, (_, cache_ref, low_ref, high_ref, start, small_ref) in enumerate(sources):
+        group = (member + groups - step) % groups
+        glu_value = jnp.dot(
+            normed, high_ref[start : start + size, :], preferred_element_type=jnp.float32
+        )
+        glu_gate = jnp.dot(
+            normed, high_ref[start + size : start + 2 * size, :], preferred_element_type=jnp.float32
+        )
+        gated = (glu_value * jax.nn.sigmoid(glu_gate)).astype(jnp.bfloat16)
+        conv_in = jnp.concatenate(
+            [
+                cache_ref[...].astype(jnp.float32),
+                gated.astype(jnp.float32).reshape(FRAMES, share, width),
+            ],
+            axis=0,
+        )
+        depthwise = jnp.zeros((FRAMES, share, width), jnp.float32)
+        for tap in range(KERNEL):
+            depthwise = depthwise + small_ref[tap : tap + 1, :][None] * conv_in[tap : tap + FRAMES]
+        shaped = depthwise * small_ref[KERNEL : KERNEL + 1, :][None]
+        shaped = shaped + small_ref[KERNEL + 1 : KERNEL + 2, :][None]
+        activated = (shaped * jax.nn.sigmoid(shaped)).astype(jnp.bfloat16)
+        grouped(activated.reshape(rows, width), low_ref, size, conv_term)
+        moved = shift_rows(
+            jnp.concatenate([conv_in[1:], conv_in[-1:]], axis=0), first, second, third
+        )
+        out_ref[group, FRAMES:, :, :] = moved.astype(jnp.bfloat16)
+    frame = lax.broadcasted_iota(jnp.int32, (FRAMES, share, width), 0)
+    for n in range(groups):
+        total = (middle[n].astype(jnp.float32) + conv_term[n]).reshape(FRAMES, share, width)
+        out_ref[n, :FRAMES, :, :] = jnp.where(frame < valid[None], total, 0.0).astype(jnp.bfloat16)
+
+
+def tail(member, groups, *arrays):
+    _, share, width = arrays[0].shape
+    return pl.pallas_call(
+        tail_body,
+        in_specs=[pl.BlockSpec(memory_space=pltpu.SMEM)]
+        + [pl.BlockSpec(memory_space=pltpu.VMEM)] * len(arrays),
+        out_specs=pl.BlockSpec(memory_space=pltpu.VMEM),
+        out_shape=jax.ShapeDtypeStruct((groups, FRAMES + CONV_CACHE, share, width), jnp.bfloat16),
+        name="tail",
+    )(member[None], *arrays)
+
+
+def swap(chunks, member, count):
+    pieces = [lax.dynamic_index_in_dim(chunks, member, 0, False)]
+    for step in range(1, count):
+        chunk = lax.dynamic_index_in_dim(chunks, (member + step) % count, 0, False)
+        pieces.append(toward(chunk, step, count))
+    return pieces
+
+
+def toward(array, steps, count):
+    return lax.ppermute(array, "enc", [(i, (i + steps) % count) for i in range(count)])
 
 
 def on_device(
@@ -315,97 +489,78 @@
     valid_old = both_old // 128
     fill_old = both_old % 128
 
+    groups = lax.axis_size("enc")
+    taps = SUB * MELS
     with_bias = jnp.concatenate(
         [sub_weight, jnp.broadcast_to(sub_bias[None, :], (16, local_width))], axis=0
     )
-    with_bias = lax.all_gather(with_bias, "enc", axis=1, tiled=True)
-    model_width = with_bias.shape[1]
-    taps = SUB * MELS
-    stacked = spectra.transpose(1, 2, 0).reshape(FRAMES, taps, stream_count)
-    inputs = (
-        jnp.einsum("tks,kc->tsc", stacked, with_bias[:taps], preferred_element_type=jnp.float32)
-        + with_bias[taps].astype(jnp.float32)
-    ).astype(jnp.bfloat16)
-    flat_in = inputs.reshape(FRAMES * stream_count, model_width)
-    normed = layer_norm(flat_in.astype(jnp.float32), ln1_gain).astype(jnp.bfloat16)
-
-    def project(matrix):
+    sub_pieces = [with_bias] + [toward(with_bias, k, groups) for k in range(1, groups)]
+
+    def blocks(matrix):
         return (
-            jnp.dot(normed, matrix, preferred_element_type=jnp.float32)
-            .astype(jnp.bfloat16)
-            .reshape(FRAMES, stream_count, local_width)
-        )
-
+            matrix.reshape(local_width, groups, local_width)
+            .transpose(1, 0, 2)
+            .reshape(groups * local_width, local_width)
+        )
+
+    stack = jnp.concatenate([blocks(w_attn_out), blocks(w_conv_out), w_glu_value, w_glu_gate], axis=0)
+    half = stack.shape[0] // 2
+    near = toward(stack, 1, groups)
+    after = toward(stack, -1, groups)
+    far_low = toward(near[:half], 1, groups)
+    far_high = toward(after[half:], -1, groups)
+    small = jnp.concatenate(
+        [depth_kernel, norm_scale[None], norm_shift[None], jnp.zeros((5, local_width), jnp.float32)],
+        axis=0,
+    )
+    small_near, small_far, small_next = [toward(small, k, groups) for k in range(1, groups)]
+    share = stream_count // groups
+    cache_share = swap(
+        conv_cache.reshape(groups, share, CONV_CACHE, local_width).transpose(0, 2, 1, 3),
+        member,
+        groups,
+    )
+
+    frames = spectra.transpose(1, 2, 0).reshape(FRAMES, taps, stream_count).transpose(0, 2, 1)
+    queries, key_new, value_new, inputs = head(
+        member, frames, sub_pieces, ln1_gain, (w_query, w_key, w_value)
+    )
     context, key_rows, value_rows, leaving_rows = attend(
         valid_old,
         fill_old,
         bucket,
-        project(w_query),
-        project(w_key),
-        project(w_value),
+        queries,
+        key_new,
+        value_new,
         key_cache.transpose(1, 0, 2),
         value_cache.transpose(1, 0, 2),
         slots,
+        groups,
     )
     received = lax.all_to_all(leaving_rows, "front", split_axis=0, concat_axis=0, tiled=True)
-    partial_out = jnp.dot(
-        context.reshape(FRAMES * stream_count, local_width),
-        w_attn_out,
-        preferred_element_type=jnp.float32,
-    )
-    attended = lax.psum_scatter(
-        partial_out.astype(jnp.bfloat16), "enc", scatter_dimension=1, tiled=True
-    ).astype(jnp.float32)
-    own_inputs = lax.dynamic_slice_in_dim(flat_in, member * local_width, local_width, 1)
-    middle_slice = (own_inputs.astype(jnp.float32) + attended).astype(jnp.bfloat16)
-    middle = lax.all_gather(middle_slice, "enc", axis=1, tiled=True)
-    normed_second = layer_norm(middle.astype(jnp.float32), ln2_gain).astype(jnp.bfloat16)
-    glu_value = jnp.dot(normed_second, w_glu_value, preferred_element_type=jnp.float32)
-    glu_gate = jnp.dot(normed_second, w_glu_gate, preferred_element_type=jnp.float32)
-    gated = (
-        (glu_value * jax.nn.sigmoid(glu_gate))
-        .astype(jnp.bfloat16)
-        .reshape(FRAMES, stream_count, local_width)
-    )
-    conv_in = jnp.concatenate([conv_cache.transpose(1, 0, 2), gated], axis=0)
-    depthwise = jnp.zeros((FRAMES, stream_count, local_width), jnp.float32)
-    for kernel_tap in range(KERNEL):
-        depthwise = depthwise + depth_kernel[kernel_tap] * conv_in[
-            kernel_tap : kernel_tap + FRAMES
-        ].astype(jnp.float32)
-    shaped = depthwise * norm_scale + norm_shift
-    activated = (
-        (shaped * jax.nn.sigmoid(shaped))
-        .astype(jnp.bfloat16)
-        .reshape(FRAMES * stream_count, local_width)
-    )
-    conv_term = lax.psum_scatter(
-        jnp.dot(activated, w_conv_out, preferred_element_type=jnp.float32).astype(jnp.bfloat16),
-        "enc",
-        scatter_dimension=1,
-        tiled=True,
-    ).astype(jnp.float32)
-    frame_ok = jnp.arange(FRAMES, dtype=jnp.int32)[:, None] < valid_old[None, :]
-    encoded = jnp.where(
-        frame_ok[:, :, None],
-        (middle_slice.astype(jnp.float32) + conv_term).reshape(
-            FRAMES, stream_count, local_width
-        ),
-        0.0,
-    ).astype(jnp.bfloat16)
-    shift = (valid_old - 1)[None, :, None]
-    conv_out = shift_rows(conv_in[1:], (shift & 1) != 0, (shift & 2) != 0, (shift & 4) != 0)
-    conv_out = jnp.concatenate(
-        [
-            conv_out,
-            jnp.where(shift == 6, conv_in[14:15], jnp.where(shift == 5, conv_in[13:14],
-            jnp.where(shift == 4, conv_in[12:13], jnp.where(shift == 3, conv_in[11:12],
-            jnp.where(shift == 2, conv_in[10:11], jnp.where(shift == 1, conv_in[9:10],
-            conv_in[8:9]))))))
-        ],
-        axis=0,
-    )
-    finished = jnp.concatenate([encoded, conv_out], axis=0)
+    context = swap(context, member, groups)
+    valid_share = lax.dynamic_slice_in_dim(valid_old, member * share, share, 0)
+    ended = tail(
+        member,
+        groups,
+        *context,
+        *cache_share,
+        inputs,
+        ln2_gain[None, :],
+        jnp.broadcast_to(valid_share[:, None], (share, local_width)),
+        stack,
+        near,
+        far_low,
+        far_high,
+        after,
+        small,
+        small_near,
+        small_far,
+        small_next,
+    )
+    ended = swap(ended, member, groups)
+    ended = jnp.concatenate((ended[::-1] + ended[::-1])[:-1], axis=1)
+    finished = lax.dynamic_slice_in_dim(ended, (groups - 1 - member) * share, stream_count, 1)
     picker = (
         bucket[None, :] == jnp.arange(slots, dtype=jnp.int32)[:, None]
     ).astype(jnp.bfloat16)

time: 210 us -> 268 us (1.28)
  waiting for transfers between devices: 98.1 us -> 134 us
  Pallas kernels: 34.6 us -> 53.5 us
  blocking collectives: 0 us -> 18.7 us
  starting transfers between devices: 22.1 us -> 39.1 us
  other arithmetic: 16 us -> 0.86 us
  matrix products: 14 us -> 0.78 us
  between operations: 14.2 us -> 1.26 us
  local copies, waits for them, and re-layouts: 9.24 us -> 19.1 us
    ppermute x0 -> x19, waiting for transfers between devices: none -> 76.4 us  [toward(): lax.ppermute(array, 'enc', [(i, (i + steps) % count) for i in range(count)])]
    all_to_all x1, waiting for transfers between devices: 0.01 us -> 57.4 us  [on_device(): lax.all_to_all(leaving_rows, 'front', split_axis=0, concat_axis=0, tiled=...]
    reduce_scatter x2 -> x0, waiting for transfers between devices: 56.7 us -> none  [the longest x1 28.7 us: on_device(): lax.psum_scatter(partial_out.astype(jnp.bfloat16), 'enc', scatter_dimensi...]
    all_gather x2 -> x0, waiting for transfers between devices: 35.4 us -> none  [the longest x1 24.3 us: on_device(): middle = lax.all_gather(middle_slice, 'enc', axis=1, tiled=True)]
    ppermute x0 -> x19, starting transfers between devices: none -> 26.9 us  [toward(): lax.ppermute(array, 'enc', [(i, (i + steps) % count) for i in range(count)])]
    pallas_call x0 -> x2, Pallas kernels: none -> 18.8 us  [the longest x1 10.2 us: head(): pl.pallas_call(head_body, grid_spec=pltpu.PrefetchScalarGridSpec(num_scal...]
    all_to_all x0 -> x1, blocking collectives: none -> 18.7 us  [on_device(): lax.all_to_all(leaving_end, 'front', split_axis=0, concat_axis=0, tiled=T...]
    dot_general x7 -> x0, matrix products: 10.3 us -> none  [the longest x3 4.25 us: project(): jnp.dot(normed, matrix, preferred_element_type=jnp.float32)]
  transfers between devices with their start and end apart: 7 -> 21, of which waited for: 5 -> 10; matrix products, arithmetic and copies ran while one was open for 8% -> 5% of each run, Pallas kernels for 7% -> 12%
where the time goes in v3:
time: 268 us; the launch traced here: 267 us
  waiting for transfers between devices  134 us (50%)
  Pallas kernels  53.5 us (20%)
  starting transfers between devices  39.1 us (15%)
  local copies, waits for them, and re-layouts  19.1 us (7%)
  blocking collectives  18.7 us (7%)
    ppermute x19, waiting for transfers between devices, toward(): lax.ppermute(array, 'enc', [(i, (i + steps) % count) for i in range(count)])  76.4 us
    all_to_all x1, waiting for transfers between devices, on_device(): lax.all_to_all(leaving_rows, 'front', split_axis=0, concat_axis=0, tiled=...  57.4 us
    ppermute x19, starting transfers between devices, toward(): lax.ppermute(array, 'enc', [(i, (i + steps) % count) for i in range(count)])  26.9 us
    pallas_call x1, Pallas kernels, attend(): pl.pallas_call(attend_body, grid_spec=pltpu.PrefetchScalarGridSpec(num_sc...  21.1 us
    all_to_all x1, blocking collectives, on_device(): lax.all_to_all(leaving_end, 'front', split_axis=0, concat_axis=0, tiled=T...  18.7 us
    pallas_call x1, Pallas kernels, place(): pl.pallas_call(place_body, grid_spec=pltpu.PrefetchScalarGridSpec(num_sca...  13.6 us
    pallas_call x1, Pallas kernels, head(): pl.pallas_call(head_body, grid_spec=pltpu.PrefetchScalarGridSpec(num_scal...  10.2 us
    pallas_call x1, Pallas kernels, tail(): pl.pallas_call(tail_body, in_specs=[pl.BlockSpec(memory_space=pltpu.SMEM)...  8.65 us
  transfers between devices with their start and end apart: 21, of which 10 were waited for; matrix products, arithmetic and copies ran while one was open for 5% of the time, Pallas kernels for 12%

profile of v3, /device:TPU:0, one launch (start us, length us, event | category | flops | bytes accessed | tf_op | source)
XLA Modules:
  0.0 267.1 jit_solution(5187546083790893086)
XLA Ops:
  0.7 1.2 copy.90
  1.8 1.1 copy.89
  3.2 2.1 collective-permute-start.9
  5.3 2.2 collective-permute-start.11
  7.7 3.4 %collective-permute-start.14 = (f32[16,256]{1,0:T(8,128)S(1)}, f32[16,256]{1,0:T(8,128)S(1)}, u32[]{:S(2)}, u32[]{:S(2)}) collective-permute-start(f32[16,256]{1,0:T(8,128)S(1)} %maximum_maximum_fusion.refs_16_), channel_id=1, source_target_pairs={{0,2},{1,3},{2,0},{3,1},{4,6},{5,7},{6,4},{7,5},{8,10},{9,11},{10,... | collective-permute-start | bytes 49160 | tf_op jit(solution)/shard_map/ppermute | solution.py:442
  11.1 1.0 collective-permute-start.15
  12.5 0.7 broadcast_in_dim.117
  13.3 7.3 %all-to-all-start = ((s32[32,2,128]{2,1,0:T(2,128)}), s32[32,2,128]{2,1,0:T(2,128)S(1)}, u32[]{:S(2)}, u32[]{:S(2)}) async-start(s32[32,2,128]{2,1,0:T(2,128)} %broadcast_in_dim.117), calls=%async_computation | async-start | bytes 65536 | tf_op jit(solution)/shard_map/all_to_all | solution.py:480
  20.9 32.4 %collective-permute-done.9.refs_12_ = bf16[4096,256]{1,0:T(8,128)(2,1)} collective-permute-done((bf16[4096,256]{1,0:T(8,128)(2,1)S(1)}, bf16[4096,256]{1,0:T(8,128)(2,1)}, u32[]{:S(2)}, u32[]{:S(2)}) %collective-permute-start.9) | collective-permute-done | bytes 2097184 | tf_op jit(solution)/shard_map/ppermute | solution.py:442
  53.3 2.3 slice.21
  55.6 2.4 slice.22
  58.0 3.1 %collective-permute-start.12 = (bf16[2048,256]{1,0:T(8,128)(2,1)}, bf16[2048,256]{1,0:T(8,128)(2,1)}, u32[]{:S(2)}, u32[]{:S(2)}) collective-permute-start(bf16[2048,256]{1,0:T(8,128)(2,1)} %slice.22), channel_id=1, source_target_pairs={{0,3},{1,0},{2,1},{3,2},{4,7},{5,4},{6,5},{7,6},{8,11},{9,8},{10,9... | collective-permute-start | bytes 3145736 | tf_op jit(solution)/shard_map/ppermute | solution.py:442
  61.2 1.8 copy.63
  63.4 2.1 collective-permute-start.1
  65.5 1.2 collective-permute-start.2
  66.8 27.1 %collective-permute-done.near_ref = bf16[656,256]{1,0:T(8,128)(2,1)S(1)} collective-permute-done((bf16[656,256]{1,0:T(8,128)(2,1)S(1)}, bf16[656,256]{1,0:T(8,128)(2,1)S(1)}, u32[]{:S(2)}, u32[]{:S(2)}) %collective-permute-start) | collective-permute-done | bytes 335904 | tf_op jit(solution)/shard_map/ppermute | solution.py:442
  93.9 2.8 %collective-permute-done.1.far_ref = bf16[656,256]{1,0:T(8,128)(2,1)S(1)} collective-permute-done((bf16[656,256]{1,0:T(8,128)(2,1)S(1)}, bf16[656,256]{1,0:T(8,128)(2,1)S(1)}, u32[]{:S(2)}, u32[]{:S(2)}) %collective-permute-start.1) | collective-permute-done | bytes 335904 | tf_op jit(solution)/shard_map/ppermute | solution.py:442
  96.7 0.9 collective-permute-start.7
  97.6 0.9 collective-permute-done.2.next_ref
  98.5 3.7 %collective-permute-start.8 = (bf16[8,32,256]{2,1,0:T(8,128)(2,1)S(1)}, bf16[8,32,256]{2,1,0:T(8,128)(2,1)S(1)}, u32[]{:S(2)}, u32[]{:S(2)}) collective-permute-start(bf16[8,32,256]{2,1,0:T(8,128)(2,1)S(1)} %bitcast.89), channel_id=1, source_target_pairs={{0,3},{1,0},{2,1},{3,2},{4,7},{5,4},{6,5},{7,6},{8,11},{9,8},{10,9... | collective-permute-start | bytes 393224 | tf_op jit(solution)/shard_map/ppermute | solution.py:442
  102.2 10.2 %head.1 = (bf16[7,128,256]{2,1,0:T(8,128)(2,1)}, bf16[7,128,256]{2,1,0:T(8,128)(2,1)}, bf16[7,128,256]{2,1,0:T(8,128)(2,1)}, bf16[7,32,1024]{2,1,0:T(8,128)(2,1)}) custom-call(s32[1]{0:T(128)} %bitcast.place_s, bf16[7,128,640]{2,1,0:T(8,128)(2,1)} %bitcast.79, bf16[656,256]{1,0:T(8,128)(2,1)} %copy-done.1, bf16[656,256]{1,0:T(8,128)(2,1)} %copy-done.6, ...), custom_call_target="tpu_custom_call" | custom-call | tf_op jit(solution)/shard_map/head/pallas_call | solution.py:316
  112.4 0.7 broadcast_in_dim.121.valid_ref
  113.1 0.7 broadcast_in_dim.122.fill_ref
  113.8 21.1 %attend.1 = (bf16[4,7,32,256]{3,2,1,0:T(8,128)(2,1)}, bf16[70,128,256]{2,1,0:T(8,128)(2,1)}, bf16[70,128,256]{2,1,0:T(8,128)(2,1)}, bf16[64,2,72,256]{3,2,1,0:T(8,128)(2,1)}) custom-call(s32[128]{0:T(128)} %copy-done.21, bf16[7,128,256]{2,1,0:T(8,128)(2,1)} %get-tuple-element.14.query_ref, bf16[7,128,256]{2,1,0:T(8,128)(2,1)} %get-tuple-element.15.key_new_ref, ...), custom_call_target="tpu_custom_call" | custom-call | tf_op jit(solution)/shard_map/attend/pallas_call | solution.py:164
  135.0 1.8 dynamic-slice_bitcast_fusion.3
  136.8 2.1 collective-permute-start.4
  138.8 1.4 collective-permute-start.5
  140.2 0.7 copy.94
  141.0 3.0 %collective-permute-done.3.refs_1_ = bf16[7,32,256]{2,1,0:T(8,128)(2,1)S(1)} collective-permute-done((bf16[7,32,256]{2,1,0:T(8,128)(2,1)S(1)}, bf16[7,32,256]{2,1,0:T(8,128)(2,1)S(1)}, u32[]{:S(2)}, u32[]{:S(2)}) %collective-permute-start.3) | collective-permute-done | bytes 114720 | tf_op jit(solution)/shard_map/ppermute | solution.py:442
  144.0 0.9 collective-permute-done.5.refs_3_
  144.9 0.7 broadcast_in_dim.124.refs_10_
  145.6 8.7 %tail.1 = bf16[4,15,32,256]{3,2,1,0:T(8,128)(2,1)} custom-call(s32[1]{0:T(128)} %bitcast.place_s, bf16[7,32,256]{2,1,0:T(8,128)(2,1)} %get-tuple-element.58.refs_0_, bf16[7,32,256]{2,1,0:T(8,128)(2,1)} %copy-done.13, bf16[7,32,256]{2,1,0:T(8,128)(2,1)} %copy-done.14, bf16[7,32,256]{2,1,0:T(8,128)(2,1)} %copy-done.15, bf16[8,32,256]{2,1,0:T(8,128)(2,1)} %bitcast.85, ...), custom_call_target="tpu_custom_call" | custom-call | tf_op jit(solution)/shard_map/tail/pallas_call | solution.py:423
  154.2 1.2 dynamic-slice_bitcast_fusion
  155.5 2.7 collective-permute-start.16
  158.4 0.7 collective-permute-start.18
  159.1 5.6 %collective-permute-done.16 = bf16[15,32,256]{2,1,0:T(8,128)(2,1)S(1)} collective-permute-done((bf16[15,32,256]{2,1,0:T(8,128)(2,1)S(1)}, bf16[15,32,256]{2,1,0:T(8,128)(2,1)S(1)}, u32[]{:S(2)}, u32[]{:S(2)}) %collective-permute-start.16) | collective-permute-done | bytes 245792 | tf_op jit(solution)/shard_map/ppermute | solution.py:442
  164.7 1.2 collective-permute-done.17
  166.0 2.4 collective-permute-done.18
  168.4 1.0 bitcast_dynamic-update-slice_fusion
  169.5 0.3 convolution_convert_fusion.1
  169.8 0.3 copy.70
  170.1 18.7 %all_to_all.19 = bf16[64,15,256]{2,1,0:T(8,128)(2,1)S(1)} all-to-all(bf16[64,15,256]{2,1,0:T(8,128)(2,1)S(1)} %copy.70), channel_id=1, replica_groups=mesh['front'=32,'enc'=4] {'front'}, dimensions={0} | all-to-all | bytes 983040 | tf_op jit(solution)/shard_map/all_to_all | solution.py:570
  188.8 4.9 %all-to-all-start.2 = ((bf16[64,2,72,256]{3,2,1,0:T(8,128)(2,1)}), bf16[64,2,72,256]{3,2,1,0:T(8,128)(2,1)}, u32[]{:S(2)}, u32[]{:S(2)}) async-start(bf16[64,2,72,256]{3,2,1,0:T(8,128)(2,1)} %get-tuple-element.19), calls=%async_computation.2 | async-start | bytes 9437184 | tf_op jit(solution)/shard_map/all_to_all | solution.py:540
  193.7 0.5 fusion.1
  194.2 1.1 copy.73
  195.3 0.8 slice_bitcast_fusion.1
  196.1 57.4 %all-to-all-done.2.got_ref = bf16[64,2,72,256]{3,2,1,0:T(8,128)(2,1)} async-done(((bf16[64,2,72,256]{3,2,1,0:T(8,128)(2,1)}), bf16[64,2,72,256]{3,2,1,0:T(8,128)(2,1)}, u32[]{:S(2)}, u32[]{:S(2)}) %all-to-all-start.2) | async-done | bytes 4718624 | tf_op jit(solution)/shard_map/all_to_all | solution.py:540
  253.5 13.6 %place.1 = (bf16[70,128,256]{2,1,0:T(8,128)(2,1)}, bf16[70,128,256]{2,1,0:T(8,128)(2,1)}) custom-call(s32[128]{0:T(128)} %copy-done.23, bf16[64,2,72,256]{3,2,1,0:T(8,128)(2,1)} %all-to-all-done.2.got_ref, bf16[70,128,256]{2,1,0:T(8,128)(2,1)} %get-tuple-element.20.key_ref, bf16[70,128,256]{2,1,0:T(8,128)(2,1)} %get-tuple-element.21.value_ref), custom_call_target="tpu_custom_call" | custom-call | tf_op jit(solution)/shard_map/place/pallas_call | solution.py:252
  (110 shorter events, 2.0 us)
Async XLA Ops:
  0.6 2.3 copy-start.5
  2.9 4.6 %copy-start.20 = (f32[9,256]{1,0:T(8,128)S(1)}, f32[9,256]{1,0:T(8,128)}, u32[]{:S(2)}) copy-start(f32[9,256]{1,0:T(8,128)} %param.40) | copy-start | bytes 27652
  2.9 4.6 %copy-start.25 = (f32[256]{0:T(256)S(1)}, f32[256]{0:T(256)}, u32[]{:S(2)}) copy-start(f32[256]{0:T(256)} %param.42) | copy-start | bytes 3076
  2.9 4.6 %copy-start.26 = (f32[256]{0:T(256)S(1)}, f32[256]{0:T(256)}, u32[]{:S(2)}) copy-start(f32[256]{0:T(256)} %param.41) | copy-start | bytes 3076
  3.0 9.1 %copy-start.24 = (s32[128]{0:T(128)S(1)}, s32[128]{0:T(128)}, u32[]{:S(2)}) copy-start(s32[128]{0:T(128)} %param.29) | copy-start | bytes 1540
  3.0 9.3 %copy-start.29 = (s32[128]{0:T(128)S(1)}, s32[128]{0:T(128)}, u32[]{:S(2)}) copy-start(s32[128]{0:T(128)} %param.31) | copy-start | bytes 1540
  3.0 9.3 %copy-start.30 = (s32[128]{0:T(128)S(1)}, s32[128]{0:T(128)}, u32[]{:S(2)}) copy-start(s32[128]{0:T(128)} %param.30) | copy-start | bytes 1540
  3.0 17.6 %copy-start.28 = (s32[128]{0:T(128)S(1)}, s32[128]{0:T(128)}, u32[]{:S(2)}) copy-start(s32[128]{0:T(128)} %param.28) | copy-start | bytes 1540
  3.1 54.8 %copy-start = (bf16[4096,256]{1,0:T(8,128)(2,1)}, bf16[4096,256]{1,0:T(8,128)(2,1)S(1)}, u32[]{:S(2)}) copy-start(bf16[4096,256]{1,0:T(8,128)(2,1)S(1)} %pad_maximum_fusion.refs_11_) | copy-start | bytes 6291460
  3.2 50.1 %collective-permute-start.9 = (bf16[4096,256]{1,0:T(8,128)(2,1)S(1)}, bf16[4096,256]{1,0:T(8,128)(2,1)}, u32[]{:S(2)}, u32[]{:S(2)}) collective-permute-start(bf16[4096,256]{1,0:T(8,128)(2,1)S(1)} %pad_maximum_fusion.refs_11_), channel_id=1, source_target_pairs={{0,1},{1,2},{2,3},{3,0},{4,5},{5,6},{6,7},{7,4},{8,9},{9,10},{10,1... | collective-permute-start | bytes 6291464 | tf_op jit(solution)/shard_map/ppermute | solution.py:442
  5.3 50.3 %collective-permute-start.11 = (bf16[4096,256]{1,0:T(8,128)(2,1)S(1)}, bf16[4096,256]{1,0:T(8,128)(2,1)}, u32[]{:S(2)}, u32[]{:S(2)}) collective-permute-start(bf16[4096,256]{1,0:T(8,128)(2,1)S(1)} %pad_maximum_fusion.refs_11_), channel_id=1, source_target_pairs={{0,3},{1,0},{2,1},{3,2},{4,7},{5,4},{6,5},{7,6},{8,11},{9,8},{10,9... | collective-permute-start | bytes 6291464 | tf_op jit(solution)/shard_map/ppermute | solution.py:442
  7.6 50.4 %copy-start.16 = (f32[16,256]{1,0:T(8,128)}, f32[16,256]{1,0:T(8,128)S(1)}, u32[]{:S(2)}) copy-start(f32[16,256]{1,0:T(8,128)S(1)} %maximum_maximum_fusion.refs_16_) | copy-start | bytes 49156
  7.6 55.6 %collective-permute-start.13 = (f32[16,256]{1,0:T(8,128)S(1)}, f32[16,256]{1,0:T(8,128)S(1)}, u32[]{:S(2)}, u32[]{:S(2)}) collective-permute-start(f32[16,256]{1,0:T(8,128)S(1)} %maximum_maximum_fusion.refs_16_), channel_id=1, source_target_pairs={{0,1},{1,2},{2,3},{3,0},{4,5},{5,6},{6,7},{7,4},{8,9},{9,10},{10,1... | collective-permute-start | bytes 49160 | tf_op jit(solution)/shard_map/ppermute | solution.py:442
  7.7 55.7 %collective-permute-start.14 = (f32[16,256]{1,0:T(8,128)S(1)}, f32[16,256]{1,0:T(8,128)S(1)}, u32[]{:S(2)}, u32[]{:S(2)}) collective-permute-start(f32[16,256]{1,0:T(8,128)S(1)} %maximum_maximum_fusion.refs_16_), channel_id=1, source_target_pairs={{0,2},{1,3},{2,0},{3,1},{4,6},{5,7},{6,4},{7,5},{8,10},{9,11},{10,... | collective-permute-start | bytes 49160 | tf_op jit(solution)/shard_map/ppermute | solution.py:442
  11.1 54.4 %collective-permute-start.15 = (f32[16,256]{1,0:T(8,128)S(1)}, f32[16,256]{1,0:T(8,128)S(1)}, u32[]{:S(2)}, u32[]{:S(2)}) collective-permute-start(f32[16,256]{1,0:T(8,128)S(1)} %maximum_maximum_fusion.refs_16_), channel_id=1, source_target_pairs={{0,3},{1,0},{2,1},{3,2},{4,7},{5,4},{6,5},{7,6},{8,11},{9,8},{10,9... | collective-permute-start | bytes 49160 | tf_op jit(solution)/shard_map/ppermute | solution.py:442
  12.3 181.4 %copy-start.23 = (s32[128]{0:T(128)}, s32[128]{0:T(128)S(1)}, u32[]{:S(2)}) copy-start(s32[128]{0:T(128)S(1)} %get-tuple-element.47.arrival_s) | copy-start | bytes 1540
  13.3 49.9 %all-to-all-start = ((s32[32,2,128]{2,1,0:T(2,128)}), s32[32,2,128]{2,1,0:T(2,128)S(1)}, u32[]{:S(2)}, u32[]{:S(2)}) async-start(s32[32,2,128]{2,1,0:T(2,128)} %broadcast_in_dim.117), calls=%async_computation | async-start | bytes 65536 | tf_op jit(solution)/shard_map/all_to_all | solution.py:480
  20.8 81.3 %copy-start.21 = (s32[128]{0:T(128)}, s32[128]{0:T(128)S(1)}, u32[]{:S(2)}) copy-start(s32[128]{0:T(128)S(1)} %compare_select_fusion.1.slot_s) | copy-start | bytes 1540
  20.9 40.2 %copy-start.3 = (bf16[128,8,256]{2,1,0:T(8,128)(2,1)S(1)}, bf16[128,8,256]{2,1,0:T(8,128)(2,1)}, u32[]{:S(2)}) copy-start(bf16[128,8,256]{2,1,0:T(8,128)(2,1)} %param.27) | copy-start | bytes 1572868
  55.6 5.6 %copy-start.27 = (bf16[256]{0:T(256)(128)(2,1)S(1)}, bf16[256]{0:T(256)(128)(2,1)}, u32[]{:S(2)}) copy-start(bf16[256]{0:T(256)(128)(2,1)} %param.24) | copy-start | bytes 1540
  55.6 5.6 %copy-start.9 = (bf16[640,256]{1,0:T(8,128)(2,1)S(1)}, bf16[640,256]{1,0:T(8,128)(2,1)}, u32[]{:S(2)}) copy-start(bf16[640,256]{1,0:T(8,128)(2,1)} %param.23) | copy-start | bytes 983044
  55.6 5.7 %copy-start.2 = (bf16[128,56,80]{0,2,1:T(8,128)(2,1)S(1)}, bf16[128,56,80]{0,2,1:T(8,128)(2,1)}, u32[]{:S(2)}) copy-start(bf16[128,56,80]{0,2,1:T(8,128)(2,1)} %param.22) | copy-start | bytes 3440644
  55.6 89.3 %collective-permute-start.10 = (bf16[2048,256]{1,0:T(8,128)(2,1)}, bf16[2048,256]{1,0:T(8,128)(2,1)}, u32[]{:S(2)}, u32[]{:S(2)}) collective-permute-start(bf16[2048,256]{1,0:T(8,128)(2,1)} %slice.21), channel_id=1, source_target_pairs={{0,1},{1,2},{2,3},{3,0},{4,5},{5,6},{6,7},{7,4},{8,9},{9,10},{10,1... | collective-permute-start | bytes 3145736 | tf_op jit(solution)/shard_map/ppermute | solution.py:442
  58.0 86.9 %collective-permute-start.12 = (bf16[2048,256]{1,0:T(8,128)(2,1)}, bf16[2048,256]{1,0:T(8,128)(2,1)}, u32[]{:S(2)}, u32[]{:S(2)}) collective-permute-start(bf16[2048,256]{1,0:T(8,128)(2,1)} %slice.22), channel_id=1, source_target_pairs={{0,3},{1,0},{2,1},{3,2},{4,7},{5,4},{6,5},{7,6},{8,11},{9,8},{10,9... | collective-permute-start | bytes 3145736 | tf_op jit(solution)/shard_map/ppermute | solution.py:442
  61.2 41.0 %copy-start.1 = (bf16[656,256]{1,0:T(8,128)(2,1)}, bf16[656,256]{1,0:T(8,128)(2,1)S(1)}, u32[]{:S(2)}) copy-start(bf16[656,256]{1,0:T(8,128)(2,1)S(1)} %pad_maximum_fusion.1.own_ref) | copy-start | bytes 1007620
  63.2 49.2 %copy-start.17 = (f32[16,256]{1,0:T(8,128)}, f32[16,256]{1,0:T(8,128)S(1)}, u32[]{:S(2)}) copy-start(f32[16,256]{1,0:T(8,128)S(1)} %collective-permute-done.13.refs_17_) | copy-start | bytes 49156
  63.2 30.6 %collective-permute-start = (bf16[656,256]{1,0:T(8,128)(2,1)S(1)}, bf16[656,256]{1,0:T(8,128)(2,1)S(1)}, u32[]{:S(2)}, u32[]{:S(2)}) collective-permute-start(bf16[656,256]{1,0:T(8,128)(2,1)S(1)} %pad_maximum_fusion.1.own_ref), channel_id=1, source_target_pairs={{0,1},{1,2},{2,3},{3,0},{4,5},{5,6},{6,7},{7,4},{8,9},{9,10},{10,1... | collective-permute-start | bytes 1007624 | tf_op jit(solution)/shard_map/ppermute | solution.py:442
  63.3 71.6 %copy-start.18 = (f32[16,256]{1,0:T(8,128)}, f32[16,256]{1,0:T(8,128)S(1)}, u32[]{:S(2)}) copy-start(f32[16,256]{1,0:T(8,128)S(1)} %collective-permute-done.14.refs_18_) | copy-start | bytes 49156
  63.4 33.3 %collective-permute-start.1 = (bf16[656,256]{1,0:T(8,128)(2,1)S(1)}, bf16[656,256]{1,0:T(8,128)(2,1)S(1)}, u32[]{:S(2)}, u32[]{:S(2)}) collective-permute-start(bf16[656,256]{1,0:T(8,128)(2,1)S(1)} %pad_maximum_fusion.1.own_ref), channel_id=1, source_target_pairs={{0,2},{1,3},{2,0},{3,1},{4,6},{5,7},{6,4},{7,5},{8,10},{9,11},{10,... | collective-permute-start | bytes 1007624 | tf_op jit(solution)/shard_map/ppermute | solution.py:442
  65.5 69.5 %copy-start.19 = (f32[16,256]{1,0:T(8,128)}, f32[16,256]{1,0:T(8,128)S(1)}, u32[]{:S(2)}) copy-start(f32[16,256]{1,0:T(8,128)S(1)} %collective-permute-done.15.refs_19_) | copy-start | bytes 49156
  65.5 33.0 %collective-permute-start.2 = (bf16[656,256]{1,0:T(8,128)(2,1)S(1)}, bf16[656,256]{1,0:T(8,128)(2,1)S(1)}, u32[]{:S(2)}, u32[]{:S(2)}) collective-permute-start(bf16[656,256]{1,0:T(8,128)(2,1)S(1)} %pad_maximum_fusion.1.own_ref), channel_id=1, source_target_pairs={{0,3},{1,0},{2,1},{3,2},{4,7},{5,4},{6,5},{7,6},{8,11},{9,8},{10,9... | collective-permute-start | bytes 1007624 | tf_op jit(solution)/shard_map/ppermute | solution.py:442
  93.9 8.3 %copy-start.6 = (bf16[656,256]{1,0:T(8,128)(2,1)}, bf16[656,256]{1,0:T(8,128)(2,1)S(1)}, u32[]{:S(2)}) copy-start(bf16[656,256]{1,0:T(8,128)(2,1)S(1)} %collective-permute-done.near_ref) | copy-start | bytes 1007620
  93.9 42.8 %collective-permute-start.6 = (bf16[8,32,256]{2,1,0:T(8,128)(2,1)S(1)}, bf16[8,32,256]{2,1,0:T(8,128)(2,1)S(1)}, u32[]{:S(2)}, u32[]{:S(2)}) collective-permute-start(bf16[8,32,256]{2,1,0:T(8,128)(2,1)S(1)} %bitcast.91), channel_id=1, source_target_pairs={{0,1},{1,2},{2,3},{3,0},{4,5},{5,6},{6,7},{7,4},{8,9},{9,10},{10,1... | collective-permute-start | bytes 393224 | tf_op jit(solution)/shard_map/ppermute | solution.py:442
  96.7 5.6 %copy-start.7 = (bf16[656,256]{1,0:T(8,128)(2,1)}, bf16[656,256]{1,0:T(8,128)(2,1)S(1)}, u32[]{:S(2)}) copy-start(bf16[656,256]{1,0:T(8,128)(2,1)S(1)} %collective-permute-done.1.far_ref) | copy-start | bytes 1007620
  96.7 40.1 %collective-permute-start.7 = (bf16[8,32,256]{2,1,0:T(8,128)(2,1)S(1)}, bf16[8,32,256]{2,1,0:T(8,128)(2,1)S(1)}, u32[]{:S(2)}, u32[]{:S(2)}) collective-permute-start(bf16[8,32,256]{2,1,0:T(8,128)(2,1)S(1)} %bitcast.90), channel_id=1, source_target_pairs={{0,2},{1,3},{2,0},{3,1},{4,6},{5,7},{6,4},{7,5},{8,10},{9,11},{10,... | collective-permute-start | bytes 393224 | tf_op jit(solution)/shard_map/ppermute | solution.py:442
  98.5 3.7 %copy-start.8 = (bf16[656,256]{1,0:T(8,128)(2,1)}, bf16[656,256]{1,0:T(8,128)(2,1)S(1)}, u32[]{:S(2)}) copy-start(bf16[656,256]{1,0:T(8,128)(2,1)S(1)} %collective-permute-done.2.next_ref) | copy-start | bytes 1007620
  98.5 40.3 %collective-permute-start.8 = (bf16[8,32,256]{2,1,0:T(8,128)(2,1)S(1)}, bf16[8,32,256]{2,1,0:T(8,128)(2,1)S(1)}, u32[]{:S(2)}, u32[]{:S(2)}) collective-permute-start(bf16[8,32,256]{2,1,0:T(8,128)(2,1)S(1)} %bitcast.89), channel_id=1, source_target_pairs={{0,3},{1,0},{2,1},{3,2},{4,7},{5,4},{6,5},{7,6},{8,11},{9,8},{10,9... | collective-permute-start | bytes 393224 | tf_op jit(solution)/shard_map/ppermute | solution.py:442
  136.7 8.8 %copy-start.10 = (bf16[8,32,256]{2,1,0:T(8,128)(2,1)}, bf16[8,32,256]{2,1,0:T(8,128)(2,1)S(1)}, u32[]{:S(2)}) copy-start(bf16[8,32,256]{2,1,0:T(8,128)(2,1)S(1)} %collective-permute-done.6.refs_5_) | copy-start | bytes 393220
  136.7 7.2 %collective-permute-start.3 = (bf16[7,32,256]{2,1,0:T(8,128)(2,1)S(1)}, bf16[7,32,256]{2,1,0:T(8,128)(2,1)S(1)}, u32[]{:S(2)}, u32[]{:S(2)}) collective-permute-start(bf16[7,32,256]{2,1,0:T(8,128)(2,1)S(1)} %get-tuple-element.57), channel_id=1, source_target_pairs={{0,1},{1,2},{2,3},{3,0},{4,5},{5,6},{6,7},{7,4},{8,9},{9,10},{10,1... | collective-permute-start | bytes 344072 | tf_op jit(solution)/shard_map/ppermute | solution.py:442
  136.7 8.8 %copy-start.11 = (bf16[8,32,256]{2,1,0:T(8,128)(2,1)}, bf16[8,32,256]{2,1,0:T(8,128)(2,1)S(1)}, u32[]{:S(2)}) copy-start(bf16[8,32,256]{2,1,0:T(8,128)(2,1)S(1)} %collective-permute-done.7.refs_6_) | copy-start | bytes 393220
  136.8 7.2 %collective-permute-start.4 = (bf16[7,32,256]{2,1,0:T(8,128)(2,1)S(1)}, bf16[7,32,256]{2,1,0:T(8,128)(2,1)S(1)}, u32[]{:S(2)}, u32[]{:S(2)}) collective-permute-start(bf16[7,32,256]{2,1,0:T(8,128)(2,1)S(1)} %get-tuple-element.56), channel_id=1, source_target_pairs={{0,2},{1,3},{2,0},{3,1},{4,6},{5,7},{6,4},{7,5},{8,10},{9,11},{10,... | collective-permute-start | bytes 344072 | tf_op jit(solution)/shard_map/ppermute | solution.py:442
  138.8 6.7 %copy-start.12 = (bf16[8,32,256]{2,1,0:T(8,128)(2,1)}, bf16[8,32,256]{2,1,0:T(8,128)(2,1)S(1)}, u32[]{:S(2)}) copy-start(bf16[8,32,256]{2,1,0:T(8,128)(2,1)S(1)} %collective-permute-done.8.refs_7_) | copy-start | bytes 393220
  138.8 6.0 %collective-permute-start.5 = (bf16[7,32,256]{2,1,0:T(8,128)(2,1)S(1)}, bf16[7,32,256]{2,1,0:T(8,128)(2,1)S(1)}, u32[]{:S(2)}, u32[]{:S(2)}) collective-permute-start(bf16[7,32,256]{2,1,0:T(8,128)(2,1)S(1)} %get-tuple-element.55), channel_id=1, source_target_pairs={{0,3},{1,0},{2,1},{3,2},{4,7},{5,4},{6,5},{7,6},{8,11},{9,8},{10,9... | collective-permute-start | bytes 344072 | tf_op jit(solution)/shard_map/ppermute | solution.py:442
  155.5 9.2 %collective-permute-start.16 = (bf16[15,32,256]{2,1,0:T(8,128)(2,1)S(1)}, bf16[15,32,256]{2,1,0:T(8,128)(2,1)S(1)}, u32[]{:S(2)}, u32[]{:S(2)}) collective-permute-start(bf16[15,32,256]{2,1,0:T(8,128)(2,1)S(1)} %get-tuple-element.50), channel_id=1, source_target_pairs={{0,3},{1,0},{2,1},{3,2},{4,7},{5,4},{6,5},{7,6},{8,11},{9,8},{10,9... | collective-permute-start | bytes 737288 | tf_op jit(solution)/shard_map/ppermute | solution.py:442
  158.1 7.8 %collective-permute-start.17 = (bf16[15,32,256]{2,1,0:T(8,128)(2,1)S(1)}, bf16[15,32,256]{2,1,0:T(8,128)(2,1)S(1)}, u32[]{:S(2)}, u32[]{:S(2)}) collective-permute-start(bf16[15,32,256]{2,1,0:T(8,128)(2,1)S(1)} %get-tuple-element.49), channel_id=1, source_target_pairs={{0,2},{1,3},{2,0},{3,1},{4,6},{5,7},{6,4},{7,5},{8,10},{9,11},{10,... | collective-permute-start | bytes 737288 | tf_op jit(solution)/shard_map/ppermute | solution.py:442
  158.4 10.0 %collective-permute-start.18 = (bf16[15,32,256]{2,1,0:T(8,128)(2,1)S(1)}, bf16[15,32,256]{2,1,0:T(8,128)(2,1)S(1)}, u32[]{:S(2)}, u32[]{:S(2)}) collective-permute-start(bf16[15,32,256]{2,1,0:T(8,128)(2,1)S(1)} %get-tuple-element.48), channel_id=1, source_target_pairs={{0,1},{1,2},{2,3},{3,0},{4,5},{5,6},{6,7},{7,4},{8,9},{9,10},{10,1... | collective-permute-start | bytes 737288 | tf_op jit(solution)/shard_map/ppermute | solution.py:442
  159.1 10.4 %copy-start.22 = (s32[128]{0:T(128)S(1)}, s32[128]{0:T(128)}, u32[]{:S(2)}) copy-start(s32[128]{0:T(128)} %copy-done.21) | copy-start | bytes 1540
  188.8 64.7 %all-to-all-start.2 = ((bf16[64,2,72,256]{3,2,1,0:T(8,128)(2,1)}), bf16[64,2,72,256]{3,2,1,0:T(8,128)(2,1)}, u32[]{:S(2)}, u32[]{:S(2)}) async-start(bf16[64,2,72,256]{3,2,1,0:T(8,128)(2,1)} %get-tuple-element.19), calls=%async_computation.2 | async-start | bytes 9437184 | tf_op jit(solution)/shard_map/all_to_all | solution.py:540
  (4 other events, 6.2 us)

commit v4 on v3

--- a/solution.py
+++ b/solution.py
@@ -51,7 +51,6 @@
 
 
 def attend_body(
-    slot_s,
     query_ref,
     key_new_ref,
     value_new_ref,
@@ -62,13 +61,9 @@
     context_ref,
     key_out_ref,
     value_out_ref,
-    send_ref,
-    rows_f,
 ):
-    base = pl.program_id(0) * BLOCK
     width = query_ref.shape[2]
     heads = width // LANES
-    slots = send_ref.shape[0]
     span = SPAN * BLOCK
     valid = valid_ref[...]
     low = (CACHE - fill_ref[:, :1]) * BLOCK
@@ -113,22 +108,60 @@
     first = ((shift & 1) != 0)[None]
     second = ((shift & 2) != 0)[None]
     third = ((shift & 4) != 0)[None]
-    for kind, (old_ref, new_ref, out_ref) in enumerate(
-        ((key_ref, key_new_ref, key_out_ref), (value_ref, value_new_ref, value_out_ref))
+    edge = CACHE - FRAMES
+    for old_ref, new_ref, out_ref in (
+        (key_ref, key_new_ref, key_out_ref),
+        (value_ref, value_new_ref, value_out_ref),
     ):
         for h in range(heads):
             lanes = slice(h * LANES, (h + 1) * LANES)
-            for start in range(0, CACHE, CHUNK):
-                stop = start + CHUNK + 8
-                rows = old_ref[start + 1 : min(stop, CACHE), :, lanes].astype(jnp.float32)
-                if stop > CACHE:
-                    extra = new_ref[:, :, lanes].astype(jnp.float32)
-                    rows = jnp.concatenate([rows, extra, extra[:1]], axis=0)[: CHUNK + 7]
-                rows = shift_rows(rows, first, second, third)
-                out_ref[start : start + CHUNK, :, lanes] = rows.astype(jnp.bfloat16)
-                rows_f[kind, h, start * BLOCK : (start + CHUNK) * BLOCK, :] = rows.reshape(
-                    CHUNK * BLOCK, LANES
-                )
+            old = old_ref[edge + 1 :, :, lanes].astype(jnp.float32)
+            new = new_ref[:, :, lanes].astype(jnp.float32)
+            rows = jnp.concatenate([old, new, new[:1]], axis=0)
+            out_ref[:, :, lanes] = shift_rows(rows, first, second, third).astype(jnp.bfloat16)
+
+
+def attend(valid_old, fill_old, queries, key_new, value_new, key_cache, value_cache, groups):
+    stream_count = key_cache.shape[1]
+    width = key_cache.shape[2]
+
+    def wide(column):
+        return jnp.broadcast_to(column[:, None], (stream_count, LANES))
+
+    def block(rows):
+        return pl.BlockSpec((rows, BLOCK, width), lambda i: (0, i, 0))
+
+    per_group = stream_count // groups // BLOCK
+    scalar = pl.BlockSpec((BLOCK, LANES), lambda i: (i, 0))
+    context = pl.BlockSpec(
+        (1, FRAMES, BLOCK, width), lambda i: (i // per_group, 0, i % per_group, 0)
+    )
+    slab = jax.ShapeDtypeStruct((FRAMES, stream_count, width), jnp.bfloat16)
+    return pl.pallas_call(
+        attend_body,
+        grid=(stream_count // BLOCK,),
+        in_specs=[block(FRAMES)] * 3 + [block(CACHE)] * 2 + [scalar] * 2,
+        out_specs=[context, block(FRAMES), block(FRAMES)],
+        out_shape=[
+            jax.ShapeDtypeStruct((groups, FRAMES, stream_count // groups, width), jnp.bfloat16),
+            slab,
+            slab,
+        ],
+        name="attend",
+    )(queries, key_new, value_new, key_cache, value_cache, wide(valid_old), wide(fill_old))
+
+
+def pack_body(slot_s, key_ref, value_ref, send_ref, rows_f):
+    base = pl.program_id(0) * BLOCK
+    heads = rows_f.shape[1]
+    slots = send_ref.shape[0]
+    for kind, src in enumerate((key_ref, value_ref)):
+        for h in range(heads):
+            rows_f[kind, h, : CACHE * BLOCK, :] = (
+                src[:, :, h * LANES : (h + 1) * LANES]
+                .astype(jnp.float32)
+                .reshape(CACHE * BLOCK, LANES)
+            )
 
     def pack(s, carry):
         slot = slot_s[base + s]
@@ -146,65 +179,29 @@
     lax.fori_loop(0, BLOCK, pack, 0)
 
 
-def attend(
-    valid_old, fill_old, bucket, queries, key_new, value_new, key_cache, value_cache, slots, groups
-):
+def pack_rows(bucket, key_cache, value_cache, slots):
     stream_count = key_cache.shape[1]
     width = key_cache.shape[2]
-    heads = width // HEAD
-
-    def wide(column):
-        return jnp.broadcast_to(column[:, None], (stream_count, LANES))
-
-    def block(rows):
-        return pl.BlockSpec((rows, BLOCK, width), lambda i, *_: (0, i, 0))
-
-    per_group = stream_count // groups // BLOCK
-    scalar = pl.BlockSpec((BLOCK, LANES), lambda i, *_: (i, 0))
+    block = pl.BlockSpec((CACHE, BLOCK, width), lambda i, *_: (0, i, 0))
     return pl.pallas_call(
-        attend_body,
+        pack_body,
         grid_spec=pltpu.PrefetchScalarGridSpec(
             num_scalar_prefetch=1,
             grid=(stream_count // BLOCK,),
-            in_specs=[
-                block(FRAMES),
-                block(FRAMES),
-                block(FRAMES),
-                block(CACHE),
-                block(CACHE),
-                scalar,
-                scalar,
+            in_specs=[block, block],
+            out_specs=pl.BlockSpec((slots, 2, KEEP, width), lambda i, *_: (0, 0, 0, 0)),
+            scratch_shapes=[
+                pltpu.VMEM((2, width // HEAD, KEEP * BLOCK, LANES), jnp.float32)
             ],
-            out_specs=[
-                pl.BlockSpec(
-                    (1, FRAMES, BLOCK, width), lambda i, *_: (i // per_group, 0, i % per_group, 0)
-                ),
-                block(CACHE),
-                block(CACHE),
-                pl.BlockSpec((slots, 2, KEEP, width), lambda i, *_: (0, 0, 0, 0)),
-            ],
-            scratch_shapes=[pltpu.VMEM((2, heads, KEEP * BLOCK, LANES), jnp.float32)],
         ),
-        out_shape=[
-            jax.ShapeDtypeStruct((groups, FRAMES, stream_count // groups, width), jnp.bfloat16),
-            jax.ShapeDtypeStruct((CACHE, stream_count, width), jnp.bfloat16),
-            jax.ShapeDtypeStruct((CACHE, stream_count, width), jnp.bfloat16),
-            jax.ShapeDtypeStruct((slots, 2, KEEP, width), jnp.bfloat16),
-        ],
-        name="attend",
-    )(
-        bucket,
-        queries,
-        key_new,
-        value_new,
-        key_cache,
-        value_cache,
-        wide(valid_old),
-        wide(fill_old),
-    )
-
-
-def place_body(arrival_s, got_ref, key_ref, value_ref, key_out_ref, value_out_ref, rows_f):
+        out_shape=jax.ShapeDtypeStruct((slots, 2, KEEP, width), jnp.bfloat16),
+        name="pack",
+    )(bucket, key_cache, value_cache)
+
+
+def place_body(
+    arrival_s, got_ref, valid_ref, key_ref, value_ref, key_out_ref, value_out_ref, rows_f
+):
     base = pl.program_id(0) * BLOCK
     heads = rows_f.shape[1]
     for kind, src in enumerate((key_ref, value_ref)):
@@ -231,18 +228,22 @@
         return carry
 
     lax.fori_loop(0, BLOCK, fetch, 0)
+    shift = valid_ref[...] - 1
+    first = ((shift & 1) != 0)[None]
+    second = ((shift & 2) != 0)[None]
+    third = ((shift & 4) != 0)[None]
+    edge = CACHE - FRAMES
     for kind, dst in enumerate((key_out_ref, value_out_ref)):
         for h in range(heads):
             lanes = slice(h * LANES, (h + 1) * LANES)
-            for start in range(0, CACHE, CHUNK):
-                dst[start : start + CHUNK, :, lanes] = (
-                    rows_f[kind, h, start * BLOCK : (start + CHUNK) * BLOCK, :]
-                    .reshape(CHUNK, BLOCK, LANES)
-                    .astype(jnp.bfloat16)
-                )
-
-
-def place(arrival, received, key_rows, value_rows):
+            for start in range(0, edge, 9):
+                rows = rows_f[kind, h, (start + 1) * BLOCK : (start + 17) * BLOCK, :]
+                rows = shift_rows(rows.reshape(16, BLOCK, LANES), first, second, third)
+                dst[start : start + 9, :, lanes] = rows.astype(jnp.bfloat16)
+            dst[edge:, :, lanes] = jnp.zeros((FRAMES, BLOCK, LANES), jnp.bfloat16)
+
+
+def place(arrival, valid_new, received, key_rows, value_rows):
     stream_count = key_rows.shape[1]
     width = key_rows.shape[2]
     heads = width // HEAD
@@ -256,6 +257,7 @@
             grid=(stream_count // BLOCK,),
             in_specs=[
                 pl.BlockSpec((slots, 2, KEEP, width), lambda i, *_: (0, 0, 0, 0)),
+                pl.BlockSpec((BLOCK, LANES), lambda i, *_: (i, 0)),
                 block,
                 block,
             ],
@@ -264,7 +266,13 @@
         ),
         out_shape=[shape, shape],
         name="place",
-    )(arrival, received, key_rows, value_rows)
+    )(
+        arrival,
+        received,
+        jnp.broadcast_to(valid_new[:, None], (stream_count, LANES)),
+        key_rows,
+        value_rows,
+    )
 
 
 def head_body(
@@ -333,36 +341,53 @@
 
 
 def tail_body(place_s, *refs):
-    contexts, caches, rest = refs[:4], refs[4:8], refs[8:]
-    inputs_ref, gain_ref, valid_ref, own_ref, near_ref, far_low, far_high, next_ref = rest[:8]
-    smalls, out_ref = rest[8:12], rest[12]
+    contexts, caches, smalls, rest = refs[:4], refs[4:8], refs[8:12], refs[12:]
+    inputs_ref, gain_ref, valid_ref = rest[:3]
+    attn_ref, conv_ref, value_ref, gate_ref = rest[3:7]
+    low_refs, high_refs, out_ref = rest[7:13], rest[13:19], rest[19]
     member = place_s[0]
+    front_half = place_s[1] == 0
     groups = len(contexts)
     _, share, width = contexts[0].shape
     rows = FRAMES * share
     size = groups * width
-    half = 2 * size
-    sources = tuple(
-        zip(
-            contexts,
-            caches,
-            (own_ref, near_ref, far_low, next_ref),
-            (own_ref, near_ref, far_high, next_ref),
-            (half, half, 0, half),
-            smalls,
-        )
-    )
-
-    def grouped(operand, low_ref, start, sums):
+    half = width // 2
+
+    def ordered(operand):
+        middle_lane = operand.shape[1] // 2
+        low, high = operand[:, :middle_lane], operand[:, middle_lane:]
+        return jnp.where(front_half, low, high), jnp.where(front_half, high, low)
+
+    def dot(left, right):
+        return jnp.dot(left, right, preferred_element_type=jnp.float32)
+
+    def grouped(step, operand, own_ref, start, sums):
+        sides = ordered(operand)
         for n in range(groups):
-            block = low_ref[start + n * width : start + (n + 1) * width, :]
-            part = jnp.dot(operand, block, preferred_element_type=jnp.float32)
+            if step == 0:
+                part = dot(operand, own_ref[:, n * width : (n + 1) * width])
+            else:
+                at = start + n * half
+                part = sum(
+                    dot(side, low_refs[2 * (step - 1) + i][at : at + half, :])
+                    for i, side in enumerate(sides)
+                )
             part = part.astype(jnp.bfloat16).astype(jnp.float32)
             sums[n] = part if sums[n] is None else sums[n] + part
 
+    def wide(step, own_ref, order):
+        if step == 0:
+            return dot(normed, own_ref[...])
+        at = high_starts[step - 1] + order * (size // 2)
+        return sum(
+            dot(side, high_refs[2 * (step - 1) + i][at : at + size // 2, :])
+            for i, side in enumerate(normed_sides)
+        )
+
+    high_starts = (size, 0, size)
     attended = [None] * groups
-    for context_ref, _, low_ref, _, _, _ in sources:
-        grouped(context_ref[...].reshape(rows, width), low_ref, 0, attended)
+    for step in range(groups):
+        grouped(step, contexts[step][...].reshape(rows, width), attn_ref, 0, attended)
     middle = []
     for n in range(groups):
         inputs = inputs_ref[:, :, n * width : (n + 1) * width].reshape(rows, width)
@@ -379,20 +404,18 @@
         ],
         axis=1,
     )
+    normed_sides = ordered(normed)
     valid = valid_ref[...]
     shift = valid - 1
     first = ((shift & 1) != 0)[None]
     second = ((shift & 2) != 0)[None]
     third = ((shift & 4) != 0)[None]
     conv_term = [None] * groups
-    for step, (_, cache_ref, low_ref, high_ref, start, small_ref) in enumerate(sources):
+    for step in range(groups):
         group = (member + groups - step) % groups
-        glu_value = jnp.dot(
-            normed, high_ref[start : start + size, :], preferred_element_type=jnp.float32
-        )
-        glu_gate = jnp.dot(
-            normed, high_ref[start + size : start + 2 * size, :], preferred_element_type=jnp.float32
-        )
+        cache_ref, small_ref = caches[step], smalls[step]
+        glu_value = wide(step, value_ref, 0)
+        glu_gate = wide(step, gate_ref, 1)
         gated = (glu_value * jax.nn.sigmoid(glu_gate)).astype(jnp.bfloat16)
         conv_in = jnp.concatenate(
             [
@@ -407,7 +430,7 @@
         shaped = depthwise * small_ref[KERNEL : KERNEL + 1, :][None]
         shaped = shaped + small_ref[KERNEL + 1 : KERNEL + 2, :][None]
         activated = (shaped * jax.nn.sigmoid(shaped)).astype(jnp.bfloat16)
-        grouped(activated.reshape(rows, width), low_ref, size, conv_term)
+        grouped(step, activated.reshape(rows, width), conv_ref, size // 2, conv_term)
         moved = shift_rows(
             jnp.concatenate([conv_in[1:], conv_in[-1:]], axis=0), first, second, third
         )
@@ -418,7 +441,7 @@
         out_ref[n, :FRAMES, :, :] = jnp.where(frame < valid[None], total, 0.0).astype(jnp.bfloat16)
 
 
-def tail(member, groups, *arrays):
+def tail(where, groups, *arrays):
     _, share, width = arrays[0].shape
     return pl.pallas_call(
         tail_body,
@@ -427,7 +450,7 @@
         out_specs=pl.BlockSpec(memory_space=pltpu.VMEM),
         out_shape=jax.ShapeDtypeStruct((groups, FRAMES + CONV_CACHE, share, width), jnp.bfloat16),
         name="tail",
-    )(member[None], *arrays)
+    )(where, *arrays)
 
 
 def swap(chunks, member, count):
@@ -489,6 +512,10 @@
     valid_old = both_old // 128
     fill_old = both_old % 128
 
+    key_rows = key_cache.transpose(1, 0, 2)
+    value_rows = value_cache.transpose(1, 0, 2)
+    leaving_rows = pack_rows(bucket, key_rows, value_rows, slots)
+    received = lax.all_to_all(leaving_rows, "front", split_axis=0, concat_axis=0, tiled=True)
     groups = lax.axis_size("enc")
     taps = SUB * MELS
     with_bias = jnp.concatenate(
@@ -496,19 +523,38 @@
     )
     sub_pieces = [with_bias] + [toward(with_bias, k, groups) for k in range(1, groups)]
 
+    core = own_index % 2
+    half = local_width // 2
+
+    def core_rows(matrix):
+        count = matrix.shape[0] // 2
+        return lax.dynamic_slice_in_dim(matrix, core * count, count, 0)
+
     def blocks(matrix):
         return (
-            matrix.reshape(local_width, groups, local_width)
+            core_rows(matrix)
+            .reshape(half, groups, local_width)
             .transpose(1, 0, 2)
-            .reshape(groups * local_width, local_width)
-        )
-
-    stack = jnp.concatenate([blocks(w_attn_out), blocks(w_conv_out), w_glu_value, w_glu_gate], axis=0)
-    half = stack.shape[0] // 2
+            .reshape(groups * half, local_width)
+        )
+
+    stack = jnp.concatenate(
+        [blocks(w_attn_out), blocks(w_conv_out), core_rows(w_glu_value), core_rows(w_glu_gate)],
+        axis=0,
+    )
+    middle_row = stack.shape[0] // 2
+
+    def other_core(array):
+        return lax.ppermute(array, "front", [(i, i ^ 1) for i in range(peer_count)])
+
     near = toward(stack, 1, groups)
     after = toward(stack, -1, groups)
-    far_low = toward(near[:half], 1, groups)
-    far_high = toward(after[half:], -1, groups)
+    far_low = toward(near[:middle_row], 1, groups)
+    far_high = toward(after[middle_row:], -1, groups)
+    near_other = other_core(near)
+    after_other = other_core(after)
+    far_low_other = other_core(far_low)
+    far_high_other = other_core(far_high)
     small = jnp.concatenate(
         [depth_kernel, norm_scale[None], norm_shift[None], jnp.zeros((5, local_width), jnp.float32)],
         axis=0,
@@ -525,42 +571,44 @@
     queries, key_new, value_new, inputs = head(
         member, frames, sub_pieces, ln1_gain, (w_query, w_key, w_value)
     )
-    context, key_rows, value_rows, leaving_rows = attend(
-        valid_old,
-        fill_old,
-        bucket,
-        queries,
-        key_new,
-        value_new,
-        key_cache.transpose(1, 0, 2),
-        value_cache.transpose(1, 0, 2),
-        slots,
-        groups,
-    )
-    received = lax.all_to_all(leaving_rows, "front", split_axis=0, concat_axis=0, tiled=True)
+    context, key_slab, value_slab = attend(
+        valid_old, fill_old, queries, key_new, value_new, key_rows, value_rows, groups
+    )
     context = swap(context, member, groups)
     valid_share = lax.dynamic_slice_in_dim(valid_old, member * share, share, 0)
     ended = tail(
-        member,
+        jnp.stack([member, core]),
         groups,
         *context,
         *cache_share,
-        inputs,
-        ln2_gain[None, :],
-        jnp.broadcast_to(valid_share[:, None], (share, local_width)),
-        stack,
-        near,
-        far_low,
-        far_high,
-        after,
         small,
         small_near,
         small_far,
         small_next,
+        inputs,
+        ln2_gain[None, :],
+        jnp.broadcast_to(valid_share[:, None], (share, local_width)),
+        w_attn_out,
+        w_conv_out,
+        w_glu_value,
+        w_glu_gate,
+        near,
+        near_other,
+        far_low,
+        far_low_other,
+        after,
+        after_other,
+        near,
+        near_other,
+        far_high,
+        far_high_other,
+        after,
+        after_other,
     )
     ended = swap(ended, member, groups)
     ended = jnp.concatenate((ended[::-1] + ended[::-1])[:-1], axis=1)
     finished = lax.dynamic_slice_in_dim(ended, (groups - 1 - member) * share, stream_count, 1)
+    finished = jnp.concatenate([finished, key_slab, value_slab], axis=0)
     picker = (
         bucket[None, :] == jnp.arange(slots, dtype=jnp.int32)[:, None]
     ).astype(jnp.bfloat16)
@@ -575,12 +623,16 @@
         "sl,ltc->tsc", placer, received_end, preferred_element_type=jnp.float32
     ).astype(jnp.bfloat16)
     finished = jnp.where((arrival < 0)[None, :, None], finished, placed)
-    key_done, value_done = place(arrival, received, key_rows, value_rows)
+    key_done, value_done = place(arrival, valid_new, received, key_rows, value_rows)
+    edge = CACHE - FRAMES
+    ends = FRAMES + CONV_CACHE
+    key_done = lax.dynamic_update_slice_in_dim(key_done, finished[ends : ends + FRAMES], edge, 0)
+    value_done = lax.dynamic_update_slice_in_dim(value_done, finished[ends + FRAMES :], edge, 0)
     return (
         finished[:FRAMES].transpose(1, 0, 2),
         key_done.transpose(1, 0, 2),
         value_done.transpose(1, 0, 2),
-        finished[FRAMES:].transpose(1, 0, 2),
+        finished[FRAMES:ends].transpose(1, 0, 2),
     )
 
 

time: 268 us -> 261 us (0.974)
  blocking collectives: 18.7 us -> 0 us
  Pallas kernels: 53.5 us -> 59.4 us
  local copies, waits for them, and re-layouts: 19.1 us -> 23.9 us
  other arithmetic: 0.86 us -> 4.3 us
    all_to_all x1 -> x0, blocking collectives: 18.7 us -> none  [on_device(): lax.all_to_all(leaving_end, 'front', split_axis=0, concat_axis=0, tiled=T...]
    ppermute x19, waiting for transfers between devices: 76.4 us -> 66 us  [toward(): lax.ppermute(array, 'enc', [(i, (i + steps) % count) for i in range(count)])]
    ppermute x19, starting transfers between devices: 26.9 us -> 20.8 us  [toward(): lax.ppermute(array, 'enc', [(i, (i + steps) % count) for i in range(count)])]
    all_to_all x0 -> x1, waiting for transfers between devices: none -> 5.74 us  [on_device(): lax.all_to_all(leaving_end, 'front', split_axis=0, concat_axis=0, tiled=T...]
    all_to_all x0 -> x1, starting transfers between devices: none -> 3.93 us  [on_device(): lax.all_to_all(leaving_end, 'front', split_axis=0, concat_axis=0, tiled=T...]
    all_to_all x1, waiting for transfers between devices: 0.01 us -> 3.81 us  [on_device(): lax.all_to_all(jnp.broadcast_to(asked[:, None], (slots, LANES)), 'front',...]
    unnamed x73 -> x71, local copies, waits for them, and re-layouts: 3.04 us -> 6.25 us
    pallas_call x1 -> x2, Pallas kernels: 21.1 us -> 24.2 us  [the longest x1 12.7 us: attend(): pl.pallas_call(attend_body, grid=(stream_count // BLOCK,), in_specs=[bloc...]
  transfers between devices with their start and end apart: 21 -> 26, of which waited for: 10 -> 12; matrix products, arithmetic and copies ran while one was open for 5% -> 7% of each run, Pallas kernels for 12% -> 13%
where the time goes in v4:
time: 261 us; the launch traced here: 260 us
  waiting for transfers between devices  132 us (51%)
  Pallas kernels  59.4 us (23%)
  starting transfers between devices  38 us (15%)
  local copies, waits for them, and re-layouts  23.9 us (9%)
  other arithmetic  4.3 us (2%)
    ppermute x19, waiting for transfers between devices, toward(): lax.ppermute(array, 'enc', [(i, (i + steps) % count) for i in range(count)])  66 us
    all_to_all x1, waiting for transfers between devices, on_device(): lax.all_to_all(leaving_rows, 'front', split_axis=0, concat_axis=0, tiled=...  56.3 us
    ppermute x19, starting transfers between devices, toward(): lax.ppermute(array, 'enc', [(i, (i + steps) % count) for i in range(count)])  20.8 us
    pallas_call x1, Pallas kernels, place(): pl.pallas_call(place_body, grid_spec=pltpu.PrefetchScalarGridSpec(num_sca...  14.5 us
    pallas_call x1, Pallas kernels, attend(): pl.pallas_call(attend_body, grid=(stream_count // BLOCK,), in_specs=[bloc...  12.7 us
    pallas_call x1, Pallas kernels, pack_rows(): pl.pallas_call(pack_body, grid_spec=pltpu.PrefetchScalarGridSpec(num_scal...  11.5 us
    pallas_call x1, Pallas kernels, tail(): pl.pallas_call(tail_body, in_specs=[pl.BlockSpec(memory_space=pltpu.SMEM)...  10.5 us
    pallas_call x1, Pallas kernels, head(): pl.pallas_call(head_body, grid_spec=pltpu.PrefetchScalarGridSpec(num_scal...  10.2 us
  transfers between devices with their start and end apart: 26, of which 12 were waited for; matrix products, arithmetic and copies ran while one was open for 7% of the time, Pallas kernels for 13%

profile of v4, /device:TPU:0, one launch (start us, length us, event | category | flops | bytes accessed | tf_op | source)
XLA Modules:
  0.0 260.1 jit_solution(10531862958902511572)
XLA Ops:
  1.3 1.1 pad_maximum_fusion.3.own_ref
  2.4 2.1 collective-permute-start
  4.5 3.6 %collective-permute-start.1 = (bf16[656,256]{1,0:T(8,128)(2,1)S(1)}, bf16[656,256]{1,0:T(8,128)(2,1)}, u32[]{:S(2)}, u32[]{:S(2)}) collective-permute-start(bf16[656,256]{1,0:T(8,128)(2,1)S(1)} %pad_maximum_fusion.3.own_ref), channel_id=1, source_target_pairs={{0,2},{1,3},{2,0},{3,1},{4,6},{5,7},{6,4},{7,5},{8,10},{9,11},{10,... | collective-permute-start | bytes 1007624 | tf_op jit(solution)/shard_map/ppermute | solution.py:465
  8.1 1.1 constant_dynamic-slice_fusion.3
  10.1 3.2 %collective-permute-start.16 = (bf16[2048,256]{1,0:T(8,128)(2,1)S(1)}, bf16[2048,256]{1,0:T(8,128)(2,1)S(1)}, u32[]{:S(2)}, u32[]{:S(2)}) collective-permute-start(bf16[2048,256]{1,0:T(8,128)(2,1)S(1)} %pad_maximum_fusion.1), channel_id=1, source_target_pairs={{0,3},{1,0},{2,1},{3,2},{4,7},{5,4},{6,5},{7,6},{8,11},{9,8},{10,9... | collective-permute-start | bytes 3145736 | tf_op jit(solution)/shard_map/ppermute | solution.py:465
  13.8 1.8 constant_dynamic-slice_fusion.5
  16.6 29.2 %collective-permute-done.10.refs_10_ = f32[16,256]{1,0:T(8,128)S(1)} collective-permute-done((f32[16,256]{1,0:T(8,128)S(1)}, f32[16,256]{1,0:T(8,128)S(1)}, u32[]{:S(2)}, u32[]{:S(2)}) %collective-permute-start.10) | collective-permute-done | bytes 16416 | tf_op jit(solution)/shard_map/ppermute | solution.py:465
  45.8 2.0 collective-permute-start.9
  47.9 1.2 broadcast_compare_fusion
  49.1 0.8 slice.29
  49.9 0.8 slice.30
  50.8 2.6 %collective-permute-start.7 = (bf16[8,32,256]{2,1,0:T(8,128)(2,1)S(1)}, bf16[8,32,256]{2,1,0:T(8,128)(2,1)}, u32[]{:S(2)}, u32[]{:S(2)}) collective-permute-start(bf16[8,32,256]{2,1,0:T(8,128)(2,1)S(1)} %bitcast.88), channel_id=1, source_target_pairs={{0,2},{1,3},{2,0},{3,1},{4,6},{5,7},{6,4},{7,5},{8,10},{9,11},{10,... | collective-permute-start | bytes 393224 | tf_op jit(solution)/shard_map/ppermute | solution.py:465
  53.4 1.3 collective-permute-start.14
  54.7 0.8 collective-permute-done.6.refs_5_
  55.6 1.1 collective-permute-start.18
  56.9 0.7 broadcast_in_dim.71
  57.6 7.3 %all-to-all-start = ((s32[32,2,128]{2,1,0:T(2,128)}), s32[32,2,128]{2,1,0:T(2,128)S(1)}, u32[]{:S(2)}, u32[]{:S(2)}) async-start(s32[32,2,128]{2,1,0:T(2,128)} %broadcast_in_dim.71), calls=%async_computation | async-start | bytes 65536 | tf_op jit(solution)/shard_map/all_to_all | solution.py:503
  64.9 2.4 copy.63
  68.5 3.8 %all-to-all-done = s32[32,2,128]{2,1,0:T(2,128)S(1)} async-done(((s32[32,2,128]{2,1,0:T(2,128)}), s32[32,2,128]{2,1,0:T(2,128)S(1)}, u32[]{:S(2)}, u32[]{:S(2)}) %all-to-all-start) | async-done | bytes 32800 | tf_op jit(solution)/shard_map/all_to_all | solution.py:503
  72.6 9.8 %collective-permute-done.2.next_ref = bf16[656,256]{1,0:T(8,128)(2,1)S(1)} collective-permute-done((bf16[656,256]{1,0:T(8,128)(2,1)S(1)}, bf16[656,256]{1,0:T(8,128)(2,1)S(1)}, u32[]{:S(2)}, u32[]{:S(2)}) %collective-permute-start.2) | collective-permute-done | bytes 335904 | tf_op jit(solution)/shard_map/ppermute | solution.py:465
  82.4 0.7 copy-done.10
  83.1 1.5 collective-permute-start.8
  85.2 10.2 %head.1 = (bf16[7,128,256]{2,1,0:T(8,128)(2,1)}, bf16[7,128,256]{2,1,0:T(8,128)(2,1)}, bf16[7,128,256]{2,1,0:T(8,128)(2,1)}, bf16[7,32,1024]{2,1,0:T(8,128)(2,1)}) custom-call(s32[1]{0:T(128)} %bitcast.place_s, bf16[7,128,640]{2,1,0:T(8,128)(2,1)} %bitcast.78, bf16[656,256]{1,0:T(8,128)(2,1)} %copy-done.5, bf16[656,256]{1,0:T(8,128)(2,1)} %collective-permute-done.near_ref, ...), custom_call_target="tpu_custom_call" | custom-call | tf_op jit(solution)/shard_map/head/pallas_call | solution.py:324
  96.7 12.7 %attend.1 = (bf16[4,7,32,256]{3,2,1,0:T(8,128)(2,1)}, bf16[7,128,256]{2,1,0:T(8,128)(2,1)}, bf16[7,128,256]{2,1,0:T(8,128)(2,1)}) custom-call(bf16[7,128,256]{2,1,0:T(8,128)(2,1)} %get-tuple-element.13.query_ref, bf16[7,128,256]{2,1,0:T(8,128)(2,1)} %get-tuple-element.14.key_new_ref, bf16[7,128,256]{2,1,0:T(8,128)(2,1)} %get-tuple-element.15.value_new_ref, ...), custom_call_target="tpu_custom_call" | custom-call | tf_op jit(solution)/shard_map/attend/pallas_call | solution.py:140
  109.5 1.8 dynamic-slice_bitcast_fusion.3
  111.8 5.9 %collective-permute-done.3.refs_1_ = bf16[7,32,256]{2,1,0:T(8,128)(2,1)} collective-permute-done((bf16[7,32,256]{2,1,0:T(8,128)(2,1)S(1)}, bf16[7,32,256]{2,1,0:T(8,128)(2,1)}, u32[]{:S(2)}, u32[]{:S(2)}) %collective-permute-start.3) | collective-permute-done | bytes 114720 | tf_op jit(solution)/shard_map/ppermute | solution.py:465
  118.1 6.1 %collective-permute-done.4.refs_2_ = bf16[7,32,256]{2,1,0:T(8,128)(2,1)} collective-permute-done((bf16[7,32,256]{2,1,0:T(8,128)(2,1)S(1)}, bf16[7,32,256]{2,1,0:T(8,128)(2,1)}, u32[]{:S(2)}, u32[]{:S(2)}) %collective-permute-start.4) | collective-permute-done | bytes 114720 | tf_op jit(solution)/shard_map/ppermute | solution.py:465
  125.5 3.8 %collective-permute-done.5.refs_3_ = bf16[7,32,256]{2,1,0:T(8,128)(2,1)} collective-permute-done((bf16[7,32,256]{2,1,0:T(8,128)(2,1)}, bf16[7,32,256]{2,1,0:T(8,128)(2,1)}, u32[]{:S(2)}, u32[]{:S(2)}) %collective-permute-start.5) | collective-permute-done | bytes 114720 | tf_op jit(solution)/shard_map/ppermute | solution.py:465
  129.3 0.8 broadcast_in_dim.129.refs_14_
  130.3 10.5 %tail.1 = bf16[4,15,32,256]{3,2,1,0:T(8,128)(2,1)} custom-call(s32[2]{0:T(128)} %pad_add_fusion.place_s, bf16[7,32,256]{2,1,0:T(8,128)(2,1)} %get-tuple-element.59.refs_0_, bf16[7,32,256]{2,1,0:T(8,128)(2,1)} %collective-permute-done.3.refs_1_, bf16[7,32,256]{2,1,0:T(8,128)(2,1)} %collective-permute-done.4.refs_2_, ...), custom_call_target="tpu_custom_call" | custom-call | tf_op jit(solution)/shard_map/tail/pallas_call | solution.py:446
  140.8 1.2 dynamic-slice_bitcast_fusion
  142.1 1.3 collective-permute-start.20
  144.3 5.2 %collective-permute-done.20 = bf16[15,32,256]{2,1,0:T(8,128)(2,1)S(1)} collective-permute-done((bf16[15,32,256]{2,1,0:T(8,128)(2,1)S(1)}, bf16[15,32,256]{2,1,0:T(8,128)(2,1)S(1)}, u32[]{:S(2)}, u32[]{:S(2)}) %collective-permute-start.20) | collective-permute-done | bytes 245792 | tf_op jit(solution)/shard_map/ppermute | solution.py:465
  149.5 2.8 %collective-permute-done.21 = bf16[15,32,256]{2,1,0:T(8,128)(2,1)S(1)} collective-permute-done((bf16[15,32,256]{2,1,0:T(8,128)(2,1)S(1)}, bf16[15,32,256]{2,1,0:T(8,128)(2,1)S(1)}, u32[]{:S(2)}, u32[]{:S(2)}) %collective-permute-start.21) | collective-permute-done | bytes 245792 | tf_op jit(solution)/shard_map/ppermute | solution.py:465
  152.4 2.4 collective-permute-done.22
  154.8 1.0 bitcast_dynamic-update-slice_fusion
  156.5 1.5 copy.72
  158.0 3.9 %all-to-all-start.1 = ((bf16[64,29,256]{2,1,0:T(8,128)(2,1)}), bf16[64,29,256]{2,1,0:T(8,128)(2,1)S(1)}, u32[]{:S(2)}, u32[]{:S(2)}) async-start(bf16[64,29,256]{2,1,0:T(8,128)(2,1)} %copy.72), calls=%async_computation.1 | async-start | bytes 2097152 | tf_op jit(solution)/shard_map/all_to_all | solution.py:618
  161.9 11.5 %pack.1 = bf16[64,2,72,256]{3,2,1,0:T(8,128)(2,1)} custom-call(s32[128]{0:T(128)} %copy-done.17, bf16[70,128,256]{2,1,0:T(8,128)(2,1)} %bitcast.73, bf16[70,128,256]{2,1,0:T(8,128)(2,1)} %bitcast.76), custom_call_target="tpu_custom_call" | custom-call | tf_op jit(solution)/shard_map/pack/pallas_call | solution.py:186
  173.4 5.7 %all-to-all-done.1 = bf16[64,29,256]{2,1,0:T(8,128)(2,1)S(1)} async-done(((bf16[64,29,256]{2,1,0:T(8,128)(2,1)}), bf16[64,29,256]{2,1,0:T(8,128)(2,1)S(1)}, u32[]{:S(2)}, u32[]{:S(2)}) %all-to-all-start.1) | async-done | bytes 950304 | tf_op jit(solution)/shard_map/all_to_all | solution.py:618
  179.1 4.9 %all-to-all-start.2 = ((bf16[64,2,72,256]{3,2,1,0:T(8,128)(2,1)}), bf16[64,2,72,256]{3,2,1,0:T(8,128)(2,1)}, u32[]{:S(2)}, u32[]{:S(2)}) async-start(bf16[64,2,72,256]{3,2,1,0:T(8,128)(2,1)} %pack.1), calls=%async_computation.2 | async-start | bytes 9437184 | tf_op jit(solution)/shard_map/all_to_all | solution.py:518
  184.0 1.2 bitcast_select_fusion
  185.2 1.3 copy-done.3
  186.5 1.1 copy.75
  187.6 56.3 %all-to-all-done.2.got_ref = bf16[64,2,72,256]{3,2,1,0:T(8,128)(2,1)} async-done(((bf16[64,2,72,256]{3,2,1,0:T(8,128)(2,1)}), bf16[64,2,72,256]{3,2,1,0:T(8,128)(2,1)}, u32[]{:S(2)}, u32[]{:S(2)}) %all-to-all-start.2) | async-done | bytes 4718624 | tf_op jit(solution)/shard_map/all_to_all | solution.py:518
  243.9 0.7 broadcast_in_dim.130.valid_ref
  244.6 14.5 %place.1 = (bf16[70,128,256]{2,1,0:T(8,128)(2,1)}, bf16[70,128,256]{2,1,0:T(8,128)(2,1)}) custom-call(s32[128]{0:T(128)} %copy-done.21, bf16[64,2,72,256]{3,2,1,0:T(8,128)(2,1)} %all-to-all-done.2.got_ref, s32[128,128]{1,0:T(8,128)} %broadcast_in_dim.130.valid_ref, bf16[70,128,256]{2,1,0:T(8,128)(2,1)} %bitcast.74, bf16[70,128,256]{2,1,0:T(8,128)(2,1)} %bitcast.77), custom_call_target="tpu_custom_call" | custom-call | tf_op jit(solution)/shard_map/place/pallas_call | solution.py:253
  259.0 1.1 slice_dynamic-update-slice_fusion
  (122 shorter events, 10.6 us)
Async XLA Ops:
  1.3 8.6 %copy-start.6 = (bf16[1024,256]{1,0:T(8,128)(2,1)S(1)}, bf16[1024,256]{1,0:T(8,128)(2,1)}, u32[]{:S(2)}) copy-start(bf16[1024,256]{1,0:T(8,128)(2,1)} %refs_17_.1) | copy-start | bytes 1572868
  1.3 8.6 %copy-start.7 = (bf16[1024,256]{1,0:T(8,128)(2,1)S(1)}, bf16[1024,256]{1,0:T(8,128)(2,1)}, u32[]{:S(2)}) copy-start(bf16[1024,256]{1,0:T(8,128)(2,1)} %refs_18_.1) | copy-start | bytes 1572868
  2.4 70.1 %copy-start.5 = (bf16[656,256]{1,0:T(8,128)(2,1)}, bf16[656,256]{1,0:T(8,128)(2,1)S(1)}, u32[]{:S(2)}) copy-start(bf16[656,256]{1,0:T(8,128)(2,1)S(1)} %pad_maximum_fusion.3.own_ref) | copy-start | bytes 1007620
  2.4 65.9 %collective-permute-start = (bf16[656,256]{1,0:T(8,128)(2,1)S(1)}, bf16[656,256]{1,0:T(8,128)(2,1)}, u32[]{:S(2)}, u32[]{:S(2)}) collective-permute-start(bf16[656,256]{1,0:T(8,128)(2,1)S(1)} %pad_maximum_fusion.3.own_ref), channel_id=1, source_target_pairs={{0,1},{1,2},{2,3},{3,0},{4,5},{5,6},{6,7},{7,4},{8,9},{9,10},{10,1... | collective-permute-start | bytes 1007624 | tf_op jit(solution)/shard_map/ppermute | solution.py:465
  4.5 67.9 %collective-permute-start.1 = (bf16[656,256]{1,0:T(8,128)(2,1)S(1)}, bf16[656,256]{1,0:T(8,128)(2,1)}, u32[]{:S(2)}, u32[]{:S(2)}) collective-permute-start(bf16[656,256]{1,0:T(8,128)(2,1)S(1)} %pad_maximum_fusion.3.own_ref), channel_id=1, source_target_pairs={{0,2},{1,3},{2,0},{3,1},{4,6},{5,7},{6,4},{7,5},{8,10},{9,11},{10,... | collective-permute-start | bytes 1007624 | tf_op jit(solution)/shard_map/ppermute | solution.py:465
  9.6 3.8 %copy-start.16 = (f32[9,256]{1,0:T(8,128)S(1)}, f32[9,256]{1,0:T(8,128)}, u32[]{:S(2)}) copy-start(f32[9,256]{1,0:T(8,128)} %param.40) | copy-start | bytes 27652
  9.7 3.9 %copy-start.25 = (s32[128]{0:T(128)S(1)}, s32[128]{0:T(128)}, u32[]{:S(2)}) copy-start(s32[128]{0:T(128)} %param.28) | copy-start | bytes 1540
  9.9 5.7 %copy-start.18 = (s32[128]{0:T(128)S(1)}, s32[128]{0:T(128)}, u32[]{:S(2)}) copy-start(s32[128]{0:T(128)} %param.29) | copy-start | bytes 1540
  9.9 5.7 %copy-start.19 = (s32[128]{0:T(128)S(1)}, s32[128]{0:T(128)}, u32[]{:S(2)}) copy-start(s32[128]{0:T(128)} %param.30) | copy-start | bytes 1540
  10.0 35.7 %collective-permute-start.12 = (bf16[2048,256]{1,0:T(8,128)(2,1)S(1)}, bf16[2048,256]{1,0:T(8,128)(2,1)S(1)}, u32[]{:S(2)}, u32[]{:S(2)}) collective-permute-start(bf16[2048,256]{1,0:T(8,128)(2,1)S(1)} %pad_maximum_fusion.1), channel_id=1, source_target_pairs={{0,1},{1,2},{2,3},{3,0},{4,5},{5,6},{6,7},{7,4},{8,9},{9,10},{10,1... | collective-permute-start | bytes 3145736 | tf_op jit(solution)/shard_map/ppermute | solution.py:465
  10.1 37.7 %collective-permute-start.16 = (bf16[2048,256]{1,0:T(8,128)(2,1)S(1)}, bf16[2048,256]{1,0:T(8,128)(2,1)S(1)}, u32[]{:S(2)}, u32[]{:S(2)}) collective-permute-start(bf16[2048,256]{1,0:T(8,128)(2,1)S(1)} %pad_maximum_fusion.1), channel_id=1, source_target_pairs={{0,3},{1,0},{2,1},{3,2},{4,7},{5,4},{6,5},{7,6},{8,11},{9,8},{10,9... | collective-permute-start | bytes 3145736 | tf_op jit(solution)/shard_map/ppermute | solution.py:465
  13.5 43.4 %copy-start.12 = (f32[16,256]{1,0:T(8,128)}, f32[16,256]{1,0:T(8,128)S(1)}, u32[]{:S(2)}) copy-start(f32[16,256]{1,0:T(8,128)S(1)} %maximum_maximum_fusion.refs_8_) | copy-start | bytes 49156
  13.5 32.2 %collective-permute-start.10 = (f32[16,256]{1,0:T(8,128)S(1)}, f32[16,256]{1,0:T(8,128)S(1)}, u32[]{:S(2)}, u32[]{:S(2)}) collective-permute-start(f32[16,256]{1,0:T(8,128)S(1)} %maximum_maximum_fusion.refs_8_), channel_id=1, source_target_pairs={{0,2},{1,3},{2,0},{3,1},{4,6},{5,7},{6,4},{7,5},{8,10},{9,11},{10,... | collective-permute-start | bytes 49160 | tf_op jit(solution)/shard_map/ppermute | solution.py:465
  16.3 139.7 %copy-start.17 = (s32[128]{0:T(128)}, s32[128]{0:T(128)S(1)}, u32[]{:S(2)}) copy-start(s32[128]{0:T(128)S(1)} %get-tuple-element.60.slot_s) | copy-start | bytes 1540
  45.7 21.6 %copy-start.13 = (f32[16,256]{1,0:T(8,128)}, f32[16,256]{1,0:T(8,128)S(1)}, u32[]{:S(2)}) copy-start(f32[16,256]{1,0:T(8,128)S(1)} %collective-permute-done.10.refs_10_) | copy-start | bytes 49156
  45.7 5.0 %collective-permute-start.11 = (f32[16,256]{1,0:T(8,128)S(1)}, f32[16,256]{1,0:T(8,128)S(1)}, u32[]{:S(2)}, u32[]{:S(2)}) collective-permute-start(f32[16,256]{1,0:T(8,128)S(1)} %maximum_maximum_fusion.refs_8_), channel_id=1, source_target_pairs={{0,3},{1,0},{2,1},{3,2},{4,7},{5,4},{6,5},{7,6},{8,11},{9,8},{10,9... | collective-permute-start | bytes 49160 | tf_op jit(solution)/shard_map/ppermute | solution.py:465
  45.7 22.2 %copy-start = (bf16[2048,256]{1,0:T(8,128)(2,1)}, bf16[2048,256]{1,0:T(8,128)(2,1)S(1)}, u32[]{:S(2)}) copy-start(bf16[2048,256]{1,0:T(8,128)(2,1)S(1)} %collective-permute-done.12.refs_19_.refs_25_) | copy-start | bytes 3145732
  45.8 7.6 %collective-permute-start.9 = (f32[16,256]{1,0:T(8,128)S(1)}, f32[16,256]{1,0:T(8,128)S(1)}, u32[]{:S(2)}, u32[]{:S(2)}) collective-permute-start(f32[16,256]{1,0:T(8,128)S(1)} %maximum_maximum_fusion.refs_8_), channel_id=1, source_target_pairs={{0,1},{1,2},{2,3},{3,0},{4,5},{5,6},{6,7},{7,4},{8,9},{9,10},{10,1... | collective-permute-start | bytes 49160 | tf_op jit(solution)/shard_map/ppermute | solution.py:465
  47.8 20.5 %copy-start.1 = (bf16[2048,256]{1,0:T(8,128)(2,1)}, bf16[2048,256]{1,0:T(8,128)(2,1)S(1)}, u32[]{:S(2)}) copy-start(bf16[2048,256]{1,0:T(8,128)(2,1)S(1)} %collective-permute-done.16.refs_23_.refs_29_) | copy-start | bytes 3145732
  47.8 7.8 %collective-permute-start.6 = (bf16[8,32,256]{2,1,0:T(8,128)(2,1)S(1)}, bf16[8,32,256]{2,1,0:T(8,128)(2,1)}, u32[]{:S(2)}, u32[]{:S(2)}) collective-permute-start(bf16[8,32,256]{2,1,0:T(8,128)(2,1)S(1)} %bitcast.87), channel_id=1, source_target_pairs={{0,1},{1,2},{2,3},{3,0},{4,5},{5,6},{6,7},{7,4},{8,9},{9,10},{10,1... | collective-permute-start | bytes 393224 | tf_op jit(solution)/shard_map/ppermute | solution.py:465
  49.1 7.6 %copy-start.21 = (s32[128]{0:T(128)}, s32[128]{0:T(128)S(1)}, u32[]{:S(2)}) copy-start(s32[128]{0:T(128)S(1)} %get-tuple-element.45.arrival_s) | copy-start | bytes 1540
  49.9 17.4 %copy-start.9 = (bf16[1,32,8,256]{3,2,1,0:T(8,128)(2,1)S(1)}, bf16[1,32,8,256]{3,2,1,0:T(8,128)(2,1)}, u32[]{:S(2)}) copy-start(bf16[1,32,8,256]{3,2,1,0:T(8,128)(2,1)} %get-tuple-element.52) | copy-start | bytes 393220
  50.8 6.8 %copy-start.14 = (f32[16,256]{1,0:T(8,128)}, f32[16,256]{1,0:T(8,128)S(1)}, u32[]{:S(2)}) copy-start(f32[16,256]{1,0:T(8,128)S(1)} %collective-permute-done.11.refs_11_) | copy-start | bytes 49156
  50.8 17.2 %collective-permute-start.7 = (bf16[8,32,256]{2,1,0:T(8,128)(2,1)S(1)}, bf16[8,32,256]{2,1,0:T(8,128)(2,1)}, u32[]{:S(2)}, u32[]{:S(2)}) collective-permute-start(bf16[8,32,256]{2,1,0:T(8,128)(2,1)S(1)} %bitcast.88), channel_id=1, source_target_pairs={{0,2},{1,3},{2,0},{3,1},{4,6},{5,7},{6,4},{7,5},{8,10},{9,11},{10,... | collective-permute-start | bytes 393224 | tf_op jit(solution)/shard_map/ppermute | solution.py:465
  53.4 4.2 %copy-start.15 = (f32[16,256]{1,0:T(8,128)}, f32[16,256]{1,0:T(8,128)S(1)}, u32[]{:S(2)}) copy-start(f32[16,256]{1,0:T(8,128)S(1)} %collective-permute-done.9.refs_9_) | copy-start | bytes 49156
  53.4 31.2 %collective-permute-start.14 = (bf16[1024,256]{1,0:T(8,128)(2,1)}, bf16[1024,256]{1,0:T(8,128)(2,1)}, u32[]{:S(2)}, u32[]{:S(2)}) collective-permute-start(bf16[1024,256]{1,0:T(8,128)(2,1)} %slice.29), channel_id=1, source_target_pairs={{0,1},{1,2},{2,3},{3,0},{4,5},{5,6},{6,7},{7,4},{8,9},{9,10},{10,1... | collective-permute-start | bytes 1572872 | tf_op jit(solution)/shard_map/ppermute | solution.py:465
  55.6 29.1 %collective-permute-start.18 = (bf16[1024,256]{1,0:T(8,128)(2,1)}, bf16[1024,256]{1,0:T(8,128)(2,1)}, u32[]{:S(2)}, u32[]{:S(2)}) collective-permute-start(bf16[1024,256]{1,0:T(8,128)(2,1)} %slice.30), channel_id=1, source_target_pairs={{0,3},{1,0},{2,1},{3,2},{4,7},{5,4},{6,5},{7,6},{8,11},{9,8},{10,9... | collective-permute-start | bytes 1572872 | tf_op jit(solution)/shard_map/ppermute | solution.py:465
  57.6 14.7 %all-to-all-start = ((s32[32,2,128]{2,1,0:T(2,128)}), s32[32,2,128]{2,1,0:T(2,128)S(1)}, u32[]{:S(2)}, u32[]{:S(2)}) async-start(s32[32,2,128]{2,1,0:T(2,128)} %broadcast_in_dim.71), calls=%async_computation | async-start | bytes 65536 | tf_op jit(solution)/shard_map/all_to_all | solution.py:503
  68.0 61.3 %collective-permute-start.13 = (bf16[2048,256]{1,0:T(8,128)(2,1)S(1)}, bf16[2048,256]{1,0:T(8,128)(2,1)S(1)}, u32[]{:S(2)}, u32[]{:S(2)}) collective-permute-start(bf16[2048,256]{1,0:T(8,128)(2,1)S(1)} %collective-permute-done.12.refs_19_.refs_25_), channel_id=1, source_target_pairs={{0,4},{4,0},{8,12},{12,8},{16,20},{20,16},{24,28},{28,24},{32,36},... | collective-permute-start | bytes 3145736 | tf_op jit(solution)/shard_map/ppermute | solution.py:548
  68.3 61.0 %collective-permute-start.17 = (bf16[2048,256]{1,0:T(8,128)(2,1)S(1)}, bf16[2048,256]{1,0:T(8,128)(2,1)}, u32[]{:S(2)}, u32[]{:S(2)}) collective-permute-start(bf16[2048,256]{1,0:T(8,128)(2,1)S(1)} %collective-permute-done.16.refs_23_.refs_29_), channel_id=1, source_target_pairs={{0,4},{4,0},{8,12},{12,8},{16,20},{20,16},{24,28},{28,24},{32,36},... | collective-permute-start | bytes 3145736 | tf_op jit(solution)/shard_map/ppermute | solution.py:548
  72.5 10.0 %collective-permute-start.2 = (bf16[656,256]{1,0:T(8,128)(2,1)S(1)}, bf16[656,256]{1,0:T(8,128)(2,1)S(1)}, u32[]{:S(2)}, u32[]{:S(2)}) collective-permute-start(bf16[656,256]{1,0:T(8,128)(2,1)S(1)} %pad_maximum_fusion.3.own_ref), channel_id=1, source_target_pairs={{0,3},{1,0},{2,1},{3,2},{4,7},{5,4},{6,5},{7,6},{8,11},{9,8},{10,9... | collective-permute-start | bytes 1007624 | tf_op jit(solution)/shard_map/ppermute | solution.py:465
  83.1 28.1 %collective-permute-start.8 = (bf16[8,32,256]{2,1,0:T(8,128)(2,1)}, bf16[8,32,256]{2,1,0:T(8,128)(2,1)S(1)}, u32[]{:S(2)}, u32[]{:S(2)}) collective-permute-start(bf16[8,32,256]{2,1,0:T(8,128)(2,1)} %bitcast.86), channel_id=1, source_target_pairs={{0,3},{1,0},{2,1},{3,2},{4,7},{5,4},{6,5},{7,6},{8,11},{9,8},{10,9... | collective-permute-start | bytes 393224 | tf_op jit(solution)/shard_map/ppermute | solution.py:465
  84.6 44.6 %collective-permute-start.15 = (bf16[1024,256]{1,0:T(8,128)(2,1)}, bf16[1024,256]{1,0:T(8,128)(2,1)}, u32[]{:S(2)}, u32[]{:S(2)}) collective-permute-start(bf16[1024,256]{1,0:T(8,128)(2,1)} %collective-permute-done.14.refs_21_), channel_id=1, source_target_pairs={{0,4},{4,0},{8,12},{12,8},{16,20},{20,16},{24,28},{28,24},{32,36},... | collective-permute-start | bytes 1572872 | tf_op jit(solution)/shard_map/ppermute | solution.py:548
  84.7 44.6 %collective-permute-start.19 = (bf16[1024,256]{1,0:T(8,128)(2,1)}, bf16[1024,256]{1,0:T(8,128)(2,1)}, u32[]{:S(2)}, u32[]{:S(2)}) collective-permute-start(bf16[1024,256]{1,0:T(8,128)(2,1)} %collective-permute-done.18.refs_27_), channel_id=1, source_target_pairs={{0,4},{4,0},{8,12},{12,8},{16,20},{20,16},{24,28},{28,24},{32,36},... | collective-permute-start | bytes 1572872 | tf_op jit(solution)/shard_map/ppermute | solution.py:548
  96.7 27.4 %copy-start.8 = (bf16[1,32,8,256]{3,2,1,0:T(8,128)(2,1)S(1)}, bf16[1,32,8,256]{3,2,1,0:T(8,128)(2,1)}, u32[]{:S(2)}) copy-start(bf16[1,32,8,256]{3,2,1,0:T(8,128)(2,1)} %get-tuple-element.55) | copy-start | bytes 393220
  111.3 18.8 %copy-start.11 = (bf16[8,32,256]{2,1,0:T(8,128)(2,1)}, bf16[8,32,256]{2,1,0:T(8,128)(2,1)S(1)}, u32[]{:S(2)}) copy-start(bf16[8,32,256]{2,1,0:T(8,128)(2,1)S(1)} %collective-permute-done.8.refs_7_) | copy-start | bytes 393220
  111.3 6.5 %collective-permute-start.3 = (bf16[7,32,256]{2,1,0:T(8,128)(2,1)S(1)}, bf16[7,32,256]{2,1,0:T(8,128)(2,1)}, u32[]{:S(2)}, u32[]{:S(2)}) collective-permute-start(bf16[7,32,256]{2,1,0:T(8,128)(2,1)S(1)} %get-tuple-element.58), channel_id=1, source_target_pairs={{0,1},{1,2},{2,3},{3,0},{4,5},{5,6},{6,7},{7,4},{8,9},{9,10},{10,1... | collective-permute-start | bytes 344072 | tf_op jit(solution)/shard_map/ppermute | solution.py:465
  117.8 6.4 %collective-permute-start.4 = (bf16[7,32,256]{2,1,0:T(8,128)(2,1)S(1)}, bf16[7,32,256]{2,1,0:T(8,128)(2,1)}, u32[]{:S(2)}, u32[]{:S(2)}) collective-permute-start(bf16[7,32,256]{2,1,0:T(8,128)(2,1)S(1)} %get-tuple-element.57), channel_id=1, source_target_pairs={{0,2},{1,3},{2,0},{3,1},{4,6},{5,7},{6,4},{7,5},{8,10},{9,11},{10,... | collective-permute-start | bytes 344072 | tf_op jit(solution)/shard_map/ppermute | solution.py:465
  124.2 5.1 %collective-permute-start.5 = (bf16[7,32,256]{2,1,0:T(8,128)(2,1)}, bf16[7,32,256]{2,1,0:T(8,128)(2,1)}, u32[]{:S(2)}, u32[]{:S(2)}) collective-permute-start(bf16[7,32,256]{2,1,0:T(8,128)(2,1)} %get-tuple-element.56), channel_id=1, source_target_pairs={{0,3},{1,0},{2,1},{3,2},{4,7},{5,4},{6,5},{7,6},{8,11},{9,8},{10,9... | collective-permute-start | bytes 344072 | tf_op jit(solution)/shard_map/ppermute | solution.py:465
  142.1 7.5 %collective-permute-start.20 = (bf16[15,32,256]{2,1,0:T(8,128)(2,1)S(1)}, bf16[15,32,256]{2,1,0:T(8,128)(2,1)S(1)}, u32[]{:S(2)}, u32[]{:S(2)}) collective-permute-start(bf16[15,32,256]{2,1,0:T(8,128)(2,1)S(1)} %get-tuple-element.51), channel_id=1, source_target_pairs={{0,3},{1,0},{2,1},{3,2},{4,7},{5,4},{6,5},{7,6},{8,11},{9,8},{10,9... | collective-permute-start | bytes 737288 | tf_op jit(solution)/shard_map/ppermute | solution.py:465
  143.3 9.1 %collective-permute-start.21 = (bf16[15,32,256]{2,1,0:T(8,128)(2,1)S(1)}, bf16[15,32,256]{2,1,0:T(8,128)(2,1)S(1)}, u32[]{:S(2)}, u32[]{:S(2)}) collective-permute-start(bf16[15,32,256]{2,1,0:T(8,128)(2,1)S(1)} %get-tuple-element.50), channel_id=1, source_target_pairs={{0,2},{1,3},{2,0},{3,1},{4,6},{5,7},{6,4},{7,5},{8,10},{9,11},{10,... | collective-permute-start | bytes 737288 | tf_op jit(solution)/shard_map/ppermute | solution.py:465
  143.8 11.0 %collective-permute-start.22 = (bf16[15,32,256]{2,1,0:T(8,128)(2,1)S(1)}, bf16[15,32,256]{2,1,0:T(8,128)(2,1)S(1)}, u32[]{:S(2)}, u32[]{:S(2)}) collective-permute-start(bf16[15,32,256]{2,1,0:T(8,128)(2,1)S(1)} %get-tuple-element.49), channel_id=1, source_target_pairs={{0,1},{1,2},{2,3},{3,0},{4,5},{5,6},{6,7},{7,4},{8,9},{9,10},{10,1... | collective-permute-start | bytes 737288 | tf_op jit(solution)/shard_map/ppermute | solution.py:465
  158.0 21.1 %all-to-all-start.1 = ((bf16[64,29,256]{2,1,0:T(8,128)(2,1)}), bf16[64,29,256]{2,1,0:T(8,128)(2,1)S(1)}, u32[]{:S(2)}, u32[]{:S(2)}) async-start(bf16[64,29,256]{2,1,0:T(8,128)(2,1)} %copy.72), calls=%async_computation.1 | async-start | bytes 2097152 | tf_op jit(solution)/shard_map/all_to_all | solution.py:618
  173.4 10.6 %copy-start.22 = (s32[128]{0:T(128)S(1)}, s32[128]{0:T(128)}, u32[]{:S(2)}) copy-start(s32[128]{0:T(128)} %copy-done.21) | copy-start | bytes 1540
  173.4 10.6 %copy-start.26 = (pred[128]{0:T(512)(128)(4,1)S(1)}, pred[128]{0:T(512)(128)(4,1)}, u32[]{:S(2)}) copy-start(pred[128]{0:T(512)(128)(4,1)} %get-tuple-element.44) | copy-start | bytes 388
  179.1 64.7 %all-to-all-start.2 = ((bf16[64,2,72,256]{3,2,1,0:T(8,128)(2,1)}), bf16[64,2,72,256]{3,2,1,0:T(8,128)(2,1)}, u32[]{:S(2)}, u32[]{:S(2)}) async-start(bf16[64,2,72,256]{3,2,1,0:T(8,128)(2,1)} %pack.1), calls=%async_computation.2 | async-start | bytes 9437184 | tf_op jit(solution)/shard_map/all_to_all | solution.py:518
  186.5 57.4 %copy-start.20 = (s32[128]{0:T(128)S(1)}, s32[128]{0:T(128)}, u32[]{:S(2)}) copy-start(s32[128]{0:T(128)} %param.30) | copy-start | bytes 1540
  244.6 14.5 %copy-start.4 = (bf16[29,128,256]{2,1,0:T(8,128)(2,1)S(1)}, bf16[29,128,256]{2,1,0:T(8,128)(2,1)}, u32[]{:S(2)}) copy-start(bf16[29,128,256]{2,1,0:T(8,128)(2,1)} %copy-done.3) | copy-start | bytes 5701636
  (7 other events, 13.0 us)

commit v5 on v4

--- a/solution.py
+++ b/solution.py
@@ -21,27 +21,52 @@
 SPAN = 80
 KEEP = 72
 CHUNK = 10
+FIELD = 7
 
 masked_score = -1e30
 
 
-def send_slots(new_slot, own_index, peer_count):
-    stream_count = new_slot.shape[0]
-    target = new_slot // stream_count
-    leaving = target != own_index
-    order = jnp.arange(stream_count, dtype=jnp.int32)
-    earlier = (target[None, :] == target[:, None]) & (order[None, :] < order[:, None])
-    position = jnp.sum(earlier.astype(jnp.int32), axis=1)
-    return jnp.where(leaving, target * CAP + position, peer_count * CAP)
-
-
-def arrival_slots(old_slot, own_index):
-    stream_count = old_slot.shape[0]
-    source = old_slot // stream_count
-    staying = source == own_index
-    earlier = (source[None, :] == source[:, None]) & (old_slot[None, :] < old_slot[:, None])
-    position = jnp.sum(earlier.astype(jnp.int32), axis=1)
-    return jnp.where(staying, -1, source * CAP + position)
+def route_body(own_s, new_ref, old_ref, both_ref, bucket_ref, arrival_ref, asked_ref):
+    own = own_s[0]
+    slots, count = asked_ref.shape
+    bits = count.bit_length() - 1
+
+    def column(row):
+        return jnp.transpose(jnp.broadcast_to(row, (count, count)))
+
+    def ranked(group_column, group_row, before):
+        same = jnp.where((group_column == group_row) & before, 1.0, 0.0)
+        return jnp.sum(same, axis=0, keepdims=True).astype(jnp.int32)
+
+    target = new_ref[...] >> bits
+    first = lax.broadcasted_iota(jnp.int32, (count, count), 0)
+    second = lax.broadcasted_iota(jnp.int32, (count, count), 1)
+    position = ranked(column(target), target, first < second)
+    bucket_ref[...] = jnp.where(target != own, target * CAP + position, slots)
+    old_row = old_ref[...]
+    old_column = column(old_row)
+    source = old_row >> bits
+    position = ranked(old_column >> bits, source, old_column < old_row)
+    arrival = jnp.where(source == own, -1, source * CAP + position)
+    arrival_ref[...] = arrival
+    slot = lax.broadcasted_iota(jnp.int32, (slots, count), 0)
+    hit = jnp.where(arrival == slot, both_ref[...].astype(jnp.float32), 0.0)
+    asked = jnp.sum(hit, axis=1, keepdims=True).astype(jnp.int32)
+    asked_ref[...] = jnp.broadcast_to(asked, (slots, count))
+
+
+def route(own_index, new_slot, old_slot, both, slots):
+    count = new_slot.shape[0]
+    row = jax.ShapeDtypeStruct((1, count), jnp.int32)
+    bucket, arrival, asked = pl.pallas_call(
+        route_body,
+        in_specs=[pl.BlockSpec(memory_space=pltpu.SMEM)]
+        + [pl.BlockSpec(memory_space=pltpu.VMEM)] * 3,
+        out_specs=[pl.BlockSpec(memory_space=pltpu.VMEM)] * 3,
+        out_shape=[row, row, jax.ShapeDtypeStruct((slots, count), jnp.int32)],
+        name="route",
+    )(own_index[None], new_slot[None], old_slot[None], both[None])
+    return bucket[0], arrival[0], asked
 
 
 def shift_rows(rows, first, second, third):
@@ -51,22 +76,33 @@
 
 
 def attend_body(
+    bucket_s,
+    both_s,
+    told_ref,
     query_ref,
     key_new_ref,
     value_new_ref,
     key_ref,
     value_ref,
-    valid_ref,
-    fill_ref,
     context_ref,
     key_out_ref,
     value_out_ref,
+    packed_ref,
 ):
+    base = pl.program_id(0) * BLOCK
+    slots = told_ref.shape[0]
+    for s in range(BLOCK):
+        slot = bucket_s[base + s]
+        told = told_ref[pl.ds(jnp.minimum(slot, slots - 1), 1), :]
+        packed_ref[s : s + 1, :] = jnp.where(
+            slot < slots, told, jnp.full_like(told, both_s[base + s])
+        )
+    packed = packed_ref[...]
     width = query_ref.shape[2]
     heads = width // LANES
     span = SPAN * BLOCK
-    valid = valid_ref[...]
-    low = (CACHE - fill_ref[:, :1]) * BLOCK
+    valid = packed >> FIELD
+    low = (CACHE - (packed[:, :1] & ((1 << FIELD) - 1))) * BLOCK
     high = (CACHE + valid[:, :1]) * BLOCK
     offset = lax.broadcasted_iota(jnp.int32, (BLOCK, span), 1) - lax.broadcasted_iota(
         jnp.int32, (BLOCK, span), 0
@@ -121,34 +157,41 @@
             out_ref[:, :, lanes] = shift_rows(rows, first, second, third).astype(jnp.bfloat16)
 
 
-def attend(valid_old, fill_old, queries, key_new, value_new, key_cache, value_cache, groups):
+def attend(bucket, both, told, queries, key_new, value_new, key_cache, value_cache, groups):
     stream_count = key_cache.shape[1]
     width = key_cache.shape[2]
 
-    def wide(column):
-        return jnp.broadcast_to(column[:, None], (stream_count, LANES))
-
     def block(rows):
-        return pl.BlockSpec((rows, BLOCK, width), lambda i: (0, i, 0))
+        return pl.BlockSpec((rows, BLOCK, width), lambda i, *_: (0, i, 0))
 
     per_group = stream_count // groups // BLOCK
-    scalar = pl.BlockSpec((BLOCK, LANES), lambda i: (i, 0))
     context = pl.BlockSpec(
-        (1, FRAMES, BLOCK, width), lambda i: (i // per_group, 0, i % per_group, 0)
+        (1, FRAMES, BLOCK, width), lambda i, *_: (i // per_group, 0, i % per_group, 0)
     )
     slab = jax.ShapeDtypeStruct((FRAMES, stream_count, width), jnp.bfloat16)
     return pl.pallas_call(
         attend_body,
-        grid=(stream_count // BLOCK,),
-        in_specs=[block(FRAMES)] * 3 + [block(CACHE)] * 2 + [scalar] * 2,
-        out_specs=[context, block(FRAMES), block(FRAMES)],
+        grid_spec=pltpu.PrefetchScalarGridSpec(
+            num_scalar_prefetch=2,
+            grid=(stream_count // BLOCK,),
+            in_specs=[pl.BlockSpec(told.shape, lambda i, *_: (0, 0))]
+            + [block(FRAMES)] * 3
+            + [block(CACHE)] * 2,
+            out_specs=[
+                context,
+                block(FRAMES),
+                block(FRAMES),
+                pl.BlockSpec((BLOCK, LANES), lambda i, *_: (i, 0)),
+            ],
+        ),
         out_shape=[
             jax.ShapeDtypeStruct((groups, FRAMES, stream_count // groups, width), jnp.bfloat16),
             slab,
             slab,
+            jax.ShapeDtypeStruct((stream_count, LANES), jnp.int32),
         ],
         name="attend",
-    )(queries, key_new, value_new, key_cache, value_cache, wide(valid_old), wide(fill_old))
+    )(bucket, both, told, queries, key_new, value_new, key_cache, value_cache)
 
 
 def pack_body(slot_s, key_ref, value_ref, send_ref, rows_f):
@@ -281,9 +324,9 @@
     weights, outs, inputs_ref, raw = rest[:3], rest[3:6], rest[6], rest[7]
     member = place_s[0]
     groups = raw.shape[0]
-    taps = frames_ref.shape[2]
+    taps = frames_ref.shape[1]
     width = raw.shape[2]
-    frames = frames_ref[0]
+    frames = jnp.transpose(frames_ref[0])
     for offset, piece in enumerate((own_ref, near_ref, far_ref, next_ref)):
         total = jnp.dot(frames, piece[:taps, :], preferred_element_type=jnp.float32)
         total = total + piece[taps : taps + 16, :].astype(jnp.float32)[:1]
@@ -311,7 +354,7 @@
 
 
 def head(member, frames, pieces, gain, matrices):
-    count, streams, taps = frames.shape
+    count, taps, streams = frames.shape
     width = matrices[0].shape[1]
     groups = len(pieces)
 
@@ -326,8 +369,8 @@
         grid_spec=pltpu.PrefetchScalarGridSpec(
             num_scalar_prefetch=1,
             grid=(count,),
-            in_specs=[pl.BlockSpec((1, streams, taps), lambda i, *_: (i, 0, 0))]
-            + [whole(p) for p in pieces]
+            in_specs=[pl.BlockSpec((1, taps, streams), lambda i, *_: (i, 0, 0))]
+            + [pl.BlockSpec((taps + 16, width), lambda i, *_: (0, 0))] * groups
             + [whole(gain)]
             + [whole(w) for w in matrices],
             out_specs=[per_frame, per_frame, per_frame]
@@ -341,10 +384,11 @@
 
 
 def tail_body(place_s, *refs):
-    contexts, caches, smalls, rest = refs[:4], refs[4:8], refs[8:12], refs[12:]
-    inputs_ref, gain_ref, valid_ref = rest[:3]
+    contexts, pieces, rest = refs[:4], refs[4:8], refs[8:]
+    inputs_ref, gain_ref, packed_ref = rest[:3]
     attn_ref, conv_ref, value_ref, gate_ref = rest[3:7]
-    low_refs, high_refs, out_ref = rest[7:13], rest[13:19], rest[19]
+    low_refs, high_refs, outs = rest[7:13], rest[13:19], rest[19:23]
+    out_ref, cache_f = rest[23:]
     member = place_s[0]
     front_half = place_s[1] == 0
     groups = len(contexts)
@@ -405,30 +449,47 @@
         axis=1,
     )
     normed_sides = ordered(normed)
-    valid = valid_ref[...]
+    valid = packed_ref[pl.ds(pl.multiple_of(member * share, share), share), :] >> FIELD
+    valid = jnp.concatenate([valid] * (width // LANES), axis=1)
     shift = valid - 1
     first = ((shift & 1) != 0)[None]
     second = ((shift & 2) != 0)[None]
     third = ((shift & 4) != 0)[None]
     conv_term = [None] * groups
+    extra = SUB * MELS + 16
+    tail_rows = extra + 3 * 16
     for step in range(groups):
         group = (member + groups - step) % groups
-        cache_ref, small_ref = caches[step], smalls[step]
+        piece = pieces[step]
+        small = sum(
+            piece[extra + 16 * i : extra + 16 * (i + 1), :].astype(jnp.float32) for i in range(3)
+        )
+        for h in range(width // LANES):
+            cache_f[h] = piece[tail_rows:, h * LANES : (h + 1) * LANES].astype(jnp.float32)
+        cached = jnp.concatenate(
+            [
+                jnp.stack(
+                    [cache_f[h, pl.ds(t, share, stride=CONV_CACHE), :] for t in range(CONV_CACHE)]
+                )
+                for h in range(width // LANES)
+            ],
+            axis=2,
+        )
         glu_value = wide(step, value_ref, 0)
         glu_gate = wide(step, gate_ref, 1)
         gated = (glu_value * jax.nn.sigmoid(glu_gate)).astype(jnp.bfloat16)
         conv_in = jnp.concatenate(
             [
-                cache_ref[...].astype(jnp.float32),
+                cached,
                 gated.astype(jnp.float32).reshape(FRAMES, share, width),
             ],
             axis=0,
         )
         depthwise = jnp.zeros((FRAMES, share, width), jnp.float32)
         for tap in range(KERNEL):
-            depthwise = depthwise + small_ref[tap : tap + 1, :][None] * conv_in[tap : tap + FRAMES]
-        shaped = depthwise * small_ref[KERNEL : KERNEL + 1, :][None]
-        shaped = shaped + small_ref[KERNEL + 1 : KERNEL + 2, :][None]
+            depthwise = depthwise + small[tap : tap + 1, :][None] * conv_in[tap : tap + FRAMES]
+        shaped = depthwise * small[KERNEL : KERNEL + 1, :][None]
+        shaped = shaped + small[KERNEL + 1 : KERNEL + 2, :][None]
         activated = (shaped * jax.nn.sigmoid(shaped)).astype(jnp.bfloat16)
         grouped(step, activated.reshape(rows, width), conv_ref, size // 2, conv_term)
         moved = shift_rows(
@@ -441,16 +502,152 @@
         out_ref[n, :FRAMES, :, :] = jnp.where(frame < valid[None], total, 0.0).astype(jnp.bfloat16)
 
 
+    for step, out in enumerate(outs):
+        out[...] = out_ref[(member + step) % groups]
+
+
 def tail(where, groups, *arrays):
     _, share, width = arrays[0].shape
+    shape = (FRAMES + CONV_CACHE, share, width)
+    vmem = pl.BlockSpec(memory_space=pltpu.VMEM)
     return pl.pallas_call(
         tail_body,
-        in_specs=[pl.BlockSpec(memory_space=pltpu.SMEM)]
-        + [pl.BlockSpec(memory_space=pltpu.VMEM)] * len(arrays),
-        out_specs=pl.BlockSpec(memory_space=pltpu.VMEM),
-        out_shape=jax.ShapeDtypeStruct((groups, FRAMES + CONV_CACHE, share, width), jnp.bfloat16),
+        in_specs=[pl.BlockSpec(memory_space=pltpu.SMEM)] + [vmem] * len(arrays),
+        out_specs=[vmem] * groups,
+        out_shape=[jax.ShapeDtypeStruct(shape, jnp.bfloat16)] * groups,
+        scratch_shapes=[
+            pltpu.VMEM((groups,) + shape, jnp.bfloat16),
+            pltpu.VMEM((width // LANES, CONV_CACHE * share, LANES), jnp.float32),
+        ],
         name="tail",
     )(where, *arrays)
+
+
+def collect_body(bucket_s, place_s, *refs):
+    pieces, slabs, (all_ref, send_ref, rows_f) = refs[:4], refs[4:6], refs[6:]
+    member = place_s[0]
+    groups = len(pieces)
+    frames, share, _ = pieces[0].shape
+    heads, _, _ = rows_f.shape
+    slots, keep, _ = send_ref.shape
+    count = groups * share
+    for step, piece in enumerate(pieces):
+        start = pl.multiple_of(((member + groups - step) % groups) * share, share)
+        all_ref[:frames, pl.ds(start, share), :] = piece[...]
+        for h in range(heads):
+            for t in range(frames):
+                rows_f[h, pl.ds(pl.multiple_of(t * count + start, share), share), :] = piece[
+                    t, :, h * LANES : (h + 1) * LANES
+                ].astype(jnp.float32)
+    for slab in slabs:
+        all_ref[frames : frames + FRAMES] = slab[...]
+        for h in range(heads):
+            rows_f[h, frames * count : (frames + FRAMES) * count, :] = (
+                slab[:, :, h * LANES : (h + 1) * LANES]
+                .astype(jnp.float32)
+                .reshape(FRAMES * count, LANES)
+            )
+        frames += FRAMES
+
+    def pack(s, carry):
+        slot = bucket_s[s]
+
+        @pl.when(slot < slots)
+        def _():
+            for h in range(heads):
+                send_ref[slot, :, h * LANES : (h + 1) * LANES] = rows_f[
+                    h, pl.ds(s, keep, stride=count), :
+                ].astype(jnp.bfloat16)
+
+        return carry
+
+    lax.fori_loop(0, count, pack, 0)
+
+
+def collect(bucket, member, pieces, slabs, slots):
+    frames = FRAMES + CONV_CACHE + 2 * FRAMES
+    keep = -(-frames // 16) * 16
+    _, count, width = slabs[0].shape
+    smem = pl.BlockSpec(memory_space=pltpu.SMEM)
+    vmem = pl.BlockSpec(memory_space=pltpu.VMEM)
+    return pl.pallas_call(
+        collect_body,
+        in_specs=[smem, smem] + [vmem] * 6,
+        out_specs=[vmem, vmem],
+        out_shape=[
+            jax.ShapeDtypeStruct((frames, count, width), jnp.bfloat16),
+            jax.ShapeDtypeStruct((slots, keep, width), jnp.bfloat16),
+        ],
+        scratch_shapes=[pltpu.VMEM((width // LANES, keep * count, LANES), jnp.float32)],
+        name="collect",
+    )(bucket, member[None], *pieces, *slabs)
+
+
+def finish_body(
+    arrival_s, all_ref, got_ref, _, __, encoded_ref, conv_ref, key_ref, value_ref, rows_f, conv_f
+):
+    heads = rows_f.shape[0]
+    frames, count, _ = all_ref.shape
+    keep = got_ref.shape[1]
+    for h in range(heads):
+        rows_f[h, : frames * count, :] = (
+            all_ref[:, :, h * LANES : (h + 1) * LANES]
+            .astype(jnp.float32)
+            .reshape(frames * count, LANES)
+        )
+
+    def fetch(s, carry):
+        slot = arrival_s[s]
+
+        @pl.when(slot >= 0)
+        def _():
+            for h in range(heads):
+                rows_f[h, pl.ds(s, keep, stride=count), :] = got_ref[
+                    slot, :, h * LANES : (h + 1) * LANES
+                ].astype(jnp.float32)
+
+        return carry
+
+    lax.fori_loop(0, count, fetch, 0)
+    ends = FRAMES + CONV_CACHE
+    for h in range(heads):
+        lanes = slice(h * LANES, (h + 1) * LANES)
+        for start, out in ((0, encoded_ref), (ends, key_ref), (ends + FRAMES, value_ref)):
+            rows = rows_f[h, start * count : (start + FRAMES) * count, :]
+            out[:, :, lanes] = rows.reshape(FRAMES, count, LANES).astype(jnp.bfloat16)
+        for t in range(CONV_CACHE):
+            at = (FRAMES + t) * count
+            conv_f[pl.ds(t, count, stride=CONV_CACHE), :] = rows_f[h, at : at + count, :]
+        conv_ref[:, :, lanes] = (
+            conv_f[...].reshape(count, CONV_CACHE, LANES).astype(jnp.bfloat16)
+        )
+
+
+def finish(arrival, everything, received, key_done, value_done):
+    _, count, width = everything.shape
+    keep = received.shape[1]
+    smem = pl.BlockSpec(memory_space=pltpu.SMEM)
+    vmem = pl.BlockSpec(memory_space=pltpu.VMEM)
+    kept = pl.BlockSpec(memory_space=pl.ANY)
+    slab = pl.BlockSpec((FRAMES, count, width), lambda i: (CACHE // FRAMES - 1, 0, 0))
+    return pl.pallas_call(
+        finish_body,
+        grid=(1,),
+        in_specs=[smem, vmem, vmem, kept, kept],
+        out_specs=[vmem, vmem, slab, slab],
+        out_shape=[
+            jax.ShapeDtypeStruct((FRAMES, count, width), jnp.bfloat16),
+            jax.ShapeDtypeStruct((count, CONV_CACHE, width), jnp.bfloat16),
+            jax.ShapeDtypeStruct(key_done.shape, jnp.bfloat16),
+            jax.ShapeDtypeStruct(value_done.shape, jnp.bfloat16),
+        ],
+        scratch_shapes=[
+            pltpu.VMEM((width // LANES, keep * count, LANES), jnp.float32),
+            pltpu.VMEM((CONV_CACHE * count, LANES), jnp.float32),
+        ],
+        input_output_aliases={3: 2, 4: 3},
+        name="finish",
+    )(arrival, everything, received, key_done, value_done)
 
 
 def swap(chunks, member, count):
@@ -495,33 +692,33 @@
     stream_count = spectra.shape[0]
     local_width = w_query.shape[1]
     slots = peer_count * CAP
-    bucket = send_slots(new_slot, own_index, peer_count)
-    arrival = arrival_slots(old_slot, own_index)
-    slot_ids = jnp.arange(slots, dtype=jnp.int32)
-    both = valid_new * 128 + cache_fill
-    asked = jnp.sum(jnp.where(arrival[None, :] == slot_ids[:, None], both[None, :], 0), axis=1)
-    told = lax.all_to_all(
-        jnp.broadcast_to(asked[:, None], (slots, LANES)),
-        "front",
-        split_axis=0,
-        concat_axis=0,
-        tiled=True,
-    )[:, 0]
-    told = jnp.sum(jnp.where(bucket[:, None] == slot_ids[None, :], told[None, :], 0), axis=1)
-    both_old = jnp.where(bucket < slots, told, both)
-    valid_old = both_old // 128
-    fill_old = both_old % 128
-
+    both = valid_new * (1 << FIELD) + cache_fill
+    bucket, arrival, asked = route(own_index, new_slot, old_slot, both, slots)
+    told = lax.all_to_all(asked, "front", split_axis=0, concat_axis=0, tiled=True)
     key_rows = key_cache.transpose(1, 0, 2)
     value_rows = value_cache.transpose(1, 0, 2)
     leaving_rows = pack_rows(bucket, key_rows, value_rows, slots)
     received = lax.all_to_all(leaving_rows, "front", split_axis=0, concat_axis=0, tiled=True)
     groups = lax.axis_size("enc")
     taps = SUB * MELS
-    with_bias = jnp.concatenate(
-        [sub_weight, jnp.broadcast_to(sub_bias[None, :], (16, local_width))], axis=0
-    )
-    sub_pieces = [with_bias] + [toward(with_bias, k, groups) for k in range(1, groups)]
+    share = stream_count // groups
+    small = jnp.concatenate(
+        [depth_kernel, norm_scale[None], norm_shift[None], jnp.zeros((5, local_width), jnp.float32)],
+        axis=0,
+    )
+    small_high = lax.reduce_precision(small, 8, 7)
+    small_rest = small - small_high
+    small_mid = lax.reduce_precision(small_rest, 8, 7)
+    common = [sub_weight, jnp.broadcast_to(sub_bias[None, :], (16, local_width))] + [
+        part.astype(jnp.bfloat16) for part in (small_high, small_mid, small_rest - small_mid)
+    ]
+    chunks = conv_cache.reshape(groups, share * CONV_CACHE, local_width)
+
+    def payload(step):
+        chunk = lax.dynamic_index_in_dim(chunks, (member + step) % groups, 0, False)
+        return jnp.concatenate(common + [chunk], axis=0)
+
+    pieces = [payload(0)] + [toward(payload(k), k, groups) for k in range(1, groups)]
 
     core = own_index % 2
     half = local_width // 2
@@ -555,39 +752,22 @@
     after_other = other_core(after)
     far_low_other = other_core(far_low)
     far_high_other = other_core(far_high)
-    small = jnp.concatenate(
-        [depth_kernel, norm_scale[None], norm_shift[None], jnp.zeros((5, local_width), jnp.float32)],
-        axis=0,
-    )
-    small_near, small_far, small_next = [toward(small, k, groups) for k in range(1, groups)]
-    share = stream_count // groups
-    cache_share = swap(
-        conv_cache.reshape(groups, share, CONV_CACHE, local_width).transpose(0, 2, 1, 3),
-        member,
-        groups,
-    )
-
-    frames = spectra.transpose(1, 2, 0).reshape(FRAMES, taps, stream_count).transpose(0, 2, 1)
+    frames = spectra.transpose(1, 2, 0).reshape(FRAMES, taps, stream_count)
     queries, key_new, value_new, inputs = head(
-        member, frames, sub_pieces, ln1_gain, (w_query, w_key, w_value)
-    )
-    context, key_slab, value_slab = attend(
-        valid_old, fill_old, queries, key_new, value_new, key_rows, value_rows, groups
+        member, frames, pieces, ln1_gain, (w_query, w_key, w_value)
+    )
+    context, key_slab, value_slab, packed = attend(
+        bucket, both, told, queries, key_new, value_new, key_rows, value_rows, groups
     )
     context = swap(context, member, groups)
-    valid_share = lax.dynamic_slice_in_dim(valid_old, member * share, share, 0)
     ended = tail(
         jnp.stack([member, core]),
         groups,
         *context,
-        *cache_share,
-        small,
-        small_near,
-        small_far,
-        small_next,
+        *pieces,
         inputs,
         ln2_gain[None, :],
-        jnp.broadcast_to(valid_share[:, None], (share, local_width)),
+        packed,
         w_attn_out,
         w_conv_out,
         w_glu_value,
@@ -605,34 +785,18 @@
         after,
         after_other,
     )
-    ended = swap(ended, member, groups)
-    ended = jnp.concatenate((ended[::-1] + ended[::-1])[:-1], axis=1)
-    finished = lax.dynamic_slice_in_dim(ended, (groups - 1 - member) * share, stream_count, 1)
-    finished = jnp.concatenate([finished, key_slab, value_slab], axis=0)
-    picker = (
-        bucket[None, :] == jnp.arange(slots, dtype=jnp.int32)[:, None]
-    ).astype(jnp.bfloat16)
-    leaving_end = jnp.einsum(
-        "ls,tsc->ltc", picker, finished, preferred_element_type=jnp.float32
-    ).astype(jnp.bfloat16)
+    ended = [ended[0]] + [toward(ended[k], k, groups) for k in range(1, groups)]
+    everything, leaving_end = collect(bucket, member, ended, (key_slab, value_slab), slots)
     received_end = lax.all_to_all(leaving_end, "front", split_axis=0, concat_axis=0, tiled=True)
-    placer = (
-        arrival[:, None] == jnp.arange(slots, dtype=jnp.int32)[None, :]
-    ).astype(jnp.bfloat16)
-    placed = jnp.einsum(
-        "sl,ltc->tsc", placer, received_end, preferred_element_type=jnp.float32
-    ).astype(jnp.bfloat16)
-    finished = jnp.where((arrival < 0)[None, :, None], finished, placed)
     key_done, value_done = place(arrival, valid_new, received, key_rows, value_rows)
-    edge = CACHE - FRAMES
-    ends = FRAMES + CONV_CACHE
-    key_done = lax.dynamic_update_slice_in_dim(key_done, finished[ends : ends + FRAMES], edge, 0)
-    value_done = lax.dynamic_update_slice_in_dim(value_done, finished[ends + FRAMES :], edge, 0)
+    encoded, conv_out, key_done, value_done = finish(
+        arrival, everything, received_end, key_done, value_done
+    )
     return (
-        finished[:FRAMES].transpose(1, 0, 2),
+        encoded.transpose(1, 0, 2),
         key_done.transpose(1, 0, 2),
         value_done.transpose(1, 0, 2),
-        finished[FRAMES:ends].transpose(1, 0, 2),
+        conv_out,
     )
 
 

time: 261 us -> 207 us (0.79)
  waiting for transfers between devices: 132 us -> 69.3 us
  Pallas kernels: 59.4 us -> 74.2 us
  local copies, waits for them, and re-layouts: 23.9 us -> 16.5 us
  starting transfers between devices: 38 us -> 40.9 us
    all_to_all x1, waiting for transfers between devices: 56.3 us -> 0.01 us  [on_device(): lax.all_to_all(leaving_rows, 'front', split_axis=0, concat_axis=0, tiled=...]
    pallas_call x1 -> x4, Pallas kernels: 12.7 us -> 27.2 us  [the longest x1 13.6 us: attend(): pl.pallas_call(attend_body, grid_spec=pltpu.PrefetchScalarGridSpec(num_sc...]
    concatenate x1 -> x4, local copies, waits for them, and re-layouts: 0.02 us -> 5.71 us  [payload(): return jnp.concatenate(common + [chunk], axis=0)]
    all_to_all x1, waiting for transfers between devices: 3.81 us -> 0.01 us  [on_device(): lax.all_to_all(asked, 'front', split_axis=0, concat_axis=0, tiled=True)]
    broadcast_in_dim x6 -> x0, local copies, waits for them, and re-layouts: 3.67 us -> none  [the longest x2 1.4 us: wide(): return jnp.broadcast_to(column[:, None], (stream_count, LANES))]
    all_to_all x1, waiting for transfers between devices: 5.74 us -> 2.16 us  [on_device(): lax.all_to_all(leaving_end, 'front', split_axis=0, concat_axis=0, tiled=T...]
    all_to_all x1, starting transfers between devices: 3.93 us -> 7.32 us  [on_device(): lax.all_to_all(leaving_end, 'front', split_axis=0, concat_axis=0, tiled=T...]
    ppermute x19 -> x13, starting transfers between devices: 20.8 us -> 18.5 us  [toward(): lax.ppermute(array, 'enc', [(i, (i + steps) % count) for i in range(count)])]
  transfers between devices with their start and end apart: 26 -> 20, of which waited for: 12 -> 11; matrix products, arithmetic and copies ran while one was open for 7% -> 7% of each run, Pallas kernels for 13% -> 33%
where the time goes in v5:
time: 207 us; the launch traced here: 205 us
  Pallas kernels  74.2 us (36%)
  waiting for transfers between devices  69.3 us (33%)
  starting transfers between devices  40.9 us (20%)
  local copies, waits for them, and re-layouts  16.5 us (8%)
  other arithmetic  2.9 us (1%)
    ppermute x13, waiting for transfers between devices, toward(): lax.ppermute(array, 'enc', [(i, (i + steps) % count) for i in range(count)])  67.1 us
    ppermute x13, starting transfers between devices, toward(): lax.ppermute(array, 'enc', [(i, (i + steps) % count) for i in range(count)])  18.5 us
    pallas_call x1, Pallas kernels, place(): pl.pallas_call(place_body, grid_spec=pltpu.PrefetchScalarGridSpec(num_sca...  14.3 us
    pallas_call x1, Pallas kernels, attend(): pl.pallas_call(attend_body, grid_spec=pltpu.PrefetchScalarGridSpec(num_sc...  13.6 us
    pallas_call x1, Pallas kernels, pack_rows(): pl.pallas_call(pack_body, grid_spec=pltpu.PrefetchScalarGridSpec(num_scal...  11.5 us
    pallas_call x1, Pallas kernels, tail(): pl.pallas_call(tail_body, in_specs=[pl.BlockSpec(memory_space=pltpu.SMEM)...  10.8 us
    pallas_call x1, Pallas kernels, head(): pl.pallas_call(head_body, grid_spec=pltpu.PrefetchScalarGridSpec(num_scal...  10.4 us
    all_to_all x1, starting transfers between devices, on_device(): lax.all_to_all(asked, 'front', split_axis=0, concat_axis=0, tiled=True)  7.43 us
  transfers between devices with their start and end apart: 20, of which 11 were waited for; matrix products, arithmetic and copies ran while one was open for 7% of the time, Pallas kernels for 33%

profile of v5, /device:TPU:0, one launch (start us, length us, event | category | flops | bytes accessed | tf_op | source)
XLA Modules:
  0.0 204.9 jit_solution(14863479226248230056)
XLA Ops:
  0.6 1.2 multiply_add_fusion.both_s
  1.8 1.5 route.1
  3.3 7.4 %all-to-all-start = ((s32[32,2,128]{2,1,0:T(2,128)}), s32[32,2,128]{2,1,0:T(2,128)S(1)}, u32[]{:S(2)}, u32[]{:S(2)}) async-start(s32[32,2,128]{2,1,0:T(2,128)} %bitcast.65), calls=%async_computation | async-start | bytes 65536 | tf_op jit(solution)/shard_map/all_to_all | solution.py:697
  10.8 11.5 %pack.1 = bf16[64,2,72,256]{3,2,1,0:T(8,128)(2,1)} custom-call(s32[128]{0:T(128)} %bitcast.66, bf16[70,128,256]{2,1,0:T(8,128)(2,1)} %bitcast.47, bf16[70,128,256]{2,1,0:T(8,128)(2,1)} %bitcast.50), custom_call_target="tpu_custom_call" | custom-call | tf_op jit(solution)/shard_map/pack/pallas_call | solution.py:229
  22.2 0.6 copy-done.13
  22.8 7.2 %all-to-all-start.2 = ((bf16[64,2,72,256]{3,2,1,0:T(8,128)(2,1)}), bf16[64,2,72,256]{3,2,1,0:T(8,128)(2,1)}, u32[]{:S(2)}, u32[]{:S(2)}) async-start(bf16[64,2,72,256]{3,2,1,0:T(8,128)(2,1)} %pack.1), calls=%async_computation.2 | async-start | bytes 9437184 | tf_op jit(solution)/shard_map/all_to_all | solution.py:701
  30.9 0.2 copy-done.7
  31.3 1.0 pad_maximum_fusion
  32.3 4.0 %collective-permute-start.10 = (bf16[2048,256]{1,0:T(8,128)(2,1)}, bf16[2048,256]{1,0:T(8,128)(2,1)S(1)}, u32[]{:S(2)}, u32[]{:S(2)}) collective-permute-start(bf16[2048,256]{1,0:T(8,128)(2,1)} %pad_maximum_fusion), channel_id=1, source_target_pairs={{0,3},{1,0},{2,1},{3,2},{4,7},{5,4},{6,5},{7,6},{8,11},{9,8},{10,9... | collective-permute-start | bytes 3145736 | tf_op jit(solution)/shard_map/ppermute | solution.py:662
  36.6 0.8 copy.39
  37.4 1.6 bitcast_dynamic-update-slice_fusion.2
  39.0 0.8 copy.40
  39.8 1.6 bitcast_dynamic-update-slice_fusion.1
  41.4 4.7 %collective-permute-start.1 = (bf16[960,256]{1,0:T(8,128)(2,1)}, bf16[960,256]{1,0:T(8,128)(2,1)}, u32[]{:S(2)}, u32[]{:S(2)}) collective-permute-start(bf16[960,256]{1,0:T(8,128)(2,1)} %bitcast_dynamic-update-slice_fusion.1), channel_id=1, source_target_pairs={{0,2},{1,3},{2,0},{3,1},{4,6},{5,7},{6,4},{7,5},{8,10},{9,11},{10,... | collective-permute-start | bytes 1474568 | tf_op jit(solution)/shard_map/ppermute | solution.py:662
  46.0 23.9 %collective-permute-done.10.refs_19_.refs_25_ = bf16[2048,256]{1,0:T(8,128)(2,1)S(1)} collective-permute-done((bf16[2048,256]{1,0:T(8,128)(2,1)}, bf16[2048,256]{1,0:T(8,128)(2,1)S(1)}, u32[]{:S(2)}, u32[]{:S(2)}) %collective-permute-start.10) | collective-permute-done | bytes 1048608 | tf_op jit(solution)/shard_map/ppermute | solution.py:662
  70.0 0.9 slice.9
  70.9 3.6 %collective-permute-start.12 = (bf16[1024,256]{1,0:T(8,128)(2,1)}, bf16[1024,256]{1,0:T(8,128)(2,1)}, u32[]{:S(2)}, u32[]{:S(2)}) collective-permute-start(bf16[1024,256]{1,0:T(8,128)(2,1)} %slice.9), channel_id=1, source_target_pairs={{0,3},{1,0},{2,1},{3,2},{4,7},{5,4},{6,5},{7,6},{8,11},{9,8},{10,9... | collective-permute-start | bytes 1572872 | tf_op jit(solution)/shard_map/ppermute | solution.py:662
  74.5 0.9 slice.8
  75.4 0.8 copy.41
  76.2 8.7 %collective-permute-done.near_ref.refs_5_ = bf16[960,256]{1,0:T(8,128)(2,1)S(1)} collective-permute-done((bf16[960,256]{1,0:T(8,128)(2,1)}, bf16[960,256]{1,0:T(8,128)(2,1)S(1)}, u32[]{:S(2)}, u32[]{:S(2)}) %collective-permute-start) | collective-permute-done | bytes 491552 | tf_op jit(solution)/shard_map/ppermute | solution.py:662
  84.9 1.7 bitcast_dynamic-update-slice_fusion
  86.6 0.5 collective-permute-start.13
  87.0 8.1 %collective-permute-done.8.refs_17_ = bf16[1024,256]{1,0:T(8,128)(2,1)} collective-permute-done((bf16[1024,256]{1,0:T(8,128)(2,1)}, bf16[1024,256]{1,0:T(8,128)(2,1)}, u32[]{:S(2)}, u32[]{:S(2)}) %collective-permute-start.8) | collective-permute-done | bytes 524320 | tf_op jit(solution)/shard_map/ppermute | solution.py:662
  95.2 0.9 bitcast_dynamic-update-slice_fusion.3.own_ref.refs_4_
  96.1 4.3 %collective-permute-done.2.next_ref.refs_7_ = bf16[960,256]{1,0:T(8,128)(2,1)} collective-permute-done((bf16[960,256]{1,0:T(8,128)(2,1)}, bf16[960,256]{1,0:T(8,128)(2,1)}, u32[]{:S(2)}, u32[]{:S(2)}) %collective-permute-start.2) | collective-permute-done | bytes 491552 | tf_op jit(solution)/shard_map/ppermute | solution.py:662
  100.4 10.4 %head.1 = (bf16[7,128,256]{2,1,0:T(8,128)(2,1)}, bf16[7,128,256]{2,1,0:T(8,128)(2,1)}, bf16[7,128,256]{2,1,0:T(8,128)(2,1)}, bf16[7,32,1024]{2,1,0:T(8,128)(2,1)}) custom-call(s32[1]{0:T(128)} %bitcast.6.place_s, bf16[7,640,128]{2,1,0:T(8,128)(2,1)} %bitcast.55, bf16[960,256]{1,0:T(8,128)(2,1)} %copy-done, bf16[960,256]{1,0:T(8,128)(2,1)} %copy-done.4, ...), custom_call_target="tpu_custom_call" | custom-call | tf_op jit(solution)/shard_map/head/pallas_call | solution.py:367
  110.8 13.6 %attend.1 = (bf16[4,7,32,256]{3,2,1,0:T(8,128)(2,1)}, bf16[7,128,256]{2,1,0:T(8,128)(2,1)}, bf16[7,128,256]{2,1,0:T(8,128)(2,1)}, s32[128,128]{1,0:T(8,128)}) custom-call(s32[128]{0:T(128)} %bitcast.67, s32[128]{0:T(128)} %multiply_add_fusion.both_s, s32[64,128]{1,0:T(8,128)} %bitcast.64, bf16[7,128,256]{2,1,0:T(8,128)(2,1)} %get-tuple-element.30.query_ref, ...), custom_call_target="tpu_custom_call" | custom-call | tf_op jit(solution)/shard_map/attend/pallas_call | solution.py:172
  124.4 1.7 dynamic-slice_bitcast_fusion
  126.1 1.5 collective-permute-start.5
  127.6 3.3 %collective-permute-done.5.refs_3_ = bf16[7,32,256]{2,1,0:T(8,128)(2,1)S(1)} collective-permute-done((bf16[7,32,256]{2,1,0:T(8,128)(2,1)S(1)}, bf16[7,32,256]{2,1,0:T(8,128)(2,1)S(1)}, u32[]{:S(2)}, u32[]{:S(2)}) %collective-permute-start.5) | collective-permute-done | bytes 114720 | tf_op jit(solution)/shard_map/ppermute | solution.py:662
  130.9 1.3 collective-permute-start.4
  132.2 5.0 %collective-permute-done.4.refs_2_ = bf16[7,32,256]{2,1,0:T(8,128)(2,1)S(1)} collective-permute-done((bf16[7,32,256]{2,1,0:T(8,128)(2,1)S(1)}, bf16[7,32,256]{2,1,0:T(8,128)(2,1)S(1)}, u32[]{:S(2)}, u32[]{:S(2)}) %collective-permute-start.4) | collective-permute-done | bytes 114720 | tf_op jit(solution)/shard_map/ppermute | solution.py:662
  137.3 0.6 pad_add_fusion.place_s
  137.9 5.3 %collective-permute-done.3.refs_1_ = bf16[7,32,256]{2,1,0:T(8,128)(2,1)S(1)} collective-permute-done((bf16[7,32,256]{2,1,0:T(8,128)(2,1)S(1)}, bf16[7,32,256]{2,1,0:T(8,128)(2,1)S(1)}, u32[]{:S(2)}, u32[]{:S(2)}) %collective-permute-start.3) | collective-permute-done | bytes 114720 | tf_op jit(solution)/shard_map/ppermute | solution.py:662
  143.3 0.6 copy-done.16
  143.9 10.8 %tail.1 = (bf16[15,32,256]{2,1,0:T(8,128)(2,1)}, bf16[15,32,256]{2,1,0:T(8,128)(2,1)}, bf16[15,32,256]{2,1,0:T(8,128)(2,1)}, bf16[15,32,256]{2,1,0:T(8,128)(2,1)}) custom-call(s32[2]{0:T(128)} %pad_add_fusion.place_s, bf16[7,32,256]{2,1,0:T(8,128)(2,1)} %get-tuple-element.53.refs_0_, bf16[7,32,256]{2,1,0:T(8,128)(2,1)} %copy-done.16, ...), custom_call_target="tpu_custom_call" | custom-call | tf_op jit(solution)/shard_map/tail/pallas_call | solution.py:513
  154.8 3.0 %collective-permute-start.15 = (bf16[15,32,256]{2,1,0:T(8,128)(2,1)}, bf16[15,32,256]{2,1,0:T(8,128)(2,1)S(1)}, u32[]{:S(2)}, u32[]{:S(2)}) collective-permute-start(bf16[15,32,256]{2,1,0:T(8,128)(2,1)} %get-tuple-element.38), channel_id=1, source_target_pairs={{0,2},{1,3},{2,0},{3,1},{4,6},{5,7},{6,4},{7,5},{8,10},{9,11},{10,... | collective-permute-start | bytes 737288 | tf_op jit(solution)/shard_map/ppermute | solution.py:662
  158.0 5.2 %collective-permute-done.14.refs_1_ = bf16[15,32,256]{2,1,0:T(8,128)(2,1)S(1)} collective-permute-done((bf16[15,32,256]{2,1,0:T(8,128)(2,1)}, bf16[15,32,256]{2,1,0:T(8,128)(2,1)S(1)}, u32[]{:S(2)}, u32[]{:S(2)}) %collective-permute-start.14) | collective-permute-done | bytes 245792 | tf_op jit(solution)/shard_map/ppermute | solution.py:662
  163.3 2.6 %collective-permute-done.15.refs_2_ = bf16[15,32,256]{2,1,0:T(8,128)(2,1)S(1)} collective-permute-done((bf16[15,32,256]{2,1,0:T(8,128)(2,1)}, bf16[15,32,256]{2,1,0:T(8,128)(2,1)S(1)}, u32[]{:S(2)}, u32[]{:S(2)}) %collective-permute-start.15) | collective-permute-done | bytes 245792 | tf_op jit(solution)/shard_map/ppermute | solution.py:662
  165.9 0.6 collective-permute-done.16.refs_3_
  166.6 0.6 copy-done.12
  167.2 6.3 %collect.1 = (bf16[29,128,256]{2,1,0:T(8,128)(2,1)}, bf16[64,32,256]{2,1,0:T(8,128)(2,1)}) custom-call(s32[128]{0:T(128)} %bitcast.68, s32[1]{0:T(128)} %bitcast.6.place_s, bf16[15,32,256]{2,1,0:T(8,128)(2,1)} %get-tuple-element.36.refs_0_, bf16[15,32,256]{2,1,0:T(8,128)(2,1)} %copy-done.10, bf16[15,32,256]{2,1,0:T(8,128)(2,1)} %copy-done.11, ...), custom_call_target="tpu_custom_call" | custom-call | tf_op jit(solution)/shard_map/collect/pallas_call | solution.py:573
  173.4 7.3 %all-to-all-start.1 = ((bf16[64,32,256]{2,1,0:T(8,128)(2,1)}), bf16[64,32,256]{2,1,0:T(8,128)(2,1)S(1)}, u32[]{:S(2)}, u32[]{:S(2)}) async-start(bf16[64,32,256]{2,1,0:T(8,128)(2,1)} %get-tuple-element.43), calls=%async_computation.1 | async-start | bytes 2097152 | tf_op jit(solution)/shard_map/all_to_all | solution.py:790
  180.8 0.7 broadcast_in_dim.54.valid_ref
  181.5 14.3 %place.1 = (bf16[70,128,256]{2,1,0:T(8,128)(2,1)}, bf16[70,128,256]{2,1,0:T(8,128)(2,1)}) custom-call(s32[128]{0:T(128)} %bitcast.71, bf16[64,2,72,256]{3,2,1,0:T(8,128)(2,1)} %all-to-all-done.2.got_ref, s32[128,128]{1,0:T(8,128)} %broadcast_in_dim.54.valid_ref, bf16[70,128,256]{2,1,0:T(8,128)(2,1)} %bitcast.49, bf16[70,128,256]{2,1,0:T(8,128)(2,1)} %bitcast.52), custom_call_target="tpu_custom_call" | custom-call | tf_op jit(solution)/shard_map/place/pallas_call | solution.py:296
  195.8 2.2 %all-to-all-done.1.got_ref = bf16[64,32,256]{2,1,0:T(8,128)(2,1)S(1)} async-done(((bf16[64,32,256]{2,1,0:T(8,128)(2,1)}), bf16[64,32,256]{2,1,0:T(8,128)(2,1)S(1)}, u32[]{:S(2)}, u32[]{:S(2)}) %all-to-all-start.1) | async-done | bytes 1048608 | tf_op jit(solution)/shard_map/all_to_all | solution.py:790
  198.0 1.0 copy-done.3
  199.0 5.9 %finish.1 = (bf16[7,128,256]{2,1,0:T(8,128)(2,1)}, bf16[128,8,256]{2,1,0:T(8,128)(2,1)}, bf16[70,128,256]{2,1,0:T(8,128)(2,1)}, bf16[70,128,256]{2,1,0:T(8,128)(2,1)}) custom-call(s32[128]{0:T(128)} %bitcast.72, bf16[29,128,256]{2,1,0:T(8,128)(2,1)} %get-tuple-element.42.all_ref, ...), custom_call_target="tpu_custom_call", output_to_operand_aliasing={{2}: (3, {}), {3}: (4, {})} | custom-call | tf_op jit(solution)/shard_map/finish/pallas_call | solution.py:633
  (72 shorter events, 1.7 us)
Async XLA Ops:
  3.3 18.9 %all-to-all-start = ((s32[32,2,128]{2,1,0:T(2,128)}), s32[32,2,128]{2,1,0:T(2,128)S(1)}, u32[]{:S(2)}, u32[]{:S(2)}) async-start(s32[32,2,128]{2,1,0:T(2,128)} %bitcast.65), calls=%async_computation | async-start | bytes 65536 | tf_op jit(solution)/shard_map/all_to_all | solution.py:697
  22.2 7.8 %copy-start.5 = (bf16[256,1024]{1,0:T(8,128)(2,1)S(1)}, bf16[256,1024]{1,0:T(8,128)(2,1)}, u32[]{:S(2)}) copy-start(bf16[256,1024]{1,0:T(8,128)(2,1)} %refs_11_.1) | copy-start | bytes 1572868
  22.2 7.9 %copy-start.6 = (bf16[256,1024]{1,0:T(8,128)(2,1)S(1)}, bf16[256,1024]{1,0:T(8,128)(2,1)}, u32[]{:S(2)}) copy-start(bf16[256,1024]{1,0:T(8,128)(2,1)} %refs_12_.1) | copy-start | bytes 1572868
  22.2 0.6 copy-start.13
  22.8 150.6 %all-to-all-start.2 = ((bf16[64,2,72,256]{3,2,1,0:T(8,128)(2,1)}), bf16[64,2,72,256]{3,2,1,0:T(8,128)(2,1)}, u32[]{:S(2)}, u32[]{:S(2)}) async-start(bf16[64,2,72,256]{3,2,1,0:T(8,128)(2,1)} %pack.1), calls=%async_computation.2 | async-start | bytes 9437184 | tf_op jit(solution)/shard_map/all_to_all | solution.py:701
  30.0 1.0 copy-start.7
  30.0 1.2 copy-start.8
  30.5 6.0 %copy-start.9 = (bf16[640,256]{1,0:T(8,128)(2,1)S(1)}, bf16[640,256]{1,0:T(8,128)(2,1)}, u32[]{:S(2)}) copy-start(bf16[640,256]{1,0:T(8,128)(2,1)} %param.23) | copy-start | bytes 983044
  30.7 5.8 %copy-start.17 = (f32[9,256]{1,0:T(8,128)S(1)}, f32[9,256]{1,0:T(8,128)}, u32[]{:S(2)}) copy-start(f32[9,256]{1,0:T(8,128)} %param.40) | copy-start | bytes 27652
  30.7 5.8 %copy-start.18 = (f32[256]{0:T(256)S(1)}, f32[256]{0:T(256)}, u32[]{:S(2)}) copy-start(f32[256]{0:T(256)} %param.42) | copy-start | bytes 3076
  30.7 5.8 %copy-start.19 = (f32[256]{0:T(256)S(1)}, f32[256]{0:T(256)}, u32[]{:S(2)}) copy-start(f32[256]{0:T(256)} %param.41) | copy-start | bytes 3076
  30.7 5.9 %copy-start.21 = (bf16[256]{0:T(256)(128)(2,1)S(1)}, bf16[256]{0:T(256)(128)(2,1)}, u32[]{:S(2)}) copy-start(bf16[256]{0:T(256)(128)(2,1)} %param.24) | copy-start | bytes 1540
  32.3 37.7 %collective-permute-start.10 = (bf16[2048,256]{1,0:T(8,128)(2,1)}, bf16[2048,256]{1,0:T(8,128)(2,1)S(1)}, u32[]{:S(2)}, u32[]{:S(2)}) collective-permute-start(bf16[2048,256]{1,0:T(8,128)(2,1)} %pad_maximum_fusion), channel_id=1, source_target_pairs={{0,3},{1,0},{2,1},{3,2},{4,7},{5,4},{6,5},{7,6},{8,11},{9,8},{10,9... | collective-permute-start | bytes 3145736 | tf_op jit(solution)/shard_map/ppermute | solution.py:662
  36.4 38.1 %collective-permute-start.6 = (bf16[2048,256]{1,0:T(8,128)(2,1)}, bf16[2048,256]{1,0:T(8,128)(2,1)S(1)}, u32[]{:S(2)}, u32[]{:S(2)}) collective-permute-start(bf16[2048,256]{1,0:T(8,128)(2,1)} %pad_maximum_fusion), channel_id=1, source_target_pairs={{0,1},{1,2},{2,3},{3,0},{4,5},{5,6},{6,7},{7,4},{8,9},{9,10},{10,1... | collective-permute-start | bytes 3145736 | tf_op jit(solution)/shard_map/ppermute | solution.py:662
  39.0 45.9 %collective-permute-start = (bf16[960,256]{1,0:T(8,128)(2,1)}, bf16[960,256]{1,0:T(8,128)(2,1)S(1)}, u32[]{:S(2)}, u32[]{:S(2)}) collective-permute-start(bf16[960,256]{1,0:T(8,128)(2,1)} %bitcast_dynamic-update-slice_fusion.2), channel_id=1, source_target_pairs={{0,1},{1,2},{2,3},{3,0},{4,5},{5,6},{6,7},{7,4},{8,9},{9,10},{10,1... | collective-permute-start | bytes 1474568 | tf_op jit(solution)/shard_map/ppermute | solution.py:662
  41.4 45.2 %collective-permute-start.1 = (bf16[960,256]{1,0:T(8,128)(2,1)}, bf16[960,256]{1,0:T(8,128)(2,1)}, u32[]{:S(2)}, u32[]{:S(2)}) collective-permute-start(bf16[960,256]{1,0:T(8,128)(2,1)} %bitcast_dynamic-update-slice_fusion.1), channel_id=1, source_target_pairs={{0,2},{1,3},{2,0},{3,1},{4,6},{5,7},{6,4},{7,5},{8,10},{9,11},{10,... | collective-permute-start | bytes 1474568 | tf_op jit(solution)/shard_map/ppermute | solution.py:662
  70.0 40.8 %copy-start.1 = (bf16[2048,256]{1,0:T(8,128)(2,1)}, bf16[2048,256]{1,0:T(8,128)(2,1)S(1)}, u32[]{:S(2)}) copy-start(bf16[2048,256]{1,0:T(8,128)(2,1)S(1)} %collective-permute-done.10.refs_19_.refs_25_) | copy-start | bytes 3145732
  70.9 15.7 %collective-permute-start.12 = (bf16[1024,256]{1,0:T(8,128)(2,1)}, bf16[1024,256]{1,0:T(8,128)(2,1)}, u32[]{:S(2)}, u32[]{:S(2)}) collective-permute-start(bf16[1024,256]{1,0:T(8,128)(2,1)} %slice.9), channel_id=1, source_target_pairs={{0,3},{1,0},{2,1},{3,2},{4,7},{5,4},{6,5},{7,6},{8,11},{9,8},{10,9... | collective-permute-start | bytes 1572872 | tf_op jit(solution)/shard_map/ppermute | solution.py:662
  74.5 36.3 %copy-start.2 = (bf16[2048,256]{1,0:T(8,128)(2,1)}, bf16[2048,256]{1,0:T(8,128)(2,1)S(1)}, u32[]{:S(2)}) copy-start(bf16[2048,256]{1,0:T(8,128)(2,1)S(1)} %collective-permute-done.6.refs_15_.refs_21_) | copy-start | bytes 3145732
  75.4 19.8 %collective-permute-start.8 = (bf16[1024,256]{1,0:T(8,128)(2,1)}, bf16[1024,256]{1,0:T(8,128)(2,1)}, u32[]{:S(2)}, u32[]{:S(2)}) collective-permute-start(bf16[1024,256]{1,0:T(8,128)(2,1)} %slice.8), channel_id=1, source_target_pairs={{0,1},{1,2},{2,3},{3,0},{4,5},{5,6},{6,7},{7,4},{8,9},{9,10},{10,1... | collective-permute-start | bytes 1572872 | tf_op jit(solution)/shard_map/ppermute | solution.py:662
  76.2 67.1 %collective-permute-start.11 = (bf16[2048,256]{1,0:T(8,128)(2,1)S(1)}, bf16[2048,256]{1,0:T(8,128)(2,1)}, u32[]{:S(2)}, u32[]{:S(2)}) collective-permute-start(bf16[2048,256]{1,0:T(8,128)(2,1)S(1)} %collective-permute-done.10.refs_19_.refs_25_), channel_id=1, source_target_pairs={{0,4},{4,0},{8,12},{12,8},{16,20},{20,16},{24,28},{28,24},{32,36},... | collective-permute-start | bytes 3145736 | tf_op jit(solution)/shard_map/ppermute | solution.py:745
  84.9 15.5 %copy-start.4 = (bf16[960,256]{1,0:T(8,128)(2,1)}, bf16[960,256]{1,0:T(8,128)(2,1)S(1)}, u32[]{:S(2)}) copy-start(bf16[960,256]{1,0:T(8,128)(2,1)S(1)} %collective-permute-done.near_ref.refs_5_) | copy-start | bytes 1474564
  84.9 58.4 %collective-permute-start.7 = (bf16[2048,256]{1,0:T(8,128)(2,1)S(1)}, bf16[2048,256]{1,0:T(8,128)(2,1)}, u32[]{:S(2)}, u32[]{:S(2)}) collective-permute-start(bf16[2048,256]{1,0:T(8,128)(2,1)S(1)} %collective-permute-done.6.refs_15_.refs_21_), channel_id=1, source_target_pairs={{0,4},{4,0},{8,12},{12,8},{16,20},{20,16},{24,28},{28,24},{32,36},... | collective-permute-start | bytes 3145736 | tf_op jit(solution)/shard_map/ppermute | solution.py:745
  86.6 13.8 %collective-permute-start.2 = (bf16[960,256]{1,0:T(8,128)(2,1)}, bf16[960,256]{1,0:T(8,128)(2,1)}, u32[]{:S(2)}, u32[]{:S(2)}) collective-permute-start(bf16[960,256]{1,0:T(8,128)(2,1)} %bitcast_dynamic-update-slice_fusion), channel_id=1, source_target_pairs={{0,3},{1,0},{2,1},{3,2},{4,7},{5,4},{6,5},{7,6},{8,11},{9,8},{10,9... | collective-permute-start | bytes 1474568 | tf_op jit(solution)/shard_map/ppermute | solution.py:662
  86.6 56.7 %collective-permute-start.13 = (bf16[1024,256]{1,0:T(8,128)(2,1)}, bf16[1024,256]{1,0:T(8,128)(2,1)}, u32[]{:S(2)}, u32[]{:S(2)}) collective-permute-start(bf16[1024,256]{1,0:T(8,128)(2,1)} %collective-permute-done.12.refs_23_), channel_id=1, source_target_pairs={{0,4},{4,0},{8,12},{12,8},{16,20},{20,16},{24,28},{28,24},{32,36},... | collective-permute-start | bytes 1572872 | tf_op jit(solution)/shard_map/ppermute | solution.py:745
  95.2 48.1 %collective-permute-start.9 = (bf16[1024,256]{1,0:T(8,128)(2,1)}, bf16[1024,256]{1,0:T(8,128)(2,1)}, u32[]{:S(2)}, u32[]{:S(2)}) collective-permute-start(bf16[1024,256]{1,0:T(8,128)(2,1)} %collective-permute-done.8.refs_17_), channel_id=1, source_target_pairs={{0,4},{4,0},{8,12},{12,8},{16,20},{20,16},{24,28},{28,24},{32,36},... | collective-permute-start | bytes 1572872 | tf_op jit(solution)/shard_map/ppermute | solution.py:745
  96.1 4.3 %copy-start = (bf16[960,256]{1,0:T(8,128)(2,1)}, bf16[960,256]{1,0:T(8,128)(2,1)S(1)}, u32[]{:S(2)}) copy-start(bf16[960,256]{1,0:T(8,128)(2,1)S(1)} %bitcast_dynamic-update-slice_fusion.3.own_ref.refs_4_) | copy-start | bytes 1474564
  126.1 4.8 %collective-permute-start.5 = (bf16[7,32,256]{2,1,0:T(8,128)(2,1)S(1)}, bf16[7,32,256]{2,1,0:T(8,128)(2,1)S(1)}, u32[]{:S(2)}, u32[]{:S(2)}) collective-permute-start(bf16[7,32,256]{2,1,0:T(8,128)(2,1)S(1)} %get-tuple-element.50), channel_id=1, source_target_pairs={{0,3},{1,0},{2,1},{3,2},{4,7},{5,4},{6,5},{7,6},{8,11},{9,8},{10,9... | collective-permute-start | bytes 344072 | tf_op jit(solution)/shard_map/ppermute | solution.py:662
  130.9 12.3 %copy-start.14 = (bf16[7,32,256]{2,1,0:T(8,128)(2,1)}, bf16[7,32,256]{2,1,0:T(8,128)(2,1)S(1)}, u32[]{:S(2)}) copy-start(bf16[7,32,256]{2,1,0:T(8,128)(2,1)S(1)} %collective-permute-done.5.refs_3_) | copy-start | bytes 344068
  130.9 6.3 %collective-permute-start.4 = (bf16[7,32,256]{2,1,0:T(8,128)(2,1)S(1)}, bf16[7,32,256]{2,1,0:T(8,128)(2,1)S(1)}, u32[]{:S(2)}, u32[]{:S(2)}) collective-permute-start(bf16[7,32,256]{2,1,0:T(8,128)(2,1)S(1)} %get-tuple-element.51), channel_id=1, source_target_pairs={{0,2},{1,3},{2,0},{3,1},{4,6},{5,7},{6,4},{7,5},{8,10},{9,11},{10,... | collective-permute-start | bytes 344072 | tf_op jit(solution)/shard_map/ppermute | solution.py:662
  137.2 6.0 %copy-start.15 = (bf16[7,32,256]{2,1,0:T(8,128)(2,1)}, bf16[7,32,256]{2,1,0:T(8,128)(2,1)S(1)}, u32[]{:S(2)}) copy-start(bf16[7,32,256]{2,1,0:T(8,128)(2,1)S(1)} %collective-permute-done.4.refs_2_) | copy-start | bytes 344068
  137.2 6.0 %collective-permute-start.3 = (bf16[7,32,256]{2,1,0:T(8,128)(2,1)S(1)}, bf16[7,32,256]{2,1,0:T(8,128)(2,1)S(1)}, u32[]{:S(2)}, u32[]{:S(2)}) collective-permute-start(bf16[7,32,256]{2,1,0:T(8,128)(2,1)S(1)} %get-tuple-element.52), channel_id=1, source_target_pairs={{0,1},{1,2},{2,3},{3,0},{4,5},{5,6},{6,7},{7,4},{8,9},{9,10},{10,1... | collective-permute-start | bytes 344072 | tf_op jit(solution)/shard_map/ppermute | solution.py:662
  143.2 0.6 copy-start.16
  154.7 26.1 %copy-start.20 = (s32[128]{0:T(128)S(1)}, s32[128]{0:T(128)}, u32[]{:S(2)}) copy-start(s32[128]{0:T(128)} %param.30) | copy-start | bytes 1540
  154.7 8.5 %collective-permute-start.14 = (bf16[15,32,256]{2,1,0:T(8,128)(2,1)}, bf16[15,32,256]{2,1,0:T(8,128)(2,1)S(1)}, u32[]{:S(2)}, u32[]{:S(2)}) collective-permute-start(bf16[15,32,256]{2,1,0:T(8,128)(2,1)} %get-tuple-element.37), channel_id=1, source_target_pairs={{0,1},{1,2},{2,3},{3,0},{4,5},{5,6},{6,7},{7,4},{8,9},{9,10},{10,1... | collective-permute-start | bytes 737288 | tf_op jit(solution)/shard_map/ppermute | solution.py:662
  154.8 11.1 %collective-permute-start.15 = (bf16[15,32,256]{2,1,0:T(8,128)(2,1)}, bf16[15,32,256]{2,1,0:T(8,128)(2,1)S(1)}, u32[]{:S(2)}, u32[]{:S(2)}) collective-permute-start(bf16[15,32,256]{2,1,0:T(8,128)(2,1)} %get-tuple-element.38), channel_id=1, source_target_pairs={{0,2},{1,3},{2,0},{3,1},{4,6},{5,7},{6,4},{7,5},{8,10},{9,11},{10,... | collective-permute-start | bytes 737288 | tf_op jit(solution)/shard_map/ppermute | solution.py:662
  157.8 8.6 %collective-permute-start.16 = (bf16[15,32,256]{2,1,0:T(8,128)(2,1)}, bf16[15,32,256]{2,1,0:T(8,128)(2,1)S(1)}, u32[]{:S(2)}, u32[]{:S(2)}) collective-permute-start(bf16[15,32,256]{2,1,0:T(8,128)(2,1)} %get-tuple-element.39), channel_id=1, source_target_pairs={{0,3},{1,0},{2,1},{3,2},{4,7},{5,4},{6,5},{7,6},{8,11},{9,8},{10,9... | collective-permute-start | bytes 737288 | tf_op jit(solution)/shard_map/ppermute | solution.py:662
  163.3 3.2 %copy-start.10 = (bf16[15,32,256]{2,1,0:T(8,128)(2,1)}, bf16[15,32,256]{2,1,0:T(8,128)(2,1)S(1)}, u32[]{:S(2)}) copy-start(bf16[15,32,256]{2,1,0:T(8,128)(2,1)S(1)} %collective-permute-done.14.refs_1_) | copy-start | bytes 737284
  165.9 0.7 copy-start.11
  166.5 0.7 copy-start.12
  173.4 24.5 %all-to-all-start.1 = ((bf16[64,32,256]{2,1,0:T(8,128)(2,1)}), bf16[64,32,256]{2,1,0:T(8,128)(2,1)S(1)}, u32[]{:S(2)}, u32[]{:S(2)}) async-start(bf16[64,32,256]{2,1,0:T(8,128)(2,1)} %get-tuple-element.43), calls=%async_computation.1 | async-start | bytes 2097152 | tf_op jit(solution)/shard_map/all_to_all | solution.py:790
  198.0 1.0 copy-start.3

commit v6 on v5

--- a/solution.py
+++ b/solution.py
@@ -26,10 +26,59 @@
 masked_score = -1e30
 
 
-def route_body(own_s, new_ref, old_ref, both_ref, bucket_ref, arrival_ref, asked_ref):
-    own = own_s[0]
+def prepare_body(
+    place_s,
+    new_ref,
+    old_ref,
+    both_ref,
+    weight_ref,
+    bias_ref,
+    kernel_ref,
+    scale_ref,
+    shift_ref,
+    cache_ref,
+    attn_ref,
+    conv_ref,
+    value_ref,
+    gate_ref,
+    *refs,
+):
+    payloads, (bucket_ref, arrival_ref, out_ref, in_ref, asked_ref, stack_ref, small) = (
+        refs[:4],
+        refs[4:],
+    )
+    member, own = place_s[0], place_s[2]
+    groups = len(payloads)
+    taps, width = weight_ref.shape
     slots, count = asked_ref.shape
     bits = count.bit_length() - 1
+
+    small[:KERNEL, :] = kernel_ref[...]
+    small[KERNEL : KERNEL + 1, :] = scale_ref[...]
+    small[KERNEL + 1 : KERNEL + 2, :] = shift_ref[...]
+    small[KERNEL + 2 :, :] = jnp.zeros((16 - KERNEL - 2, width), jnp.float32)
+    rest = small[...]
+    bias = jnp.broadcast_to(bias_ref[...].astype(jnp.float32), (16, width)).astype(jnp.bfloat16)
+    parts = []
+    for _ in range(3):
+        part = rest.astype(jnp.bfloat16)
+        parts.append(part)
+        rest = rest - part.astype(jnp.float32)
+    for step, payload in enumerate(payloads):
+        payload[:taps, :] = weight_ref[...]
+        payload[taps : taps + 16, :] = bias
+        for i, part in enumerate(parts):
+            payload[taps + 16 * (i + 1) : taps + 16 * (i + 2), :] = part
+        payload[taps + 64 :, :] = cache_ref[(member + step) % groups]
+
+    half = attn_ref.shape[0]
+    for start, source in ((0, attn_ref), (groups * half, conv_ref)):
+        for n in range(groups):
+            at = start + n * half
+            stack_ref[at : at + half, :] = source[:, n * width : (n + 1) * width]
+    at = 2 * groups * half
+    stack_ref[at : at + value_ref.shape[0], :] = value_ref[...]
+    stack_ref[at + value_ref.shape[0] :, :] = gate_ref[...]
 
     def column(row):
         return jnp.transpose(jnp.broadcast_to(row, (count, count)))
@@ -38,35 +87,66 @@
         same = jnp.where((group_column == group_row) & before, 1.0, 0.0)
         return jnp.sum(same, axis=0, keepdims=True).astype(jnp.int32)
 
-    target = new_ref[...] >> bits
     first = lax.broadcasted_iota(jnp.int32, (count, count), 0)
     second = lax.broadcasted_iota(jnp.int32, (count, count), 1)
+
+    def inverse(row):
+        hit = jnp.where(column(row) == second, (first + 1).astype(jnp.float32), 0.0)
+        return jnp.sum(hit, axis=0, keepdims=True).astype(jnp.int32) - 1
+
+    target = new_ref[...] >> bits
     position = ranked(column(target), target, first < second)
-    bucket_ref[...] = jnp.where(target != own, target * CAP + position, slots)
+    bucket = jnp.where(target != own, target * CAP + position, slots)
+    bucket_ref[...] = bucket
+    out_ref[...] = inverse(bucket)
     old_row = old_ref[...]
     old_column = column(old_row)
     source = old_row >> bits
     position = ranked(old_column >> bits, source, old_column < old_row)
     arrival = jnp.where(source == own, -1, source * CAP + position)
     arrival_ref[...] = arrival
+    in_ref[...] = inverse(arrival)
     slot = lax.broadcasted_iota(jnp.int32, (slots, count), 0)
     hit = jnp.where(arrival == slot, both_ref[...].astype(jnp.float32), 0.0)
     asked = jnp.sum(hit, axis=1, keepdims=True).astype(jnp.int32)
     asked_ref[...] = jnp.broadcast_to(asked, (slots, count))
 
 
-def route(own_index, new_slot, old_slot, both, slots):
-    count = new_slot.shape[0]
+def prepare(where, rows, sub, conv, chunks, columns, tall, slots):
+    count = rows[0].shape[0]
+    groups, chunk_rows, width = chunks.shape
+    taps = sub[0].shape[0]
+    whole = [r[None] for r in rows] + [sub[0], sub[1][None], conv[0], conv[1][None], conv[2][None]]
+
+    def full(array):
+        zeros = (0,) * array.ndim
+        return pl.BlockSpec(array.shape, lambda i, place_s: zeros)
+
+    def my_half(array):
+        return pl.BlockSpec(
+            (array.shape[0] // 2, array.shape[1]), lambda i, place_s: (place_s[1], 0)
+        )
+
     row = jax.ShapeDtypeStruct((1, count), jnp.int32)
-    bucket, arrival, asked = pl.pallas_call(
-        route_body,
-        in_specs=[pl.BlockSpec(memory_space=pltpu.SMEM)]
-        + [pl.BlockSpec(memory_space=pltpu.VMEM)] * 3,
-        out_specs=[pl.BlockSpec(memory_space=pltpu.VMEM)] * 3,
-        out_shape=[row, row, jax.ShapeDtypeStruct((slots, count), jnp.int32)],
-        name="route",
-    )(own_index[None], new_slot[None], old_slot[None], both[None])
-    return bucket[0], arrival[0], asked
+    payload = jax.ShapeDtypeStruct((taps + 64 + chunk_rows, width), jnp.bfloat16)
+    shapes = [payload] * groups + [row] * 4
+    shapes.append(jax.ShapeDtypeStruct((slots, count), jnp.int32))
+    shapes.append(jax.ShapeDtypeStruct((2 * groups * width, width), jnp.bfloat16))
+    outs = pl.pallas_call(
+        prepare_body,
+        grid_spec=pltpu.PrefetchScalarGridSpec(
+            num_scalar_prefetch=1,
+            grid=(1,),
+            in_specs=[full(a) for a in whole]
+            + [full(chunks)]
+            + [my_half(a) for a in columns + tall],
+            out_specs=[full(a) for a in shapes],
+            scratch_shapes=[pltpu.VMEM((16, width), jnp.float32)],
+        ),
+        out_shape=shapes,
+        name="prepare",
+    )(where, *whole, chunks, *columns, *tall)
+    return outs[:groups], [r[0] for r in outs[groups : groups + 4]], outs[-2], outs[-1]
 
 
 def shift_rows(rows, first, second, third):
@@ -321,66 +401,69 @@
 def head_body(
     place_s, frames_ref, own_ref, near_ref, far_ref, next_ref, gain_ref, *rest
 ):
-    weights, outs, inputs_ref, raw = rest[:3], rest[3:6], rest[6], rest[7]
+    weights, outs, inputs_ref, flat, raw, normed = rest[:3], rest[3:6], *rest[6:]
     member = place_s[0]
     groups = raw.shape[0]
-    taps = frames_ref.shape[1]
     width = raw.shape[2]
-    frames = jnp.transpose(frames_ref[0])
+    count, taps, streams = frames_ref.shape
+    for t in range(count):
+        flat[t * streams : (t + 1) * streams, :] = jnp.transpose(frames_ref[t])
     for offset, piece in enumerate((own_ref, near_ref, far_ref, next_ref)):
-        total = jnp.dot(frames, piece[:taps, :], preferred_element_type=jnp.float32)
+        total = jnp.dot(flat[...], piece[:taps, :], preferred_element_type=jnp.float32)
         total = total + piece[taps : taps + 16, :].astype(jnp.float32)[:1]
         raw[(member + groups - offset) % groups] = total.astype(jnp.bfloat16)
-    values = [raw[g].astype(jnp.float32) for g in range(groups)]
     model_width = groups * width
-    average = sum(jnp.sum(v, axis=1, keepdims=True) for v in values) * (1.0 / model_width)
-    values = [v - average for v in values]
-    spread = sum(jnp.sum(v * v, axis=1, keepdims=True) for v in values) * (1.0 / model_width)
-    scale = lax.rsqrt(spread + 1e-05)
-    normed = [
-        (v * scale * gain_ref[:, g * width : (g + 1) * width]).astype(jnp.bfloat16)
-        for g, v in enumerate(values)
-    ]
-    normed = jnp.concatenate(normed, axis=1)
+    share = inputs_ref.shape[1]
+    for t in range(count):
+        lines = slice(t * streams, (t + 1) * streams)
+        values = [raw[g, lines, :].astype(jnp.float32) for g in range(groups)]
+        average = sum(jnp.sum(v, axis=1, keepdims=True) for v in values) * (1.0 / model_width)
+        values = [v - average for v in values]
+        spread = sum(jnp.sum(v * v, axis=1, keepdims=True) for v in values) * (1.0 / model_width)
+        scale = lax.rsqrt(spread + 1e-05)
+        for g, v in enumerate(values):
+            columns = slice(g * width, (g + 1) * width)
+            normed[lines, columns] = (v * scale * gain_ref[:, columns]).astype(jnp.bfloat16)
+            start = pl.multiple_of(t * streams + member * share, share)
+            inputs_ref[t, :, columns] = raw[g, pl.ds(start, share), :]
     for matrix, out in zip(weights, outs):
-        out[0] = jnp.dot(normed, matrix[...], preferred_element_type=jnp.float32).astype(
-            jnp.bfloat16
-        )
-    share = inputs_ref.shape[1]
-    for g in range(groups):
-        inputs_ref[0, :, g * width : (g + 1) * width] = raw[
-            g, pl.ds(pl.multiple_of(member * share, share), share), :
-        ]
-
-
-def head(member, frames, pieces, gain, matrices):
+        product = jnp.dot(normed[...], matrix[...], preferred_element_type=jnp.float32)
+        out[...] = product.astype(jnp.bfloat16).reshape(count, streams, width)
+
+
+def head(where, frames, pieces, gain, matrices):
     count, taps, streams = frames.shape
     width = matrices[0].shape[1]
     groups = len(pieces)
 
     def whole(array):
-        return pl.BlockSpec(array.shape, lambda i, *_: (0, 0))
-
-    per_frame = pl.BlockSpec((1, streams, width), lambda i, *_: (i, 0, 0))
-    shape = jax.ShapeDtypeStruct((count, streams, width), jnp.bfloat16)
+        zeros = (0,) * array.ndim
+        return pl.BlockSpec(array.shape, lambda i, *_: zeros)
+
     gain = gain[None, :]
+    shapes = [jax.ShapeDtypeStruct((count, streams, width), jnp.bfloat16)] * 3
+    shapes.append(
+        jax.ShapeDtypeStruct((count, streams // groups, groups * width), jnp.bfloat16)
+    )
     return pl.pallas_call(
         head_body,
         grid_spec=pltpu.PrefetchScalarGridSpec(
             num_scalar_prefetch=1,
-            grid=(count,),
-            in_specs=[pl.BlockSpec((1, taps, streams), lambda i, *_: (i, 0, 0))]
+            grid=(1,),
+            in_specs=[whole(frames)]
             + [pl.BlockSpec((taps + 16, width), lambda i, *_: (0, 0))] * groups
             + [whole(gain)]
             + [whole(w) for w in matrices],
-            out_specs=[per_frame, per_frame, per_frame]
-            + [pl.BlockSpec((1, streams // groups, groups * width), lambda i, *_: (i, 0, 0))],
-            scratch_shapes=[pltpu.VMEM((groups, streams, width), jnp.bfloat16)],
+            out_specs=[whole(a) for a in shapes],
+            scratch_shapes=[
+                pltpu.VMEM((count * streams, taps), jnp.bfloat16),
+                pltpu.VMEM((groups, count * streams, width), jnp.bfloat16),
+                pltpu.VMEM((count * streams, groups * width), jnp.bfloat16),
+            ],
         ),
-        out_shape=[shape, shape, shape]
-        + [jax.ShapeDtypeStruct((count, streams // groups, groups * width), jnp.bfloat16)],
+        out_shape=shapes,
         name="head",
-    )(member[None], frames, *pieces, gain, *matrices)
+    )(where, frames, *pieces, gain, *matrices)
 
 
 def tail_body(place_s, *refs):
@@ -523,7 +606,7 @@
     )(where, *arrays)
 
 
-def collect_body(bucket_s, place_s, *refs):
+def collect_body(leaving_s, place_s, *refs):
     pieces, slabs, (all_ref, send_ref, rows_f) = refs[:4], refs[4:6], refs[6:]
     member = place_s[0]
     groups = len(pieces)
@@ -549,10 +632,10 @@
             )
         frames += FRAMES
 
-    def pack(s, carry):
-        slot = bucket_s[s]
-
-        @pl.when(slot < slots)
+    def pack(slot, carry):
+        s = leaving_s[slot]
+
+        @pl.when(s >= 0)
         def _():
             for h in range(heads):
                 send_ref[slot, :, h * LANES : (h + 1) * LANES] = rows_f[
@@ -561,10 +644,10 @@
 
         return carry
 
-    lax.fori_loop(0, count, pack, 0)
-
-
-def collect(bucket, member, pieces, slabs, slots):
+    lax.fori_loop(0, slots, pack, 0)
+
+
+def collect(leaving, where, pieces, slabs, slots):
     frames = FRAMES + CONV_CACHE + 2 * FRAMES
     keep = -(-frames // 16) * 16
     _, count, width = slabs[0].shape
@@ -580,11 +663,11 @@
         ],
         scratch_shapes=[pltpu.VMEM((width // LANES, keep * count, LANES), jnp.float32)],
         name="collect",
-    )(bucket, member[None], *pieces, *slabs)
+    )(leaving, where, *pieces, *slabs)
 
 
 def finish_body(
-    arrival_s, all_ref, got_ref, _, __, encoded_ref, conv_ref, key_ref, value_ref, rows_f, conv_f
+    coming_s, all_ref, got_ref, _, __, encoded_ref, conv_ref, key_ref, value_ref, rows_f, conv_f
 ):
     heads = rows_f.shape[0]
     frames, count, _ = all_ref.shape
@@ -596,10 +679,10 @@
             .reshape(frames * count, LANES)
         )
 
-    def fetch(s, carry):
-        slot = arrival_s[s]
-
-        @pl.when(slot >= 0)
+    def fetch(slot, carry):
+        s = coming_s[slot]
+
+        @pl.when(s >= 0)
         def _():
             for h in range(heads):
                 rows_f[h, pl.ds(s, keep, stride=count), :] = got_ref[
@@ -608,7 +691,7 @@
 
         return carry
 
-    lax.fori_loop(0, count, fetch, 0)
+    lax.fori_loop(0, got_ref.shape[0], fetch, 0)
     ends = FRAMES + CONV_CACHE
     for h in range(heads):
         lanes = slice(h * LANES, (h + 1) * LANES)
@@ -623,7 +706,7 @@
         )
 
 
-def finish(arrival, everything, received, key_done, value_done):
+def finish(coming, everything, received, key_done, value_done):
     _, count, width = everything.shape
     keep = received.shape[1]
     smem = pl.BlockSpec(memory_space=pltpu.SMEM)
@@ -647,7 +730,7 @@
         ],
         input_output_aliases={3: 2, 4: 3},
         name="finish",
-    )(arrival, everything, received, key_done, value_done)
+    )(coming, everything, received, key_done, value_done)
 
 
 def swap(chunks, member, count):
@@ -692,53 +775,29 @@
     stream_count = spectra.shape[0]
     local_width = w_query.shape[1]
     slots = peer_count * CAP
+    groups = lax.axis_size("enc")
+    core = own_index % 2
+    where = jnp.stack([member, core, own_index])
     both = valid_new * (1 << FIELD) + cache_fill
-    bucket, arrival, asked = route(own_index, new_slot, old_slot, both, slots)
+    share = stream_count // groups
+    payloads, maps, asked, stack = prepare(
+        where,
+        (new_slot, old_slot, both),
+        (sub_weight, sub_bias),
+        (depth_kernel, norm_scale, norm_shift),
+        conv_cache.reshape(groups, share * CONV_CACHE, local_width),
+        (w_attn_out, w_conv_out),
+        (w_glu_value, w_glu_gate),
+        slots,
+    )
+    bucket, arrival, leaving, coming = maps
+    pieces = [payloads[0]] + [toward(payloads[k], k, groups) for k in range(1, groups)]
     told = lax.all_to_all(asked, "front", split_axis=0, concat_axis=0, tiled=True)
     key_rows = key_cache.transpose(1, 0, 2)
     value_rows = value_cache.transpose(1, 0, 2)
     leaving_rows = pack_rows(bucket, key_rows, value_rows, slots)
     received = lax.all_to_all(leaving_rows, "front", split_axis=0, concat_axis=0, tiled=True)
-    groups = lax.axis_size("enc")
     taps = SUB * MELS
-    share = stream_count // groups
-    small = jnp.concatenate(
-        [depth_kernel, norm_scale[None], norm_shift[None], jnp.zeros((5, local_width), jnp.float32)],
-        axis=0,
-    )
-    small_high = lax.reduce_precision(small, 8, 7)
-    small_rest = small - small_high
-    small_mid = lax.reduce_precision(small_rest, 8, 7)
-    common = [sub_weight, jnp.broadcast_to(sub_bias[None, :], (16, local_width))] + [
-        part.astype(jnp.bfloat16) for part in (small_high, small_mid, small_rest - small_mid)
-    ]
-    chunks = conv_cache.reshape(groups, share * CONV_CACHE, local_width)
-
-    def payload(step):
-        chunk = lax.dynamic_index_in_dim(chunks, (member + step) % groups, 0, False)
-        return jnp.concatenate(common + [chunk], axis=0)
-
-    pieces = [payload(0)] + [toward(payload(k), k, groups) for k in range(1, groups)]
-
-    core = own_index % 2
-    half = local_width // 2
-
-    def core_rows(matrix):
-        count = matrix.shape[0] // 2
-        return lax.dynamic_slice_in_dim(matrix, core * count, count, 0)
-
-    def blocks(matrix):
-        return (
-            core_rows(matrix)
-            .reshape(half, groups, local_width)
-            .transpose(1, 0, 2)
-            .reshape(groups * half, local_width)
-        )
-
-    stack = jnp.concatenate(
-        [blocks(w_attn_out), blocks(w_conv_out), core_rows(w_glu_value), core_rows(w_glu_gate)],
-        axis=0,
-    )
     middle_row = stack.shape[0] // 2
 
     def other_core(array):
@@ -754,14 +813,14 @@
     far_high_other = other_core(far_high)
     frames = spectra.transpose(1, 2, 0).reshape(FRAMES, taps, stream_count)
     queries, key_new, value_new, inputs = head(
-        member, frames, pieces, ln1_gain, (w_query, w_key, w_value)
+        where, frames, pieces, ln1_gain, (w_query, w_key, w_value)
     )
     context, key_slab, value_slab, packed = attend(
         bucket, both, told, queries, key_new, value_new, key_rows, value_rows, groups
     )
     context = swap(context, member, groups)
     ended = tail(
-        jnp.stack([member, core]),
+        where,
         groups,
         *context,
         *pieces,
@@ -786,11 +845,11 @@
         after_other,
     )
     ended = [ended[0]] + [toward(ended[k], k, groups) for k in range(1, groups)]
-    everything, leaving_end = collect(bucket, member, ended, (key_slab, value_slab), slots)
+    everything, leaving_end = collect(leaving, where, ended, (key_slab, value_slab), slots)
     received_end = lax.all_to_all(leaving_end, "front", split_axis=0, concat_axis=0, tiled=True)
     key_done, value_done = place(arrival, valid_new, received, key_rows, value_rows)
     encoded, conv_out, key_done, value_done = finish(
-        arrival, everything, received_end, key_done, value_done
+        coming, everything, received_end, key_done, value_done
     )
     return (
         encoded.transpose(1, 0, 2),

time: 207 us -> 204 us (0.986)
  local copies, waits for them, and re-layouts: 16.5 us -> 7 us
  waiting for transfers between devices: 69.3 us -> 77.8 us
    ppermute x13, waiting for transfers between devices: 67.1 us -> 75.6 us  [toward(): lax.ppermute(array, 'enc', [(i, (i + steps) % count) for i in range(count)])]
    concatenate x5 -> x0, local copies, waits for them, and re-layouts: 5.79 us -> none  [the longest x4 5.71 us: payload(): return jnp.concatenate(common + [chunk], axis=0)]
    unnamed x54 -> x26, local copies, waits for them, and re-layouts: 6.14 us -> 3.25 us
    pallas_call x1, Pallas kernels: 1.49 us -> 4.07 us  [prepare(): pl.pallas_call(prepare_body, grid_spec=pltpu.PrefetchScalarGridSpec(num_s...]
  transfers between devices with their start and end apart: 20 -> 20, of which waited for: 11 -> 11; matrix products, arithmetic and copies ran while one was open for 7% -> 1% of each run, Pallas kernels for 33% -> 32%
where the time goes in v6:
time: 204 us; the launch traced here: 202 us
  waiting for transfers between devices  77.8 us (38%)
  Pallas kernels  73.2 us (36%)
  starting transfers between devices  41.7 us (20%)
  local copies, waits for them, and re-layouts  7 us (3%)
    ppermute x13, waiting for transfers between devices, toward(): lax.ppermute(array, 'enc', [(i, (i + steps) % count) for i in range(count)])  75.6 us
    ppermute x13, starting transfers between devices, toward(): lax.ppermute(array, 'enc', [(i, (i + steps) % count) for i in range(count)])  19.2 us
    pallas_call x1, Pallas kernels, place(): pl.pallas_call(place_body, grid_spec=pltpu.PrefetchScalarGridSpec(num_sca...  14.3 us
    pallas_call x1, Pallas kernels, attend(): pl.pallas_call(attend_body, grid_spec=pltpu.PrefetchScalarGridSpec(num_sc...  13.6 us
    pallas_call x1, Pallas kernels, pack_rows(): pl.pallas_call(pack_body, grid_spec=pltpu.PrefetchScalarGridSpec(num_scal...  11.4 us
    pallas_call x1, Pallas kernels, tail(): pl.pallas_call(tail_body, in_specs=[pl.BlockSpec(memory_space=pltpu.SMEM)...  10.8 us
    pallas_call x1, Pallas kernels, head(): pl.pallas_call(head_body, grid_spec=pltpu.PrefetchScalarGridSpec(num_scal...  8.62 us
    all_to_all x1, starting transfers between devices, on_device(): lax.all_to_all(asked, 'front', split_axis=0, concat_axis=0, tiled=True)  7.43 us
  transfers between devices with their start and end apart: 20, of which 11 were waited for; matrix products, arithmetic and copies ran while one was open for 1% of the time, Pallas kernels for 32%

profile of v6, /device:TPU:0, one launch (start us, length us, event | category | flops | bytes accessed | tf_op | source)
XLA Modules:
  0.0 202.4 jit_solution(7410450904159119389)
XLA Ops:
  0.6 1.2 broadcast_in_dim.33.bias_ref
  1.9 1.2 multiply_add_fusion.both_s
  3.1 0.6 pad_add_fusion.place_s
  3.8 4.1 %prepare.1 = (bf16[960,256]{1,0:T(8,128)(2,1)}, bf16[960,256]{1,0:T(8,128)(2,1)}, bf16[960,256]{1,0:T(8,128)(2,1)}, bf16[960,256]{1,0:T(8,128)(2,1)}, s32[1,128]...) custom-call(s32[3]{0:T(128)} %pad_add_fusion.place_s, ...), custom_call_target="tpu_custom_call" | custom-call | tf_op jit(solution)/shard_map/prepare/pallas_call | solution.py:135
  7.8 7.4 %all-to-all-start = ((s32[32,2,128]{2,1,0:T(2,128)}), s32[32,2,128]{2,1,0:T(2,128)S(1)}, u32[]{:S(2)}, u32[]{:S(2)}) async-start(s32[32,2,128]{2,1,0:T(2,128)} %bitcast.44), calls=%async_computation | async-start | bytes 65536 | tf_op jit(solution)/shard_map/all_to_all | solution.py:795
  15.3 11.4 %pack.1 = bf16[64,2,72,256]{3,2,1,0:T(8,128)(2,1)} custom-call(s32[128]{0:T(128)} %bitcast.47, bf16[70,128,256]{2,1,0:T(8,128)(2,1)} %bitcast.33, bf16[70,128,256]{2,1,0:T(8,128)(2,1)} %bitcast.36), custom_call_target="tpu_custom_call" | custom-call | tf_op jit(solution)/shard_map/pack/pallas_call | solution.py:309
  26.7 0.0 all-to-all-done
  26.7 0.6 copy-done.7
  27.3 7.2 %all-to-all-start.2 = ((bf16[64,2,72,256]{3,2,1,0:T(8,128)(2,1)}), bf16[64,2,72,256]{3,2,1,0:T(8,128)(2,1)}, u32[]{:S(2)}, u32[]{:S(2)}) async-start(bf16[64,2,72,256]{3,2,1,0:T(8,128)(2,1)} %pack.1), calls=%async_computation.2 | async-start | bytes 9437184 | tf_op jit(solution)/shard_map/all_to_all | solution.py:799
  34.5 4.1 %collective-permute-start.10 = (bf16[2048,256]{1,0:T(8,128)(2,1)S(1)}, bf16[2048,256]{1,0:T(8,128)(2,1)S(1)}, u32[]{:S(2)}, u32[]{:S(2)}) collective-permute-start(bf16[2048,256]{1,0:T(8,128)(2,1)S(1)} %copy-done.12), channel_id=1, source_target_pairs={{0,3},{1,0},{2,1},{3,2},{4,7},{5,4},{6,5},{7,6},{8,11},{9,8},{10,9... | collective-permute-start | bytes 3145736 | tf_op jit(solution)/shard_map/ppermute | solution.py:745
  38.6 0.0 collective-permute-start.6
  38.6 0.0 collective-permute-start
  38.6 4.7 %collective-permute-start.1 = (bf16[960,256]{1,0:T(8,128)(2,1)}, bf16[960,256]{1,0:T(8,128)(2,1)}, u32[]{:S(2)}, u32[]{:S(2)}) collective-permute-start(bf16[960,256]{1,0:T(8,128)(2,1)} %get-tuple-element.40), channel_id=1, source_target_pairs={{0,2},{1,3},{2,0},{3,1},{4,6},{5,7},{6,4},{7,5},{8,10},{9,11},{10,... | collective-permute-start | bytes 1474568 | tf_op jit(solution)/shard_map/ppermute | solution.py:745
  43.3 28.6 %collective-permute-done.10.refs_19_.refs_25_ = bf16[2048,256]{1,0:T(8,128)(2,1)S(1)} collective-permute-done((bf16[2048,256]{1,0:T(8,128)(2,1)S(1)}, bf16[2048,256]{1,0:T(8,128)(2,1)S(1)}, u32[]{:S(2)}, u32[]{:S(2)}) %collective-permute-start.10) | collective-permute-done | bytes 1048608 | tf_op jit(solution)/shard_map/ppermute | solution.py:745
  72.0 3.8 %collective-permute-start.12 = (bf16[1024,256]{1,0:T(8,128)(2,1)S(1)}, bf16[1024,256]{1,0:T(8,128)(2,1)}, u32[]{:S(2)}, u32[]{:S(2)}) collective-permute-start(bf16[1024,256]{1,0:T(8,128)(2,1)S(1)} %slice.9), channel_id=1, source_target_pairs={{0,3},{1,0},{2,1},{3,2},{4,7},{5,4},{6,5},{7,6},{8,11},{9,8},{10,9... | collective-permute-start | bytes 1572872 | tf_op jit(solution)/shard_map/ppermute | solution.py:745
  75.8 0.1 collective-permute-start.8
  75.9 0.1 collective-permute-start.11
  76.0 11.1 %collective-permute-done.near_ref.refs_5_ = bf16[960,256]{1,0:T(8,128)(2,1)} collective-permute-done((bf16[960,256]{1,0:T(8,128)(2,1)}, bf16[960,256]{1,0:T(8,128)(2,1)}, u32[]{:S(2)}, u32[]{:S(2)}) %collective-permute-start) | collective-permute-done | bytes 491552 | tf_op jit(solution)/shard_map/ppermute | solution.py:745
  87.1 0.6 collective-permute-start.13
  87.6 9.6 %collective-permute-done.8.refs_17_ = bf16[1024,256]{1,0:T(8,128)(2,1)} collective-permute-done((bf16[1024,256]{1,0:T(8,128)(2,1)S(1)}, bf16[1024,256]{1,0:T(8,128)(2,1)}, u32[]{:S(2)}, u32[]{:S(2)}) %collective-permute-start.8) | collective-permute-done | bytes 524320 | tf_op jit(solution)/shard_map/ppermute | solution.py:745
  97.2 3.8 %collective-permute-done.2.next_ref.refs_7_ = bf16[960,256]{1,0:T(8,128)(2,1)} collective-permute-done((bf16[960,256]{1,0:T(8,128)(2,1)}, bf16[960,256]{1,0:T(8,128)(2,1)}, u32[]{:S(2)}, u32[]{:S(2)}) %collective-permute-start.2) | collective-permute-done | bytes 491552 | tf_op jit(solution)/shard_map/ppermute | solution.py:745
  101.0 8.6 %head.1 = (bf16[7,128,256]{2,1,0:T(8,128)(2,1)}, bf16[7,128,256]{2,1,0:T(8,128)(2,1)}, bf16[7,128,256]{2,1,0:T(8,128)(2,1)}, bf16[7,32,1024]{2,1,0:T(8,128)(2,1)}) custom-call(s32[3]{0:T(128)} %pad_add_fusion.place_s, bf16[7,640,128]{2,1,0:T(8,128)(2,1)} %bitcast.41, bf16[960,256]{1,0:T(8,128)(2,1)} %get-tuple-element.38.own_ref.refs_4_, ...), custom_call_target="tpu_custom_call" | custom-call | tf_op jit(solution)/shard_map/head/pallas_call | solution.py:448
  109.6 13.6 %attend.1 = (bf16[4,7,32,256]{3,2,1,0:T(8,128)(2,1)}, bf16[7,128,256]{2,1,0:T(8,128)(2,1)}, bf16[7,128,256]{2,1,0:T(8,128)(2,1)}, s32[128,128]{1,0:T(8,128)}) custom-call(s32[128]{0:T(128)} %bitcast.48, s32[128]{0:T(128)} %multiply_add_fusion.both_s, s32[64,128]{1,0:T(8,128)} %bitcast.43, bf16[7,128,256]{2,1,0:T(8,128)(2,1)} %get-tuple-element.42.query_ref, ...), custom_call_target="tpu_custom_call" | custom-call | tf_op jit(solution)/shard_map/attend/pallas_call | solution.py:252
  123.2 1.7 dynamic-slice_bitcast_fusion
  124.9 1.5 collective-permute-start.5
  126.4 3.3 %collective-permute-done.5.refs_3_ = bf16[7,32,256]{2,1,0:T(8,128)(2,1)S(1)} collective-permute-done((bf16[7,32,256]{2,1,0:T(8,128)(2,1)S(1)}, bf16[7,32,256]{2,1,0:T(8,128)(2,1)S(1)}, u32[]{:S(2)}, u32[]{:S(2)}) %collective-permute-start.5) | collective-permute-done | bytes 114720 | tf_op jit(solution)/shard_map/ppermute | solution.py:745
  129.7 1.4 collective-permute-start.4
  131.1 4.9 %collective-permute-done.4.refs_2_ = bf16[7,32,256]{2,1,0:T(8,128)(2,1)S(1)} collective-permute-done((bf16[7,32,256]{2,1,0:T(8,128)(2,1)S(1)}, bf16[7,32,256]{2,1,0:T(8,128)(2,1)S(1)}, u32[]{:S(2)}, u32[]{:S(2)}) %collective-permute-start.4) | collective-permute-done | bytes 114720 | tf_op jit(solution)/shard_map/ppermute | solution.py:745
  136.0 0.2 collective-permute-start.3
  136.3 5.8 %collective-permute-done.3.refs_1_ = bf16[7,32,256]{2,1,0:T(8,128)(2,1)S(1)} collective-permute-done((bf16[7,32,256]{2,1,0:T(8,128)(2,1)S(1)}, bf16[7,32,256]{2,1,0:T(8,128)(2,1)S(1)}, u32[]{:S(2)}, u32[]{:S(2)}) %collective-permute-start.3) | collective-permute-done | bytes 114720 | tf_op jit(solution)/shard_map/ppermute | solution.py:745
  142.1 0.6 copy-done.10
  142.7 0.4 copy-done.2
  143.1 10.8 %tail.1 = (bf16[15,32,256]{2,1,0:T(8,128)(2,1)}, bf16[15,32,256]{2,1,0:T(8,128)(2,1)}, bf16[15,32,256]{2,1,0:T(8,128)(2,1)}, bf16[15,32,256]{2,1,0:T(8,128)(2,1)}) custom-call(s32[3]{0:T(128)} %pad_add_fusion.place_s, bf16[7,32,256]{2,1,0:T(8,128)(2,1)} %get-tuple-element.67.refs_0_, bf16[7,32,256]{2,1,0:T(8,128)(2,1)} %copy-done.10, ...), custom_call_target="tpu_custom_call" | custom-call | tf_op jit(solution)/shard_map/tail/pallas_call | solution.py:596
  153.9 0.1 collective-permute-start.14
  154.0 3.1 %collective-permute-start.15 = (bf16[15,32,256]{2,1,0:T(8,128)(2,1)}, bf16[15,32,256]{2,1,0:T(8,128)(2,1)S(1)}, u32[]{:S(2)}, u32[]{:S(2)}) collective-permute-start(bf16[15,32,256]{2,1,0:T(8,128)(2,1)} %get-tuple-element.51), channel_id=1, source_target_pairs={{0,2},{1,3},{2,0},{3,1},{4,6},{5,7},{6,4},{7,5},{8,10},{9,11},{10,... | collective-permute-start | bytes 737288 | tf_op jit(solution)/shard_map/ppermute | solution.py:745
  157.1 0.2 collective-permute-start.16
  157.3 5.3 %collective-permute-done.14.refs_1_ = bf16[15,32,256]{2,1,0:T(8,128)(2,1)S(1)} collective-permute-done((bf16[15,32,256]{2,1,0:T(8,128)(2,1)}, bf16[15,32,256]{2,1,0:T(8,128)(2,1)S(1)}, u32[]{:S(2)}, u32[]{:S(2)}) %collective-permute-start.14) | collective-permute-done | bytes 245792 | tf_op jit(solution)/shard_map/ppermute | solution.py:745
  162.6 2.6 %collective-permute-done.15.refs_2_ = bf16[15,32,256]{2,1,0:T(8,128)(2,1)S(1)} collective-permute-done((bf16[15,32,256]{2,1,0:T(8,128)(2,1)}, bf16[15,32,256]{2,1,0:T(8,128)(2,1)S(1)}, u32[]{:S(2)}, u32[]{:S(2)}) %collective-permute-start.15) | collective-permute-done | bytes 245792 | tf_op jit(solution)/shard_map/ppermute | solution.py:745
  165.2 0.7 collective-permute-done.16.refs_3_
  165.9 0.0 copy-done.5
  165.9 0.7 copy-done.6
  166.6 5.3 %collect.1 = (bf16[29,128,256]{2,1,0:T(8,128)(2,1)}, bf16[64,32,256]{2,1,0:T(8,128)(2,1)}) custom-call(s32[128]{0:T(128)} %bitcast.54, s32[3]{0:T(128)} %pad_add_fusion.place_s, bf16[15,32,256]{2,1,0:T(8,128)(2,1)} %get-tuple-element.49.refs_0_, bf16[15,32,256]{2,1,0:T(8,128)(2,1)} %copy-done.4, bf16[15,32,256]{2,1,0:T(8,128)(2,1)} %copy-done.5, ...), custom_call_target="tpu_custom_call" | custom-call | tf_op jit(solution)/shard_map/collect/pallas_call | solution.py:656
  171.9 7.3 %all-to-all-start.1 = ((bf16[64,32,256]{2,1,0:T(8,128)(2,1)}), bf16[64,32,256]{2,1,0:T(8,128)(2,1)S(1)}, u32[]{:S(2)}, u32[]{:S(2)}) async-start(bf16[64,32,256]{2,1,0:T(8,128)(2,1)} %get-tuple-element.56), calls=%async_computation.1 | async-start | bytes 2097152 | tf_op jit(solution)/shard_map/all_to_all | solution.py:849
  179.2 0.7 broadcast_in_dim.38.valid_ref
  179.9 14.3 %place.1 = (bf16[70,128,256]{2,1,0:T(8,128)(2,1)}, bf16[70,128,256]{2,1,0:T(8,128)(2,1)}) custom-call(s32[128]{0:T(128)} %bitcast.53, bf16[64,2,72,256]{3,2,1,0:T(8,128)(2,1)} %all-to-all-done.2.got_ref, s32[128,128]{1,0:T(8,128)} %broadcast_in_dim.38.valid_ref, bf16[70,128,256]{2,1,0:T(8,128)(2,1)} %bitcast.35, bf16[70,128,256]{2,1,0:T(8,128)(2,1)} %bitcast.38), custom_call_target="tpu_custom_call" | custom-call | tf_op jit(solution)/shard_map/place/pallas_call | solution.py:376
  194.2 2.2 %all-to-all-done.1.got_ref = bf16[64,32,256]{2,1,0:T(8,128)(2,1)S(1)} async-done(((bf16[64,32,256]{2,1,0:T(8,128)(2,1)}), bf16[64,32,256]{2,1,0:T(8,128)(2,1)S(1)}, u32[]{:S(2)}, u32[]{:S(2)}) %all-to-all-start.1) | async-done | bytes 1048608 | tf_op jit(solution)/shard_map/all_to_all | solution.py:849
  196.4 1.0 copy-done.3
  197.4 5.0 %finish.1 = (bf16[7,128,256]{2,1,0:T(8,128)(2,1)}, bf16[128,8,256]{2,1,0:T(8,128)(2,1)}, bf16[70,128,256]{2,1,0:T(8,128)(2,1)}, bf16[70,128,256]{2,1,0:T(8,128)(2,1)}) custom-call(s32[128]{0:T(128)} %bitcast.52, bf16[29,128,256]{2,1,0:T(8,128)(2,1)} %get-tuple-element.55.all_ref, ...), custom_call_target="tpu_custom_call", output_to_operand_aliasing={{2}: (3, {}), {3}: (4, {})} | custom-call | tf_op jit(solution)/shard_map/finish/pallas_call | solution.py:716
  (33 shorter events, 0.1 us)
Async XLA Ops:
  7.8 18.9 %all-to-all-start = ((s32[32,2,128]{2,1,0:T(2,128)}), s32[32,2,128]{2,1,0:T(2,128)S(1)}, u32[]{:S(2)}, u32[]{:S(2)}) async-start(s32[32,2,128]{2,1,0:T(2,128)} %bitcast.44), calls=%async_computation | async-start | bytes 65536 | tf_op jit(solution)/shard_map/all_to_all | solution.py:795
  26.7 7.8 %copy-start.12 = (bf16[2048,256]{1,0:T(8,128)(2,1)S(1)}, bf16[2048,256]{1,0:T(8,128)(2,1)}, u32[]{:S(2)}) copy-start(bf16[2048,256]{1,0:T(8,128)(2,1)} %get-tuple-element.48) | copy-start | bytes 3145732
  26.7 0.6 copy-start.7
  27.3 144.6 %all-to-all-start.2 = ((bf16[64,2,72,256]{3,2,1,0:T(8,128)(2,1)}), bf16[64,2,72,256]{3,2,1,0:T(8,128)(2,1)}, u32[]{:S(2)}, u32[]{:S(2)}) async-start(bf16[64,2,72,256]{3,2,1,0:T(8,128)(2,1)} %pack.1), calls=%async_computation.2 | async-start | bytes 9437184 | tf_op jit(solution)/shard_map/all_to_all | solution.py:799
  34.5 37.4 %collective-permute-start.10 = (bf16[2048,256]{1,0:T(8,128)(2,1)S(1)}, bf16[2048,256]{1,0:T(8,128)(2,1)S(1)}, u32[]{:S(2)}, u32[]{:S(2)}) collective-permute-start(bf16[2048,256]{1,0:T(8,128)(2,1)S(1)} %copy-done.12), channel_id=1, source_target_pairs={{0,3},{1,0},{2,1},{3,2},{4,7},{5,4},{6,5},{7,6},{8,11},{9,8},{10,9... | collective-permute-start | bytes 3145736 | tf_op jit(solution)/shard_map/ppermute | solution.py:745
  38.6 37.1 %collective-permute-start.6 = (bf16[2048,256]{1,0:T(8,128)(2,1)S(1)}, bf16[2048,256]{1,0:T(8,128)(2,1)S(1)}, u32[]{:S(2)}, u32[]{:S(2)}) collective-permute-start(bf16[2048,256]{1,0:T(8,128)(2,1)S(1)} %copy-done.12), channel_id=1, source_target_pairs={{0,1},{1,2},{2,3},{3,0},{4,5},{5,6},{6,7},{7,4},{8,9},{9,10},{10,1... | collective-permute-start | bytes 3145736 | tf_op jit(solution)/shard_map/ppermute | solution.py:745
  38.6 48.4 %collective-permute-start = (bf16[960,256]{1,0:T(8,128)(2,1)}, bf16[960,256]{1,0:T(8,128)(2,1)}, u32[]{:S(2)}, u32[]{:S(2)}) collective-permute-start(bf16[960,256]{1,0:T(8,128)(2,1)} %get-tuple-element.39), channel_id=1, source_target_pairs={{0,1},{1,2},{2,3},{3,0},{4,5},{5,6},{6,7},{7,4},{8,9},{9,10},{10,1... | collective-permute-start | bytes 1474568 | tf_op jit(solution)/shard_map/ppermute | solution.py:745
  38.6 48.4 %collective-permute-start.1 = (bf16[960,256]{1,0:T(8,128)(2,1)}, bf16[960,256]{1,0:T(8,128)(2,1)}, u32[]{:S(2)}, u32[]{:S(2)}) collective-permute-start(bf16[960,256]{1,0:T(8,128)(2,1)} %get-tuple-element.40), channel_id=1, source_target_pairs={{0,2},{1,3},{2,0},{3,1},{4,6},{5,7},{6,4},{7,5},{8,10},{9,11},{10,... | collective-permute-start | bytes 1474568 | tf_op jit(solution)/shard_map/ppermute | solution.py:745
  71.9 51.2 %copy-start = (bf16[2048,256]{1,0:T(8,128)(2,1)}, bf16[2048,256]{1,0:T(8,128)(2,1)S(1)}, u32[]{:S(2)}) copy-start(bf16[2048,256]{1,0:T(8,128)(2,1)S(1)} %collective-permute-done.10.refs_19_.refs_25_) | copy-start | bytes 3145732
  72.0 15.1 %collective-permute-start.12 = (bf16[1024,256]{1,0:T(8,128)(2,1)S(1)}, bf16[1024,256]{1,0:T(8,128)(2,1)}, u32[]{:S(2)}, u32[]{:S(2)}) collective-permute-start(bf16[1024,256]{1,0:T(8,128)(2,1)S(1)} %slice.9), channel_id=1, source_target_pairs={{0,3},{1,0},{2,1},{3,2},{4,7},{5,4},{6,5},{7,6},{8,11},{9,8},{10,9... | collective-permute-start | bytes 1572872 | tf_op jit(solution)/shard_map/ppermute | solution.py:745
  75.7 47.4 %copy-start.1 = (bf16[2048,256]{1,0:T(8,128)(2,1)}, bf16[2048,256]{1,0:T(8,128)(2,1)S(1)}, u32[]{:S(2)}) copy-start(bf16[2048,256]{1,0:T(8,128)(2,1)S(1)} %collective-permute-done.6.refs_15_.refs_21_) | copy-start | bytes 3145732
  75.8 21.4 %collective-permute-start.8 = (bf16[1024,256]{1,0:T(8,128)(2,1)S(1)}, bf16[1024,256]{1,0:T(8,128)(2,1)}, u32[]{:S(2)}, u32[]{:S(2)}) collective-permute-start(bf16[1024,256]{1,0:T(8,128)(2,1)S(1)} %slice.8), channel_id=1, source_target_pairs={{0,1},{1,2},{2,3},{3,0},{4,5},{5,6},{6,7},{7,4},{8,9},{9,10},{10,1... | collective-permute-start | bytes 1572872 | tf_op jit(solution)/shard_map/ppermute | solution.py:745
  75.9 66.2 %collective-permute-start.11 = (bf16[2048,256]{1,0:T(8,128)(2,1)S(1)}, bf16[2048,256]{1,0:T(8,128)(2,1)S(1)}, u32[]{:S(2)}, u32[]{:S(2)}) collective-permute-start(bf16[2048,256]{1,0:T(8,128)(2,1)S(1)} %collective-permute-done.10.refs_19_.refs_25_), channel_id=1, source_target_pairs={{0,4},{4,0},{8,12},{12,8},{16,20},{20,16},{24,28},{28,24},{32,36},... | collective-permute-start | bytes 3145736 | tf_op jit(solution)/shard_map/ppermute | solution.py:804
  87.0 55.0 %collective-permute-start.7 = (bf16[2048,256]{1,0:T(8,128)(2,1)S(1)}, bf16[2048,256]{1,0:T(8,128)(2,1)}, u32[]{:S(2)}, u32[]{:S(2)}) collective-permute-start(bf16[2048,256]{1,0:T(8,128)(2,1)S(1)} %collective-permute-done.6.refs_15_.refs_21_), channel_id=1, source_target_pairs={{0,4},{4,0},{8,12},{12,8},{16,20},{20,16},{24,28},{28,24},{32,36},... | collective-permute-start | bytes 3145736 | tf_op jit(solution)/shard_map/ppermute | solution.py:804
  87.0 14.0 %collective-permute-start.2 = (bf16[960,256]{1,0:T(8,128)(2,1)}, bf16[960,256]{1,0:T(8,128)(2,1)}, u32[]{:S(2)}, u32[]{:S(2)}) collective-permute-start(bf16[960,256]{1,0:T(8,128)(2,1)} %get-tuple-element.41), channel_id=1, source_target_pairs={{0,3},{1,0},{2,1},{3,2},{4,7},{5,4},{6,5},{7,6},{8,11},{9,8},{10,9... | collective-permute-start | bytes 1474568 | tf_op jit(solution)/shard_map/ppermute | solution.py:745
  87.1 55.0 %collective-permute-start.13 = (bf16[1024,256]{1,0:T(8,128)(2,1)}, bf16[1024,256]{1,0:T(8,128)(2,1)}, u32[]{:S(2)}, u32[]{:S(2)}) collective-permute-start(bf16[1024,256]{1,0:T(8,128)(2,1)} %collective-permute-done.12.refs_23_), channel_id=1, source_target_pairs={{0,4},{4,0},{8,12},{12,8},{16,20},{20,16},{24,28},{28,24},{32,36},... | collective-permute-start | bytes 1572872 | tf_op jit(solution)/shard_map/ppermute | solution.py:804
  97.2 44.8 %collective-permute-start.9 = (bf16[1024,256]{1,0:T(8,128)(2,1)}, bf16[1024,256]{1,0:T(8,128)(2,1)}, u32[]{:S(2)}, u32[]{:S(2)}) collective-permute-start(bf16[1024,256]{1,0:T(8,128)(2,1)} %collective-permute-done.8.refs_17_), channel_id=1, source_target_pairs={{0,4},{4,0},{8,12},{12,8},{16,20},{20,16},{24,28},{28,24},{32,36},... | collective-permute-start | bytes 1572872 | tf_op jit(solution)/shard_map/ppermute | solution.py:804
  124.9 4.8 %collective-permute-start.5 = (bf16[7,32,256]{2,1,0:T(8,128)(2,1)S(1)}, bf16[7,32,256]{2,1,0:T(8,128)(2,1)S(1)}, u32[]{:S(2)}, u32[]{:S(2)}) collective-permute-start(bf16[7,32,256]{2,1,0:T(8,128)(2,1)S(1)} %get-tuple-element.64), channel_id=1, source_target_pairs={{0,3},{1,0},{2,1},{3,2},{4,7},{5,4},{6,5},{7,6},{8,11},{9,8},{10,9... | collective-permute-start | bytes 344072 | tf_op jit(solution)/shard_map/ppermute | solution.py:745
  129.7 12.3 %copy-start.8 = (bf16[7,32,256]{2,1,0:T(8,128)(2,1)}, bf16[7,32,256]{2,1,0:T(8,128)(2,1)S(1)}, u32[]{:S(2)}) copy-start(bf16[7,32,256]{2,1,0:T(8,128)(2,1)S(1)} %collective-permute-done.5.refs_3_) | copy-start | bytes 344068
  129.7 6.3 %collective-permute-start.4 = (bf16[7,32,256]{2,1,0:T(8,128)(2,1)S(1)}, bf16[7,32,256]{2,1,0:T(8,128)(2,1)S(1)}, u32[]{:S(2)}, u32[]{:S(2)}) collective-permute-start(bf16[7,32,256]{2,1,0:T(8,128)(2,1)S(1)} %get-tuple-element.65), channel_id=1, source_target_pairs={{0,2},{1,3},{2,0},{3,1},{4,6},{5,7},{6,4},{7,5},{8,10},{9,11},{10,... | collective-permute-start | bytes 344072 | tf_op jit(solution)/shard_map/ppermute | solution.py:745
  136.0 6.1 %copy-start.9 = (bf16[7,32,256]{2,1,0:T(8,128)(2,1)}, bf16[7,32,256]{2,1,0:T(8,128)(2,1)S(1)}, u32[]{:S(2)}) copy-start(bf16[7,32,256]{2,1,0:T(8,128)(2,1)S(1)} %collective-permute-done.4.refs_2_) | copy-start | bytes 344068
  136.0 6.0 %collective-permute-start.3 = (bf16[7,32,256]{2,1,0:T(8,128)(2,1)S(1)}, bf16[7,32,256]{2,1,0:T(8,128)(2,1)S(1)}, u32[]{:S(2)}, u32[]{:S(2)}) collective-permute-start(bf16[7,32,256]{2,1,0:T(8,128)(2,1)S(1)} %get-tuple-element.66), channel_id=1, source_target_pairs={{0,1},{1,2},{2,3},{3,0},{4,5},{5,6},{6,7},{7,4},{8,9},{9,10},{10,1... | collective-permute-start | bytes 344072 | tf_op jit(solution)/shard_map/ppermute | solution.py:745
  142.0 0.6 copy-start.10
  142.1 1.0 copy-start.2
  143.1 36.2 %copy-start.11 = (s32[128]{0:T(128)S(1)}, s32[128]{0:T(128)}, u32[]{:S(2)}) copy-start(s32[128]{0:T(128)} %param.30) | copy-start | bytes 1540
  153.9 8.7 %collective-permute-start.14 = (bf16[15,32,256]{2,1,0:T(8,128)(2,1)}, bf16[15,32,256]{2,1,0:T(8,128)(2,1)S(1)}, u32[]{:S(2)}, u32[]{:S(2)}) collective-permute-start(bf16[15,32,256]{2,1,0:T(8,128)(2,1)} %get-tuple-element.50), channel_id=1, source_target_pairs={{0,1},{1,2},{2,3},{3,0},{4,5},{5,6},{6,7},{7,4},{8,9},{9,10},{10,1... | collective-permute-start | bytes 737288 | tf_op jit(solution)/shard_map/ppermute | solution.py:745
  154.0 11.3 %collective-permute-start.15 = (bf16[15,32,256]{2,1,0:T(8,128)(2,1)}, bf16[15,32,256]{2,1,0:T(8,128)(2,1)S(1)}, u32[]{:S(2)}, u32[]{:S(2)}) collective-permute-start(bf16[15,32,256]{2,1,0:T(8,128)(2,1)} %get-tuple-element.51), channel_id=1, source_target_pairs={{0,2},{1,3},{2,0},{3,1},{4,6},{5,7},{6,4},{7,5},{8,10},{9,11},{10,... | collective-permute-start | bytes 737288 | tf_op jit(solution)/shard_map/ppermute | solution.py:745
  157.1 8.8 %collective-permute-start.16 = (bf16[15,32,256]{2,1,0:T(8,128)(2,1)}, bf16[15,32,256]{2,1,0:T(8,128)(2,1)S(1)}, u32[]{:S(2)}, u32[]{:S(2)}) collective-permute-start(bf16[15,32,256]{2,1,0:T(8,128)(2,1)} %get-tuple-element.52), channel_id=1, source_target_pairs={{0,3},{1,0},{2,1},{3,2},{4,7},{5,4},{6,5},{7,6},{8,11},{9,8},{10,9... | collective-permute-start | bytes 737288 | tf_op jit(solution)/shard_map/ppermute | solution.py:745
  162.6 3.3 %copy-start.4 = (bf16[15,32,256]{2,1,0:T(8,128)(2,1)}, bf16[15,32,256]{2,1,0:T(8,128)(2,1)S(1)}, u32[]{:S(2)}) copy-start(bf16[15,32,256]{2,1,0:T(8,128)(2,1)S(1)} %collective-permute-done.14.refs_1_) | copy-start | bytes 737284
  165.2 0.7 copy-start.5
  165.9 0.7 copy-start.6
  171.9 24.5 %all-to-all-start.1 = ((bf16[64,32,256]{2,1,0:T(8,128)(2,1)}), bf16[64,32,256]{2,1,0:T(8,128)(2,1)S(1)}, u32[]{:S(2)}, u32[]{:S(2)}) async-start(bf16[64,32,256]{2,1,0:T(8,128)(2,1)} %get-tuple-element.56), calls=%async_computation.1 | async-start | bytes 2097152 | tf_op jit(solution)/shard_map/all_to_all | solution.py:849
  196.4 1.0 copy-start.3

commit v7 on v6

--- a/solution.py
+++ b/solution.py
@@ -1,3 +1,4 @@
+import functools
 import math
 
 import jax
@@ -30,7 +31,8 @@
     place_s,
     new_ref,
     old_ref,
-    both_ref,
+    valid_ref,
+    fill_ref,
     weight_ref,
     bias_ref,
     kernel_ref,
@@ -43,10 +45,8 @@
     gate_ref,
     *refs,
 ):
-    payloads, (bucket_ref, arrival_ref, out_ref, in_ref, asked_ref, stack_ref, small) = (
-        refs[:4],
-        refs[4:],
-    )
+    payloads, maps, (wide_ref, asked_ref, stack_ref, small) = refs[:4], refs[4:11], refs[11:]
+    both_ref, bucket_ref, out_ref, out_rank_ref, arrival_ref, in_ref, in_rank_ref = maps
     member, own = place_s[0], place_s[2]
     groups = len(payloads)
     taps, width = weight_ref.shape
@@ -94,20 +94,31 @@
         hit = jnp.where(column(row) == second, (first + 1).astype(jnp.float32), 0.0)
         return jnp.sum(hit, axis=0, keepdims=True).astype(jnp.int32) - 1
 
+    def listed(chosen, list_ref, rank_ref):
+        marks = column(jnp.where(chosen, 1, 0)).astype(jnp.float32)
+        rank = jnp.sum(jnp.where(first <= second, marks, 0.0), axis=0, keepdims=True)
+        rank = rank.astype(jnp.int32)
+        rank_ref[...] = rank
+        list_ref[...] = inverse(jnp.where(chosen, rank - 1, -1))
+
+    valid = valid_ref[...]
+    wide_ref[...] = column(valid)
+    both = valid * (1 << FIELD) + fill_ref[...]
+    both_ref[...] = both
     target = new_ref[...] >> bits
     position = ranked(column(target), target, first < second)
     bucket = jnp.where(target != own, target * CAP + position, slots)
     bucket_ref[...] = bucket
-    out_ref[...] = inverse(bucket)
+    listed(target != own, out_ref, out_rank_ref)
     old_row = old_ref[...]
     old_column = column(old_row)
     source = old_row >> bits
     position = ranked(old_column >> bits, source, old_column < old_row)
     arrival = jnp.where(source == own, -1, source * CAP + position)
     arrival_ref[...] = arrival
-    in_ref[...] = inverse(arrival)
+    listed(source != own, in_ref, in_rank_ref)
     slot = lax.broadcasted_iota(jnp.int32, (slots, count), 0)
-    hit = jnp.where(arrival == slot, both_ref[...].astype(jnp.float32), 0.0)
+    hit = jnp.where(arrival == slot, both.astype(jnp.float32), 0.0)
     asked = jnp.sum(hit, axis=1, keepdims=True).astype(jnp.int32)
     asked_ref[...] = jnp.broadcast_to(asked, (slots, count))
 
@@ -129,7 +140,8 @@
 
     row = jax.ShapeDtypeStruct((1, count), jnp.int32)
     payload = jax.ShapeDtypeStruct((taps + 64 + chunk_rows, width), jnp.bfloat16)
-    shapes = [payload] * groups + [row] * 4
+    shapes = [payload] * groups + [row] * 7
+    shapes.append(jax.ShapeDtypeStruct((count, count), jnp.int32))
     shapes.append(jax.ShapeDtypeStruct((slots, count), jnp.int32))
     shapes.append(jax.ShapeDtypeStruct((2 * groups * width, width), jnp.bfloat16))
     outs = pl.pallas_call(
@@ -146,7 +158,7 @@
         out_shape=shapes,
         name="prepare",
     )(where, *whole, chunks, *columns, *tall)
-    return outs[:groups], [r[0] for r in outs[groups : groups + 4]], outs[-2], outs[-1]
+    return outs[:groups], [r[0] for r in outs[groups : groups + 7]], *outs[-3:]
 
 
 def shift_rows(rows, first, second, third):
@@ -156,6 +168,7 @@
 
 
 def attend_body(
+    place_s,
     bucket_s,
     both_s,
     told_ref,
@@ -164,12 +177,14 @@
     value_new_ref,
     key_ref,
     value_ref,
-    context_ref,
-    key_out_ref,
-    value_out_ref,
-    packed_ref,
+    *rest,
+    begin,
+    groups,
+    per_group,
 ):
-    base = pl.program_id(0) * BLOCK
+    near_ref, far_ref, key_out_ref, value_out_ref, packed_ref = rest[-5:]
+    step = pl.program_id(0)
+    base = chosen_block(step, place_s, begin, groups, per_group) * BLOCK
     slots = told_ref.shape[0]
     for s in range(BLOCK):
         slot = bucket_s[base + s]
@@ -218,7 +233,15 @@
             (((1,), (0,)), ((), ())),
             preferred_element_type=jnp.float32,
         )
-        context_ref[0, :, :, lanes] = context.reshape(FRAMES, BLOCK, LANES).astype(jnp.bfloat16)
+        context = context.reshape(FRAMES, BLOCK, LANES).astype(jnp.bfloat16)
+
+        @pl.when(step < per_group)
+        def _():
+            near_ref[:, :, lanes] = context
+
+        @pl.when(step >= per_group)
+        def _():
+            far_ref[:, :, lanes] = context
 
     shift = valid - 1
     first = ((shift & 1) != 0)[None]
@@ -237,47 +260,61 @@
             out_ref[:, :, lanes] = shift_rows(rows, first, second, third).astype(jnp.bfloat16)
 
 
-def attend(bucket, both, told, queries, key_new, value_new, key_cache, value_cache, groups):
-    stream_count = key_cache.shape[1]
-    width = key_cache.shape[2]
+def chosen_block(i, place_s, begin, groups, per_group):
+    return ((place_s[0] + begin + i // per_group) % groups) * per_group + i % per_group
+
+
+def attend(begin, where, bucket, both, told, new, caches, groups, earlier=()):
+    stream_count = caches[0].shape[1]
+    width = caches[0].shape[2]
+    share = stream_count // groups
+    per_group = share // BLOCK
+
+    def at(i, place_s):
+        return chosen_block(i, place_s, begin, groups, per_group)
 
     def block(rows):
-        return pl.BlockSpec((rows, BLOCK, width), lambda i, *_: (0, i, 0))
-
-    per_group = stream_count // groups // BLOCK
-    context = pl.BlockSpec(
-        (1, FRAMES, BLOCK, width), lambda i, *_: (i // per_group, 0, i % per_group, 0)
-    )
+        return pl.BlockSpec((rows, BLOCK, width), lambda i, p, *_: (0, at(i, p), 0))
+
+    part = (FRAMES, BLOCK, width)
+    context = jax.ShapeDtypeStruct((FRAMES, share, width), jnp.bfloat16)
     slab = jax.ShapeDtypeStruct((FRAMES, stream_count, width), jnp.bfloat16)
     return pl.pallas_call(
-        attend_body,
+        functools.partial(attend_body, begin=begin, groups=groups, per_group=per_group),
         grid_spec=pltpu.PrefetchScalarGridSpec(
-            num_scalar_prefetch=2,
-            grid=(stream_count // BLOCK,),
+            num_scalar_prefetch=3,
+            grid=(2 * per_group,),
             in_specs=[pl.BlockSpec(told.shape, lambda i, *_: (0, 0))]
             + [block(FRAMES)] * 3
-            + [block(CACHE)] * 2,
+            + [block(CACHE)] * 2
+            + [pl.BlockSpec(memory_space=pl.ANY)] * len(earlier),
             out_specs=[
-                context,
+                pl.BlockSpec(part, lambda i, *_: (0, jnp.minimum(i, per_group - 1), 0)),
+                pl.BlockSpec(part, lambda i, *_: (0, jnp.maximum(i - per_group, 0), 0)),
                 block(FRAMES),
                 block(FRAMES),
-                pl.BlockSpec((BLOCK, LANES), lambda i, *_: (i, 0)),
+                pl.BlockSpec((BLOCK, LANES), lambda i, p, *_: (at(i, p), 0)),
             ],
         ),
         out_shape=[
-            jax.ShapeDtypeStruct((groups, FRAMES, stream_count // groups, width), jnp.bfloat16),
+            context,
+            context,
             slab,
             slab,
             jax.ShapeDtypeStruct((stream_count, LANES), jnp.int32),
         ],
-        name="attend",
-    )(bucket, both, told, queries, key_new, value_new, key_cache, value_cache)
-
-
-def pack_body(slot_s, key_ref, value_ref, send_ref, rows_f):
+        input_output_aliases={9 + k: 2 + k for k in range(len(earlier))},
+        name="attend_b" if earlier else "attend_a",
+    )(where, bucket, both, told, *new, *caches, *earlier)
+
+
+def bounds(rank_s, base):
+    return jnp.where(base == 0, 0, rank_s[jnp.maximum(base - 1, 0)]), rank_s[base + BLOCK - 1]
+
+
+def pack_body(slot_s, list_s, rank_s, key_ref, value_ref, send_ref, rows_f):
     base = pl.program_id(0) * BLOCK
     heads = rows_f.shape[1]
-    slots = send_ref.shape[0]
     for kind, src in enumerate((key_ref, value_ref)):
         for h in range(heads):
             rows_f[kind, h, : CACHE * BLOCK, :] = (
@@ -286,30 +323,27 @@
                 .reshape(CACHE * BLOCK, LANES)
             )
 
-    def pack(s, carry):
+    def pack(k, carry):
+        s = list_s[k] - base
         slot = slot_s[base + s]
-
-        @pl.when(slot < slots)
-        def _():
-            for kind in range(2):
-                for h in range(heads):
-                    send_ref[slot, kind, :, h * LANES : (h + 1) * LANES] = rows_f[
-                        kind, h, pl.ds(s, KEEP, stride=BLOCK), :
-                    ].astype(jnp.bfloat16)
-
+        for kind in range(2):
+            for h in range(heads):
+                send_ref[slot, kind, :, h * LANES : (h + 1) * LANES] = rows_f[
+                    kind, h, pl.ds(s, KEEP, stride=BLOCK), :
+                ].astype(jnp.bfloat16)
         return carry
 
-    lax.fori_loop(0, BLOCK, pack, 0)
-
-
-def pack_rows(bucket, key_cache, value_cache, slots):
+    lax.fori_loop(*bounds(rank_s, base), pack, 0)
+
+
+def pack_rows(leaving, key_cache, value_cache, slots):
     stream_count = key_cache.shape[1]
     width = key_cache.shape[2]
     block = pl.BlockSpec((CACHE, BLOCK, width), lambda i, *_: (0, i, 0))
     return pl.pallas_call(
         pack_body,
         grid_spec=pltpu.PrefetchScalarGridSpec(
-            num_scalar_prefetch=1,
+            num_scalar_prefetch=3,
             grid=(stream_count // BLOCK,),
             in_specs=[block, block],
             out_specs=pl.BlockSpec((slots, 2, KEEP, width), lambda i, *_: (0, 0, 0, 0)),
@@ -319,11 +353,11 @@
         ),
         out_shape=jax.ShapeDtypeStruct((slots, 2, KEEP, width), jnp.bfloat16),
         name="pack",
-    )(bucket, key_cache, value_cache)
+    )(*leaving, key_cache, value_cache)
 
 
 def place_body(
-    arrival_s, got_ref, valid_ref, key_ref, value_ref, key_out_ref, value_out_ref, rows_f
+    arrival_s, list_s, rank_s, got_ref, valid_ref, key_ref, value_ref, key_out_ref, value_out_ref, rows_f
 ):
     base = pl.program_id(0) * BLOCK
     heads = rows_f.shape[1]
@@ -337,20 +371,17 @@
                     .reshape(CHUNK * BLOCK, LANES)
                 )
 
-    def fetch(s, carry):
+    def fetch(k, carry):
+        s = list_s[k] - base
         slot = arrival_s[base + s]
-
-        @pl.when(slot >= 0)
-        def _():
-            for kind in range(2):
-                for h in range(heads):
-                    rows_f[kind, h, pl.ds(s, KEEP, stride=BLOCK), :] = got_ref[
-                        slot, kind, :, h * LANES : (h + 1) * LANES
-                    ].astype(jnp.float32)
-
+        for kind in range(2):
+            for h in range(heads):
+                rows_f[kind, h, pl.ds(s, KEEP, stride=BLOCK), :] = got_ref[
+                    slot, kind, :, h * LANES : (h + 1) * LANES
+                ].astype(jnp.float32)
         return carry
 
-    lax.fori_loop(0, BLOCK, fetch, 0)
+    lax.fori_loop(*bounds(rank_s, base), fetch, 0)
     shift = valid_ref[...] - 1
     first = ((shift & 1) != 0)[None]
     second = ((shift & 2) != 0)[None]
@@ -366,7 +397,7 @@
             dst[edge:, :, lanes] = jnp.zeros((FRAMES, BLOCK, LANES), jnp.bfloat16)
 
 
-def place(arrival, valid_new, received, key_rows, value_rows):
+def place(coming, valid_wide, received, key_rows, value_rows):
     stream_count = key_rows.shape[1]
     width = key_rows.shape[2]
     heads = width // HEAD
@@ -376,7 +407,7 @@
     return pl.pallas_call(
         place_body,
         grid_spec=pltpu.PrefetchScalarGridSpec(
-            num_scalar_prefetch=1,
+            num_scalar_prefetch=3,
             grid=(stream_count // BLOCK,),
             in_specs=[
                 pl.BlockSpec((slots, 2, KEEP, width), lambda i, *_: (0, 0, 0, 0)),
@@ -390,9 +421,9 @@
         out_shape=[shape, shape],
         name="place",
     )(
-        arrival,
+        *coming,
         received,
-        jnp.broadcast_to(valid_new[:, None], (stream_count, LANES)),
+        valid_wide,
         key_rows,
         value_rows,
     )
@@ -606,13 +637,13 @@
     )(where, *arrays)
 
 
-def collect_body(leaving_s, place_s, *refs):
+def collect_body(slot_s, list_s, rank_s, place_s, *refs):
     pieces, slabs, (all_ref, send_ref, rows_f) = refs[:4], refs[4:6], refs[6:]
     member = place_s[0]
     groups = len(pieces)
     frames, share, _ = pieces[0].shape
     heads, _, _ = rows_f.shape
-    slots, keep, _ = send_ref.shape
+    _, keep, _ = send_ref.shape
     count = groups * share
     for step, piece in enumerate(pieces):
         start = pl.multiple_of(((member + groups - step) % groups) * share, share)
@@ -632,19 +663,16 @@
             )
         frames += FRAMES
 
-    def pack(slot, carry):
-        s = leaving_s[slot]
-
-        @pl.when(s >= 0)
-        def _():
-            for h in range(heads):
-                send_ref[slot, :, h * LANES : (h + 1) * LANES] = rows_f[
-                    h, pl.ds(s, keep, stride=count), :
-                ].astype(jnp.bfloat16)
-
+    def pack(k, carry):
+        s = list_s[k]
+        slot = slot_s[s]
+        for h in range(heads):
+            send_ref[slot, :, h * LANES : (h + 1) * LANES] = rows_f[
+                h, pl.ds(s, keep, stride=count), :
+            ].astype(jnp.bfloat16)
         return carry
 
-    lax.fori_loop(0, slots, pack, 0)
+    lax.fori_loop(0, rank_s[count - 1], pack, 0)
 
 
 def collect(leaving, where, pieces, slabs, slots):
@@ -655,7 +683,7 @@
     vmem = pl.BlockSpec(memory_space=pltpu.VMEM)
     return pl.pallas_call(
         collect_body,
-        in_specs=[smem, smem] + [vmem] * 6,
+        in_specs=[smem] * 4 + [vmem] * 6,
         out_specs=[vmem, vmem],
         out_shape=[
             jax.ShapeDtypeStruct((frames, count, width), jnp.bfloat16),
@@ -663,11 +691,11 @@
         ],
         scratch_shapes=[pltpu.VMEM((width // LANES, keep * count, LANES), jnp.float32)],
         name="collect",
-    )(leaving, where, *pieces, *slabs)
+    )(*leaving, where, *pieces, *slabs)
 
 
 def finish_body(
-    coming_s, all_ref, got_ref, _, __, encoded_ref, conv_ref, key_ref, value_ref, rows_f, conv_f
+    slot_s, list_s, rank_s, all_ref, got_ref, _, __, encoded_ref, conv_ref, key_ref, value_ref, rows_f, conv_f
 ):
     heads = rows_f.shape[0]
     frames, count, _ = all_ref.shape
@@ -679,19 +707,16 @@
             .reshape(frames * count, LANES)
         )
 
-    def fetch(slot, carry):
-        s = coming_s[slot]
-
-        @pl.when(s >= 0)
-        def _():
-            for h in range(heads):
-                rows_f[h, pl.ds(s, keep, stride=count), :] = got_ref[
-                    slot, :, h * LANES : (h + 1) * LANES
-                ].astype(jnp.float32)
-
+    def fetch(k, carry):
+        s = list_s[k]
+        slot = slot_s[s]
+        for h in range(heads):
+            rows_f[h, pl.ds(s, keep, stride=count), :] = got_ref[
+                slot, :, h * LANES : (h + 1) * LANES
+            ].astype(jnp.float32)
         return carry
 
-    lax.fori_loop(0, got_ref.shape[0], fetch, 0)
+    lax.fori_loop(0, rank_s[count - 1], fetch, 0)
     ends = FRAMES + CONV_CACHE
     for h in range(heads):
         lanes = slice(h * LANES, (h + 1) * LANES)
@@ -716,7 +741,7 @@
     return pl.pallas_call(
         finish_body,
         grid=(1,),
-        in_specs=[smem, vmem, vmem, kept, kept],
+        in_specs=[smem] * 3 + [vmem, vmem, kept, kept],
         out_specs=[vmem, vmem, slab, slab],
         out_shape=[
             jax.ShapeDtypeStruct((FRAMES, count, width), jnp.bfloat16),
@@ -728,17 +753,9 @@
             pltpu.VMEM((width // LANES, keep * count, LANES), jnp.float32),
             pltpu.VMEM((CONV_CACHE * count, LANES), jnp.float32),
         ],
-        input_output_aliases={3: 2, 4: 3},
+        input_output_aliases={5: 2, 6: 3},
         name="finish",
-    )(coming, everything, received, key_done, value_done)
-
-
-def swap(chunks, member, count):
-    pieces = [lax.dynamic_index_in_dim(chunks, member, 0, False)]
-    for step in range(1, count):
-        chunk = lax.dynamic_index_in_dim(chunks, (member + step) % count, 0, False)
-        pieces.append(toward(chunk, step, count))
-    return pieces
+    )(*coming, everything, received, key_done, value_done)
 
 
 def toward(array, steps, count):
@@ -778,11 +795,10 @@
     groups = lax.axis_size("enc")
     core = own_index % 2
     where = jnp.stack([member, core, own_index])
-    both = valid_new * (1 << FIELD) + cache_fill
     share = stream_count // groups
-    payloads, maps, asked, stack = prepare(
+    payloads, maps, valid_wide, asked, stack = prepare(
         where,
-        (new_slot, old_slot, both),
+        (new_slot, old_slot, valid_new, cache_fill),
         (sub_weight, sub_bias),
         (depth_kernel, norm_scale, norm_shift),
         conv_cache.reshape(groups, share * CONV_CACHE, local_width),
@@ -790,12 +806,12 @@
         (w_glu_value, w_glu_gate),
         slots,
     )
-    bucket, arrival, leaving, coming = maps
+    both, bucket, leaving, coming = maps[0], maps[1], maps[1:4], maps[4:7]
     pieces = [payloads[0]] + [toward(payloads[k], k, groups) for k in range(1, groups)]
     told = lax.all_to_all(asked, "front", split_axis=0, concat_axis=0, tiled=True)
     key_rows = key_cache.transpose(1, 0, 2)
     value_rows = value_cache.transpose(1, 0, 2)
-    leaving_rows = pack_rows(bucket, key_rows, value_rows, slots)
+    leaving_rows = pack_rows(leaving, key_rows, value_rows, slots)
     received = lax.all_to_all(leaving_rows, "front", split_axis=0, concat_axis=0, tiled=True)
     taps = SUB * MELS
     middle_row = stack.shape[0] // 2
@@ -815,10 +831,14 @@
     queries, key_new, value_new, inputs = head(
         where, frames, pieces, ln1_gain, (w_query, w_key, w_value)
     )
-    context, key_slab, value_slab, packed = attend(
-        bucket, both, told, queries, key_new, value_new, key_rows, value_rows, groups
-    )
-    context = swap(context, member, groups)
+    new = (queries, key_new, value_new)
+    caches = (key_rows, value_rows)
+    first, second, *earlier = attend(1, where, bucket, both, told, new, caches, groups)
+    context = [toward(first, 1, groups), toward(second, 2, groups)]
+    third, own, key_slab, value_slab, packed = attend(
+        groups - 1, where, bucket, both, told, new, caches, groups, earlier
+    )
+    context = [own] + context + [toward(third, groups - 1, groups)]
     ended = tail(
         where,
         groups,
@@ -847,7 +867,7 @@
     ended = [ended[0]] + [toward(ended[k], k, groups) for k in range(1, groups)]
     everything, leaving_end = collect(leaving, where, ended, (key_slab, value_slab), slots)
     received_end = lax.all_to_all(leaving_end, "front", split_axis=0, concat_axis=0, tiled=True)
-    key_done, value_done = place(arrival, valid_new, received, key_rows, value_rows)
+    key_done, value_done = place(coming, valid_wide, received, key_rows, value_rows)
     encoded, conv_out, key_done, value_done = finish(
         coming, everything, received_end, key_done, value_done
     )

time: 204 us -> 205 us (level)
  waiting for transfers between devices: 77.8 us -> 80.6 us
  Pallas kernels: 73.2 us -> 75.7 us
  local copies, waits for them, and re-layouts: 7 us -> 4.54 us
    pallas_call x3 -> x4, Pallas kernels: 23.9 us -> 28.1 us  [the longest x2 19 us: attend(): pl.pallas_call(functools.partial(attend_body, begin=begin, groups=groups,...]
  transfers between devices with their start and end apart: 20 -> 20, of which waited for: 11 -> 11; matrix products, arithmetic and copies ran while one was open for 1% -> 0% of each run, Pallas kernels for 32% -> 33%
where the time goes in v7:
time: 205 us; the launch traced here: 203 us
  waiting for transfers between devices  80.6 us (39%)
  Pallas kernels  75.7 us (37%)
  starting transfers between devices  40.9 us (20%)
  local copies, waits for them, and re-layouts  4.54 us (2%)
    ppermute x13, waiting for transfers between devices, toward(): lax.ppermute(array, 'enc', [(i, (i + steps) % count) for i in range(count)])  76.9 us
    pallas_call x2, Pallas kernels, attend(): pl.pallas_call(functools.partial(attend_body, begin=begin, groups=groups,...  19 us
    ppermute x13, starting transfers between devices, toward(): lax.ppermute(array, 'enc', [(i, (i + steps) % count) for i in range(count)])  18.3 us
    pallas_call x1, Pallas kernels, place(): pl.pallas_call(place_body, grid_spec=pltpu.PrefetchScalarGridSpec(num_sca...  13.5 us
    pallas_call x1, Pallas kernels, tail(): pl.pallas_call(tail_body, in_specs=[pl.BlockSpec(memory_space=pltpu.SMEM)...  10.8 us
    pallas_call x1, Pallas kernels, pack_rows(): pl.pallas_call(pack_body, grid_spec=pltpu.PrefetchScalarGridSpec(num_scal...  10.5 us
    pallas_call x1, Pallas kernels, head(): pl.pallas_call(head_body, grid_spec=pltpu.PrefetchScalarGridSpec(num_scal...  8.62 us
    all_to_all x1, starting transfers between devices, on_device(): lax.all_to_all(asked, 'front', split_axis=0, concat_axis=0, tiled=True)  7.44 us
  transfers between devices with their start and end apart: 20, of which 11 were waited for; matrix products, arithmetic and copies ran while one was open for 0% of the time, Pallas kernels for 33%

profile of v7, /device:TPU:0, one launch (start us, length us, event | category | flops | bytes accessed | tf_op | source)
XLA Modules:
  0.0 203.2 jit_solution(10367594061255774595)
XLA Ops:
  0.6 1.2 broadcast_in_dim.31.bias_ref
  1.9 0.6 pad_add_fusion.place_s
  2.5 4.1 %prepare.1 = (bf16[960,256]{1,0:T(8,128)(2,1)}, bf16[960,256]{1,0:T(8,128)(2,1)}, bf16[960,256]{1,0:T(8,128)(2,1)}, bf16[960,256]{1,0:T(8,128)(2,1)}, s32[1,128]...) custom-call(s32[3]{0:T(128)} %pad_add_fusion.place_s, ...), custom_call_target="tpu_custom_call" | custom-call | tf_op jit(solution)/shard_map/prepare/pallas_call | solution.py:147
  6.6 7.4 %all-to-all-start = ((s32[32,2,128]{2,1,0:T(2,128)}), s32[32,2,128]{2,1,0:T(2,128)S(1)}, u32[]{:S(2)}, u32[]{:S(2)}) async-start(s32[32,2,128]{2,1,0:T(2,128)} %bitcast.43), calls=%async_computation | async-start | bytes 65536 | tf_op jit(solution)/shard_map/all_to_all | solution.py:811
  14.0 10.5 %pack.1 = bf16[64,2,72,256]{3,2,1,0:T(8,128)(2,1)} custom-call(s32[128]{0:T(128)} %bitcast.44, s32[128]{0:T(128)} %bitcast.56, s32[128]{0:T(128)} %bitcast.58, bf16[70,128,256]{2,1,0:T(8,128)(2,1)} %bitcast.29, bf16[70,128,256]{2,1,0:T(8,128)(2,1)} %bitcast.33), custom_call_target="tpu_custom_call" | custom-call | tf_op jit(solution)/shard_map/pack/pallas_call | solution.py:343
  24.5 0.0 all-to-all-done
  24.5 0.6 copy-done.4
  25.1 7.2 %all-to-all-start.2 = ((bf16[64,2,72,256]{3,2,1,0:T(8,128)(2,1)}), bf16[64,2,72,256]{3,2,1,0:T(8,128)(2,1)}, u32[]{:S(2)}, u32[]{:S(2)}) async-start(bf16[64,2,72,256]{3,2,1,0:T(8,128)(2,1)} %pack.1), calls=%async_computation.2 | async-start | bytes 9437184 | tf_op jit(solution)/shard_map/all_to_all | solution.py:815
  32.3 4.1 %collective-permute-start.10 = (bf16[2048,256]{1,0:T(8,128)(2,1)S(1)}, bf16[2048,256]{1,0:T(8,128)(2,1)S(1)}, u32[]{:S(2)}, u32[]{:S(2)}) collective-permute-start(bf16[2048,256]{1,0:T(8,128)(2,1)S(1)} %copy-done.11), channel_id=1, source_target_pairs={{0,3},{1,0},{2,1},{3,2},{4,7},{5,4},{6,5},{7,6},{8,11},{9,8},{10,9... | collective-permute-start | bytes 3145736 | tf_op jit(solution)/shard_map/ppermute | solution.py:762
  36.4 0.0 collective-permute-start.6
  36.4 0.0 collective-permute-start
  36.4 4.7 %collective-permute-start.1 = (bf16[960,256]{1,0:T(8,128)(2,1)}, bf16[960,256]{1,0:T(8,128)(2,1)}, u32[]{:S(2)}, u32[]{:S(2)}) collective-permute-start(bf16[960,256]{1,0:T(8,128)(2,1)} %get-tuple-element.54), channel_id=1, source_target_pairs={{0,2},{1,3},{2,0},{3,1},{4,6},{5,7},{6,4},{7,5},{8,10},{9,11},{10,... | collective-permute-start | bytes 1474568 | tf_op jit(solution)/shard_map/ppermute | solution.py:762
  41.1 28.6 %collective-permute-done.10.refs_19_.refs_25_ = bf16[2048,256]{1,0:T(8,128)(2,1)S(1)} collective-permute-done((bf16[2048,256]{1,0:T(8,128)(2,1)S(1)}, bf16[2048,256]{1,0:T(8,128)(2,1)S(1)}, u32[]{:S(2)}, u32[]{:S(2)}) %collective-permute-start.10) | collective-permute-done | bytes 1048608 | tf_op jit(solution)/shard_map/ppermute | solution.py:762
  69.8 3.8 %collective-permute-start.12 = (bf16[1024,256]{1,0:T(8,128)(2,1)S(1)}, bf16[1024,256]{1,0:T(8,128)(2,1)}, u32[]{:S(2)}, u32[]{:S(2)}) collective-permute-start(bf16[1024,256]{1,0:T(8,128)(2,1)S(1)} %slice.9), channel_id=1, source_target_pairs={{0,3},{1,0},{2,1},{3,2},{4,7},{5,4},{6,5},{7,6},{8,11},{9,8},{10,9... | collective-permute-start | bytes 1572872 | tf_op jit(solution)/shard_map/ppermute | solution.py:762
  73.6 0.1 collective-permute-start.8
  73.7 0.1 collective-permute-start.11
  73.8 11.1 %collective-permute-done.near_ref.refs_5_ = bf16[960,256]{1,0:T(8,128)(2,1)} collective-permute-done((bf16[960,256]{1,0:T(8,128)(2,1)}, bf16[960,256]{1,0:T(8,128)(2,1)}, u32[]{:S(2)}, u32[]{:S(2)}) %collective-permute-start) | collective-permute-done | bytes 491552 | tf_op jit(solution)/shard_map/ppermute | solution.py:762
  84.8 0.0 collective-permute-done.1.far_ref.refs_6_
  84.8 0.0 collective-permute-start.2
  84.9 0.6 collective-permute-start.13
  85.4 9.6 %collective-permute-done.8.refs_17_ = bf16[1024,256]{1,0:T(8,128)(2,1)} collective-permute-done((bf16[1024,256]{1,0:T(8,128)(2,1)S(1)}, bf16[1024,256]{1,0:T(8,128)(2,1)}, u32[]{:S(2)}, u32[]{:S(2)}) %collective-permute-start.8) | collective-permute-done | bytes 524320 | tf_op jit(solution)/shard_map/ppermute | solution.py:762
  95.0 0.0 collective-permute-start.9
  95.0 3.8 %collective-permute-done.2.next_ref.refs_7_ = bf16[960,256]{1,0:T(8,128)(2,1)} collective-permute-done((bf16[960,256]{1,0:T(8,128)(2,1)}, bf16[960,256]{1,0:T(8,128)(2,1)}, u32[]{:S(2)}, u32[]{:S(2)}) %collective-permute-start.2) | collective-permute-done | bytes 491552 | tf_op jit(solution)/shard_map/ppermute | solution.py:762
  98.8 8.6 %head.1 = (bf16[7,128,256]{2,1,0:T(8,128)(2,1)}, bf16[7,128,256]{2,1,0:T(8,128)(2,1)}, bf16[7,128,256]{2,1,0:T(8,128)(2,1)}, bf16[7,32,1024]{2,1,0:T(8,128)(2,1)}) custom-call(s32[3]{0:T(128)} %pad_add_fusion.place_s, bf16[7,640,128]{2,1,0:T(8,128)(2,1)} %bitcast.39, bf16[960,256]{1,0:T(8,128)(2,1)} %get-tuple-element.52.own_ref.refs_4_, ...), custom_call_target="tpu_custom_call" | custom-call | tf_op jit(solution)/shard_map/head/pallas_call | solution.py:479
  107.4 9.4 %attend_a.1 = (bf16[7,32,256]{2,1,0:T(8,128)(2,1)}, bf16[7,32,256]{2,1,0:T(8,128)(2,1)}, bf16[7,128,256]{2,1,0:T(8,128)(2,1)}, bf16[7,128,256]{2,1,0:T(8,128)(2,1)}, s32[128,128]{1,0:T(8,128)}) custom-call(s32[3]{0:T(128)} %pad_add_fusion.place_s, s32[128]{0:T(128)} %bitcast.45, s32[128]{0:T(128)} %bitcast.60, s32[64,128]{1,0:T(8,128)} %bitcast.41, ...), custom_call_target="tpu_custom_call" | custom-call | tf_op jit(solution)/shard_map/attend_a/pallas_call | solution.py:282
  116.8 9.6 %attend_b.1 = (bf16[7,32,256]{2,1,0:T(8,128)(2,1)}, bf16[7,32,256]{2,1,0:T(8,128)(2,1)}, bf16[7,128,256]{2,1,0:T(8,128)(2,1)}, bf16[7,128,256]{2,1,0:T(8,128)(2,1)}, s32[128,128]{1,0:T(8,128)}) custom-call(s32[3]{0:T(128)} %pad_add_fusion.place_s, s32[128]{0:T(128)} %bitcast.46, ...), custom_call_target="tpu_custom_call", output_to_operand_aliasing={{2}: (9, {}), {3}: (10, {}), {4}: (11, {})} | custom-call | tf_op jit(solution)/shard_map/attend_b/pallas_call | solution.py:282
  126.4 1.5 collective-permute-start.5
  127.9 3.5 %collective-permute-done.5.refs_3_ = bf16[7,32,256]{2,1,0:T(8,128)(2,1)S(1)} collective-permute-done((bf16[7,32,256]{2,1,0:T(8,128)(2,1)}, bf16[7,32,256]{2,1,0:T(8,128)(2,1)S(1)}, u32[]{:S(2)}, u32[]{:S(2)}) %collective-permute-start.5) | collective-permute-done | bytes 114720 | tf_op jit(solution)/shard_map/ppermute | solution.py:762
  131.5 6.0 %collective-permute-done.3.refs_1_ = bf16[7,32,256]{2,1,0:T(8,128)(2,1)S(1)} collective-permute-done((bf16[7,32,256]{2,1,0:T(8,128)(2,1)S(1)}, bf16[7,32,256]{2,1,0:T(8,128)(2,1)S(1)}, u32[]{:S(2)}, u32[]{:S(2)}) %collective-permute-start.3) | collective-permute-done | bytes 114720 | tf_op jit(solution)/shard_map/ppermute | solution.py:762
  137.5 0.7 collective-permute-start.4
  138.2 5.8 %collective-permute-done.4.refs_2_ = bf16[7,32,256]{2,1,0:T(8,128)(2,1)S(1)} collective-permute-done((bf16[7,32,256]{2,1,0:T(8,128)(2,1)}, bf16[7,32,256]{2,1,0:T(8,128)(2,1)S(1)}, u32[]{:S(2)}, u32[]{:S(2)}) %collective-permute-start.4) | collective-permute-done | bytes 114720 | tf_op jit(solution)/shard_map/ppermute | solution.py:762
  144.0 0.6 copy-done.10
  144.6 0.4 copy-done.2
  145.0 10.8 %tail.1 = (bf16[15,32,256]{2,1,0:T(8,128)(2,1)}, bf16[15,32,256]{2,1,0:T(8,128)(2,1)}, bf16[15,32,256]{2,1,0:T(8,128)(2,1)}, bf16[15,32,256]{2,1,0:T(8,128)(2,1)}) custom-call(s32[3]{0:T(128)} %pad_add_fusion.place_s, bf16[7,32,256]{2,1,0:T(8,128)(2,1)} %get-tuple-element.62.refs_0_, bf16[7,32,256]{2,1,0:T(8,128)(2,1)} %copy-done.9, ...), custom_call_target="tpu_custom_call" | custom-call | tf_op jit(solution)/shard_map/tail/pallas_call | solution.py:627
  155.8 0.1 collective-permute-start.14
  155.9 3.1 %collective-permute-start.15 = (bf16[15,32,256]{2,1,0:T(8,128)(2,1)}, bf16[15,32,256]{2,1,0:T(8,128)(2,1)S(1)}, u32[]{:S(2)}, u32[]{:S(2)}) collective-permute-start(bf16[15,32,256]{2,1,0:T(8,128)(2,1)} %get-tuple-element.71), channel_id=1, source_target_pairs={{0,2},{1,3},{2,0},{3,1},{4,6},{5,7},{6,4},{7,5},{8,10},{9,11},{10,... | collective-permute-start | bytes 737288 | tf_op jit(solution)/shard_map/ppermute | solution.py:762
  159.0 0.2 collective-permute-start.16
  159.2 5.3 %collective-permute-done.14.refs_1_ = bf16[15,32,256]{2,1,0:T(8,128)(2,1)S(1)} collective-permute-done((bf16[15,32,256]{2,1,0:T(8,128)(2,1)}, bf16[15,32,256]{2,1,0:T(8,128)(2,1)S(1)}, u32[]{:S(2)}, u32[]{:S(2)}) %collective-permute-start.14) | collective-permute-done | bytes 245792 | tf_op jit(solution)/shard_map/ppermute | solution.py:762
  164.5 2.6 %collective-permute-done.15.refs_2_ = bf16[15,32,256]{2,1,0:T(8,128)(2,1)S(1)} collective-permute-done((bf16[15,32,256]{2,1,0:T(8,128)(2,1)}, bf16[15,32,256]{2,1,0:T(8,128)(2,1)S(1)}, u32[]{:S(2)}, u32[]{:S(2)}) %collective-permute-start.15) | collective-permute-done | bytes 245792 | tf_op jit(solution)/shard_map/ppermute | solution.py:762
  167.1 0.6 collective-permute-done.16.refs_3_
  167.8 0.0 copy-done.6
  167.8 0.6 copy-done.7
  168.5 4.6 %collect.1 = (bf16[29,128,256]{2,1,0:T(8,128)(2,1)}, bf16[64,32,256]{2,1,0:T(8,128)(2,1)}) custom-call(s32[128]{0:T(128)} %bitcast.47, s32[128]{0:T(128)} %bitcast.57, s32[128]{0:T(128)} %bitcast.59, s32[3]{0:T(128)} %pad_add_fusion.place_s, bf16[15,32,256]{2,1,0:T(8,128)(2,1)} %get-tuple-element.69.refs_0_, bf16[15,32,256]{2,1,0:T(8,128)(2,1)} %copy-done.5, ...), custom_call_target="tpu_custom_call" | custom-call | tf_op jit(solution)/shard_map/collect/pallas_call | solution.py:684
  173.1 7.4 %all-to-all-start.1 = ((bf16[64,32,256]{2,1,0:T(8,128)(2,1)}), bf16[64,32,256]{2,1,0:T(8,128)(2,1)S(1)}, u32[]{:S(2)}, u32[]{:S(2)}) async-start(bf16[64,32,256]{2,1,0:T(8,128)(2,1)} %get-tuple-element.76), calls=%async_computation.1 | async-start | bytes 2097152 | tf_op jit(solution)/shard_map/all_to_all | solution.py:869
  180.5 13.5 %place.1 = (bf16[70,128,256]{2,1,0:T(8,128)(2,1)}, bf16[70,128,256]{2,1,0:T(8,128)(2,1)}) custom-call(s32[128]{0:T(128)} %bitcast.50, s32[128]{0:T(128)} %bitcast.52, s32[128]{0:T(128)} %bitcast.54, bf16[64,2,72,256]{3,2,1,0:T(8,128)(2,1)} %all-to-all-done.2.got_ref, s32[128,128]{1,0:T(8,128)} %get-tuple-element.77.valid_ref, ...), custom_call_target="tpu_custom_call" | custom-call | tf_op jit(solution)/shard_map/place/pallas_call | solution.py:407
  194.0 3.7 %all-to-all-done.1.got_ref = bf16[64,32,256]{2,1,0:T(8,128)(2,1)S(1)} async-done(((bf16[64,32,256]{2,1,0:T(8,128)(2,1)}), bf16[64,32,256]{2,1,0:T(8,128)(2,1)S(1)}, u32[]{:S(2)}, u32[]{:S(2)}) %all-to-all-start.1) | async-done | bytes 1048608 | tf_op jit(solution)/shard_map/all_to_all | solution.py:869
  197.7 1.0 copy-done.3
  198.7 4.5 %finish.1 = (bf16[7,128,256]{2,1,0:T(8,128)(2,1)}, bf16[128,8,256]{2,1,0:T(8,128)(2,1)}, bf16[70,128,256]{2,1,0:T(8,128)(2,1)}, bf16[70,128,256]{2,1,0:T(8,128)(2,1)}) custom-call(s32[128]{0:T(128)} %bitcast.51, s32[128]{0:T(128)} %bitcast.53, s32[128]{0:T(128)} %bitcast.55, ...), custom_call_target="tpu_custom_call", output_to_operand_aliasing={{2}: (5, {}), {3}: (6, {})} | custom-call | tf_op jit(solution)/shard_map/finish/pallas_call | solution.py:741
  (31 shorter events, 0.1 us)
Async XLA Ops:
  6.6 18.0 %all-to-all-start = ((s32[32,2,128]{2,1,0:T(2,128)}), s32[32,2,128]{2,1,0:T(2,128)S(1)}, u32[]{:S(2)}, u32[]{:S(2)}) async-start(s32[32,2,128]{2,1,0:T(2,128)} %bitcast.43), calls=%async_computation | async-start | bytes 65536 | tf_op jit(solution)/shard_map/all_to_all | solution.py:811
  24.5 7.8 %copy-start.11 = (bf16[2048,256]{1,0:T(8,128)(2,1)S(1)}, bf16[2048,256]{1,0:T(8,128)(2,1)}, u32[]{:S(2)}) copy-start(bf16[2048,256]{1,0:T(8,128)(2,1)} %get-tuple-element.68) | copy-start | bytes 3145732
  24.5 0.6 copy-start.4
  25.1 148.0 %all-to-all-start.2 = ((bf16[64,2,72,256]{3,2,1,0:T(8,128)(2,1)}), bf16[64,2,72,256]{3,2,1,0:T(8,128)(2,1)}, u32[]{:S(2)}, u32[]{:S(2)}) async-start(bf16[64,2,72,256]{3,2,1,0:T(8,128)(2,1)} %pack.1), calls=%async_computation.2 | async-start | bytes 9437184 | tf_op jit(solution)/shard_map/all_to_all | solution.py:815
  32.3 37.4 %collective-permute-start.10 = (bf16[2048,256]{1,0:T(8,128)(2,1)S(1)}, bf16[2048,256]{1,0:T(8,128)(2,1)S(1)}, u32[]{:S(2)}, u32[]{:S(2)}) collective-permute-start(bf16[2048,256]{1,0:T(8,128)(2,1)S(1)} %copy-done.11), channel_id=1, source_target_pairs={{0,3},{1,0},{2,1},{3,2},{4,7},{5,4},{6,5},{7,6},{8,11},{9,8},{10,9... | collective-permute-start | bytes 3145736 | tf_op jit(solution)/shard_map/ppermute | solution.py:762
  36.4 37.1 %collective-permute-start.6 = (bf16[2048,256]{1,0:T(8,128)(2,1)S(1)}, bf16[2048,256]{1,0:T(8,128)(2,1)S(1)}, u32[]{:S(2)}, u32[]{:S(2)}) collective-permute-start(bf16[2048,256]{1,0:T(8,128)(2,1)S(1)} %copy-done.11), channel_id=1, source_target_pairs={{0,1},{1,2},{2,3},{3,0},{4,5},{5,6},{6,7},{7,4},{8,9},{9,10},{10,1... | collective-permute-start | bytes 3145736 | tf_op jit(solution)/shard_map/ppermute | solution.py:762
  36.4 48.4 %collective-permute-start = (bf16[960,256]{1,0:T(8,128)(2,1)}, bf16[960,256]{1,0:T(8,128)(2,1)}, u32[]{:S(2)}, u32[]{:S(2)}) collective-permute-start(bf16[960,256]{1,0:T(8,128)(2,1)} %get-tuple-element.53), channel_id=1, source_target_pairs={{0,1},{1,2},{2,3},{3,0},{4,5},{5,6},{6,7},{7,4},{8,9},{9,10},{10,1... | collective-permute-start | bytes 1474568 | tf_op jit(solution)/shard_map/ppermute | solution.py:762
  36.4 48.4 %collective-permute-start.1 = (bf16[960,256]{1,0:T(8,128)(2,1)}, bf16[960,256]{1,0:T(8,128)(2,1)}, u32[]{:S(2)}, u32[]{:S(2)}) collective-permute-start(bf16[960,256]{1,0:T(8,128)(2,1)} %get-tuple-element.54), channel_id=1, source_target_pairs={{0,2},{1,3},{2,0},{3,1},{4,6},{5,7},{6,4},{7,5},{8,10},{9,11},{10,... | collective-permute-start | bytes 1474568 | tf_op jit(solution)/shard_map/ppermute | solution.py:762
  69.7 47.1 %copy-start = (bf16[2048,256]{1,0:T(8,128)(2,1)}, bf16[2048,256]{1,0:T(8,128)(2,1)S(1)}, u32[]{:S(2)}) copy-start(bf16[2048,256]{1,0:T(8,128)(2,1)S(1)} %collective-permute-done.10.refs_19_.refs_25_) | copy-start | bytes 3145732
  69.8 15.1 %collective-permute-start.12 = (bf16[1024,256]{1,0:T(8,128)(2,1)S(1)}, bf16[1024,256]{1,0:T(8,128)(2,1)}, u32[]{:S(2)}, u32[]{:S(2)}) collective-permute-start(bf16[1024,256]{1,0:T(8,128)(2,1)S(1)} %slice.9), channel_id=1, source_target_pairs={{0,3},{1,0},{2,1},{3,2},{4,7},{5,4},{6,5},{7,6},{8,11},{9,8},{10,9... | collective-permute-start | bytes 1572872 | tf_op jit(solution)/shard_map/ppermute | solution.py:762
  73.6 43.3 %copy-start.1 = (bf16[2048,256]{1,0:T(8,128)(2,1)}, bf16[2048,256]{1,0:T(8,128)(2,1)S(1)}, u32[]{:S(2)}) copy-start(bf16[2048,256]{1,0:T(8,128)(2,1)S(1)} %collective-permute-done.6.refs_15_.refs_21_) | copy-start | bytes 3145732
  73.6 21.4 %collective-permute-start.8 = (bf16[1024,256]{1,0:T(8,128)(2,1)S(1)}, bf16[1024,256]{1,0:T(8,128)(2,1)}, u32[]{:S(2)}, u32[]{:S(2)}) collective-permute-start(bf16[1024,256]{1,0:T(8,128)(2,1)S(1)} %slice.8), channel_id=1, source_target_pairs={{0,1},{1,2},{2,3},{3,0},{4,5},{5,6},{6,7},{7,4},{8,9},{9,10},{10,1... | collective-permute-start | bytes 1572872 | tf_op jit(solution)/shard_map/ppermute | solution.py:762
  73.7 70.3 %collective-permute-start.11 = (bf16[2048,256]{1,0:T(8,128)(2,1)S(1)}, bf16[2048,256]{1,0:T(8,128)(2,1)S(1)}, u32[]{:S(2)}, u32[]{:S(2)}) collective-permute-start(bf16[2048,256]{1,0:T(8,128)(2,1)S(1)} %collective-permute-done.10.refs_19_.refs_25_), channel_id=1, source_target_pairs={{0,4},{4,0},{8,12},{12,8},{16,20},{20,16},{24,28},{28,24},{32,36},... | collective-permute-start | bytes 3145736 | tf_op jit(solution)/shard_map/ppermute | solution.py:820
  84.8 59.2 %collective-permute-start.7 = (bf16[2048,256]{1,0:T(8,128)(2,1)S(1)}, bf16[2048,256]{1,0:T(8,128)(2,1)}, u32[]{:S(2)}, u32[]{:S(2)}) collective-permute-start(bf16[2048,256]{1,0:T(8,128)(2,1)S(1)} %collective-permute-done.6.refs_15_.refs_21_), channel_id=1, source_target_pairs={{0,4},{4,0},{8,12},{12,8},{16,20},{20,16},{24,28},{28,24},{32,36},... | collective-permute-start | bytes 3145736 | tf_op jit(solution)/shard_map/ppermute | solution.py:820
  84.8 14.0 %collective-permute-start.2 = (bf16[960,256]{1,0:T(8,128)(2,1)}, bf16[960,256]{1,0:T(8,128)(2,1)}, u32[]{:S(2)}, u32[]{:S(2)}) collective-permute-start(bf16[960,256]{1,0:T(8,128)(2,1)} %get-tuple-element.55), channel_id=1, source_target_pairs={{0,3},{1,0},{2,1},{3,2},{4,7},{5,4},{6,5},{7,6},{8,11},{9,8},{10,9... | collective-permute-start | bytes 1474568 | tf_op jit(solution)/shard_map/ppermute | solution.py:762
  84.9 59.1 %collective-permute-start.13 = (bf16[1024,256]{1,0:T(8,128)(2,1)}, bf16[1024,256]{1,0:T(8,128)(2,1)}, u32[]{:S(2)}, u32[]{:S(2)}) collective-permute-start(bf16[1024,256]{1,0:T(8,128)(2,1)} %collective-permute-done.12.refs_23_), channel_id=1, source_target_pairs={{0,4},{4,0},{8,12},{12,8},{16,20},{20,16},{24,28},{28,24},{32,36},... | collective-permute-start | bytes 1572872 | tf_op jit(solution)/shard_map/ppermute | solution.py:820
  95.0 49.0 %collective-permute-start.9 = (bf16[1024,256]{1,0:T(8,128)(2,1)}, bf16[1024,256]{1,0:T(8,128)(2,1)}, u32[]{:S(2)}, u32[]{:S(2)}) collective-permute-start(bf16[1024,256]{1,0:T(8,128)(2,1)} %collective-permute-done.8.refs_17_), channel_id=1, source_target_pairs={{0,4},{4,0},{8,12},{12,8},{16,20},{20,16},{24,28},{28,24},{32,36},... | collective-permute-start | bytes 1572872 | tf_op jit(solution)/shard_map/ppermute | solution.py:820
  116.8 14.6 %copy-start.12 = (bf16[7,32,256]{2,1,0:T(8,128)(2,1)S(1)}, bf16[7,32,256]{2,1,0:T(8,128)(2,1)}, u32[]{:S(2)}) copy-start(bf16[7,32,256]{2,1,0:T(8,128)(2,1)} %get-tuple-element.63) | copy-start | bytes 344068
  126.4 5.1 %collective-permute-start.5 = (bf16[7,32,256]{2,1,0:T(8,128)(2,1)}, bf16[7,32,256]{2,1,0:T(8,128)(2,1)S(1)}, u32[]{:S(2)}, u32[]{:S(2)}) collective-permute-start(bf16[7,32,256]{2,1,0:T(8,128)(2,1)} %get-tuple-element.65), channel_id=1, source_target_pairs={{0,3},{1,0},{2,1},{3,2},{4,7},{5,4},{6,5},{7,6},{8,11},{9,8},{10,9... | collective-permute-start | bytes 344072 | tf_op jit(solution)/shard_map/ppermute | solution.py:762
  131.5 12.6 %copy-start.8 = (bf16[7,32,256]{2,1,0:T(8,128)(2,1)}, bf16[7,32,256]{2,1,0:T(8,128)(2,1)S(1)}, u32[]{:S(2)}) copy-start(bf16[7,32,256]{2,1,0:T(8,128)(2,1)S(1)} %collective-permute-done.5.refs_3_) | copy-start | bytes 344068
  131.5 6.0 %collective-permute-start.3 = (bf16[7,32,256]{2,1,0:T(8,128)(2,1)S(1)}, bf16[7,32,256]{2,1,0:T(8,128)(2,1)S(1)}, u32[]{:S(2)}, u32[]{:S(2)}) collective-permute-start(bf16[7,32,256]{2,1,0:T(8,128)(2,1)S(1)} %copy-done.12), channel_id=1, source_target_pairs={{0,1},{1,2},{2,3},{3,0},{4,5},{5,6},{6,7},{7,4},{8,9},{9,10},{10,1... | collective-permute-start | bytes 344072 | tf_op jit(solution)/shard_map/ppermute | solution.py:762
  137.5 6.6 %copy-start.9 = (bf16[7,32,256]{2,1,0:T(8,128)(2,1)}, bf16[7,32,256]{2,1,0:T(8,128)(2,1)S(1)}, u32[]{:S(2)}) copy-start(bf16[7,32,256]{2,1,0:T(8,128)(2,1)S(1)} %collective-permute-done.3.refs_1_) | copy-start | bytes 344068
  137.5 6.5 %collective-permute-start.4 = (bf16[7,32,256]{2,1,0:T(8,128)(2,1)}, bf16[7,32,256]{2,1,0:T(8,128)(2,1)S(1)}, u32[]{:S(2)}, u32[]{:S(2)}) collective-permute-start(bf16[7,32,256]{2,1,0:T(8,128)(2,1)} %get-tuple-element.64), channel_id=1, source_target_pairs={{0,2},{1,3},{2,0},{3,1},{4,6},{5,7},{6,4},{7,5},{8,10},{9,11},{10,... | collective-permute-start | bytes 344072 | tf_op jit(solution)/shard_map/ppermute | solution.py:762
  144.0 0.6 copy-start.10
  144.0 1.0 copy-start.2
  155.8 8.7 %collective-permute-start.14 = (bf16[15,32,256]{2,1,0:T(8,128)(2,1)}, bf16[15,32,256]{2,1,0:T(8,128)(2,1)S(1)}, u32[]{:S(2)}, u32[]{:S(2)}) collective-permute-start(bf16[15,32,256]{2,1,0:T(8,128)(2,1)} %get-tuple-element.70), channel_id=1, source_target_pairs={{0,1},{1,2},{2,3},{3,0},{4,5},{5,6},{6,7},{7,4},{8,9},{9,10},{10,1... | collective-permute-start | bytes 737288 | tf_op jit(solution)/shard_map/ppermute | solution.py:762
  155.9 11.3 %collective-permute-start.15 = (bf16[15,32,256]{2,1,0:T(8,128)(2,1)}, bf16[15,32,256]{2,1,0:T(8,128)(2,1)S(1)}, u32[]{:S(2)}, u32[]{:S(2)}) collective-permute-start(bf16[15,32,256]{2,1,0:T(8,128)(2,1)} %get-tuple-element.71), channel_id=1, source_target_pairs={{0,2},{1,3},{2,0},{3,1},{4,6},{5,7},{6,4},{7,5},{8,10},{9,11},{10,... | collective-permute-start | bytes 737288 | tf_op jit(solution)/shard_map/ppermute | solution.py:762
  159.0 8.8 %collective-permute-start.16 = (bf16[15,32,256]{2,1,0:T(8,128)(2,1)}, bf16[15,32,256]{2,1,0:T(8,128)(2,1)S(1)}, u32[]{:S(2)}, u32[]{:S(2)}) collective-permute-start(bf16[15,32,256]{2,1,0:T(8,128)(2,1)} %get-tuple-element.72), channel_id=1, source_target_pairs={{0,3},{1,0},{2,1},{3,2},{4,7},{5,4},{6,5},{7,6},{8,11},{9,8},{10,9... | collective-permute-start | bytes 737288 | tf_op jit(solution)/shard_map/ppermute | solution.py:762
  164.5 3.3 %copy-start.5 = (bf16[15,32,256]{2,1,0:T(8,128)(2,1)}, bf16[15,32,256]{2,1,0:T(8,128)(2,1)S(1)}, u32[]{:S(2)}) copy-start(bf16[15,32,256]{2,1,0:T(8,128)(2,1)S(1)} %collective-permute-done.14.refs_1_) | copy-start | bytes 737284
  167.1 0.7 copy-start.6
  167.8 0.7 copy-start.7
  173.1 24.6 %all-to-all-start.1 = ((bf16[64,32,256]{2,1,0:T(8,128)(2,1)}), bf16[64,32,256]{2,1,0:T(8,128)(2,1)S(1)}, u32[]{:S(2)}, u32[]{:S(2)}) async-start(bf16[64,32,256]{2,1,0:T(8,128)(2,1)} %get-tuple-element.76), calls=%async_computation.1 | async-start | bytes 2097152 | tf_op jit(solution)/shard_map/all_to_all | solution.py:869
  197.7 1.0 copy-start.3

commit v8 on v7

--- a/solution.py
+++ b/solution.py
@@ -58,7 +58,8 @@
     small[KERNEL + 1 : KERNEL + 2, :] = shift_ref[...]
     small[KERNEL + 2 :, :] = jnp.zeros((16 - KERNEL - 2, width), jnp.float32)
     rest = small[...]
-    bias = jnp.broadcast_to(bias_ref[...].astype(jnp.float32), (16, width)).astype(jnp.bfloat16)
+    bias = bias_ref[...].astype(jnp.float32).reshape(1, width)
+    bias = jnp.broadcast_to(bias, (16, width)).astype(jnp.bfloat16)
     parts = []
     for _ in range(3):
         part = rest.astype(jnp.bfloat16)
@@ -127,7 +128,7 @@
     count = rows[0].shape[0]
     groups, chunk_rows, width = chunks.shape
     taps = sub[0].shape[0]
-    whole = [r[None] for r in rows] + [sub[0], sub[1][None], conv[0], conv[1][None], conv[2][None]]
+    whole = [r[None] for r in rows] + [sub[0], sub[1], conv[0], conv[1][None], conv[2][None]]
 
     def full(array):
         zeros = (0,) * array.ndim
@@ -216,6 +217,7 @@
             axis=0,
         )
 
+    contexts = []
     for h in range(heads):
         lanes = slice(h * LANES, (h + 1) * LANES)
         scores = lax.dot_general(
@@ -233,15 +235,7 @@
             (((1,), (0,)), ((), ())),
             preferred_element_type=jnp.float32,
         )
-        context = context.reshape(FRAMES, BLOCK, LANES).astype(jnp.bfloat16)
-
-        @pl.when(step < per_group)
-        def _():
-            near_ref[:, :, lanes] = context
-
-        @pl.when(step >= per_group)
-        def _():
-            far_ref[:, :, lanes] = context
+        contexts.append(context.reshape(FRAMES, BLOCK, LANES).astype(jnp.bfloat16))
 
     shift = valid - 1
     first = ((shift & 1) != 0)[None]
@@ -258,6 +252,16 @@
             new = new_ref[:, :, lanes].astype(jnp.float32)
             rows = jnp.concatenate([old, new, new[:1]], axis=0)
             out_ref[:, :, lanes] = shift_rows(rows, first, second, third).astype(jnp.bfloat16)
+
+    @pl.when(step < per_group)
+    def _():
+        for h, context in enumerate(contexts):
+            near_ref[:, :, h * LANES : (h + 1) * LANES] = context
+
+    @pl.when(step >= per_group)
+    def _():
+        for h, context in enumerate(contexts):
+            far_ref[:, :, h * LANES : (h + 1) * LANES] = context
 
 
 def chosen_block(i, place_s, begin, groups, per_group):
@@ -501,8 +505,8 @@
     contexts, pieces, rest = refs[:4], refs[4:8], refs[8:]
     inputs_ref, gain_ref, packed_ref = rest[:3]
     attn_ref, conv_ref, value_ref, gate_ref = rest[3:7]
-    low_refs, high_refs, outs = rest[7:13], rest[13:19], rest[19:23]
-    out_ref, cache_f = rest[23:]
+    ring_refs, outs = rest[7:13], rest[13:17]
+    out_ref, cache_f = rest[17:]
     member = place_s[0]
     front_half = place_s[1] == 0
     groups = len(contexts)
@@ -527,7 +531,7 @@
             else:
                 at = start + n * half
                 part = sum(
-                    dot(side, low_refs[2 * (step - 1) + i][at : at + half, :])
+                    dot(side, ring_refs[2 * (step - 1) + i][at : at + half, :])
                     for i, side in enumerate(sides)
                 )
             part = part.astype(jnp.bfloat16).astype(jnp.float32)
@@ -536,13 +540,12 @@
     def wide(step, own_ref, order):
         if step == 0:
             return dot(normed, own_ref[...])
-        at = high_starts[step - 1] + order * (size // 2)
+        at = size + order * (size // 2)
         return sum(
-            dot(side, high_refs[2 * (step - 1) + i][at : at + size // 2, :])
+            dot(side, ring_refs[2 * (step - 1) + i][at : at + size // 2, :])
             for i, side in enumerate(normed_sides)
         )
 
-    high_starts = (size, 0, size)
     attended = [None] * groups
     for step in range(groups):
         grouped(step, contexts[step][...].reshape(rows, width), attn_ref, 0, attended)
@@ -814,19 +817,16 @@
     leaving_rows = pack_rows(leaving, key_rows, value_rows, slots)
     received = lax.all_to_all(leaving_rows, "front", split_axis=0, concat_axis=0, tiled=True)
     taps = SUB * MELS
-    middle_row = stack.shape[0] // 2
 
     def other_core(array):
         return lax.ppermute(array, "front", [(i, i ^ 1) for i in range(peer_count)])
 
     near = toward(stack, 1, groups)
     after = toward(stack, -1, groups)
-    far_low = toward(near[:middle_row], 1, groups)
-    far_high = toward(after[middle_row:], -1, groups)
+    far = toward(after, -1, groups)
+    after_other = other_core(after)
     near_other = other_core(near)
-    after_other = other_core(after)
-    far_low_other = other_core(far_low)
-    far_high_other = other_core(far_high)
+    far_other = other_core(far)
     frames = spectra.transpose(1, 2, 0).reshape(FRAMES, taps, stream_count)
     queries, key_new, value_new, inputs = head(
         where, frames, pieces, ln1_gain, (w_query, w_key, w_value)
@@ -853,14 +853,8 @@
         w_glu_gate,
         near,
         near_other,
-        far_low,
-        far_low_other,
-        after,
-        after_other,
-        near,
-        near_other,
-        far_high,
-        far_high_other,
+        far,
+        far_other,
         after,
         after_other,
     )

time: 205 us -> 210 us (1.024)
  waiting for transfers between devices: 80.6 us -> 87 us
  Pallas kernels: 75.7 us -> 72.8 us
  starting transfers between devices: 40.9 us -> 43.1 us
    ppermute x13 -> x12, waiting for transfers between devices: 76.9 us -> 83.3 us  [toward(): lax.ppermute(array, 'enc', [(i, (i + steps) % count) for i in range(count)])]
    ppermute x13 -> x12, starting transfers between devices: 18.3 us -> 20.9 us  [toward(): lax.ppermute(array, 'enc', [(i, (i + steps) % count) for i in range(count)])]
  transfers between devices with their start and end apart: 20 -> 18, of which waited for: 11 -> 10; matrix products, arithmetic and copies ran while one was open for 0% -> 0% of each run, Pallas kernels for 33% -> 31%
where the time goes in v8:
time: 210 us; the launch traced here: 208 us
  waiting for transfers between devices  87 us (41%)
  Pallas kernels  72.8 us (35%)
  starting transfers between devices  43.1 us (21%)
  local copies, waits for them, and re-layouts  3.76 us (2%)
    ppermute x12, waiting for transfers between devices, toward(): lax.ppermute(array, 'enc', [(i, (i + steps) % count) for i in range(count)])  83.3 us
    ppermute x12, starting transfers between devices, toward(): lax.ppermute(array, 'enc', [(i, (i + steps) % count) for i in range(count)])  20.9 us
    pallas_call x2, Pallas kernels, attend(): pl.pallas_call(functools.partial(attend_body, begin=begin, groups=groups,...  17.3 us
    pallas_call x1, Pallas kernels, place(): pl.pallas_call(place_body, grid_spec=pltpu.PrefetchScalarGridSpec(num_sca...  13.5 us
    pallas_call x1, Pallas kernels, pack_rows(): pl.pallas_call(pack_body, grid_spec=pltpu.PrefetchScalarGridSpec(num_scal...  10.5 us
    pallas_call x1, Pallas kernels, tail(): pl.pallas_call(tail_body, in_specs=[pl.BlockSpec(memory_space=pltpu.SMEM)...  9.61 us
    pallas_call x1, Pallas kernels, head(): pl.pallas_call(head_body, grid_spec=pltpu.PrefetchScalarGridSpec(num_scal...  8.63 us
    all_to_all x1, starting transfers between devices, on_device(): lax.all_to_all(asked, 'front', split_axis=0, concat_axis=0, tiled=True)  7.44 us
  transfers between devices with their start and end apart: 18, of which 10 were waited for; matrix products, arithmetic and copies ran while one was open for 0% of the time, Pallas kernels for 31%

profile of v8, /device:TPU:0, one launch (start us, length us, event | category | flops | bytes accessed | tf_op | source)
XLA Modules:
  0.0 208.0 jit_solution(16312984877751071807)
XLA Ops:
  0.6 0.7 pad_add_fusion.place_s
  1.3 4.1 %prepare.1 = (bf16[960,256]{1,0:T(8,128)(2,1)}, bf16[960,256]{1,0:T(8,128)(2,1)}, bf16[960,256]{1,0:T(8,128)(2,1)}, bf16[960,256]{1,0:T(8,128)(2,1)}, s32[1,128]...) custom-call(s32[3]{0:T(128)} %pad_add_fusion.place_s, ...), custom_call_target="tpu_custom_call" | custom-call | tf_op jit(solution)/shard_map/prepare/pallas_call | solution.py:148
  5.4 7.4 %all-to-all-start = ((s32[32,2,128]{2,1,0:T(2,128)}), s32[32,2,128]{2,1,0:T(2,128)S(1)}, u32[]{:S(2)}, u32[]{:S(2)}) async-start(s32[32,2,128]{2,1,0:T(2,128)} %bitcast.43), calls=%async_computation | async-start | bytes 65536 | tf_op jit(solution)/shard_map/all_to_all | solution.py:814
  12.9 10.5 %pack.1 = bf16[64,2,72,256]{3,2,1,0:T(8,128)(2,1)} custom-call(s32[128]{0:T(128)} %bitcast.44, s32[128]{0:T(128)} %bitcast.56, s32[128]{0:T(128)} %bitcast.58, bf16[70,128,256]{2,1,0:T(8,128)(2,1)} %bitcast.29, bf16[70,128,256]{2,1,0:T(8,128)(2,1)} %bitcast.33), custom_call_target="tpu_custom_call" | custom-call | tf_op jit(solution)/shard_map/pack/pallas_call | solution.py:347
  23.4 0.0 all-to-all-done
  23.4 0.6 copy-done.5
  24.0 7.2 %all-to-all-start.2 = ((bf16[64,2,72,256]{3,2,1,0:T(8,128)(2,1)}), bf16[64,2,72,256]{3,2,1,0:T(8,128)(2,1)}, u32[]{:S(2)}, u32[]{:S(2)}) async-start(bf16[64,2,72,256]{3,2,1,0:T(8,128)(2,1)} %pack.1), calls=%async_computation.2 | async-start | bytes 9437184 | tf_op jit(solution)/shard_map/all_to_all | solution.py:818
  31.2 4.1 %collective-permute-start.8 = (bf16[2048,256]{1,0:T(8,128)(2,1)S(1)}, bf16[2048,256]{1,0:T(8,128)(2,1)S(1)}, u32[]{:S(2)}, u32[]{:S(2)}) collective-permute-start(bf16[2048,256]{1,0:T(8,128)(2,1)S(1)} %copy-done.12), channel_id=1, source_target_pairs={{0,3},{1,0},{2,1},{3,2},{4,7},{5,4},{6,5},{7,6},{8,11},{9,8},{10,9... | collective-permute-start | bytes 3145736 | tf_op jit(solution)/shard_map/ppermute | solution.py:765
  35.3 0.0 collective-permute-start.6
  35.3 22.8 %collective-permute-done.8.refs_19_ = bf16[2048,256]{1,0:T(8,128)(2,1)S(1)} collective-permute-done((bf16[2048,256]{1,0:T(8,128)(2,1)S(1)}, bf16[2048,256]{1,0:T(8,128)(2,1)S(1)}, u32[]{:S(2)}, u32[]{:S(2)}) %collective-permute-start.8) | collective-permute-done | bytes 1048608 | tf_op jit(solution)/shard_map/ppermute | solution.py:765
  58.1 3.7 %collective-permute-start.9 = (bf16[2048,256]{1,0:T(8,128)(2,1)S(1)}, bf16[2048,256]{1,0:T(8,128)(2,1)}, u32[]{:S(2)}, u32[]{:S(2)}) collective-permute-start(bf16[2048,256]{1,0:T(8,128)(2,1)S(1)} %collective-permute-done.8.refs_19_), channel_id=1, source_target_pairs={{0,3},{1,0},{2,1},{3,2},{4,7},{5,4},{6,5},{7,6},{8,11},{9,8},{10,9... | collective-permute-start | bytes 3145736 | tf_op jit(solution)/shard_map/ppermute | solution.py:765
  61.8 0.0 collective-permute-start
  61.8 0.0 collective-permute-start.11
  61.8 0.0 collective-permute-done.6.refs_15_
  61.8 0.5 collective-permute-start.7
  62.3 21.5 %collective-permute-done.9.refs_17_ = bf16[2048,256]{1,0:T(8,128)(2,1)} collective-permute-done((bf16[2048,256]{1,0:T(8,128)(2,1)S(1)}, bf16[2048,256]{1,0:T(8,128)(2,1)}, u32[]{:S(2)}, u32[]{:S(2)}) %collective-permute-start.9) | collective-permute-done | bytes 1048608 | tf_op jit(solution)/shard_map/ppermute | solution.py:765
  83.8 0.0 collective-permute-start.10
  83.8 2.3 %collective-permute-start.1 = (bf16[960,256]{1,0:T(8,128)(2,1)}, bf16[960,256]{1,0:T(8,128)(2,1)S(1)}, u32[]{:S(2)}, u32[]{:S(2)}) collective-permute-start(bf16[960,256]{1,0:T(8,128)(2,1)} %get-tuple-element.54), channel_id=1, source_target_pairs={{0,2},{1,3},{2,0},{3,1},{4,6},{5,7},{6,4},{7,5},{8,10},{9,11},{10,... | collective-permute-start | bytes 1474568 | tf_op jit(solution)/shard_map/ppermute | solution.py:765
  86.1 0.0 collective-permute-done.near_ref.refs_5_
  86.1 1.6 collective-permute-start.2
  87.7 11.5 %collective-permute-done.1.far_ref.refs_6_ = bf16[960,256]{1,0:T(8,128)(2,1)S(1)} collective-permute-done((bf16[960,256]{1,0:T(8,128)(2,1)}, bf16[960,256]{1,0:T(8,128)(2,1)S(1)}, u32[]{:S(2)}, u32[]{:S(2)}) %collective-permute-start.1) | collective-permute-done | bytes 491552 | tf_op jit(solution)/shard_map/ppermute | solution.py:765
  99.2 11.7 %collective-permute-done.2.next_ref.refs_7_ = bf16[960,256]{1,0:T(8,128)(2,1)S(1)} collective-permute-done((bf16[960,256]{1,0:T(8,128)(2,1)S(1)}, bf16[960,256]{1,0:T(8,128)(2,1)S(1)}, u32[]{:S(2)}, u32[]{:S(2)}) %collective-permute-start.2) | collective-permute-done | bytes 491552 | tf_op jit(solution)/shard_map/ppermute | solution.py:765
  110.9 0.8 copy-done.3
  111.6 8.6 %head.1 = (bf16[7,128,256]{2,1,0:T(8,128)(2,1)}, bf16[7,128,256]{2,1,0:T(8,128)(2,1)}, bf16[7,128,256]{2,1,0:T(8,128)(2,1)}, bf16[7,32,1024]{2,1,0:T(8,128)(2,1)}) custom-call(s32[3]{0:T(128)} %pad_add_fusion.place_s, bf16[7,640,128]{2,1,0:T(8,128)(2,1)} %bitcast.39, bf16[960,256]{1,0:T(8,128)(2,1)} %get-tuple-element.52.own_ref.refs_4_, ...), custom_call_target="tpu_custom_call" | custom-call | tf_op jit(solution)/shard_map/head/pallas_call | solution.py:483
  120.3 8.6 %attend_a.1 = (bf16[7,32,256]{2,1,0:T(8,128)(2,1)}, bf16[7,32,256]{2,1,0:T(8,128)(2,1)}, bf16[7,128,256]{2,1,0:T(8,128)(2,1)}, bf16[7,128,256]{2,1,0:T(8,128)(2,1)}, s32[128,128]{1,0:T(8,128)}) custom-call(s32[3]{0:T(128)} %pad_add_fusion.place_s, s32[128]{0:T(128)} %bitcast.45, s32[128]{0:T(128)} %bitcast.60, s32[64,128]{1,0:T(8,128)} %bitcast.41, ...), custom_call_target="tpu_custom_call" | custom-call | tf_op jit(solution)/shard_map/attend_a/pallas_call | solution.py:286
  128.8 8.7 %attend_b.1 = (bf16[7,32,256]{2,1,0:T(8,128)(2,1)}, bf16[7,32,256]{2,1,0:T(8,128)(2,1)}, bf16[7,128,256]{2,1,0:T(8,128)(2,1)}, bf16[7,128,256]{2,1,0:T(8,128)(2,1)}, s32[128,128]{1,0:T(8,128)}) custom-call(s32[3]{0:T(128)} %pad_add_fusion.place_s, s32[128]{0:T(128)} %bitcast.46, ...), custom_call_target="tpu_custom_call", output_to_operand_aliasing={{2}: (9, {}), {3}: (10, {}), {4}: (11, {})} | custom-call | tf_op jit(solution)/shard_map/attend_b/pallas_call | solution.py:286
  137.6 2.3 %collective-permute-start.5 = (bf16[7,32,256]{2,1,0:T(8,128)(2,1)}, bf16[7,32,256]{2,1,0:T(8,128)(2,1)S(1)}, u32[]{:S(2)}, u32[]{:S(2)}) collective-permute-start(bf16[7,32,256]{2,1,0:T(8,128)(2,1)} %get-tuple-element.65), channel_id=1, source_target_pairs={{0,3},{1,0},{2,1},{3,2},{4,7},{5,4},{6,5},{7,6},{8,11},{9,8},{10,9... | collective-permute-start | bytes 344072 | tf_op jit(solution)/shard_map/ppermute | solution.py:765
  139.9 0.0 collective-permute-start.3
  139.9 2.7 %collective-permute-done.5.refs_3_ = bf16[7,32,256]{2,1,0:T(8,128)(2,1)S(1)} collective-permute-done((bf16[7,32,256]{2,1,0:T(8,128)(2,1)}, bf16[7,32,256]{2,1,0:T(8,128)(2,1)S(1)}, u32[]{:S(2)}, u32[]{:S(2)}) %collective-permute-start.5) | collective-permute-done | bytes 114720 | tf_op jit(solution)/shard_map/ppermute | solution.py:765
  142.6 1.9 collective-permute-start.4
  144.6 2.6 %collective-permute-done.3.refs_1_ = bf16[7,32,256]{2,1,0:T(8,128)(2,1)S(1)} collective-permute-done((bf16[7,32,256]{2,1,0:T(8,128)(2,1)S(1)}, bf16[7,32,256]{2,1,0:T(8,128)(2,1)S(1)}, u32[]{:S(2)}, u32[]{:S(2)}) %collective-permute-start.3) | collective-permute-done | bytes 114720 | tf_op jit(solution)/shard_map/ppermute | solution.py:765
  147.1 1.8 collective-permute-done.4.refs_2_
  149.0 0.0 collective-permute-done.10.refs_18_
  149.0 0.6 copy-done.11
  149.6 9.6 %tail.1 = (bf16[15,32,256]{2,1,0:T(8,128)(2,1)}, bf16[15,32,256]{2,1,0:T(8,128)(2,1)}, bf16[15,32,256]{2,1,0:T(8,128)(2,1)}, bf16[15,32,256]{2,1,0:T(8,128)(2,1)}) custom-call(s32[3]{0:T(128)} %pad_add_fusion.place_s, bf16[7,32,256]{2,1,0:T(8,128)(2,1)} %get-tuple-element.62.refs_0_, bf16[7,32,256]{2,1,0:T(8,128)(2,1)} %copy-done.10, ...), custom_call_target="tpu_custom_call" | custom-call | tf_op jit(solution)/shard_map/tail/pallas_call | solution.py:630
  159.2 0.9 collective-permute-start.12
  160.1 4.1 %collective-permute-start.13 = (bf16[15,32,256]{2,1,0:T(8,128)(2,1)}, bf16[15,32,256]{2,1,0:T(8,128)(2,1)S(1)}, u32[]{:S(2)}, u32[]{:S(2)}) collective-permute-start(bf16[15,32,256]{2,1,0:T(8,128)(2,1)} %get-tuple-element.71), channel_id=1, source_target_pairs={{0,2},{1,3},{2,0},{3,1},{4,6},{5,7},{6,4},{7,5},{8,10},{9,11},{10,... | collective-permute-start | bytes 737288 | tf_op jit(solution)/shard_map/ppermute | solution.py:765
  164.2 0.0 collective-permute-start.14
  164.2 5.6 %collective-permute-done.12.refs_1_ = bf16[15,32,256]{2,1,0:T(8,128)(2,1)S(1)} collective-permute-done((bf16[15,32,256]{2,1,0:T(8,128)(2,1)}, bf16[15,32,256]{2,1,0:T(8,128)(2,1)S(1)}, u32[]{:S(2)}, u32[]{:S(2)}) %collective-permute-start.12) | collective-permute-done | bytes 245792 | tf_op jit(solution)/shard_map/ppermute | solution.py:765
  169.8 3.1 %collective-permute-done.13.refs_2_ = bf16[15,32,256]{2,1,0:T(8,128)(2,1)S(1)} collective-permute-done((bf16[15,32,256]{2,1,0:T(8,128)(2,1)}, bf16[15,32,256]{2,1,0:T(8,128)(2,1)S(1)}, u32[]{:S(2)}, u32[]{:S(2)}) %collective-permute-start.13) | collective-permute-done | bytes 245792 | tf_op jit(solution)/shard_map/ppermute | solution.py:765
  172.9 0.7 copy-done.7
  173.6 0.1 copy-done.8
  173.7 4.6 %collect.1 = (bf16[29,128,256]{2,1,0:T(8,128)(2,1)}, bf16[64,32,256]{2,1,0:T(8,128)(2,1)}) custom-call(s32[128]{0:T(128)} %bitcast.47, s32[128]{0:T(128)} %bitcast.57, s32[128]{0:T(128)} %bitcast.59, s32[3]{0:T(128)} %pad_add_fusion.place_s, bf16[15,32,256]{2,1,0:T(8,128)(2,1)} %get-tuple-element.69.refs_0_, bf16[15,32,256]{2,1,0:T(8,128)(2,1)} %copy-done.6, ...), custom_call_target="tpu_custom_call" | custom-call | tf_op jit(solution)/shard_map/collect/pallas_call | solution.py:687
  178.3 7.0 %all-to-all-start.1 = ((bf16[64,32,256]{2,1,0:T(8,128)(2,1)}), bf16[64,32,256]{2,1,0:T(8,128)(2,1)S(1)}, u32[]{:S(2)}, u32[]{:S(2)}) async-start(bf16[64,32,256]{2,1,0:T(8,128)(2,1)} %get-tuple-element.76), calls=%async_computation.1 | async-start | bytes 2097152 | tf_op jit(solution)/shard_map/all_to_all | solution.py:863
  185.4 13.5 %place.1 = (bf16[70,128,256]{2,1,0:T(8,128)(2,1)}, bf16[70,128,256]{2,1,0:T(8,128)(2,1)}) custom-call(s32[128]{0:T(128)} %bitcast.50, s32[128]{0:T(128)} %bitcast.52, s32[128]{0:T(128)} %bitcast.54, bf16[64,2,72,256]{3,2,1,0:T(8,128)(2,1)} %all-to-all-done.2.got_ref, s32[128,128]{1,0:T(8,128)} %get-tuple-element.77.valid_ref, ...), custom_call_target="tpu_custom_call" | custom-call | tf_op jit(solution)/shard_map/place/pallas_call | solution.py:411
  198.9 3.7 %all-to-all-done.1.got_ref = bf16[64,32,256]{2,1,0:T(8,128)(2,1)S(1)} async-done(((bf16[64,32,256]{2,1,0:T(8,128)(2,1)}), bf16[64,32,256]{2,1,0:T(8,128)(2,1)S(1)}, u32[]{:S(2)}, u32[]{:S(2)}) %all-to-all-start.1) | async-done | bytes 1048608 | tf_op jit(solution)/shard_map/all_to_all | solution.py:863
  202.6 1.0 copy-done
  203.6 4.5 %finish.1 = (bf16[7,128,256]{2,1,0:T(8,128)(2,1)}, bf16[128,8,256]{2,1,0:T(8,128)(2,1)}, bf16[70,128,256]{2,1,0:T(8,128)(2,1)}, bf16[70,128,256]{2,1,0:T(8,128)(2,1)}) custom-call(s32[128]{0:T(128)} %bitcast.51, s32[128]{0:T(128)} %bitcast.53, s32[128]{0:T(128)} %bitcast.55, ...), custom_call_target="tpu_custom_call", output_to_operand_aliasing={{2}: (5, {}), {3}: (6, {})} | custom-call | tf_op jit(solution)/shard_map/finish/pallas_call | solution.py:744
  (30 shorter events, 0.1 us)
Async XLA Ops:
  5.4 18.0 %all-to-all-start = ((s32[32,2,128]{2,1,0:T(2,128)}), s32[32,2,128]{2,1,0:T(2,128)S(1)}, u32[]{:S(2)}, u32[]{:S(2)}) async-start(s32[32,2,128]{2,1,0:T(2,128)} %bitcast.43), calls=%async_computation | async-start | bytes 65536 | tf_op jit(solution)/shard_map/all_to_all | solution.py:814
  23.4 7.8 %copy-start.12 = (bf16[2048,256]{1,0:T(8,128)(2,1)S(1)}, bf16[2048,256]{1,0:T(8,128)(2,1)}, u32[]{:S(2)}) copy-start(bf16[2048,256]{1,0:T(8,128)(2,1)} %get-tuple-element.68) | copy-start | bytes 3145732
  23.4 62.7 %copy-start.13 = (bf16[960,256]{1,0:T(8,128)(2,1)S(1)}, bf16[960,256]{1,0:T(8,128)(2,1)}, u32[]{:S(2)}) copy-start(bf16[960,256]{1,0:T(8,128)(2,1)} %get-tuple-element.55) | copy-start | bytes 1474564
  23.4 0.6 copy-start.5
  24.0 154.3 %all-to-all-start.2 = ((bf16[64,2,72,256]{3,2,1,0:T(8,128)(2,1)}), bf16[64,2,72,256]{3,2,1,0:T(8,128)(2,1)}, u32[]{:S(2)}, u32[]{:S(2)}) async-start(bf16[64,2,72,256]{3,2,1,0:T(8,128)(2,1)} %pack.1), calls=%async_computation.2 | async-start | bytes 9437184 | tf_op jit(solution)/shard_map/all_to_all | solution.py:818
  31.2 26.9 %collective-permute-start.8 = (bf16[2048,256]{1,0:T(8,128)(2,1)S(1)}, bf16[2048,256]{1,0:T(8,128)(2,1)S(1)}, u32[]{:S(2)}, u32[]{:S(2)}) collective-permute-start(bf16[2048,256]{1,0:T(8,128)(2,1)S(1)} %copy-done.12), channel_id=1, source_target_pairs={{0,3},{1,0},{2,1},{3,2},{4,7},{5,4},{6,5},{7,6},{8,11},{9,8},{10,9... | collective-permute-start | bytes 3145736 | tf_op jit(solution)/shard_map/ppermute | solution.py:765
  35.3 26.5 %collective-permute-start.6 = (bf16[2048,256]{1,0:T(8,128)(2,1)S(1)}, bf16[2048,256]{1,0:T(8,128)(2,1)}, u32[]{:S(2)}, u32[]{:S(2)}) collective-permute-start(bf16[2048,256]{1,0:T(8,128)(2,1)S(1)} %copy-done.12), channel_id=1, source_target_pairs={{0,1},{1,2},{2,3},{3,0},{4,5},{5,6},{6,7},{7,4},{8,9},{9,10},{10,1... | collective-permute-start | bytes 3145736 | tf_op jit(solution)/shard_map/ppermute | solution.py:765
  58.1 90.9 %copy-start.4 = (bf16[2048,256]{1,0:T(8,128)(2,1)}, bf16[2048,256]{1,0:T(8,128)(2,1)S(1)}, u32[]{:S(2)}) copy-start(bf16[2048,256]{1,0:T(8,128)(2,1)S(1)} %collective-permute-done.8.refs_19_) | copy-start | bytes 3145732
  58.1 25.7 %collective-permute-start.9 = (bf16[2048,256]{1,0:T(8,128)(2,1)S(1)}, bf16[2048,256]{1,0:T(8,128)(2,1)}, u32[]{:S(2)}, u32[]{:S(2)}) collective-permute-start(bf16[2048,256]{1,0:T(8,128)(2,1)S(1)} %collective-permute-done.8.refs_19_), channel_id=1, source_target_pairs={{0,3},{1,0},{2,1},{3,2},{4,7},{5,4},{6,5},{7,6},{8,11},{9,8},{10,9... | collective-permute-start | bytes 3145736 | tf_op jit(solution)/shard_map/ppermute | solution.py:765
  61.8 24.4 %collective-permute-start = (bf16[960,256]{1,0:T(8,128)(2,1)}, bf16[960,256]{1,0:T(8,128)(2,1)S(1)}, u32[]{:S(2)}, u32[]{:S(2)}) collective-permute-start(bf16[960,256]{1,0:T(8,128)(2,1)} %get-tuple-element.53), channel_id=1, source_target_pairs={{0,1},{1,2},{2,3},{3,0},{4,5},{5,6},{6,7},{7,4},{8,9},{9,10},{10,1... | collective-permute-start | bytes 1474568 | tf_op jit(solution)/shard_map/ppermute | solution.py:765
  61.8 87.2 %collective-permute-start.11 = (bf16[2048,256]{1,0:T(8,128)(2,1)S(1)}, bf16[2048,256]{1,0:T(8,128)(2,1)}, u32[]{:S(2)}, u32[]{:S(2)}) collective-permute-start(bf16[2048,256]{1,0:T(8,128)(2,1)S(1)} %collective-permute-done.8.refs_19_), channel_id=1, source_target_pairs={{0,4},{4,0},{8,12},{12,8},{16,20},{20,16},{24,28},{28,24},{32,36},... | collective-permute-start | bytes 3145736 | tf_op jit(solution)/shard_map/ppermute | solution.py:822
  61.8 87.2 %collective-permute-start.7 = (bf16[2048,256]{1,0:T(8,128)(2,1)}, bf16[2048,256]{1,0:T(8,128)(2,1)}, u32[]{:S(2)}, u32[]{:S(2)}) collective-permute-start(bf16[2048,256]{1,0:T(8,128)(2,1)} %collective-permute-done.6.refs_15_), channel_id=1, source_target_pairs={{0,4},{4,0},{8,12},{12,8},{16,20},{20,16},{24,28},{28,24},{32,36},... | collective-permute-start | bytes 3145736 | tf_op jit(solution)/shard_map/ppermute | solution.py:822
  83.8 65.2 %collective-permute-start.10 = (bf16[2048,256]{1,0:T(8,128)(2,1)}, bf16[2048,256]{1,0:T(8,128)(2,1)}, u32[]{:S(2)}, u32[]{:S(2)}) collective-permute-start(bf16[2048,256]{1,0:T(8,128)(2,1)} %collective-permute-done.9.refs_17_), channel_id=1, source_target_pairs={{0,4},{4,0},{8,12},{12,8},{16,20},{20,16},{24,28},{28,24},{32,36},... | collective-permute-start | bytes 3145736 | tf_op jit(solution)/shard_map/ppermute | solution.py:822
  83.8 15.3 %collective-permute-start.1 = (bf16[960,256]{1,0:T(8,128)(2,1)}, bf16[960,256]{1,0:T(8,128)(2,1)S(1)}, u32[]{:S(2)}, u32[]{:S(2)}) collective-permute-start(bf16[960,256]{1,0:T(8,128)(2,1)} %get-tuple-element.54), channel_id=1, source_target_pairs={{0,2},{1,3},{2,0},{3,1},{4,6},{5,7},{6,4},{7,5},{8,10},{9,11},{10,... | collective-permute-start | bytes 1474568 | tf_op jit(solution)/shard_map/ppermute | solution.py:765
  86.1 24.7 %copy-start.1 = (bf16[960,256]{1,0:T(8,128)(2,1)}, bf16[960,256]{1,0:T(8,128)(2,1)S(1)}, u32[]{:S(2)}) copy-start(bf16[960,256]{1,0:T(8,128)(2,1)S(1)} %collective-permute-done.near_ref.refs_5_) | copy-start | bytes 1474564
  86.1 24.7 %collective-permute-start.2 = (bf16[960,256]{1,0:T(8,128)(2,1)S(1)}, bf16[960,256]{1,0:T(8,128)(2,1)S(1)}, u32[]{:S(2)}, u32[]{:S(2)}) collective-permute-start(bf16[960,256]{1,0:T(8,128)(2,1)S(1)} %copy-done.13), channel_id=1, source_target_pairs={{0,3},{1,0},{2,1},{3,2},{4,7},{5,4},{6,5},{7,6},{8,11},{9,8},{10,9... | collective-permute-start | bytes 1474568 | tf_op jit(solution)/shard_map/ppermute | solution.py:765
  99.2 11.7 %copy-start.2 = (bf16[960,256]{1,0:T(8,128)(2,1)}, bf16[960,256]{1,0:T(8,128)(2,1)S(1)}, u32[]{:S(2)}) copy-start(bf16[960,256]{1,0:T(8,128)(2,1)S(1)} %collective-permute-done.1.far_ref.refs_6_) | copy-start | bytes 1474564
  110.9 0.8 copy-start.3
  128.8 11.1 %copy-start.15 = (bf16[7,32,256]{2,1,0:T(8,128)(2,1)S(1)}, bf16[7,32,256]{2,1,0:T(8,128)(2,1)}, u32[]{:S(2)}) copy-start(bf16[7,32,256]{2,1,0:T(8,128)(2,1)} %get-tuple-element.63) | copy-start | bytes 344068
  128.8 13.8 %copy-start.14 = (bf16[7,32,256]{2,1,0:T(8,128)(2,1)S(1)}, bf16[7,32,256]{2,1,0:T(8,128)(2,1)}, u32[]{:S(2)}) copy-start(bf16[7,32,256]{2,1,0:T(8,128)(2,1)} %get-tuple-element.64) | copy-start | bytes 344068
  137.6 5.1 %collective-permute-start.5 = (bf16[7,32,256]{2,1,0:T(8,128)(2,1)}, bf16[7,32,256]{2,1,0:T(8,128)(2,1)S(1)}, u32[]{:S(2)}, u32[]{:S(2)}) collective-permute-start(bf16[7,32,256]{2,1,0:T(8,128)(2,1)} %get-tuple-element.65), channel_id=1, source_target_pairs={{0,3},{1,0},{2,1},{3,2},{4,7},{5,4},{6,5},{7,6},{8,11},{9,8},{10,9... | collective-permute-start | bytes 344072 | tf_op jit(solution)/shard_map/ppermute | solution.py:765
  139.9 7.2 %collective-permute-start.3 = (bf16[7,32,256]{2,1,0:T(8,128)(2,1)S(1)}, bf16[7,32,256]{2,1,0:T(8,128)(2,1)S(1)}, u32[]{:S(2)}, u32[]{:S(2)}) collective-permute-start(bf16[7,32,256]{2,1,0:T(8,128)(2,1)S(1)} %copy-done.15), channel_id=1, source_target_pairs={{0,1},{1,2},{2,3},{3,0},{4,5},{5,6},{6,7},{7,4},{8,9},{9,10},{10,1... | collective-permute-start | bytes 344072 | tf_op jit(solution)/shard_map/ppermute | solution.py:765
  142.6 6.3 %copy-start.9 = (bf16[7,32,256]{2,1,0:T(8,128)(2,1)}, bf16[7,32,256]{2,1,0:T(8,128)(2,1)S(1)}, u32[]{:S(2)}) copy-start(bf16[7,32,256]{2,1,0:T(8,128)(2,1)S(1)} %collective-permute-done.5.refs_3_) | copy-start | bytes 344068
  142.6 6.3 %collective-permute-start.4 = (bf16[7,32,256]{2,1,0:T(8,128)(2,1)S(1)}, bf16[7,32,256]{2,1,0:T(8,128)(2,1)S(1)}, u32[]{:S(2)}, u32[]{:S(2)}) collective-permute-start(bf16[7,32,256]{2,1,0:T(8,128)(2,1)S(1)} %copy-done.14), channel_id=1, source_target_pairs={{0,2},{1,3},{2,0},{3,1},{4,6},{5,7},{6,4},{7,5},{8,10},{9,11},{10,... | collective-permute-start | bytes 344072 | tf_op jit(solution)/shard_map/ppermute | solution.py:765
  147.1 1.8 copy-start.10
  148.9 0.6 copy-start.11
  159.2 10.5 %collective-permute-start.12 = (bf16[15,32,256]{2,1,0:T(8,128)(2,1)}, bf16[15,32,256]{2,1,0:T(8,128)(2,1)S(1)}, u32[]{:S(2)}, u32[]{:S(2)}) collective-permute-start(bf16[15,32,256]{2,1,0:T(8,128)(2,1)} %get-tuple-element.70), channel_id=1, source_target_pairs={{0,1},{1,2},{2,3},{3,0},{4,5},{5,6},{6,7},{7,4},{8,9},{9,10},{10,1... | collective-permute-start | bytes 737288 | tf_op jit(solution)/shard_map/ppermute | solution.py:765
  160.1 12.8 %collective-permute-start.13 = (bf16[15,32,256]{2,1,0:T(8,128)(2,1)}, bf16[15,32,256]{2,1,0:T(8,128)(2,1)S(1)}, u32[]{:S(2)}, u32[]{:S(2)}) collective-permute-start(bf16[15,32,256]{2,1,0:T(8,128)(2,1)} %get-tuple-element.71), channel_id=1, source_target_pairs={{0,2},{1,3},{2,0},{3,1},{4,6},{5,7},{6,4},{7,5},{8,10},{9,11},{10,... | collective-permute-start | bytes 737288 | tf_op jit(solution)/shard_map/ppermute | solution.py:765
  164.2 8.7 %collective-permute-start.14 = (bf16[15,32,256]{2,1,0:T(8,128)(2,1)}, bf16[15,32,256]{2,1,0:T(8,128)(2,1)S(1)}, u32[]{:S(2)}, u32[]{:S(2)}) collective-permute-start(bf16[15,32,256]{2,1,0:T(8,128)(2,1)} %get-tuple-element.72), channel_id=1, source_target_pairs={{0,3},{1,0},{2,1},{3,2},{4,7},{5,4},{6,5},{7,6},{8,11},{9,8},{10,9... | collective-permute-start | bytes 737288 | tf_op jit(solution)/shard_map/ppermute | solution.py:765
  169.8 3.2 %copy-start.6 = (bf16[15,32,256]{2,1,0:T(8,128)(2,1)}, bf16[15,32,256]{2,1,0:T(8,128)(2,1)S(1)}, u32[]{:S(2)}) copy-start(bf16[15,32,256]{2,1,0:T(8,128)(2,1)S(1)} %collective-permute-done.12.refs_1_) | copy-start | bytes 737284
  172.9 0.7 copy-start.7
  172.9 0.8 copy-start.8
  178.3 24.2 %all-to-all-start.1 = ((bf16[64,32,256]{2,1,0:T(8,128)(2,1)}), bf16[64,32,256]{2,1,0:T(8,128)(2,1)S(1)}, u32[]{:S(2)}, u32[]{:S(2)}) async-start(bf16[64,32,256]{2,1,0:T(8,128)(2,1)} %get-tuple-element.76), calls=%async_computation.1 | async-start | bytes 2097152 | tf_op jit(solution)/shard_map/all_to_all | solution.py:863
  202.6 1.0 copy-start

commit v9 on v7

--- a/solution.py
+++ b/solution.py
@@ -58,7 +58,8 @@
     small[KERNEL + 1 : KERNEL + 2, :] = shift_ref[...]
     small[KERNEL + 2 :, :] = jnp.zeros((16 - KERNEL - 2, width), jnp.float32)
     rest = small[...]
-    bias = jnp.broadcast_to(bias_ref[...].astype(jnp.float32), (16, width)).astype(jnp.bfloat16)
+    bias = bias_ref[...].astype(jnp.float32).reshape(1, width)
+    bias = jnp.broadcast_to(bias, (16, width)).astype(jnp.bfloat16)
     parts = []
     for _ in range(3):
         part = rest.astype(jnp.bfloat16)
@@ -127,7 +128,7 @@
     count = rows[0].shape[0]
     groups, chunk_rows, width = chunks.shape
     taps = sub[0].shape[0]
-    whole = [r[None] for r in rows] + [sub[0], sub[1][None], conv[0], conv[1][None], conv[2][None]]
+    whole = [r[None] for r in rows] + [sub[0], sub[1], conv[0], conv[1][None], conv[2][None]]
 
     def full(array):
         zeros = (0,) * array.ndim
@@ -216,6 +217,7 @@
             axis=0,
         )
 
+    contexts = []
     for h in range(heads):
         lanes = slice(h * LANES, (h + 1) * LANES)
         scores = lax.dot_general(
@@ -233,15 +235,7 @@
             (((1,), (0,)), ((), ())),
             preferred_element_type=jnp.float32,
         )
-        context = context.reshape(FRAMES, BLOCK, LANES).astype(jnp.bfloat16)
-
-        @pl.when(step < per_group)
-        def _():
-            near_ref[:, :, lanes] = context
-
-        @pl.when(step >= per_group)
-        def _():
-            far_ref[:, :, lanes] = context
+        contexts.append(context.reshape(FRAMES, BLOCK, LANES).astype(jnp.bfloat16))
 
     shift = valid - 1
     first = ((shift & 1) != 0)[None]
@@ -258,6 +252,16 @@
             new = new_ref[:, :, lanes].astype(jnp.float32)
             rows = jnp.concatenate([old, new, new[:1]], axis=0)
             out_ref[:, :, lanes] = shift_rows(rows, first, second, third).astype(jnp.bfloat16)
+
+    @pl.when(step < per_group)
+    def _():
+        for h, context in enumerate(contexts):
+            near_ref[:, :, h * LANES : (h + 1) * LANES] = context
+
+    @pl.when(step >= per_group)
+    def _():
+        for h, context in enumerate(contexts):
+            far_ref[:, :, h * LANES : (h + 1) * LANES] = context
 
 
 def chosen_block(i, place_s, begin, groups, per_group):
@@ -510,6 +514,7 @@
     rows = FRAMES * share
     size = groups * width
     half = width // 2
+    high_starts = (size, 0, size)
 
     def ordered(operand):
         middle_lane = operand.shape[1] // 2
@@ -542,7 +547,6 @@
             for i, side in enumerate(normed_sides)
         )
 
-    high_starts = (size, 0, size)
     attended = [None] * groups
     for step in range(groups):
         grouped(step, contexts[step][...].reshape(rows, width), attn_ref, 0, attended)
@@ -814,11 +818,11 @@
     leaving_rows = pack_rows(leaving, key_rows, value_rows, slots)
     received = lax.all_to_all(leaving_rows, "front", split_axis=0, concat_axis=0, tiled=True)
     taps = SUB * MELS
-    middle_row = stack.shape[0] // 2
 
     def other_core(array):
         return lax.ppermute(array, "front", [(i, i ^ 1) for i in range(peer_count)])
 
+    middle_row = stack.shape[0] // 2
     near = toward(stack, 1, groups)
     after = toward(stack, -1, groups)
     far_low = toward(near[:middle_row], 1, groups)

time: 205 us -> 202 us (0.985)
  no operation moved by 1% of the time
where the time goes in v9:
time: 202 us; the launch traced here: 200 us
  waiting for transfers between devices  80.6 us (40%)
  Pallas kernels  74 us (37%)
  starting transfers between devices  40.8 us (20%)
  local copies, waits for them, and re-layouts  3.32 us (2%)
    ppermute x13, waiting for transfers between devices, toward(): lax.ppermute(array, 'enc', [(i, (i + steps) % count) for i in range(count)])  76.9 us
    ppermute x13, starting transfers between devices, toward(): lax.ppermute(array, 'enc', [(i, (i + steps) % count) for i in range(count)])  18.3 us
    pallas_call x2, Pallas kernels, attend(): pl.pallas_call(functools.partial(attend_body, begin=begin, groups=groups,...  17.3 us
    pallas_call x1, Pallas kernels, place(): pl.pallas_call(place_body, grid_spec=pltpu.PrefetchScalarGridSpec(num_sca...  13.5 us
    pallas_call x1, Pallas kernels, tail(): pl.pallas_call(tail_body, in_specs=[pl.BlockSpec(memory_space=pltpu.SMEM)...  10.8 us
    pallas_call x1, Pallas kernels, pack_rows(): pl.pallas_call(pack_body, grid_spec=pltpu.PrefetchScalarGridSpec(num_scal...  10.5 us
    pallas_call x1, Pallas kernels, head(): pl.pallas_call(head_body, grid_spec=pltpu.PrefetchScalarGridSpec(num_scal...  8.62 us
    all_to_all x1, starting transfers between devices, on_device(): lax.all_to_all(asked, 'front', split_axis=0, concat_axis=0, tiled=True)  7.44 us
  transfers between devices with their start and end apart: 20, of which 11 were waited for; matrix products, arithmetic and copies ran while one was open for 0% of the time, Pallas kernels for 33%

profile of v9, /device:TPU:0, one launch (start us, length us, event | category | flops | bytes accessed | tf_op | source)
XLA Modules:
  0.0 200.2 jit_solution(10402944736395935857)
XLA Ops:
  0.6 0.6 pad_add_fusion.place_s
  1.2 4.1 %prepare.1 = (bf16[960,256]{1,0:T(8,128)(2,1)}, bf16[960,256]{1,0:T(8,128)(2,1)}, bf16[960,256]{1,0:T(8,128)(2,1)}, bf16[960,256]{1,0:T(8,128)(2,1)}, s32[1,128]...) custom-call(s32[3]{0:T(128)} %pad_add_fusion.place_s, ...), custom_call_target="tpu_custom_call" | custom-call | tf_op jit(solution)/shard_map/prepare/pallas_call | solution.py:148
  5.4 7.4 %all-to-all-start = ((s32[32,2,128]{2,1,0:T(2,128)}), s32[32,2,128]{2,1,0:T(2,128)S(1)}, u32[]{:S(2)}, u32[]{:S(2)}) async-start(s32[32,2,128]{2,1,0:T(2,128)} %bitcast.43), calls=%async_computation | async-start | bytes 65536 | tf_op jit(solution)/shard_map/all_to_all | solution.py:815
  12.8 10.5 %pack.1 = bf16[64,2,72,256]{3,2,1,0:T(8,128)(2,1)} custom-call(s32[128]{0:T(128)} %bitcast.44, s32[128]{0:T(128)} %bitcast.56, s32[128]{0:T(128)} %bitcast.58, bf16[70,128,256]{2,1,0:T(8,128)(2,1)} %bitcast.29, bf16[70,128,256]{2,1,0:T(8,128)(2,1)} %bitcast.33), custom_call_target="tpu_custom_call" | custom-call | tf_op jit(solution)/shard_map/pack/pallas_call | solution.py:347
  23.3 0.0 all-to-all-done
  23.3 0.6 copy-done.4
  23.9 7.2 %all-to-all-start.2 = ((bf16[64,2,72,256]{3,2,1,0:T(8,128)(2,1)}), bf16[64,2,72,256]{3,2,1,0:T(8,128)(2,1)}, u32[]{:S(2)}, u32[]{:S(2)}) async-start(bf16[64,2,72,256]{3,2,1,0:T(8,128)(2,1)} %pack.1), calls=%async_computation.2 | async-start | bytes 9437184 | tf_op jit(solution)/shard_map/all_to_all | solution.py:819
  31.1 4.1 %collective-permute-start.10 = (bf16[2048,256]{1,0:T(8,128)(2,1)S(1)}, bf16[2048,256]{1,0:T(8,128)(2,1)S(1)}, u32[]{:S(2)}, u32[]{:S(2)}) collective-permute-start(bf16[2048,256]{1,0:T(8,128)(2,1)S(1)} %copy-done.11), channel_id=1, source_target_pairs={{0,3},{1,0},{2,1},{3,2},{4,7},{5,4},{6,5},{7,6},{8,11},{9,8},{10,9... | collective-permute-start | bytes 3145736 | tf_op jit(solution)/shard_map/ppermute | solution.py:766
  35.2 0.0 collective-permute-start
  35.2 4.7 %collective-permute-start.1 = (bf16[960,256]{1,0:T(8,128)(2,1)}, bf16[960,256]{1,0:T(8,128)(2,1)}, u32[]{:S(2)}, u32[]{:S(2)}) collective-permute-start(bf16[960,256]{1,0:T(8,128)(2,1)} %get-tuple-element.54), channel_id=1, source_target_pairs={{0,2},{1,3},{2,0},{3,1},{4,6},{5,7},{6,4},{7,5},{8,10},{9,11},{10,... | collective-permute-start | bytes 1474568 | tf_op jit(solution)/shard_map/ppermute | solution.py:766
  39.9 28.6 %collective-permute-done.10.refs_19_.refs_25_ = bf16[2048,256]{1,0:T(8,128)(2,1)S(1)} collective-permute-done((bf16[2048,256]{1,0:T(8,128)(2,1)S(1)}, bf16[2048,256]{1,0:T(8,128)(2,1)S(1)}, u32[]{:S(2)}, u32[]{:S(2)}) %collective-permute-start.10) | collective-permute-done | bytes 1048608 | tf_op jit(solution)/shard_map/ppermute | solution.py:766
  68.6 3.8 %collective-permute-start.12 = (bf16[1024,256]{1,0:T(8,128)(2,1)S(1)}, bf16[1024,256]{1,0:T(8,128)(2,1)}, u32[]{:S(2)}, u32[]{:S(2)}) collective-permute-start(bf16[1024,256]{1,0:T(8,128)(2,1)S(1)} %slice.9), channel_id=1, source_target_pairs={{0,3},{1,0},{2,1},{3,2},{4,7},{5,4},{6,5},{7,6},{8,11},{9,8},{10,9... | collective-permute-start | bytes 1572872 | tf_op jit(solution)/shard_map/ppermute | solution.py:766
  72.3 0.0 collective-permute-done.6.refs_15_.refs_21_
  72.4 0.1 collective-permute-start.8
  72.5 0.1 collective-permute-start.11
  72.6 11.1 %collective-permute-done.near_ref.refs_5_ = bf16[960,256]{1,0:T(8,128)(2,1)} collective-permute-done((bf16[960,256]{1,0:T(8,128)(2,1)}, bf16[960,256]{1,0:T(8,128)(2,1)}, u32[]{:S(2)}, u32[]{:S(2)}) %collective-permute-start) | collective-permute-done | bytes 491552 | tf_op jit(solution)/shard_map/ppermute | solution.py:766
  83.6 0.0 collective-permute-done.12.refs_23_
  83.6 0.6 collective-permute-start.13
  84.2 9.6 %collective-permute-done.8.refs_17_ = bf16[1024,256]{1,0:T(8,128)(2,1)} collective-permute-done((bf16[1024,256]{1,0:T(8,128)(2,1)S(1)}, bf16[1024,256]{1,0:T(8,128)(2,1)}, u32[]{:S(2)}, u32[]{:S(2)}) %collective-permute-start.8) | collective-permute-done | bytes 524320 | tf_op jit(solution)/shard_map/ppermute | solution.py:766
  93.8 0.0 collective-permute-start.9
  93.8 3.8 %collective-permute-done.2.next_ref.refs_7_ = bf16[960,256]{1,0:T(8,128)(2,1)} collective-permute-done((bf16[960,256]{1,0:T(8,128)(2,1)}, bf16[960,256]{1,0:T(8,128)(2,1)}, u32[]{:S(2)}, u32[]{:S(2)}) %collective-permute-start.2) | collective-permute-done | bytes 491552 | tf_op jit(solution)/shard_map/ppermute | solution.py:766
  97.6 8.6 %head.1 = (bf16[7,128,256]{2,1,0:T(8,128)(2,1)}, bf16[7,128,256]{2,1,0:T(8,128)(2,1)}, bf16[7,128,256]{2,1,0:T(8,128)(2,1)}, bf16[7,32,1024]{2,1,0:T(8,128)(2,1)}) custom-call(s32[3]{0:T(128)} %pad_add_fusion.place_s, bf16[7,640,128]{2,1,0:T(8,128)(2,1)} %bitcast.39, bf16[960,256]{1,0:T(8,128)(2,1)} %get-tuple-element.52.own_ref.refs_4_, ...), custom_call_target="tpu_custom_call" | custom-call | tf_op jit(solution)/shard_map/head/pallas_call | solution.py:483
  106.2 8.6 %attend_a.1 = (bf16[7,32,256]{2,1,0:T(8,128)(2,1)}, bf16[7,32,256]{2,1,0:T(8,128)(2,1)}, bf16[7,128,256]{2,1,0:T(8,128)(2,1)}, bf16[7,128,256]{2,1,0:T(8,128)(2,1)}, s32[128,128]{1,0:T(8,128)}) custom-call(s32[3]{0:T(128)} %pad_add_fusion.place_s, s32[128]{0:T(128)} %bitcast.45, s32[128]{0:T(128)} %bitcast.60, s32[64,128]{1,0:T(8,128)} %bitcast.41, ...), custom_call_target="tpu_custom_call" | custom-call | tf_op jit(solution)/shard_map/attend_a/pallas_call | solution.py:286
  114.8 8.7 %attend_b.1 = (bf16[7,32,256]{2,1,0:T(8,128)(2,1)}, bf16[7,32,256]{2,1,0:T(8,128)(2,1)}, bf16[7,128,256]{2,1,0:T(8,128)(2,1)}, bf16[7,128,256]{2,1,0:T(8,128)(2,1)}, s32[128,128]{1,0:T(8,128)}) custom-call(s32[3]{0:T(128)} %pad_add_fusion.place_s, s32[128]{0:T(128)} %bitcast.46, ...), custom_call_target="tpu_custom_call", output_to_operand_aliasing={{2}: (9, {}), {3}: (10, {}), {4}: (11, {})} | custom-call | tf_op jit(solution)/shard_map/attend_b/pallas_call | solution.py:286
  123.5 1.5 collective-permute-start.5
  125.0 3.5 %collective-permute-done.5.refs_3_ = bf16[7,32,256]{2,1,0:T(8,128)(2,1)S(1)} collective-permute-done((bf16[7,32,256]{2,1,0:T(8,128)(2,1)}, bf16[7,32,256]{2,1,0:T(8,128)(2,1)S(1)}, u32[]{:S(2)}, u32[]{:S(2)}) %collective-permute-start.5) | collective-permute-done | bytes 114720 | tf_op jit(solution)/shard_map/ppermute | solution.py:766
  128.6 0.0 collective-permute-start.3
  128.6 6.0 %collective-permute-done.3.refs_1_ = bf16[7,32,256]{2,1,0:T(8,128)(2,1)S(1)} collective-permute-done((bf16[7,32,256]{2,1,0:T(8,128)(2,1)S(1)}, bf16[7,32,256]{2,1,0:T(8,128)(2,1)S(1)}, u32[]{:S(2)}, u32[]{:S(2)}) %collective-permute-start.3) | collective-permute-done | bytes 114720 | tf_op jit(solution)/shard_map/ppermute | solution.py:766
  134.6 0.7 collective-permute-start.4
  135.3 5.8 %collective-permute-done.4.refs_2_ = bf16[7,32,256]{2,1,0:T(8,128)(2,1)S(1)} collective-permute-done((bf16[7,32,256]{2,1,0:T(8,128)(2,1)}, bf16[7,32,256]{2,1,0:T(8,128)(2,1)S(1)}, u32[]{:S(2)}, u32[]{:S(2)}) %collective-permute-start.4) | collective-permute-done | bytes 114720 | tf_op jit(solution)/shard_map/ppermute | solution.py:766
  141.1 0.0 collective-permute-done.13.refs_24_
  141.1 0.6 copy-done.10
  141.7 0.4 copy-done.2
  142.1 10.8 %tail.1 = (bf16[15,32,256]{2,1,0:T(8,128)(2,1)}, bf16[15,32,256]{2,1,0:T(8,128)(2,1)}, bf16[15,32,256]{2,1,0:T(8,128)(2,1)}, bf16[15,32,256]{2,1,0:T(8,128)(2,1)}) custom-call(s32[3]{0:T(128)} %pad_add_fusion.place_s, bf16[7,32,256]{2,1,0:T(8,128)(2,1)} %get-tuple-element.62.refs_0_, bf16[7,32,256]{2,1,0:T(8,128)(2,1)} %copy-done.9, ...), custom_call_target="tpu_custom_call" | custom-call | tf_op jit(solution)/shard_map/tail/pallas_call | solution.py:631
  152.9 0.1 collective-permute-start.14
  153.0 3.1 %collective-permute-start.15 = (bf16[15,32,256]{2,1,0:T(8,128)(2,1)}, bf16[15,32,256]{2,1,0:T(8,128)(2,1)S(1)}, u32[]{:S(2)}, u32[]{:S(2)}) collective-permute-start(bf16[15,32,256]{2,1,0:T(8,128)(2,1)} %get-tuple-element.71), channel_id=1, source_target_pairs={{0,2},{1,3},{2,0},{3,1},{4,6},{5,7},{6,4},{7,5},{8,10},{9,11},{10,... | collective-permute-start | bytes 737288 | tf_op jit(solution)/shard_map/ppermute | solution.py:766
  156.1 0.2 collective-permute-start.16
  156.3 5.3 %collective-permute-done.14.refs_1_ = bf16[15,32,256]{2,1,0:T(8,128)(2,1)S(1)} collective-permute-done((bf16[15,32,256]{2,1,0:T(8,128)(2,1)}, bf16[15,32,256]{2,1,0:T(8,128)(2,1)S(1)}, u32[]{:S(2)}, u32[]{:S(2)}) %collective-permute-start.14) | collective-permute-done | bytes 245792 | tf_op jit(solution)/shard_map/ppermute | solution.py:766
  161.6 2.6 %collective-permute-done.15.refs_2_ = bf16[15,32,256]{2,1,0:T(8,128)(2,1)S(1)} collective-permute-done((bf16[15,32,256]{2,1,0:T(8,128)(2,1)}, bf16[15,32,256]{2,1,0:T(8,128)(2,1)S(1)}, u32[]{:S(2)}, u32[]{:S(2)}) %collective-permute-start.15) | collective-permute-done | bytes 245792 | tf_op jit(solution)/shard_map/ppermute | solution.py:766
  164.2 0.7 collective-permute-done.16.refs_3_
  164.9 0.0 copy-done.6
  164.9 0.7 copy-done.7
  165.6 4.6 %collect.1 = (bf16[29,128,256]{2,1,0:T(8,128)(2,1)}, bf16[64,32,256]{2,1,0:T(8,128)(2,1)}) custom-call(s32[128]{0:T(128)} %bitcast.47, s32[128]{0:T(128)} %bitcast.57, s32[128]{0:T(128)} %bitcast.59, s32[3]{0:T(128)} %pad_add_fusion.place_s, bf16[15,32,256]{2,1,0:T(8,128)(2,1)} %get-tuple-element.69.refs_0_, bf16[15,32,256]{2,1,0:T(8,128)(2,1)} %copy-done.5, ...), custom_call_target="tpu_custom_call" | custom-call | tf_op jit(solution)/shard_map/collect/pallas_call | solution.py:688
  170.2 7.3 %all-to-all-start.1 = ((bf16[64,32,256]{2,1,0:T(8,128)(2,1)}), bf16[64,32,256]{2,1,0:T(8,128)(2,1)S(1)}, u32[]{:S(2)}, u32[]{:S(2)}) async-start(bf16[64,32,256]{2,1,0:T(8,128)(2,1)} %get-tuple-element.76), calls=%async_computation.1 | async-start | bytes 2097152 | tf_op jit(solution)/shard_map/all_to_all | solution.py:873
  177.5 13.5 %place.1 = (bf16[70,128,256]{2,1,0:T(8,128)(2,1)}, bf16[70,128,256]{2,1,0:T(8,128)(2,1)}) custom-call(s32[128]{0:T(128)} %bitcast.50, s32[128]{0:T(128)} %bitcast.52, s32[128]{0:T(128)} %bitcast.54, bf16[64,2,72,256]{3,2,1,0:T(8,128)(2,1)} %all-to-all-done.2.got_ref, s32[128,128]{1,0:T(8,128)} %get-tuple-element.77.valid_ref, ...), custom_call_target="tpu_custom_call" | custom-call | tf_op jit(solution)/shard_map/place/pallas_call | solution.py:411
  191.1 3.7 %all-to-all-done.1.got_ref = bf16[64,32,256]{2,1,0:T(8,128)(2,1)S(1)} async-done(((bf16[64,32,256]{2,1,0:T(8,128)(2,1)}), bf16[64,32,256]{2,1,0:T(8,128)(2,1)S(1)}, u32[]{:S(2)}, u32[]{:S(2)}) %all-to-all-start.1) | async-done | bytes 1048608 | tf_op jit(solution)/shard_map/all_to_all | solution.py:873
  194.7 1.0 copy-done.3
  195.7 4.5 %finish.1 = (bf16[7,128,256]{2,1,0:T(8,128)(2,1)}, bf16[128,8,256]{2,1,0:T(8,128)(2,1)}, bf16[70,128,256]{2,1,0:T(8,128)(2,1)}, bf16[70,128,256]{2,1,0:T(8,128)(2,1)}) custom-call(s32[128]{0:T(128)} %bitcast.51, s32[128]{0:T(128)} %bitcast.53, s32[128]{0:T(128)} %bitcast.55, ...), custom_call_target="tpu_custom_call", output_to_operand_aliasing={{2}: (5, {}), {3}: (6, {})} | custom-call | tf_op jit(solution)/shard_map/finish/pallas_call | solution.py:745
  (30 shorter events, 0.1 us)
Async XLA Ops:
  5.4 18.0 %all-to-all-start = ((s32[32,2,128]{2,1,0:T(2,128)}), s32[32,2,128]{2,1,0:T(2,128)S(1)}, u32[]{:S(2)}, u32[]{:S(2)}) async-start(s32[32,2,128]{2,1,0:T(2,128)} %bitcast.43), calls=%async_computation | async-start | bytes 65536 | tf_op jit(solution)/shard_map/all_to_all | solution.py:815
  23.3 7.8 %copy-start.11 = (bf16[2048,256]{1,0:T(8,128)(2,1)S(1)}, bf16[2048,256]{1,0:T(8,128)(2,1)}, u32[]{:S(2)}) copy-start(bf16[2048,256]{1,0:T(8,128)(2,1)} %get-tuple-element.68) | copy-start | bytes 3145732
  23.3 0.6 copy-start.4
  23.9 146.3 %all-to-all-start.2 = ((bf16[64,2,72,256]{3,2,1,0:T(8,128)(2,1)}), bf16[64,2,72,256]{3,2,1,0:T(8,128)(2,1)}, u32[]{:S(2)}, u32[]{:S(2)}) async-start(bf16[64,2,72,256]{3,2,1,0:T(8,128)(2,1)} %pack.1), calls=%async_computation.2 | async-start | bytes 9437184 | tf_op jit(solution)/shard_map/all_to_all | solution.py:819
  31.1 37.4 %collective-permute-start.10 = (bf16[2048,256]{1,0:T(8,128)(2,1)S(1)}, bf16[2048,256]{1,0:T(8,128)(2,1)S(1)}, u32[]{:S(2)}, u32[]{:S(2)}) collective-permute-start(bf16[2048,256]{1,0:T(8,128)(2,1)S(1)} %copy-done.11), channel_id=1, source_target_pairs={{0,3},{1,0},{2,1},{3,2},{4,7},{5,4},{6,5},{7,6},{8,11},{9,8},{10,9... | collective-permute-start | bytes 3145736 | tf_op jit(solution)/shard_map/ppermute | solution.py:766
  35.2 37.1 %collective-permute-start.6 = (bf16[2048,256]{1,0:T(8,128)(2,1)S(1)}, bf16[2048,256]{1,0:T(8,128)(2,1)S(1)}, u32[]{:S(2)}, u32[]{:S(2)}) collective-permute-start(bf16[2048,256]{1,0:T(8,128)(2,1)S(1)} %copy-done.11), channel_id=1, source_target_pairs={{0,1},{1,2},{2,3},{3,0},{4,5},{5,6},{6,7},{7,4},{8,9},{9,10},{10,1... | collective-permute-start | bytes 3145736 | tf_op jit(solution)/shard_map/ppermute | solution.py:766
  35.2 48.4 %collective-permute-start = (bf16[960,256]{1,0:T(8,128)(2,1)}, bf16[960,256]{1,0:T(8,128)(2,1)}, u32[]{:S(2)}, u32[]{:S(2)}) collective-permute-start(bf16[960,256]{1,0:T(8,128)(2,1)} %get-tuple-element.53), channel_id=1, source_target_pairs={{0,1},{1,2},{2,3},{3,0},{4,5},{5,6},{6,7},{7,4},{8,9},{9,10},{10,1... | collective-permute-start | bytes 1474568 | tf_op jit(solution)/shard_map/ppermute | solution.py:766
  35.2 48.4 %collective-permute-start.1 = (bf16[960,256]{1,0:T(8,128)(2,1)}, bf16[960,256]{1,0:T(8,128)(2,1)}, u32[]{:S(2)}, u32[]{:S(2)}) collective-permute-start(bf16[960,256]{1,0:T(8,128)(2,1)} %get-tuple-element.54), channel_id=1, source_target_pairs={{0,2},{1,3},{2,0},{3,1},{4,6},{5,7},{6,4},{7,5},{8,10},{9,11},{10,... | collective-permute-start | bytes 1474568 | tf_op jit(solution)/shard_map/ppermute | solution.py:766
  68.5 46.2 %copy-start = (bf16[2048,256]{1,0:T(8,128)(2,1)}, bf16[2048,256]{1,0:T(8,128)(2,1)S(1)}, u32[]{:S(2)}) copy-start(bf16[2048,256]{1,0:T(8,128)(2,1)S(1)} %collective-permute-done.10.refs_19_.refs_25_) | copy-start | bytes 3145732
  68.6 15.1 %collective-permute-start.12 = (bf16[1024,256]{1,0:T(8,128)(2,1)S(1)}, bf16[1024,256]{1,0:T(8,128)(2,1)}, u32[]{:S(2)}, u32[]{:S(2)}) collective-permute-start(bf16[1024,256]{1,0:T(8,128)(2,1)S(1)} %slice.9), channel_id=1, source_target_pairs={{0,3},{1,0},{2,1},{3,2},{4,7},{5,4},{6,5},{7,6},{8,11},{9,8},{10,9... | collective-permute-start | bytes 1572872 | tf_op jit(solution)/shard_map/ppermute | solution.py:766
  72.3 42.4 %copy-start.1 = (bf16[2048,256]{1,0:T(8,128)(2,1)}, bf16[2048,256]{1,0:T(8,128)(2,1)S(1)}, u32[]{:S(2)}) copy-start(bf16[2048,256]{1,0:T(8,128)(2,1)S(1)} %collective-permute-done.6.refs_15_.refs_21_) | copy-start | bytes 3145732
  72.4 21.4 %collective-permute-start.8 = (bf16[1024,256]{1,0:T(8,128)(2,1)S(1)}, bf16[1024,256]{1,0:T(8,128)(2,1)}, u32[]{:S(2)}, u32[]{:S(2)}) collective-permute-start(bf16[1024,256]{1,0:T(8,128)(2,1)S(1)} %slice.8), channel_id=1, source_target_pairs={{0,1},{1,2},{2,3},{3,0},{4,5},{5,6},{6,7},{7,4},{8,9},{9,10},{10,1... | collective-permute-start | bytes 1572872 | tf_op jit(solution)/shard_map/ppermute | solution.py:766
  72.5 68.6 %collective-permute-start.11 = (bf16[2048,256]{1,0:T(8,128)(2,1)S(1)}, bf16[2048,256]{1,0:T(8,128)(2,1)S(1)}, u32[]{:S(2)}, u32[]{:S(2)}) collective-permute-start(bf16[2048,256]{1,0:T(8,128)(2,1)S(1)} %collective-permute-done.10.refs_19_.refs_25_), channel_id=1, source_target_pairs={{0,4},{4,0},{8,12},{12,8},{16,20},{20,16},{24,28},{28,24},{32,36},... | collective-permute-start | bytes 3145736 | tf_op jit(solution)/shard_map/ppermute | solution.py:823
  83.6 57.5 %collective-permute-start.7 = (bf16[2048,256]{1,0:T(8,128)(2,1)S(1)}, bf16[2048,256]{1,0:T(8,128)(2,1)}, u32[]{:S(2)}, u32[]{:S(2)}) collective-permute-start(bf16[2048,256]{1,0:T(8,128)(2,1)S(1)} %collective-permute-done.6.refs_15_.refs_21_), channel_id=1, source_target_pairs={{0,4},{4,0},{8,12},{12,8},{16,20},{20,16},{24,28},{28,24},{32,36},... | collective-permute-start | bytes 3145736 | tf_op jit(solution)/shard_map/ppermute | solution.py:823
  83.6 14.0 %collective-permute-start.2 = (bf16[960,256]{1,0:T(8,128)(2,1)}, bf16[960,256]{1,0:T(8,128)(2,1)}, u32[]{:S(2)}, u32[]{:S(2)}) collective-permute-start(bf16[960,256]{1,0:T(8,128)(2,1)} %get-tuple-element.55), channel_id=1, source_target_pairs={{0,3},{1,0},{2,1},{3,2},{4,7},{5,4},{6,5},{7,6},{8,11},{9,8},{10,9... | collective-permute-start | bytes 1474568 | tf_op jit(solution)/shard_map/ppermute | solution.py:766
  83.6 57.4 %collective-permute-start.13 = (bf16[1024,256]{1,0:T(8,128)(2,1)}, bf16[1024,256]{1,0:T(8,128)(2,1)}, u32[]{:S(2)}, u32[]{:S(2)}) collective-permute-start(bf16[1024,256]{1,0:T(8,128)(2,1)} %collective-permute-done.12.refs_23_), channel_id=1, source_target_pairs={{0,4},{4,0},{8,12},{12,8},{16,20},{20,16},{24,28},{28,24},{32,36},... | collective-permute-start | bytes 1572872 | tf_op jit(solution)/shard_map/ppermute | solution.py:823
  93.8 47.3 %collective-permute-start.9 = (bf16[1024,256]{1,0:T(8,128)(2,1)}, bf16[1024,256]{1,0:T(8,128)(2,1)}, u32[]{:S(2)}, u32[]{:S(2)}) collective-permute-start(bf16[1024,256]{1,0:T(8,128)(2,1)} %collective-permute-done.8.refs_17_), channel_id=1, source_target_pairs={{0,4},{4,0},{8,12},{12,8},{16,20},{20,16},{24,28},{28,24},{32,36},... | collective-permute-start | bytes 1572872 | tf_op jit(solution)/shard_map/ppermute | solution.py:823
  114.8 13.8 %copy-start.12 = (bf16[7,32,256]{2,1,0:T(8,128)(2,1)S(1)}, bf16[7,32,256]{2,1,0:T(8,128)(2,1)}, u32[]{:S(2)}) copy-start(bf16[7,32,256]{2,1,0:T(8,128)(2,1)} %get-tuple-element.63) | copy-start | bytes 344068
  123.5 5.1 %collective-permute-start.5 = (bf16[7,32,256]{2,1,0:T(8,128)(2,1)}, bf16[7,32,256]{2,1,0:T(8,128)(2,1)S(1)}, u32[]{:S(2)}, u32[]{:S(2)}) collective-permute-start(bf16[7,32,256]{2,1,0:T(8,128)(2,1)} %get-tuple-element.65), channel_id=1, source_target_pairs={{0,3},{1,0},{2,1},{3,2},{4,7},{5,4},{6,5},{7,6},{8,11},{9,8},{10,9... | collective-permute-start | bytes 344072 | tf_op jit(solution)/shard_map/ppermute | solution.py:766
  128.6 12.6 %copy-start.8 = (bf16[7,32,256]{2,1,0:T(8,128)(2,1)}, bf16[7,32,256]{2,1,0:T(8,128)(2,1)S(1)}, u32[]{:S(2)}) copy-start(bf16[7,32,256]{2,1,0:T(8,128)(2,1)S(1)} %collective-permute-done.5.refs_3_) | copy-start | bytes 344068
  128.6 6.0 %collective-permute-start.3 = (bf16[7,32,256]{2,1,0:T(8,128)(2,1)S(1)}, bf16[7,32,256]{2,1,0:T(8,128)(2,1)S(1)}, u32[]{:S(2)}, u32[]{:S(2)}) collective-permute-start(bf16[7,32,256]{2,1,0:T(8,128)(2,1)S(1)} %copy-done.12), channel_id=1, source_target_pairs={{0,1},{1,2},{2,3},{3,0},{4,5},{5,6},{6,7},{7,4},{8,9},{9,10},{10,1... | collective-permute-start | bytes 344072 | tf_op jit(solution)/shard_map/ppermute | solution.py:766
  134.6 6.6 %copy-start.9 = (bf16[7,32,256]{2,1,0:T(8,128)(2,1)}, bf16[7,32,256]{2,1,0:T(8,128)(2,1)S(1)}, u32[]{:S(2)}) copy-start(bf16[7,32,256]{2,1,0:T(8,128)(2,1)S(1)} %collective-permute-done.3.refs_1_) | copy-start | bytes 344068
  134.6 6.5 %collective-permute-start.4 = (bf16[7,32,256]{2,1,0:T(8,128)(2,1)}, bf16[7,32,256]{2,1,0:T(8,128)(2,1)S(1)}, u32[]{:S(2)}, u32[]{:S(2)}) collective-permute-start(bf16[7,32,256]{2,1,0:T(8,128)(2,1)} %get-tuple-element.64), channel_id=1, source_target_pairs={{0,2},{1,3},{2,0},{3,1},{4,6},{5,7},{6,4},{7,5},{8,10},{9,11},{10,... | collective-permute-start | bytes 344072 | tf_op jit(solution)/shard_map/ppermute | solution.py:766
  141.1 0.6 copy-start.10
  141.1 1.0 copy-start.2
  152.9 8.7 %collective-permute-start.14 = (bf16[15,32,256]{2,1,0:T(8,128)(2,1)}, bf16[15,32,256]{2,1,0:T(8,128)(2,1)S(1)}, u32[]{:S(2)}, u32[]{:S(2)}) collective-permute-start(bf16[15,32,256]{2,1,0:T(8,128)(2,1)} %get-tuple-element.70), channel_id=1, source_target_pairs={{0,1},{1,2},{2,3},{3,0},{4,5},{5,6},{6,7},{7,4},{8,9},{9,10},{10,1... | collective-permute-start | bytes 737288 | tf_op jit(solution)/shard_map/ppermute | solution.py:766
  153.0 11.2 %collective-permute-start.15 = (bf16[15,32,256]{2,1,0:T(8,128)(2,1)}, bf16[15,32,256]{2,1,0:T(8,128)(2,1)S(1)}, u32[]{:S(2)}, u32[]{:S(2)}) collective-permute-start(bf16[15,32,256]{2,1,0:T(8,128)(2,1)} %get-tuple-element.71), channel_id=1, source_target_pairs={{0,2},{1,3},{2,0},{3,1},{4,6},{5,7},{6,4},{7,5},{8,10},{9,11},{10,... | collective-permute-start | bytes 737288 | tf_op jit(solution)/shard_map/ppermute | solution.py:766
  156.1 8.8 %collective-permute-start.16 = (bf16[15,32,256]{2,1,0:T(8,128)(2,1)}, bf16[15,32,256]{2,1,0:T(8,128)(2,1)S(1)}, u32[]{:S(2)}, u32[]{:S(2)}) collective-permute-start(bf16[15,32,256]{2,1,0:T(8,128)(2,1)} %get-tuple-element.72), channel_id=1, source_target_pairs={{0,3},{1,0},{2,1},{3,2},{4,7},{5,4},{6,5},{7,6},{8,11},{9,8},{10,9... | collective-permute-start | bytes 737288 | tf_op jit(solution)/shard_map/ppermute | solution.py:766
  161.6 3.3 %copy-start.5 = (bf16[15,32,256]{2,1,0:T(8,128)(2,1)}, bf16[15,32,256]{2,1,0:T(8,128)(2,1)S(1)}, u32[]{:S(2)}) copy-start(bf16[15,32,256]{2,1,0:T(8,128)(2,1)S(1)} %collective-permute-done.14.refs_1_) | copy-start | bytes 737284
  164.2 0.7 copy-start.6
  164.9 0.7 copy-start.7
  170.2 24.5 %all-to-all-start.1 = ((bf16[64,32,256]{2,1,0:T(8,128)(2,1)}), bf16[64,32,256]{2,1,0:T(8,128)(2,1)S(1)}, u32[]{:S(2)}, u32[]{:S(2)}) async-start(bf16[64,32,256]{2,1,0:T(8,128)(2,1)} %get-tuple-element.76), calls=%async_computation.1 | async-start | bytes 2097152 | tf_op jit(solution)/shard_map/all_to_all | solution.py:873
  194.7 1.0 copy-start.3
